TPU v7x, 128 devices: a whole 4x4x4 slice. The times are simulated.
128 devices in a mesh: ctx: 8 (over z_lo, x), ch: 16 (over y, z_hi, core).
Axes of the slice: x: 4, y: 4, z: 4 (z_hi: 2, z_lo: 2; z = z_hi * 2 + z_lo), core: 2. Of those that a mesh axis runs over, the one named last changes fastest.
Arguments:
- features: bfloat16 [8192, 3, 8192], P('ctx', None, 'ch'), may hold values from -6 to 6
- short_filter: float32 [3, 3, 8192], P(None, None, 'ch'), may hold values from -3 to 3
- decay_rate: float32 [16, 8192], P(None, 'ch'), may hold values from 6.1035156e-06 to 0.0333333333
- residues: float32 [16, 8192], P(None, 'ch'), may hold values from -0.2581989 to 0.2581989
- out_weight: bfloat16 [8192, 8192], P('ch'), may hold values from -0.09375 to 0.09375
Outputs:
- mixed_out: bfloat16 [8192, 8192], P('ctx', 'ch')
All inputs are finite; a program needn't handle non-finite values.
Results may differ from a plain program's by a relative error of at most 0.02.
Values may be sent and summed in bfloat16 or wider, within the bound.
No kernel may reach another device: no remote copies, remote signals or barrier semaphores. Data moves between devices by JAX's collectives and lax.ppermute only.
A program may use at most 128 MiB of HBM per device.

v0:
```python
import jax
import jax.numpy as jnp
from jax import lax
from jax.sharding import PartitionSpec as P

SUB = 64


PREC = lax.Precision.HIGH


def passed_along(x, axis, by):
    length = lax.axis_size(axis)
    pairs = [(i, i + by) for i in range(length) if 0 <= i + by < length]
    return lax.ppermute(x, axis, pairs)


def carried(own_state, decay_rate, tok_rows):
    axis_count = lax.axis_size("ctx")

    def advance(step_no, carry_pair):
        message, running = carry_pair
        message = passed_along(message.astype(jnp.bfloat16), "ctx", 1).astype(message.dtype)
        factor = (step_no - 1).astype(jnp.float32) * tok_rows
        return (message, running + jnp.exp(-decay_rate * factor) * message)

    return lax.fori_loop(1, axis_count, advance, (own_state, jnp.zeros_like(own_state)))[1]


def long_conv(product, decay_rate, residues):
    tok_rows, chan_width = product.shape
    blocks = tok_rows // SUB
    sub_values = product.T.reshape(chan_width, blocks, SUB).astype(jnp.float32)
    rate_t = decay_rate.T
    res_t = residues.T
    lag_index = jnp.arange(SUB, dtype=jnp.float32)
    powers = jnp.exp(-rate_t[:, :, None] * lag_index[None, None, :])
    filter_taps = jnp.sum(res_t[:, :, None] * powers, axis=1)
    padded = jnp.concatenate([filter_taps, jnp.zeros_like(filter_taps)], axis=1)
    skewed = jnp.tile(padded, (1, SUB))[:, : SUB * (2 * SUB - 1)].reshape(
        chan_width, SUB, 2 * SUB - 1
    )
    toeplitz = skewed[:, :, :SUB]
    intra_part = jnp.einsum("cst,cms->cmt", toeplitz, sub_values, precision=PREC)
    tail_pow = powers[:, :, ::-1]
    summary = jnp.einsum("crs,cms->crm", tail_pow, sub_values, precision=PREC)
    block_ids = jnp.arange(blocks, dtype=jnp.int32)
    gap_count = block_ids[:, None] - block_ids[None, :] - 1
    gap_float = jnp.maximum(gap_count, 0).astype(jnp.float32)
    weights = jnp.exp(-rate_t[:, :, None, None] * SUB * gap_float[None, None])
    weights = jnp.where((gap_count >= 0)[None, None], weights, 0.0)
    local_prefix = jnp.einsum("crnm,crm->crn", weights, summary, precision=PREC)
    block_float = block_ids.astype(jnp.float32)
    end_w = jnp.exp(-rate_t[:, :, None] * SUB * (blocks - 1 - block_float)[None, None])
    own_state = jnp.sum(end_w * summary, axis=2).T
    entering = carried(own_state, decay_rate, tok_rows).T
    start_w = jnp.exp(-rate_t[:, :, None] * SUB * block_float[None, None])
    sub_state = start_w * entering[:, :, None] + local_prefix
    read_out = res_t[:, :, None] * jnp.exp(-rate_t[:, :, None] * (lag_index + 1.0)[None, None])
    cross_part = jnp.einsum("crt,crn->cnt", read_out, sub_state, precision=PREC)
    return (intra_part + cross_part).reshape(chan_width, tok_rows).T


def per_device(features, short_filter, decay_rate, residues, out_weight):
    tok_rows = features.shape[0]
    last_rows = features[tok_rows - 2 :]
    before = passed_along(last_rows, "ctx", 1)
    padded = jnp.concatenate([before, features], axis=0)
    featured = (
        short_filter[0][None] * padded[2:]
        + short_filter[1][None] * padded[1 : tok_rows + 1]
        + short_filter[2][None] * padded[:tok_rows]
    )
    product = (featured[:, 1] * featured[:, 2]).astype(jnp.bfloat16)
    conv_out = long_conv(product, decay_rate, residues)
    gated_out = (featured[:, 0] * conv_out).astype(jnp.bfloat16)
    partial_value = jnp.dot(gated_out, out_weight, preferred_element_type=jnp.float32)
    return lax.psum_scatter(
        partial_value.astype(jnp.bfloat16), "ch", scatter_dimension=1, tiled=True
    )


def solution(mesh):
    placed = (
        P("ctx", None, "ch"),
        P(None, None, "ch"),
        P(None, "ch"),
        P(None, "ch"),
        P("ch", None),
    )
    return jax.shard_map(
        per_device, mesh=mesh, in_specs=placed, out_specs=P("ctx", "ch"), check_vma=False
    )
```

profile of v0, /device:TPU:0, one launch (start us, length us, event | category | flops | bytes accessed | tf_op | source)
XLA Modules:
  0.0 350.9 jit_solution(15430403141568571677)
XLA Ops:
  6.5 0.0 reduce-scatter.2.cloned.1.call-start
  6.5 0.7 slice.35
  7.3 3.5 collective-permute-start.1
  10.8 0.5 broadcast_subtract_fusion
  11.3 0.5 iota_convert_fusion
  11.8 0.6 fusion.18
  12.4 0.8 broadcast_multiply_fusion
  13.1 0.8 fusion.19
  13.9 0.7 slice_bitcast_fusion.3
  14.6 0.1 copy.35
  14.8 0.9 copy.34
  15.7 0.0 copy-start.2
  15.7 6.9 %multiply_reduce_fusion.2 = (f32[512,64]{1,0:T(8,128)S(1)}, f32[512,16,64]{2,1,0:T(8,128)}) fusion(f32[512,16]{1,0:T(8,128)S(1)} %copy.34, f32[512,16]{1,0:T(8,128)S(1)} %copy.35), kind=kLoop, calls=%fused_computation.13 | loop fusion | flops 1540096 | bytes 2293760 | tf_op jit(solution)/shard_map/reduce_sum | solution.py:38
  22.6 0.6 iota_add_fusion
  23.1 0.8 copy.39
  24.0 0.1 copy.53
  24.1 7.2 %rev.3 = f32[512,16,64]{2,1,0:T(8,128)} reverse(f32[512,16,64]{2,1,0:T(8,128)} %get-tuple-element.183), dimensions={2} | reverse | bytes 4194304 | tf_op jit(solution)/shard_map/rev | solution.py:45
  31.3 0.0 copy-done.2
  31.3 2.1 tile.4
  33.5 6.1 %slice.49 = f32[512,8128]{0,1:T(8,128)} slice(f32[512,8192]{0,1:T(8,128)S(1)} %bitcast.38), slice={[0:512], [0:8128]} | slice | bytes 33292288 | tf_op jit(solution)/shard_map/slice | solution.py:40
  39.6 14.1 %reshape.61 = f32[512,64,127]{0,2,1:T(8,128)} reshape(f32[512,8128]{0,1:T(8,128)} %slice.49) | data formatting | bytes 33292288 | tf_op jit(solution)/shard_map/reshape | solution.py:40
  53.7 8.4 %slice.50 = f32[512,64,64]{0,2,1:T(8,128)} slice(f32[512,64,127]{0,2,1:T(8,128)} %reshape.61), slice={[0:512], [0:64], [0:64]} | slice | bytes 16777216 | tf_op jit(solution)/shard_map/slice | solution.py:43
  62.1 16.4 %copy.51 = f32[512,64,64]{2,1,0:T(8,128)} copy(f32[512,64,64]{0,2,1:T(8,128)} %slice.50) | data formatting | bytes 16777216
  78.5 0.0 collective-permute-done.1
  78.5 0.0 copy-done.1
  78.5 2.3 multiply_add_fusion
  80.8 2.7 copy-done
  83.5 0.3 fusion.9
  83.8 2.0 copy.38
  85.9 7.1 %multiply_reduce_fusion.1 = (bf16[512,16]{1,0:T(8,128)(2,1)S(1)}, f32[512,16,16]{1,2,0:T(8,128)}) fusion(f32[16]{0:T(128)S(1)} %copy-done.7, f32[512,16]{1,0:T(8,128)} %copy.39, f32[512,16,64]{2,1,0:T(8,128)} %rev.3, bf16[512,16,64]{2,1,0:T(8,128)(2,1)S(1)} %copy.38), kind=kOutput, calls=%fused_computation.10 | convolution fusion | flops 50716672 | bytes 3719232 | tf_op jit(solution)/shard_map/crs,cms->crm/dot_general | solution.py:46
  93.0 0.0 copy-start.6
  93.0 0.1 copy.41
  93.1 42.8 %while.20 = (s32[]{:T(128)}, bf16[16,512]{1,0:T(8,128)(2,1)S(1)}, f32[16,512]{1,0:T(8,128)S(1)}, f32[16,512]{1,0:T(8,128)S(1)}, s32[]{:T(128)}, /*index=5*/f32[]{:T(128)}, s32[]{:T(128)}) while((s32[]{:T(128)}, bf16[16,512]{1,0:T(8,128)(2,1)S(1)}, f32[16,512]{1,0:T(8,128)S(1)}, f32[16,512]{1,0:T(8,128)S(1)}, s32[]{:T(128)}, ...), condition=%wide.region_3.4_spmd.clone, body=%wide.region_2.3_spmd.clone.sunk | while | flops 49157 | bytes 196767 | solution.py:27
  93.1 3.4 collective-permute-start
  96.5 1.4 collective-permute-done
  97.9 4.2 %collective-permute-start = (bf16[16,512]{1,0:T(8,128)(2,1)S(1)}, bf16[16,512]{1,0:T(8,128)(2,1)S(1)}, u32[]{:S(2)}, u32[]{:S(2)}) collective-permute-start(bf16[16,512]{1,0:T(8,128)(2,1)S(1)} %get-tuple-element.230), channel_id=1, source_target_pairs={{0,16},{16,32},{32,48},{48,64},{64,80},{80,96},{96,112},{1,17},{17... | collective-permute-start | bytes 49160 | tf_op jit(solution)/shard_map/while/body/eval_jaxpr/ppermute | solution.py:15
  102.1 1.4 collective-permute-done
  103.6 4.2 %collective-permute-start = (bf16[16,512]{1,0:T(8,128)(2,1)S(1)}, bf16[16,512]{1,0:T(8,128)(2,1)S(1)}, u32[]{:S(2)}, u32[]{:S(2)}) collective-permute-start(bf16[16,512]{1,0:T(8,128)(2,1)S(1)} %get-tuple-element.230), channel_id=1, source_target_pairs={{0,16},{16,32},{32,48},{48,64},{64,80},{80,96},{96,112},{1,17},{17... | collective-permute-start | bytes 49160 | tf_op jit(solution)/shard_map/while/body/eval_jaxpr/ppermute | solution.py:15
  107.8 1.4 collective-permute-done
  109.3 4.2 %collective-permute-start = (bf16[16,512]{1,0:T(8,128)(2,1)S(1)}, bf16[16,512]{1,0:T(8,128)(2,1)S(1)}, u32[]{:S(2)}, u32[]{:S(2)}) collective-permute-start(bf16[16,512]{1,0:T(8,128)(2,1)S(1)} %get-tuple-element.230), channel_id=1, source_target_pairs={{0,16},{16,32},{32,48},{48,64},{64,80},{80,96},{96,112},{1,17},{17... | collective-permute-start | bytes 49160 | tf_op jit(solution)/shard_map/while/body/eval_jaxpr/ppermute | solution.py:15
  113.5 1.4 collective-permute-done
  114.9 4.2 %collective-permute-start = (bf16[16,512]{1,0:T(8,128)(2,1)S(1)}, bf16[16,512]{1,0:T(8,128)(2,1)S(1)}, u32[]{:S(2)}, u32[]{:S(2)}) collective-permute-start(bf16[16,512]{1,0:T(8,128)(2,1)S(1)} %get-tuple-element.230), channel_id=1, source_target_pairs={{0,16},{16,32},{32,48},{48,64},{64,80},{80,96},{96,112},{1,17},{17... | collective-permute-start | bytes 49160 | tf_op jit(solution)/shard_map/while/body/eval_jaxpr/ppermute | solution.py:15
  119.2 1.4 collective-permute-done
  120.6 6.1 %collective-permute-start = (bf16[16,512]{1,0:T(8,128)(2,1)S(1)}, bf16[16,512]{1,0:T(8,128)(2,1)S(1)}, u32[]{:S(2)}, u32[]{:S(2)}) collective-permute-start(bf16[16,512]{1,0:T(8,128)(2,1)S(1)} %get-tuple-element.230), channel_id=1, source_target_pairs={{0,16},{16,32},{32,48},{48,64},{64,80},{80,96},{96,112},{1,17},{17... | collective-permute-start | bytes 49160 | tf_op jit(solution)/shard_map/while/body/eval_jaxpr/ppermute | solution.py:15
  126.7 1.4 collective-permute-done
  128.1 6.3 %collective-permute-start = (bf16[16,512]{1,0:T(8,128)(2,1)S(1)}, bf16[16,512]{1,0:T(8,128)(2,1)S(1)}, u32[]{:S(2)}, u32[]{:S(2)}) collective-permute-start(bf16[16,512]{1,0:T(8,128)(2,1)S(1)} %get-tuple-element.230), channel_id=1, source_target_pairs={{0,16},{16,32},{32,48},{48,64},{64,80},{80,96},{96,112},{1,17},{17... | collective-permute-start | bytes 49160 | tf_op jit(solution)/shard_map/while/body/eval_jaxpr/ppermute | solution.py:15
  134.5 1.4 collective-permute-done
  135.9 0.8 copy.42
  136.7 3.1 copy.52
  139.9 0.0 copy-done.6
  139.9 0.0 copy-start.3
  139.9 0.0 copy-start.4
  139.9 0.0 copy-start.8
  139.9 0.0 copy-start.9
  139.9 3.6 %multiply_reduce_fusion = f32[512,16,16]{0,2,1:T(8,128)} fusion(f32[512,16,16]{0,2,1:T(8,128)S(1)} %copy.52, f32[16,16]{1,0:T(8,128)S(1)} %maximum_convert_fusion, f32[512,16]{0,1:T(8,128)S(1)} %broadcast_multiply_fusion, pred[16,16]{1,0:T(8,128)(4,1)S(1)} %copy-done.6), kind=kLoop, calls=%fused_computation.2 | loop fusion | flops 8257536 | bytes 1082624
  143.5 4.7 %copy.50 = f32[512,16,16]{1,2,0:T(8,128)} copy(f32[512,16,16]{0,2,1:T(8,128)} %multiply_reduce_fusion) | data formatting | bytes 1048576 | tf_op jit(solution)/shard_map/crnm,crm->crn/dot_general | solution.py:52
  148.2 0.0 copy-done.4
  148.2 7.4 %fusion = f32[512,16,64]{2,1,0:T(8,128)S(1)} fusion(f32[512,16,16]{1,2,0:T(8,128)} %copy.50, f32[64]{0:T(128)S(1)} %copy-done.9, f32[512,16]{1,0:T(8,128)S(1)} %copy-done.5, f32[16]{0:T(128)S(1)} %copy-done.8, f32[512,16]{1,0:T(8,128)S(1)} %copy-done.4, f32[512,16]{1,0:T(8,128)S(1)} %copy.35, f32[512,16]{1,0:T(8,128)S(1)} %copy-done.3), kind=kOutput, calls=%fused_computation.4 | convolution fusion | flops 51773440 | bytes 2752832 | tf_op jit(solution)/shard_map/crt,crn->cnt/dot_general | solution.py:60
  155.6 9.5 %convolution_add_fusion = f32[512,16,64]{2,1,0:T(8,128)} fusion(f32[512,16,64]{2,1,0:T(8,128)S(1)} %fusion, bf16[512,16,64]{2,1,0:T(8,128)(2,1)S(1)} %copy.38, f32[512,64,64]{2,1,0:T(8,128)} %copy.51), kind=kOutput, calls=%fused_computation.19 | convolution fusion | flops 201850880 | bytes 13631488 | tf_op jit(solution)/shard_map/cst,cms->cmt/dot_general | solution.py:44
  165.1 2.8 copy.43
  167.9 2.0 fusion.11
  169.9 15.1 %convolution_convert_fusion = bf16[1024,8192]{1,0:T(8,128)(2,1)} fusion(bf16[1024,512]{1,0:T(8,128)(2,1)S(1)} %fusion.11, bf16[512,8192]{1,0:T(8,128)(2,1)} %param.11), kind=kOutput, calls=%fused_computation.1 | convolution fusion | flops 8598323200 | bytes 26214400 | tf_op jit(solution)/shard_map/dot_general | solution.py:77
  185.0 0.0 reduce-scatter.2.cloned.1.call-update
  185.1 159.0 %reduce-scatter.2.cloned.1.call-done = bf16[1024,512]{1,0:T(8,128)(2,1)} async-done(((bf16[1024,8192]{1,0:T(8,128)(2,1)}), bf16[1024,512]{1,0:T(8,128)(2,1)}) %reduce-scatter.2.cloned.1.call-update) | async-done | bytes 1048592 | tf_op jit(solution)/shard_map/reduce_scatter | solution.py:78
  (19 shorter events, 0.2 us)
Async XLA Ops:
  6.5 337.5 %reduce-scatter.2.cloned.1.call-start = ((), (), s32[]{:S(2)}) async-start(), calls=%async_computation.1 | async-start | bytes 17825792 | tf_op jit(solution)/shard_map/reduce_scatter | solution.py:78
  7.3 71.2 %collective-permute-start.1 = (bf16[2,3,512]{2,0,1:T(2,128)(2,1)S(1)}, bf16[2,3,512]{2,0,1:T(2,128)(2,1)S(1)}, u32[]{:S(2)}, u32[]{:S(2)}) collective-permute-start(bf16[2,3,512]{2,0,1:T(2,128)(2,1)S(1)} %slice.35), channel_id=1, source_target_pairs={{0,16},{16,32},{32,48},{48,64},{64,80},{80,96},{96,112},{1,17},{17... | collective-permute-start | bytes 18440 | tf_op jit(solution)/shard_map/ppermute | solution.py:15
  15.7 15.7 %copy-start.2 = (f32[512,16]{1,0:T(8,128)}, f32[512,16]{1,0:T(8,128)S(1)}, u32[]{:S(2)}) copy-start(f32[512,16]{1,0:T(8,128)S(1)} %copy.34) | copy-start | bytes 98308
  62.1 16.4 %copy-start.1 = (bf16[1024,3,512]{2,0,1:T(8,128)(2,1)S(1)}, bf16[1024,3,512]{2,0,1:T(8,128)(2,1)}, u32[]{:S(2)}) copy-start(bf16[1024,3,512]{2,0,1:T(8,128)(2,1)} %param.7) | copy-start | bytes 9437188
  80.8 2.7 copy-start
  83.5 2.4 copy-start.7
  93.0 46.9 %copy-start.6 = (pred[16,16]{1,0:T(8,128)(4,1)S(1)}, pred[16,16]{1,0:T(8,128)(4,1)}, u32[]{:S(2)}) copy-start(pred[16,16]{1,0:T(8,128)(4,1)} %fusion.18) | copy-start | bytes 772
  93.1 4.8 %collective-permute-start = (bf16[16,512]{1,0:T(8,128)(2,1)S(1)}, bf16[16,512]{1,0:T(8,128)(2,1)S(1)}, u32[]{:S(2)}, u32[]{:S(2)}) collective-permute-start(bf16[16,512]{1,0:T(8,128)(2,1)S(1)} %get-tuple-element.230), channel_id=1, source_target_pairs={{0,16},{16,32},{32,48},{48,64},{64,80},{80,96},{96,112},{1,17},{17... | collective-permute-start | bytes 49160 | tf_op jit(solution)/shard_map/while/body/eval_jaxpr/ppermute | solution.py:15
  97.9 5.6 %collective-permute-start = (bf16[16,512]{1,0:T(8,128)(2,1)S(1)}, bf16[16,512]{1,0:T(8,128)(2,1)S(1)}, u32[]{:S(2)}, u32[]{:S(2)}) collective-permute-start(bf16[16,512]{1,0:T(8,128)(2,1)S(1)} %get-tuple-element.230), channel_id=1, source_target_pairs={{0,16},{16,32},{32,48},{48,64},{64,80},{80,96},{96,112},{1,17},{17... | collective-permute-start | bytes 49160 | tf_op jit(solution)/shard_map/while/body/eval_jaxpr/ppermute | solution.py:15
  103.6 5.6 %collective-permute-start = (bf16[16,512]{1,0:T(8,128)(2,1)S(1)}, bf16[16,512]{1,0:T(8,128)(2,1)S(1)}, u32[]{:S(2)}, u32[]{:S(2)}) collective-permute-start(bf16[16,512]{1,0:T(8,128)(2,1)S(1)} %get-tuple-element.230), channel_id=1, source_target_pairs={{0,16},{16,32},{32,48},{48,64},{64,80},{80,96},{96,112},{1,17},{17... | collective-permute-start | bytes 49160 | tf_op jit(solution)/shard_map/while/body/eval_jaxpr/ppermute | solution.py:15
  109.3 5.6 %collective-permute-start = (bf16[16,512]{1,0:T(8,128)(2,1)S(1)}, bf16[16,512]{1,0:T(8,128)(2,1)S(1)}, u32[]{:S(2)}, u32[]{:S(2)}) collective-permute-start(bf16[16,512]{1,0:T(8,128)(2,1)S(1)} %get-tuple-element.230), channel_id=1, source_target_pairs={{0,16},{16,32},{32,48},{48,64},{64,80},{80,96},{96,112},{1,17},{17... | collective-permute-start | bytes 49160 | tf_op jit(solution)/shard_map/while/body/eval_jaxpr/ppermute | solution.py:15
  114.9 5.6 %collective-permute-start = (bf16[16,512]{1,0:T(8,128)(2,1)S(1)}, bf16[16,512]{1,0:T(8,128)(2,1)S(1)}, u32[]{:S(2)}, u32[]{:S(2)}) collective-permute-start(bf16[16,512]{1,0:T(8,128)(2,1)S(1)} %get-tuple-element.230), channel_id=1, source_target_pairs={{0,16},{16,32},{32,48},{48,64},{64,80},{80,96},{96,112},{1,17},{17... | collective-permute-start | bytes 49160 | tf_op jit(solution)/shard_map/while/body/eval_jaxpr/ppermute | solution.py:15
  120.6 7.5 %collective-permute-start = (bf16[16,512]{1,0:T(8,128)(2,1)S(1)}, bf16[16,512]{1,0:T(8,128)(2,1)S(1)}, u32[]{:S(2)}, u32[]{:S(2)}) collective-permute-start(bf16[16,512]{1,0:T(8,128)(2,1)S(1)} %get-tuple-element.230), channel_id=1, source_target_pairs={{0,16},{16,32},{32,48},{48,64},{64,80},{80,96},{96,112},{1,17},{17... | collective-permute-start | bytes 49160 | tf_op jit(solution)/shard_map/while/body/eval_jaxpr/ppermute | solution.py:15
  128.1 7.7 %collective-permute-start = (bf16[16,512]{1,0:T(8,128)(2,1)S(1)}, bf16[16,512]{1,0:T(8,128)(2,1)S(1)}, u32[]{:S(2)}, u32[]{:S(2)}) collective-permute-start(bf16[16,512]{1,0:T(8,128)(2,1)S(1)} %get-tuple-element.230), channel_id=1, source_target_pairs={{0,16},{16,32},{32,48},{48,64},{64,80},{80,96},{96,112},{1,17},{17... | collective-permute-start | bytes 49160 | tf_op jit(solution)/shard_map/while/body/eval_jaxpr/ppermute | solution.py:15
  139.9 8.3 %copy-start.3 = (f32[512,16]{1,0:T(8,128)S(1)}, f32[512,16]{1,0:T(8,128)}, u32[]{:S(2)}) copy-start(f32[512,16]{1,0:T(8,128)} %copy-done.2) | copy-start | bytes 98308
  139.9 8.3 %copy-start.4 = (f32[512,16]{1,0:T(8,128)S(1)}, f32[512,16]{1,0:T(8,128)}, u32[]{:S(2)}) copy-start(f32[512,16]{1,0:T(8,128)} %copy.39) | copy-start | bytes 98308
  139.9 8.3 %copy-start.8 = (f32[16]{0:T(128)S(1)}, f32[16]{0:T(128)}, u32[]{:S(2)}) copy-start(f32[16]{0:T(128)} %iota_convert_fusion) | copy-start | bytes 196
  139.9 8.3 %copy-start.9 = (f32[64]{0:T(128)S(1)}, f32[64]{0:T(128)}, u32[]{:S(2)}) copy-start(f32[64]{0:T(128)} %iota_add_fusion) | copy-start | bytes 772
  143.5 4.7 %copy-start.5 = (f32[512,16]{1,0:T(8,128)S(1)}, f32[512,16]{1,0:T(8,128)}, u32[]{:S(2)}) copy-start(f32[512,16]{1,0:T(8,128)} %copy.42) | copy-start | bytes 98308
Sparse Core Ops, SparseCore 0:
  185.2 158.8 reduce-scatter.1
where the time goes:
time: 352 us; the launch traced here: 351 us
  waiting for transfers between devices  169 us (48%)
  local copies, waits for them, and re-layouts  74.1 us (21%)
  matrix products  39 us (11%)
  starting transfers between devices  36 us (10%)
  other arithmetic  19 us (5%)
  between operations  13.6 us (4%)
    reduce_scatter x1, waiting for transfers between devices, per_device(): lax.psum_scatter(partial_value.astype(jnp.bfloat16), 'ch', scatter_dimens...  159 us
    ppermute x8, starting transfers between devices, passed_along(): return lax.ppermute(x, axis, pairs)  36 us
    unnamed x24, local copies, waits for them, and re-layouts  22.4 us
    dot_general x1, matrix products, per_device(): jnp.dot(gated_out, out_weight, preferred_element_type=jnp.float32)  15.1 us
    reshape x1, local copies, waits for them, and re-layouts, long_conv(): jnp.tile(padded, (1, SUB))[:, :SUB * (2 * SUB - 1)]  14.1 us
    ppermute x8, waiting for transfers between devices, passed_along(): return lax.ppermute(x, axis, pairs)  9.94 us
    dot_general x1, matrix products, long_conv(): jnp.einsum('cst,cms->cmt', toeplitz, sub_values, precision=PREC)  9.46 us
    slice x1, local copies, waits for them, and re-layouts, long_conv(): toeplitz = skewed[:, :, :SUB]  8.42 us
  transfers between devices with their start and end apart: 9, of which 8 were waited for; matrix products, arithmetic and copies ran while one was open for 19% of the time, Pallas kernels for 0%

commit v1 on v0

v1 whole, which is shorter than its diff:
```python
import jax
import jax.numpy as jnp
from jax import lax
from jax.experimental import pallas as pl
from jax.experimental.pallas import tpu as pltpu
from jax.sharding import PartitionSpec as P

f32, bf16 = jnp.float32, jnp.bfloat16
LANES = 128
SUBS = 8


def row_scan(values, factor, rows):
    step = 1
    while step < SUBS:
        back = jnp.where(rows >= step, pltpu.roll(values, step, axis=0), 0.0)
        values = values + factor * back
        factor = factor * factor
        step *= 2
    return values


def state_kernel(key_ref, val_ref, halo_ref, sf_ref, rate_ref, p_ref, own_ref, start_ref, xs):
    n_modes = rate_ref.shape[0]
    steps = p_ref.shape[0]
    rows = lax.broadcasted_iota(jnp.int32, (SUBS, LANES), 0)
    for j in range(2):
        xs[j, pl.ds(8, SUBS * steps), :] = (key_ref, val_ref)[j][0].astype(f32)
        xs[j, pl.ds(6, 2), :] = halo_ref[j + 1].astype(f32)
    w = [[jnp.broadcast_to(sf_ref[k, j + 1][None], (SUBS, LANES)) for k in range(3)] for j in range(2)]
    decay = [jnp.exp(-jnp.broadcast_to(rate_ref[pl.ds(r, 1), :], (SUBS, LANES))) for r in range(n_modes)]

    def tap(j, at):
        return xs[j, pl.ds(8 + at, SUBS, stride=steps), :]

    def body(t, carry):
        k1, k2, v1, v2, state = carry
        k0, v0 = tap(0, t), tap(1, t)
        key = w[0][0] * k0 + w[0][1] * k1 + w[0][2] * k2
        val = w[1][0] * v0 + w[1][1] * v1 + w[1][2] * v2
        p = (key * val).astype(bf16).astype(f32)
        p_ref[t] = p
        state = tuple(a * s + p for a, s in zip(decay, state))
        return (k0, k1, v0, v1, state)

    zero = jnp.zeros((SUBS, LANES), f32)
    init = (tap(0, -1), tap(0, -2), tap(1, -1), tap(1, -2), (zero,) * n_modes)
    state = lax.fori_loop(0, steps, body, init, unroll=4)[4]
    for r in range(n_modes):
        rate = jnp.broadcast_to(rate_ref[pl.ds(r, 1), :], (SUBS, LANES))
        scanned = row_scan(state[r], jnp.exp(-rate * steps), rows)
        own_ref[pl.ds(r, 1), :] = scanned[SUBS - 1 :]
        start_ref[r] = jnp.where(rows >= 1, pltpu.roll(scanned, 1, axis=0), 0.0)


def gate_kernel(x_ref, halo_ref, sf_ref, rate_ref, res_ref, p_ref, start_ref, enter_ref, out_ref, xs, ys):
    n_modes = rate_ref.shape[0]
    steps = p_ref.shape[0]
    rows = lax.broadcasted_iota(jnp.int32, (SUBS, LANES), 0).astype(f32)
    xs[pl.ds(8, SUBS * steps), :] = x_ref[0].astype(f32)
    xs[pl.ds(6, 2), :] = halo_ref[0].astype(f32)
    w = [jnp.broadcast_to(sf_ref[k, 0][None], (SUBS, LANES)) for k in range(3)]
    decay, gain, state0 = [], [], []
    for r in range(n_modes):
        rate = jnp.broadcast_to(rate_ref[pl.ds(r, 1), :], (SUBS, LANES))
        enter = jnp.broadcast_to(enter_ref[pl.ds(r, 1), :], (SUBS, LANES))
        decay.append(jnp.exp(-rate))
        gain.append(jnp.broadcast_to(res_ref[pl.ds(r, 1), :], (SUBS, LANES)))
        state0.append(start_ref[r] + jnp.exp(-rate * steps * rows) * enter)

    def tap(at):
        return xs[pl.ds(8 + at, SUBS, stride=steps), :]

    def body(t, carry):
        x1, x2, state = carry
        x0 = tap(t)
        gate = w[0] * x0 + w[1] * x1 + w[2] * x2
        p = p_ref[t]
        state = tuple(a * s + p for a, s in zip(decay, state))
        parts = [c * s for c, s in zip(gain, state)]
        while len(parts) > 1:
            parts = [a + b for a, b in zip(parts[::2], parts[1::2])]
        ys[pl.ds(t, SUBS, stride=steps), :] = gate * parts[0]
        return (x0, x1, state)

    lax.fori_loop(0, steps, body, (tap(-1), tap(-2), tuple(state0)), unroll=4)
    out_ref[...] = ys[...].astype(bf16)


def states(x, halo, sf, rate):
    _, n_tok, width = x.shape
    modes = rate.shape[0]
    steps = n_tok // SUBS
    col = lambda g: (0, g)
    return pl.pallas_call(
        state_kernel,
        grid=(width // LANES,),
        in_specs=[
            pl.BlockSpec((1, n_tok, LANES), lambda g: (1, 0, g)),
            pl.BlockSpec((1, n_tok, LANES), lambda g: (2, 0, g)),
            pl.BlockSpec((3, 2, LANES), lambda g: (0, 0, g)),
            pl.BlockSpec((3, 3, LANES), lambda g: (0, 0, g)),
            pl.BlockSpec((modes, LANES), col),
        ],
        out_specs=[
            pl.BlockSpec((steps, SUBS, LANES), lambda g: (0, 0, g)),
            pl.BlockSpec((modes, LANES), col),
            pl.BlockSpec((modes, SUBS, LANES), lambda g: (0, 0, g)),
        ],
        out_shape=[
            jax.ShapeDtypeStruct((steps, SUBS, width), f32),
            jax.ShapeDtypeStruct((modes, width), f32),
            jax.ShapeDtypeStruct((modes, SUBS, width), f32),
        ],
        scratch_shapes=[pltpu.VMEM((2, n_tok + 8, LANES), f32)],
        compiler_params=pltpu.CompilerParams(vmem_limit_bytes=32 << 20),
        name="states",
    )(x, x, halo, sf, rate)


def gated(x, halo, sf, rate, res, p, start, enter):
    _, n_tok, width = x.shape
    modes = rate.shape[0]
    steps = n_tok // SUBS
    col = lambda g: (0, g)
    three = lambda g: (0, 0, g)
    return pl.pallas_call(
        gate_kernel,
        grid=(width // LANES,),
        in_specs=[
            pl.BlockSpec((1, n_tok, LANES), three),
            pl.BlockSpec((1, 2, LANES), three),
            pl.BlockSpec((3, 3, LANES), three),
            pl.BlockSpec((modes, LANES), col),
            pl.BlockSpec((modes, LANES), col),
            pl.BlockSpec((steps, SUBS, LANES), three),
            pl.BlockSpec((modes, SUBS, LANES), three),
            pl.BlockSpec((modes, LANES), col),
        ],
        out_specs=pl.BlockSpec((n_tok, LANES), col),
        out_shape=jax.ShapeDtypeStruct((n_tok, width), bf16),
        scratch_shapes=[pltpu.VMEM((n_tok + 8, LANES), f32), pltpu.VMEM((n_tok, LANES), f32)],
        compiler_params=pltpu.CompilerParams(vmem_limit_bytes=32 << 20),
        name="gated",
    )(x, halo, sf, rate, res, p, start, enter)


def passed_along(x, axis, by):
    length = lax.axis_size(axis)
    pairs = [(i, i + by) for i in range(length) if 0 <= i + by < length]
    return lax.ppermute(x, axis, pairs)


def entering_state(own, rate, n_tok):
    block = jnp.exp(-rate * n_tok)
    one, two, three = (passed_along(own, "ctx", k) for k in (1, 2, 3))
    last = one + block * (two + block * three)
    four = own + block * last
    return last + block * block * block * passed_along(four, "ctx", 4)


def per_device(features, short_filter, decay_rate, residues, out_weight):
    n_tok = features.shape[0]
    halo = passed_along(features[n_tok - 2 :], "ctx", 1).transpose(1, 0, 2)
    x = features.transpose(1, 0, 2)
    product, own, start = states(x, halo, short_filter, decay_rate)
    enter = entering_state(own, decay_rate, float(n_tok))
    gated_out = gated(x, halo, short_filter, decay_rate, residues, product, start, enter)
    partial_value = jnp.dot(gated_out, out_weight, preferred_element_type=f32)
    return lax.psum_scatter(partial_value.astype(bf16), "ch", scatter_dimension=1, tiled=True)


def solution(mesh):
    placed = (P("ctx", None, "ch"), P(None, None, "ch"), P(None, "ch"), P(None, "ch"), P("ch", None))
    return jax.shard_map(per_device, mesh=mesh, in_specs=placed, out_specs=P("ctx", "ch"), check_vma=False)
```

time: 352 us -> 223 us (0.63)
  local copies, waits for them, and re-layouts: 74.1 us -> 4.88 us
  matrix products: 39 us -> 15.1 us
  other arithmetic: 19 us -> 0.04 us
  waiting for transfers between devices: 169 us -> 152 us
  Pallas kernels: 0 us -> 15.4 us
  starting transfers between devices: 36 us -> 21 us
    dot_general x4 -> x1, matrix products: 39 us -> 15.1 us  [per_device(): partial_value = jnp.dot(gated_out, out_weight, preferred_element_type=f32)]
    unnamed x24 -> x8, local copies, waits for them, and re-layouts: 22.4 us -> 4.14 us
    reshape x2 -> x0, local copies, waits for them, and re-layouts: 16.1 us -> none  [the longest x1 14.1 us: long_conv(): jnp.tile(padded, (1, SUB))[:, :SUB * (2 * SUB - 1)]]
    pallas_call x0 -> x2, Pallas kernels: none -> 15.4 us  [the longest x1 8.58 us: gated(): pl.pallas_call(gate_kernel, grid=(width // LANES,), in_specs=[pl.BlockSpe...]
    ppermute x8 -> x5, starting transfers between devices: 36 us -> 21 us  [passed_along(): return lax.ppermute(x, axis, pairs)]
    slice x3 -> x1, local copies, waits for them, and re-layouts: 15.3 us -> 0.75 us  [per_device(): halo = passed_along(features[n_tok - 2:], 'ctx', 1).transpose(1, 0, 2)]
    reduce_scatter x1, waiting for transfers between devices: 159 us -> 148 us  [per_device(): lax.psum_scatter(partial_value.astype(bf16), 'ch', scatter_dimension=1, t...]
    rev x1 -> x0, local copies, waits for them, and re-layouts: 7.22 us -> none  [long_conv(): tail_pow = powers[:, :, ::-1]]
  transfers between devices with their start and end apart: 9 -> 6, of which waited for: 8 -> 4; matrix products, arithmetic and copies ran while one was open for 19% -> 0% of each run, Pallas kernels for 0% -> 0%
where the time goes in v1:
time: 223 us; the launch traced here: 222 us
  waiting for transfers between devices  152 us (68%)
  starting transfers between devices  21 us (9%)
  Pallas kernels  15.4 us (7%)
  matrix products  15.1 us (7%)
  between operations  13.5 us (6%)
  local copies, waits for them, and re-layouts  4.88 us (2%)
    reduce_scatter x1, waiting for transfers between devices, per_device(): lax.psum_scatter(partial_value.astype(bf16), 'ch', scatter_dimension=1, t...  148 us
    ppermute x5, starting transfers between devices, passed_along(): return lax.ppermute(x, axis, pairs)  21 us
    dot_general x1, matrix products, per_device(): partial_value = jnp.dot(gated_out, out_weight, preferred_element_type=f32)  15.1 us
    pallas_call x1, Pallas kernels, gated(): pl.pallas_call(gate_kernel, grid=(width // LANES,), in_specs=[pl.BlockSpe...  8.58 us
    pallas_call x1, Pallas kernels, states(): pl.pallas_call(state_kernel, grid=(width // LANES,), in_specs=[pl.BlockSp...  6.84 us
    ppermute x5, waiting for transfers between devices, passed_along(): return lax.ppermute(x, axis, pairs)  4.47 us
  transfers between devices with their start and end apart: 6, of which 4 were waited for; matrix products, arithmetic and copies ran while one was open for 0% of the time, Pallas kernels for 0%

profile of v1, /device:TPU:0, one launch (start us, length us, event | category | flops | bytes accessed | tf_op | source)
XLA Modules:
  0.0 222.3 jit_solution(9902482520886557637)
XLA Ops:
  6.5 0.0 reduce-scatter.2.cloned.1.call-start
  6.5 0.7 slice.3
  7.3 3.5 %collective-permute-start = (bf16[2,3,512]{2,0,1:T(2,128)(2,1)S(1)}, bf16[2,3,512]{2,0,1:T(2,128)(2,1)S(1)}, u32[]{:S(2)}, u32[]{:S(2)}) collective-permute-start(bf16[2,3,512]{2,0,1:T(2,128)(2,1)S(1)} %slice.3), channel_id=1, source_target_pairs={{0,16},{16,32},{32,48},{48,64},{64,80},{80,96},{96,112},{1,17},{17... | collective-permute-start | bytes 18440 | tf_op jit(solution)/shard_map/ppermute | solution.py:151
  10.8 1.3 collective-permute-done
  12.1 0.0 copy-start
  12.1 1.9 copy-done
  14.0 0.0 copy-start.1
  14.0 0.8 copy-done.1
  14.8 0.0 copy-start.2
  14.8 0.7 copy-done.2
  15.5 6.8 %states.1 = (f32[128,8,512]{2,1,0:T(8,128)S(1)}, f32[16,512]{1,0:T(8,128)S(1)}, f32[16,8,512]{2,1,0:T(8,128)S(1)}) custom-call(bf16[3,1024,512]{2,1,0:T(8,128)(2,1)S(1)} %bitcast.4, bf16[3,1024,512]{2,1,0:T(8,128)(2,1)S(1)} %bitcast.5, bf16[3,2,512]{2,1,0:T(2,128)(2,1)S(1)} %bitcast.7, f32[3,3,512]{2,1,0:T(4,128)S(1)} %copy-done.2, f32[16,512]{1,0:T(8,128)S(1)} %copy-done.1), custom_call_target="tpu_custom_call" | custom-call | tf_op jit(solution)/shard_map/states/pallas_call | solution.py:95
  22.3 5.5 %collective-permute-start.3 = (f32[16,512]{1,0:T(8,128)S(1)}, f32[16,512]{1,0:T(8,128)S(1)}, u32[]{:S(2)}, u32[]{:S(2)}) collective-permute-start(f32[16,512]{1,0:T(8,128)S(1)} %get-tuple-element.10), channel_id=1, source_target_pairs={{0,48},{16,64},{32,80},{48,96},{64,112},{1,49},{17,65},{33,81},{49... | collective-permute-start | bytes 98312 | tf_op jit(solution)/shard_map/ppermute | solution.py:151
  27.8 4.1 %collective-permute-start.2 = (f32[16,512]{1,0:T(8,128)S(1)}, f32[16,512]{1,0:T(8,128)S(1)}, u32[]{:S(2)}, u32[]{:S(2)}) collective-permute-start(f32[16,512]{1,0:T(8,128)S(1)} %get-tuple-element.10), channel_id=1, source_target_pairs={{0,32},{16,48},{32,64},{48,80},{64,96},{80,112},{1,33},{17,49},{33... | collective-permute-start | bytes 98312 | tf_op jit(solution)/shard_map/ppermute | solution.py:151
  31.9 2.8 %collective-permute-start.1 = (f32[16,512]{1,0:T(8,128)S(1)}, f32[16,512]{1,0:T(8,128)S(1)}, u32[]{:S(2)}, u32[]{:S(2)}) collective-permute-start(f32[16,512]{1,0:T(8,128)S(1)} %get-tuple-element.10), channel_id=1, source_target_pairs={{0,16},{16,32},{32,48},{48,64},{64,80},{80,96},{96,112},{1,17},{17... | collective-permute-start | bytes 98312 | tf_op jit(solution)/shard_map/ppermute | solution.py:151
  34.7 0.0 collective-permute-done.3
  34.7 0.0 collective-permute-done.2
  34.7 1.6 collective-permute-done.1
  36.3 5.2 %collective-permute-start.4 = (f32[16,512]{1,0:T(8,128)S(1)}, f32[16,512]{1,0:T(8,128)S(1)}, u32[]{:S(2)}, u32[]{:S(2)}) collective-permute-start(f32[16,512]{1,0:T(8,128)S(1)} %multiply_add_fusion), channel_id=1, source_target_pairs={{0,64},{16,80},{32,96},{48,112},{1,65},{17,81},{33,97},{49,113},{2... | collective-permute-start | bytes 98312 | tf_op jit(solution)/shard_map/ppermute | solution.py:151
  41.5 1.6 collective-permute-done.4
  43.1 0.0 copy-start.3
  43.1 0.7 copy-done.3
  43.9 8.6 %gated.1 = bf16[1024,512]{1,0:T(8,128)(2,1)S(1)} custom-call(bf16[3,1024,512]{2,1,0:T(8,128)(2,1)S(1)} %bitcast.6, bf16[3,2,512]{2,1,0:T(2,128)(2,1)S(1)} %bitcast.8, f32[3,3,512]{2,1,0:T(4,128)S(1)} %copy-done.2, f32[16,512]{1,0:T(8,128)S(1)} %copy-done.1, f32[16,512]{1,0:T(8,128)S(1)} %copy-done.3, f32[128,8,512]{2,1,0:T(8,128)S(1)} %get-tuple-element.8.p_ref, ...), custom_call_target="tpu_custom_call" | custom-call | tf_op jit(solution)/shard_map/gated/pallas_call | solution.py:127
  52.5 15.1 %convolution_convert_fusion = bf16[1024,8192]{1,0:T(8,128)(2,1)} fusion(bf16[1024,512]{1,0:T(8,128)(2,1)S(1)} %gated.1, bf16[512,8192]{1,0:T(8,128)(2,1)} %param.9), kind=kOutput, calls=%fused_computation | convolution fusion | flops 8598323200 | bytes 26214400 | tf_op jit(solution)/shard_map/dot_general | solution.py:169
  67.5 0.0 reduce-scatter.2.cloned.1.call-update
  67.6 147.9 %reduce-scatter.2.cloned.1.call-done = bf16[1024,512]{1,0:T(8,128)(2,1)} async-done(((bf16[1024,8192]{1,0:T(8,128)(2,1)}), bf16[1024,512]{1,0:T(8,128)(2,1)}) %reduce-scatter.2.cloned.1.call-update) | async-done | bytes 1048592 | tf_op jit(solution)/shard_map/reduce_scatter | solution.py:170
  (2 shorter events, 0.0 us)
Async XLA Ops:
  6.5 208.9 %reduce-scatter.2.cloned.1.call-start = ((), (), s32[]{:S(2)}) async-start(), calls=%async_computation.1 | async-start | bytes 17825792 | tf_op jit(solution)/shard_map/reduce_scatter | solution.py:170
  7.3 4.8 %collective-permute-start = (bf16[2,3,512]{2,0,1:T(2,128)(2,1)S(1)}, bf16[2,3,512]{2,0,1:T(2,128)(2,1)S(1)}, u32[]{:S(2)}, u32[]{:S(2)}) collective-permute-start(bf16[2,3,512]{2,0,1:T(2,128)(2,1)S(1)} %slice.3), channel_id=1, source_target_pairs={{0,16},{16,32},{32,48},{48,64},{64,80},{80,96},{96,112},{1,17},{17... | collective-permute-start | bytes 18440 | tf_op jit(solution)/shard_map/ppermute | solution.py:151
  12.1 1.9 copy-start
  14.0 0.8 copy-start.1
  14.8 0.7 copy-start.2
  22.3 12.3 %collective-permute-start.3 = (f32[16,512]{1,0:T(8,128)S(1)}, f32[16,512]{1,0:T(8,128)S(1)}, u32[]{:S(2)}, u32[]{:S(2)}) collective-permute-start(f32[16,512]{1,0:T(8,128)S(1)} %get-tuple-element.10), channel_id=1, source_target_pairs={{0,48},{16,64},{32,80},{48,96},{64,112},{1,49},{17,65},{33,81},{49... | collective-permute-start | bytes 98312 | tf_op jit(solution)/shard_map/ppermute | solution.py:151
  27.8 6.9 %collective-permute-start.2 = (f32[16,512]{1,0:T(8,128)S(1)}, f32[16,512]{1,0:T(8,128)S(1)}, u32[]{:S(2)}, u32[]{:S(2)}) collective-permute-start(f32[16,512]{1,0:T(8,128)S(1)} %get-tuple-element.10), channel_id=1, source_target_pairs={{0,32},{16,48},{32,64},{48,80},{64,96},{80,112},{1,33},{17,49},{33... | collective-permute-start | bytes 98312 | tf_op jit(solution)/shard_map/ppermute | solution.py:151
  31.9 4.4 %collective-permute-start.1 = (f32[16,512]{1,0:T(8,128)S(1)}, f32[16,512]{1,0:T(8,128)S(1)}, u32[]{:S(2)}, u32[]{:S(2)}) collective-permute-start(f32[16,512]{1,0:T(8,128)S(1)} %get-tuple-element.10), channel_id=1, source_target_pairs={{0,16},{16,32},{32,48},{48,64},{64,80},{80,96},{96,112},{1,17},{17... | collective-permute-start | bytes 98312 | tf_op jit(solution)/shard_map/ppermute | solution.py:151
  36.3 6.8 %collective-permute-start.4 = (f32[16,512]{1,0:T(8,128)S(1)}, f32[16,512]{1,0:T(8,128)S(1)}, u32[]{:S(2)}, u32[]{:S(2)}) collective-permute-start(f32[16,512]{1,0:T(8,128)S(1)} %multiply_add_fusion), channel_id=1, source_target_pairs={{0,64},{16,80},{32,96},{48,112},{1,65},{17,81},{33,97},{49,113},{2... | collective-permute-start | bytes 98312 | tf_op jit(solution)/shard_map/ppermute | solution.py:151
  43.1 0.8 copy-start.3
Sparse Core Ops, SparseCore 0:
  67.7 147.7 reduce-scatter.1

commit v2 on v1

--- a/solution.py
+++ b/solution.py
@@ -1,3 +1,5 @@
+import functools
+
 import jax
 import jax.numpy as jnp
 from jax import lax
@@ -113,7 +115,7 @@
             jax.ShapeDtypeStruct((modes, SUBS, width), f32),
         ],
         scratch_shapes=[pltpu.VMEM((2, n_tok + 8, LANES), f32)],
-        compiler_params=pltpu.CompilerParams(vmem_limit_bytes=32 << 20),
+        compiler_params=pltpu.CompilerParams(vmem_limit_bytes=60 << 20),
         name="states",
     )(x, x, halo, sf, rate)
 
@@ -140,34 +142,128 @@
         out_specs=pl.BlockSpec((n_tok, LANES), col),
         out_shape=jax.ShapeDtypeStruct((n_tok, width), bf16),
         scratch_shapes=[pltpu.VMEM((n_tok + 8, LANES), f32), pltpu.VMEM((n_tok, LANES), f32)],
-        compiler_params=pltpu.CompilerParams(vmem_limit_bytes=32 << 20),
+        compiler_params=pltpu.CompilerParams(vmem_limit_bytes=60 << 20),
         name="gated",
     )(x, halo, sf, rate, res, p, start, enter)
 
 
-def passed_along(x, axis, by):
-    length = lax.axis_size(axis)
-    pairs = [(i, i + by) for i in range(length) if 0 <= i + by < length]
-    return lax.ppermute(x, axis, pairs)
+def spread(x, axis, target):
+    pairs = [(i, target(i)) for i in range(lax.axis_size(axis))]
+    return lax.ppermute(x, axis, [(i, j) for i, j in pairs if j is not None])
+
+
+def to_core(x):
+    return spread(x, "ch", lambda i: i ^ 1)
+
+
+def to_far_z(x):
+    return spread(x, "ch", lambda i: i ^ 2)
+
+
+def to_y(x, by):
+    return spread(x, "ch", lambda i: (i + 4 * by) % 16)
+
+
+def to_x(x, by):
+    return spread(x, "ctx", lambda i: i // 4 * 4 + (i + by) % 4)
 
 
 def entering_state(own, rate, n_tok):
-    block = jnp.exp(-rate * n_tok)
-    one, two, three = (passed_along(own, "ctx", k) for k in (1, 2, 3))
-    last = one + block * (two + block * three)
-    four = own + block * last
-    return last + block * block * block * passed_along(four, "ctx", 4)
+    at = lax.axis_index("ctx") % 4
+    behind = [own] + [to_x(own, k) for k in (1, 2, 3)]
+    near = jnp.zeros_like(own)
+    whole = jnp.zeros_like(own)
+    for k, state in enumerate(behind):
+        if k:
+            near = near + jnp.where(at >= k, jnp.exp(-rate * (n_tok * (k - 1))) * state, 0.0)
+        ahead = ((3 - (at - k)) % 4).astype(f32)
+        whole = whole + jnp.exp(-rate * (n_tok * ahead)) * state
+    before = spread(whole, "ctx", lambda i: i + 4 if i < 4 else None)
+    return near + jnp.exp(-rate * (n_tok * at.astype(f32))) * before
+
+
+def project_kernel(first, n_tok, cols_ref, g_ref, gp_ref, w_ref, wp_ref, *out_refs):
+    k = pl.program_id(0)
+    rows = pl.ds(first, n_tok)
+    acc = jnp.dot(g_ref[rows, :], w_ref[...], preferred_element_type=f32)
+    acc = acc + jnp.dot(gp_ref[rows, :], wp_ref[...], preferred_element_type=f32)
+    if len(out_refs) == 1:
+        out_refs[0][0] = acc.astype(bf16)
+        return
+    for i, out_ref in enumerate(out_refs):
+
+        @pl.when(k == i)
+        def _():
+            out_ref[...] = acc.astype(bf16)
+
+
+def project(operands, first, n_tok, blocks, stacked=False):
+    g, gp, w, wp = operands
+    at = lax.axis_index("ch")
+    y, z, core = at // 4, at // 2 % 2, at % 2
+    cols = jnp.stack([(y + dy) % 4 * 4 + (z + dz) % 2 * 2 + core for dy, dz in blocks]).astype(jnp.int32)
+    tok, depth = g.shape
+    n = len(blocks)
+    if stacked:
+        out_specs = pl.BlockSpec((1, n_tok, depth), lambda k, c: (k, 0, 0))
+        out_shape = jax.ShapeDtypeStruct((n, n_tok, depth), bf16)
+    else:
+        out_specs = [pl.BlockSpec((n_tok, depth), lambda k, c: (0, 0))] * n
+        out_shape = [jax.ShapeDtypeStruct((n_tok, depth), bf16)] * n
+    return pl.pallas_call(
+        functools.partial(project_kernel, first, n_tok),
+        grid_spec=pltpu.PrefetchScalarGridSpec(
+            num_scalar_prefetch=1,
+            grid=(n,),
+            in_specs=[
+                pl.BlockSpec((tok, depth), lambda k, c: (0, 0)),
+                pl.BlockSpec((tok, depth), lambda k, c: (0, 0)),
+                pl.BlockSpec((depth, depth), lambda k, c: (0, c[k])),
+                pl.BlockSpec((depth, depth), lambda k, c: (0, c[k])),
+            ],
+            out_specs=out_specs,
+        ),
+        out_shape=out_shape,
+        compiler_params=pltpu.CompilerParams(vmem_limit_bytes=60 << 20),
+        name="project",
+    )(cols, g, gp, w, wp)
+
+
+def total(*parts):
+    return sum(p.astype(f32) for p in parts).astype(bf16)
+
+
+Z_TOK = 384
 
 
 def per_device(features, short_filter, decay_rate, residues, out_weight):
     n_tok = features.shape[0]
-    halo = passed_along(features[n_tok - 2 :], "ctx", 1).transpose(1, 0, 2)
+    halo = spread(features[n_tok - 2 :], "ctx", lambda i: i + 1 if i < 7 else None).transpose(1, 0, 2)
     x = features.transpose(1, 0, 2)
+    weight_pair = to_core(out_weight)
     product, own, start = states(x, halo, short_filter, decay_rate)
     enter = entering_state(own, decay_rate, float(n_tok))
-    gated_out = gated(x, halo, short_filter, decay_rate, residues, product, start, enter)
-    partial_value = jnp.dot(gated_out, out_weight, preferred_element_type=f32)
-    return lax.psum_scatter(partial_value.astype(bf16), "ch", scatter_dimension=1, tiled=True)
+    mine = gated(x, halo, short_filter, decay_rate, residues, product, start, enter)
+    operands = (mine, to_core(mine), out_weight, weight_pair)
+    n_y = n_tok - Z_TOK
+    half = Z_TOK // 2
+
+    p20, p21 = project(operands, 0, n_y, [(2, 0), (2, 1)])
+    r20, r21 = to_y(p20, 1), to_y(p21, -1)
+    far = to_far_z(project(operands, n_y, Z_TOK, [(0, 1), (1, 1), (2, 1), (3, 1)], True))
+    p11, p30 = project(operands, 0, n_y, [(1, 1), (3, 0)])
+    r11, r30 = to_y(p11, 1), to_y(p30, -1)
+    p10, p31, p00, p01 = project(operands, 0, n_y, [(1, 0), (3, 1), (0, 0), (0, 1)])
+    r10, r31 = to_y(total(p10, r20), 1), to_y(total(p31, r21), -1)
+    zv = to_far_z(total(p01, r11, r31))
+
+    near = project(operands, n_y, Z_TOK, [(0, 0), (1, 0), (2, 0), (3, 0)], True)
+    q2 = total(near[2], far[2])
+    s2a, s2b = to_y(q2[:half], 1), to_y(q2[half:], -1)
+    q1 = jnp.concatenate([total(near[1, :half], far[1, :half], s2a), total(near[1, half:], far[1, half:])])
+    q3 = jnp.concatenate([total(near[3, :half], far[3, :half]), total(near[3, half:], far[3, half:], s2b)])
+    s1, s3 = to_y(q1, 1), to_y(q3, -1)
+    return jnp.concatenate([total(p00, r10, r30, zv), total(near[0], far[0], s1, s3)])
 
 
 def solution(mesh):

time: 223 us -> 129 us (0.58)
  waiting for transfers between devices: 152 us -> 32.4 us
  Pallas kernels: 15.4 us -> 50 us
  matrix products: 15.1 us -> 0 us
  between operations: 13.5 us -> 0.25 us
  starting transfers between devices: 21 us -> 33.7 us
  other arithmetic: 0.04 us -> 9.7 us
  local copies, waits for them, and re-layouts: 4.88 us -> 2.4 us
    reduce_scatter x1 -> x0, waiting for transfers between devices: 148 us -> none  [per_device(): lax.psum_scatter(partial_value.astype(bf16), 'ch', scatter_dimension=1, t...]
    pallas_call x0 -> x5, Pallas kernels: none -> 32.2 us  [project(): pl.pallas_call(functools.partial(project_kernel, first, n_tok), grid_spec...]
    ppermute x5 -> x19, waiting for transfers between devices: 4.47 us -> 32.4 us  [spread(): return lax.ppermute(x, axis, [(i, j) for i, j in pairs if j is not None])]
    dot_general x1 -> x0, matrix products: 15.1 us -> none  [per_device(): partial_value = jnp.dot(gated_out, out_weight, preferred_element_type=f32)]
    ppermute x5 -> x19, starting transfers between devices: 21 us -> 33.7 us  [spread(): return lax.ppermute(x, axis, [(i, j) for i, j in pairs if j is not None])]
    convert_element_type x0 -> x8, other arithmetic: none -> 4.81 us  [total(): return sum((p.astype(f32) for p in parts)).astype(bf16)]
    unnamed x8 -> x12, local copies, waits for them, and re-layouts: 4.14 us -> 1.62 us
    another operation x0 -> x4, other arithmetic: none -> 2.38 us  [project(): jnp.stack([(y + dy) % 4 * 4 + (z + dz) % 2 * 2 + core for dy, dz in blocks])]
  transfers between devices with their start and end apart: 6 -> 19, of which waited for: 4 -> 10; matrix products, arithmetic and copies ran while one was open for 0% -> 7% of each run, Pallas kernels for 0% -> 35%
where the time goes in v2:
time: 129 us; the launch traced here: 128 us
  Pallas kernels  50 us (39%)
  starting transfers between devices  33.7 us (26%)
  waiting for transfers between devices  32.4 us (25%)
  other arithmetic  9.7 us (8%)
  local copies, waits for them, and re-layouts  2.4 us (2%)
    ppermute x19, starting transfers between devices, spread(): return lax.ppermute(x, axis, [(i, j) for i, j in pairs if j is not None])  33.7 us
    ppermute x19, waiting for transfers between devices, spread(): return lax.ppermute(x, axis, [(i, j) for i, j in pairs if j is not None])  32.4 us
    pallas_call x5, Pallas kernels, project(): pl.pallas_call(functools.partial(project_kernel, first, n_tok), grid_spec...  32.2 us
    pallas_call x1, Pallas kernels, gated(): pl.pallas_call(gate_kernel, grid=(width // LANES,), in_specs=[pl.BlockSpe...  9.73 us
    pallas_call x1, Pallas kernels, states(): pl.pallas_call(state_kernel, grid=(width // LANES,), in_specs=[pl.BlockSp...  8.07 us
    convert_element_type x8, other arithmetic, total(): return sum((p.astype(f32) for p in parts)).astype(bf16)  4.81 us
  transfers between devices with their start and end apart: 19, of which 10 were waited for; matrix products, arithmetic and copies ran while one was open for 7% of the time, Pallas kernels for 35%

profile of v2, /device:TPU:0, one launch (start us, length us, event | category | flops | bytes accessed | tf_op | source)
XLA Modules:
  0.0 128.3 jit_solution(7491254511223437683)
XLA Ops:
  0.0 0.0 collective-permute-start.6
  0.0 0.7 slice.51
  0.8 3.5 %collective-permute-start = (bf16[2,3,512]{2,0,1:T(2,128)(2,1)S(1)}, bf16[2,3,512]{2,0,1:T(2,128)(2,1)S(1)}, u32[]{:S(2)}, u32[]{:S(2)}) collective-permute-start(bf16[2,3,512]{2,0,1:T(2,128)(2,1)S(1)} %slice.51), channel_id=1, source_target_pairs={{0,16},{16,32},{32,48},{48,64},{64,80},{80,96},{96,112},{1,17},{17... | collective-permute-start | bytes 18440 | tf_op jit(solution)/shard_map/ppermute | solution.py:152
  4.2 1.3 %collective-permute-done = bf16[2,3,512]{2,0,1:T(2,128)(2,1)S(1)} collective-permute-done((bf16[2,3,512]{2,0,1:T(2,128)(2,1)S(1)}, bf16[2,3,512]{2,0,1:T(2,128)(2,1)S(1)}, u32[]{:S(2)}, u32[]{:S(2)}) %collective-permute-start) | collective-permute-done | bytes 6176 | tf_op jit(solution)/shard_map/ppermute | solution.py:152
  5.6 0.6 copy-done.5
  6.2 8.1 %states.1 = (f32[128,8,512]{2,1,0:T(8,128)}, f32[16,512]{1,0:T(8,128)}, f32[16,8,512]{2,1,0:T(8,128)}) custom-call(bf16[3,1024,512]{2,1,0:T(8,128)(2,1)} %bitcast.32, bf16[3,1024,512]{2,1,0:T(8,128)(2,1)} %bitcast.33, bf16[3,2,512]{2,1,0:T(2,128)(2,1)} %bitcast.35, f32[3,3,512]{2,1,0:T(4,128)} %sf_ref.3, f32[16,512]{1,0:T(8,128)} %rate_ref.3), custom_call_target="tpu_custom_call" | custom-call | tf_op jit(solution)/shard_map/states/pallas_call | solution.py:97
  14.2 2.3 %collective-permute-start.1 = (f32[16,512]{1,0:T(8,128)}, f32[16,512]{1,0:T(8,128)S(1)}, u32[]{:S(2)}, u32[]{:S(2)}) collective-permute-start(f32[16,512]{1,0:T(8,128)} %get-tuple-element.18), channel_id=1, source_target_pairs={{0,16},{16,32},{32,48},{48,0},{64,80},{80,96},{96,112},{112,64},{1... | collective-permute-start | bytes 98312 | tf_op jit(solution)/shard_map/ppermute | solution.py:152
  16.5 2.7 %collective-permute-start.2 = (f32[16,512]{1,0:T(8,128)}, f32[16,512]{1,0:T(8,128)S(1)}, u32[]{:S(2)}, u32[]{:S(2)}) collective-permute-start(f32[16,512]{1,0:T(8,128)} %get-tuple-element.18), channel_id=1, source_target_pairs={{0,32},{16,48},{32,0},{48,16},{64,96},{80,112},{96,64},{112,80},{1... | collective-permute-start | bytes 98312 | tf_op jit(solution)/shard_map/ppermute | solution.py:152
  19.2 1.4 %collective-permute-start.3 = (f32[16,512]{1,0:T(8,128)}, f32[16,512]{1,0:T(8,128)S(1)}, u32[]{:S(2)}, u32[]{:S(2)}) collective-permute-start(f32[16,512]{1,0:T(8,128)} %get-tuple-element.18), channel_id=1, source_target_pairs={{0,48},{16,0},{32,16},{48,32},{64,112},{80,64},{96,80},{112,96},{1... | collective-permute-start | bytes 98312 | tf_op jit(solution)/shard_map/ppermute | solution.py:152
  20.7 0.0 collective-permute-done.1
  20.7 1.5 %collective-permute-done.2 = f32[16,512]{1,0:T(8,128)S(1)} collective-permute-done((f32[16,512]{1,0:T(8,128)}, f32[16,512]{1,0:T(8,128)S(1)}, u32[]{:S(2)}, u32[]{:S(2)}) %collective-permute-start.2) | collective-permute-done | bytes 32800 | tf_op jit(solution)/shard_map/ppermute | solution.py:152
  22.1 1.2 collective-permute-done.3
  23.4 0.0 copy-done.4
  23.4 0.8 multiply_add_fusion.1
  24.2 4.1 %collective-permute-start.4 = (f32[16,512]{1,0:T(8,128)S(1)}, f32[16,512]{1,0:T(8,128)S(1)}, u32[]{:S(2)}, u32[]{:S(2)}) collective-permute-start(f32[16,512]{1,0:T(8,128)S(1)} %multiply_add_fusion.1), channel_id=1, source_target_pairs={{0,64},{16,80},{32,96},{48,112},{1,65},{17,81},{33,97},{49,113},{2... | collective-permute-start | bytes 98312 | tf_op jit(solution)/shard_map/ppermute | solution.py:152
  28.3 1.6 %collective-permute-done.4 = f32[16,512]{1,0:T(8,128)S(1)} collective-permute-done((f32[16,512]{1,0:T(8,128)S(1)}, f32[16,512]{1,0:T(8,128)S(1)}, u32[]{:S(2)}, u32[]{:S(2)}) %collective-permute-start.4) | collective-permute-done | bytes 32800 | tf_op jit(solution)/shard_map/ppermute | solution.py:152
  29.9 0.6 multiply_add_fusion.enter_ref
  30.5 9.7 %gated.1.g_ref = bf16[1024,512]{1,0:T(8,128)(2,1)} custom-call(bf16[3,1024,512]{2,1,0:T(8,128)(2,1)} %bitcast.34, bf16[3,2,512]{2,1,0:T(2,128)(2,1)} %bitcast.36, f32[3,3,512]{2,1,0:T(4,128)} %sf_ref.3, f32[16,512]{1,0:T(8,128)} %rate_ref.3, f32[16,512]{1,0:T(8,128)} %res_ref.1, f32[128,8,512]{2,1,0:T(8,128)} %get-tuple-element.16.p_ref, ...), custom_call_target="tpu_custom_call" | custom-call | tf_op jit(solution)/shard_map/gated/pallas_call | solution.py:129
  40.3 0.0 collective-permute-start.5
  40.3 0.6 pad_add_fusion.1.cols_ref
  40.9 2.2 %collective-permute-done.5.gp_ref = bf16[1024,512]{1,0:T(8,128)(2,1)S(1)} collective-permute-done((bf16[1024,512]{1,0:T(8,128)(2,1)}, bf16[1024,512]{1,0:T(8,128)(2,1)S(1)}, u32[]{:S(2)}, u32[]{:S(2)}) %collective-permute-start.5) | collective-permute-done | bytes 1048608 | tf_op jit(solution)/shard_map/ppermute | solution.py:152
  43.1 0.0 collective-permute-done.6.wp_ref
  43.1 1.0 copy-done
  44.1 5.5 %project.6 = (bf16[640,512]{1,0:T(8,128)(2,1)}, bf16[640,512]{1,0:T(8,128)(2,1)}) custom-call(s32[2]{0:T(128)} %pad_add_fusion.1.cols_ref, bf16[1024,512]{1,0:T(8,128)(2,1)} %gated.1.g_ref, bf16[1024,512]{1,0:T(8,128)(2,1)} %copy-done, bf16[512,8192]{1,0:T(8,128)(2,1)} %w_ref.9, bf16[512,8192]{1,0:T(8,128)(2,1)} %collective-permute-done.6.wp_ref), custom_call_target="tpu_custom_call" | custom-call | tf_op jit(solution)/shard_map/project/pallas_call | solution.py:213
  49.7 3.0 %collective-permute-start.11 = (bf16[640,512]{1,0:T(8,128)(2,1)}, bf16[640,512]{1,0:T(8,128)(2,1)S(1)}, u32[]{:S(2)}, u32[]{:S(2)}) collective-permute-start(bf16[640,512]{1,0:T(8,128)(2,1)} %get-tuple-element.26), channel_id=1, source_target_pairs={{0,12},{1,13},{2,14},{3,15},{4,0},{5,1},{6,2},{7,3},{8,4},{9,5},{1... | collective-permute-start | bytes 1966088 | tf_op jit(solution)/shard_map/ppermute | solution.py:152
  52.7 0.6 pad_add_fusion.4.cols_ref
  53.2 6.5 %project.9 = bf16[4,384,512]{2,1,0:T(8,128)(2,1)} custom-call(s32[4]{0:T(128)} %pad_add_fusion.4.cols_ref, bf16[1024,512]{1,0:T(8,128)(2,1)} %gated.1.g_ref, bf16[1024,512]{1,0:T(8,128)(2,1)} %copy-done, bf16[512,8192]{1,0:T(8,128)(2,1)} %w_ref.9, bf16[512,8192]{1,0:T(8,128)(2,1)} %collective-permute-done.6.wp_ref), custom_call_target="tpu_custom_call" | custom-call | tf_op jit(solution)/shard_map/project/pallas_call | solution.py:213
  59.8 3.6 %collective-permute-start.14 = (bf16[4,384,512]{2,1,0:T(8,128)(2,1)}, bf16[4,384,512]{2,1,0:T(8,128)(2,1)S(1)}, u32[]{:S(2)}, u32[]{:S(2)}) collective-permute-start(bf16[4,384,512]{2,1,0:T(8,128)(2,1)} %project.9), channel_id=1, source_target_pairs={{0,2},{1,3},{2,0},{3,1},{4,6},{5,7},{6,4},{7,5},{8,10},{9,11},{10,... | collective-permute-start | bytes 4718600 | tf_op jit(solution)/shard_map/ppermute | solution.py:152
  63.4 0.6 pad_add_fusion.2.cols_ref
  64.0 0.6 pad_add_fusion
  64.6 0.0 collective-permute-start.7
  64.6 5.5 %project.7 = (bf16[640,512]{1,0:T(8,128)(2,1)}, bf16[640,512]{1,0:T(8,128)(2,1)}) custom-call(s32[2]{0:T(128)} %pad_add_fusion.2.cols_ref, bf16[1024,512]{1,0:T(8,128)(2,1)} %gated.1.g_ref, bf16[1024,512]{1,0:T(8,128)(2,1)} %copy-done, bf16[512,8192]{1,0:T(8,128)(2,1)} %w_ref.9, bf16[512,8192]{1,0:T(8,128)(2,1)} %collective-permute-done.6.wp_ref), custom_call_target="tpu_custom_call" | custom-call | tf_op jit(solution)/shard_map/project/pallas_call | solution.py:213
  70.1 0.6 collective-permute-start.10
  70.6 8.1 %project.5 = (bf16[640,512]{1,0:T(8,128)(2,1)}, bf16[640,512]{1,0:T(8,128)(2,1)}, bf16[640,512]{1,0:T(8,128)(2,1)}, bf16[640,512]{1,0:T(8,128)(2,1)}) custom-call(s32[4]{0:T(128)} %get-tuple-element.33.cols_ref, bf16[1024,512]{1,0:T(8,128)(2,1)} %gated.1.g_ref, bf16[1024,512]{1,0:T(8,128)(2,1)} %copy-done, bf16[512,8192]{1,0:T(8,128)(2,1)} %w_ref.9, ...), custom_call_target="tpu_custom_call" | custom-call | tf_op jit(solution)/shard_map/project/pallas_call | solution.py:213
  78.8 0.0 collective-permute-done.11
  78.8 2.1 %add_convert_fusion.2 = bf16[640,512]{1,0:T(8,128)(2,1)} fusion(bf16[640,512]{1,0:T(8,128)(2,1)S(1)} %collective-permute-done.11, bf16[640,512]{1,0:T(8,128)(2,1)} %get-tuple-element.25), kind=kLoop, calls=%fused_computation.2 | loop fusion | flops 1310720 | bytes 1966080 | tf_op jit(solution)/shard_map/convert_element_type | solution.py:233
  80.9 2.7 %collective-permute-start.12 = (bf16[640,512]{1,0:T(8,128)(2,1)}, bf16[640,512]{1,0:T(8,128)(2,1)S(1)}, u32[]{:S(2)}, u32[]{:S(2)}) collective-permute-start(bf16[640,512]{1,0:T(8,128)(2,1)} %add_convert_fusion.2), channel_id=1, source_target_pairs={{0,12},{1,13},{2,14},{3,15},{4,0},{5,1},{6,2},{7,3},{8,4},{9,5},{1... | collective-permute-start | bytes 1966088 | tf_op jit(solution)/shard_map/ppermute | solution.py:152
  83.6 2.0 %collective-permute-start.9 = (bf16[640,512]{1,0:T(8,128)(2,1)}, bf16[640,512]{1,0:T(8,128)(2,1)S(1)}, u32[]{:S(2)}, u32[]{:S(2)}) collective-permute-start(bf16[640,512]{1,0:T(8,128)(2,1)} %get-tuple-element.22), channel_id=1, source_target_pairs={{0,12},{1,13},{2,14},{3,15},{4,0},{5,1},{6,2},{7,3},{8,4},{9,5},{1... | collective-permute-start | bytes 1966088 | tf_op jit(solution)/shard_map/ppermute | solution.py:152
  85.6 6.5 %project.8 = bf16[4,384,512]{2,1,0:T(8,128)(2,1)} custom-call(s32[4]{0:T(128)} %get-tuple-element.34.cols_ref, bf16[1024,512]{1,0:T(8,128)(2,1)} %gated.1.g_ref, bf16[1024,512]{1,0:T(8,128)(2,1)} %copy-done, bf16[512,8192]{1,0:T(8,128)(2,1)} %w_ref.9, bf16[512,8192]{1,0:T(8,128)(2,1)} %collective-permute-done.6.wp_ref), custom_call_target="tpu_custom_call" | custom-call | tf_op jit(solution)/shard_map/project/pallas_call | solution.py:213
  92.1 0.0 collective-permute-done.7
  92.1 1.5 %add_convert_fusion.3 = bf16[640,512]{1,0:T(8,128)(2,1)S(1)} fusion(bf16[640,512]{1,0:T(8,128)(2,1)} %collective-permute-done.7, bf16[640,512]{1,0:T(8,128)(2,1)} %get-tuple-element.20), kind=kLoop, calls=%fused_computation.3 | loop fusion | flops 1310720 | bytes 1966080 | tf_op jit(solution)/shard_map/convert_element_type | solution.py:233
  93.6 0.1 collective-permute-start.8
  93.7 2.8 %collective-permute-done.10 = bf16[640,512]{1,0:T(8,128)(2,1)S(1)} collective-permute-done((bf16[640,512]{1,0:T(8,128)(2,1)}, bf16[640,512]{1,0:T(8,128)(2,1)S(1)}, u32[]{:S(2)}, u32[]{:S(2)}) %collective-permute-start.10) | collective-permute-done | bytes 655392 | tf_op jit(solution)/shard_map/ppermute | solution.py:152
  96.5 2.5 %collective-permute-done.12 = bf16[640,512]{1,0:T(8,128)(2,1)S(1)} collective-permute-done((bf16[640,512]{1,0:T(8,128)(2,1)}, bf16[640,512]{1,0:T(8,128)(2,1)S(1)}, u32[]{:S(2)}, u32[]{:S(2)}) %collective-permute-start.12) | collective-permute-done | bytes 655392 | tf_op jit(solution)/shard_map/ppermute | solution.py:152
  99.1 0.3 add_convert_fusion.1
  99.3 0.1 collective-permute-start.13
  99.4 0.0 collective-permute-done.14
  99.4 0.1 add_convert_fusion.4
  99.6 1.8 %collective-permute-start.15 = (bf16[192,512]{1,0:T(8,128)(2,1)S(1)}, bf16[192,512]{1,0:T(8,128)(2,1)S(1)}, u32[]{:S(2)}, u32[]{:S(2)}) collective-permute-start(bf16[192,512]{1,0:T(8,128)(2,1)S(1)} %get-tuple-element.31), channel_id=1, source_target_pairs={{0,4},{1,5},{2,6},{3,7},{4,8},{5,9},{6,10},{7,11},{8,12},{9,13},{1... | collective-permute-start | bytes 589832 | tf_op jit(solution)/shard_map/ppermute | solution.py:152
  101.4 1.9 %collective-permute-start.17 = (bf16[192,512]{1,0:T(8,128)(2,1)S(1)}, bf16[192,512]{1,0:T(8,128)(2,1)S(1)}, u32[]{:S(2)}, u32[]{:S(2)}) collective-permute-start(bf16[192,512]{1,0:T(8,128)(2,1)S(1)} %get-tuple-element.32), channel_id=1, source_target_pairs={{0,12},{1,13},{2,14},{3,15},{4,0},{5,1},{6,2},{7,3},{8,4},{9,5},{1... | collective-permute-start | bytes 589832 | tf_op jit(solution)/shard_map/ppermute | solution.py:152
  103.3 0.1 fusion.4
  103.4 11.1 %collective-permute-done.15 = bf16[192,512]{1,0:T(8,128)(2,1)S(1)} collective-permute-done((bf16[192,512]{1,0:T(8,128)(2,1)S(1)}, bf16[192,512]{1,0:T(8,128)(2,1)S(1)}, u32[]{:S(2)}, u32[]{:S(2)}) %collective-permute-start.15) | collective-permute-done | bytes 196640 | tf_op jit(solution)/shard_map/ppermute | solution.py:152
  114.5 0.9 collective-permute-done.17
  115.5 0.1 fusion.3
  115.7 1.9 %collective-permute-start.16 = (bf16[384,512]{1,0:T(8,128)(2,1)S(1)}, bf16[384,512]{1,0:T(8,128)(2,1)S(1)}, u32[]{:S(2)}, u32[]{:S(2)}) collective-permute-start(bf16[384,512]{1,0:T(8,128)(2,1)S(1)} %pad_maximum_fusion.1), channel_id=1, source_target_pairs={{0,4},{1,5},{2,6},{3,7},{4,8},{5,9},{6,10},{7,11},{8,12},{9,13},{1... | collective-permute-start | bytes 1179656 | tf_op jit(solution)/shard_map/ppermute | solution.py:152
  117.6 1.9 %collective-permute-start.18 = (bf16[384,512]{1,0:T(8,128)(2,1)S(1)}, bf16[384,512]{1,0:T(8,128)(2,1)S(1)}, u32[]{:S(2)}, u32[]{:S(2)}) collective-permute-start(bf16[384,512]{1,0:T(8,128)(2,1)S(1)} %pad_maximum_fusion.2), channel_id=1, source_target_pairs={{0,12},{1,13},{2,14},{3,15},{4,0},{5,1},{6,2},{7,3},{8,4},{9,5},{1... | collective-permute-start | bytes 1179656 | tf_op jit(solution)/shard_map/ppermute | solution.py:152
  119.5 0.0 collective-permute-done.9
  119.5 0.0 collective-permute-done.8
  119.5 0.0 collective-permute-done.13
  119.6 0.4 add_convert_fusion
  119.9 7.2 %collective-permute-done.16 = bf16[384,512]{1,0:T(8,128)(2,1)S(1)} collective-permute-done((bf16[384,512]{1,0:T(8,128)(2,1)S(1)}, bf16[384,512]{1,0:T(8,128)(2,1)S(1)}, u32[]{:S(2)}, u32[]{:S(2)}) %collective-permute-start.16) | collective-permute-done | bytes 393248 | tf_op jit(solution)/shard_map/ppermute | solution.py:152
  127.1 0.0 collective-permute-done.18
  127.1 0.2 fusion.1
  127.3 1.0 pad_maximum_fusion
  (12 shorter events, 0.1 us)
Async XLA Ops:
  0.0 43.1 %collective-permute-start.6 = (bf16[512,8192]{1,0:T(8,128)(2,1)}, bf16[512,8192]{1,0:T(8,128)(2,1)}, u32[]{:S(2)}, u32[]{:S(2)}) collective-permute-start(bf16[512,8192]{1,0:T(8,128)(2,1)} %w_ref.9), channel_id=1, source_target_pairs={{0,1},{1,0},{2,3},{3,2},{4,5},{5,4},{6,7},{7,6},{8,9},{9,8},{10,11... | collective-permute-start | bytes 25165832 | tf_op jit(solution)/shard_map/ppermute | solution.py:152
  0.8 4.8 %collective-permute-start = (bf16[2,3,512]{2,0,1:T(2,128)(2,1)S(1)}, bf16[2,3,512]{2,0,1:T(2,128)(2,1)S(1)}, u32[]{:S(2)}, u32[]{:S(2)}) collective-permute-start(bf16[2,3,512]{2,0,1:T(2,128)(2,1)S(1)} %slice.51), channel_id=1, source_target_pairs={{0,16},{16,32},{32,48},{48,64},{64,80},{80,96},{96,112},{1,17},{17... | collective-permute-start | bytes 18440 | tf_op jit(solution)/shard_map/ppermute | solution.py:152
  5.6 0.6 copy-start.5
  6.2 17.2 %copy-start.4 = (f32[16,512]{1,0:T(8,128)S(1)}, f32[16,512]{1,0:T(8,128)}, u32[]{:S(2)}) copy-start(f32[16,512]{1,0:T(8,128)} %rate_ref.3) | copy-start | bytes 98308
  14.2 6.5 %collective-permute-start.1 = (f32[16,512]{1,0:T(8,128)}, f32[16,512]{1,0:T(8,128)S(1)}, u32[]{:S(2)}, u32[]{:S(2)}) collective-permute-start(f32[16,512]{1,0:T(8,128)} %get-tuple-element.18), channel_id=1, source_target_pairs={{0,16},{16,32},{32,48},{48,0},{64,80},{80,96},{96,112},{112,64},{1... | collective-permute-start | bytes 98312 | tf_op jit(solution)/shard_map/ppermute | solution.py:152
  16.5 5.6 %collective-permute-start.2 = (f32[16,512]{1,0:T(8,128)}, f32[16,512]{1,0:T(8,128)S(1)}, u32[]{:S(2)}, u32[]{:S(2)}) collective-permute-start(f32[16,512]{1,0:T(8,128)} %get-tuple-element.18), channel_id=1, source_target_pairs={{0,32},{16,48},{32,0},{48,16},{64,96},{80,112},{96,64},{112,80},{1... | collective-permute-start | bytes 98312 | tf_op jit(solution)/shard_map/ppermute | solution.py:152
  19.2 4.1 %collective-permute-start.3 = (f32[16,512]{1,0:T(8,128)}, f32[16,512]{1,0:T(8,128)S(1)}, u32[]{:S(2)}, u32[]{:S(2)}) collective-permute-start(f32[16,512]{1,0:T(8,128)} %get-tuple-element.18), channel_id=1, source_target_pairs={{0,48},{16,0},{32,16},{48,32},{64,112},{80,64},{96,80},{112,96},{1... | collective-permute-start | bytes 98312 | tf_op jit(solution)/shard_map/ppermute | solution.py:152
  24.2 5.7 %collective-permute-start.4 = (f32[16,512]{1,0:T(8,128)S(1)}, f32[16,512]{1,0:T(8,128)S(1)}, u32[]{:S(2)}, u32[]{:S(2)}) collective-permute-start(f32[16,512]{1,0:T(8,128)S(1)} %multiply_add_fusion.1), channel_id=1, source_target_pairs={{0,64},{16,80},{32,96},{48,112},{1,65},{17,81},{33,97},{49,113},{2... | collective-permute-start | bytes 98312 | tf_op jit(solution)/shard_map/ppermute | solution.py:152
  40.3 2.9 %collective-permute-start.5 = (bf16[1024,512]{1,0:T(8,128)(2,1)}, bf16[1024,512]{1,0:T(8,128)(2,1)S(1)}, u32[]{:S(2)}, u32[]{:S(2)}) collective-permute-start(bf16[1024,512]{1,0:T(8,128)(2,1)} %gated.1.g_ref), channel_id=1, source_target_pairs={{0,1},{1,0},{2,3},{3,2},{4,5},{5,4},{6,7},{7,6},{8,9},{9,8},{10,11... | collective-permute-start | bytes 3145736 | tf_op jit(solution)/shard_map/ppermute | solution.py:152
  43.1 1.0 copy-start
  49.7 29.1 %collective-permute-start.11 = (bf16[640,512]{1,0:T(8,128)(2,1)}, bf16[640,512]{1,0:T(8,128)(2,1)S(1)}, u32[]{:S(2)}, u32[]{:S(2)}) collective-permute-start(bf16[640,512]{1,0:T(8,128)(2,1)} %get-tuple-element.26), channel_id=1, source_target_pairs={{0,12},{1,13},{2,14},{3,15},{4,0},{5,1},{6,2},{7,3},{8,4},{9,5},{1... | collective-permute-start | bytes 1966088 | tf_op jit(solution)/shard_map/ppermute | solution.py:152
  59.8 39.6 %collective-permute-start.14 = (bf16[4,384,512]{2,1,0:T(8,128)(2,1)}, bf16[4,384,512]{2,1,0:T(8,128)(2,1)S(1)}, u32[]{:S(2)}, u32[]{:S(2)}) collective-permute-start(bf16[4,384,512]{2,1,0:T(8,128)(2,1)} %project.9), channel_id=1, source_target_pairs={{0,2},{1,3},{2,0},{3,1},{4,6},{5,7},{6,4},{7,5},{8,10},{9,11},{10,... | collective-permute-start | bytes 4718600 | tf_op jit(solution)/shard_map/ppermute | solution.py:152
  64.6 27.5 %collective-permute-start.7 = (bf16[640,512]{1,0:T(8,128)(2,1)}, bf16[640,512]{1,0:T(8,128)(2,1)}, u32[]{:S(2)}, u32[]{:S(2)}) collective-permute-start(bf16[640,512]{1,0:T(8,128)(2,1)} %get-tuple-element.21), channel_id=1, source_target_pairs={{0,4},{1,5},{2,6},{3,7},{4,8},{5,9},{6,10},{7,11},{8,12},{9,13},{1... | collective-permute-start | bytes 1966088 | tf_op jit(solution)/shard_map/ppermute | solution.py:152
  70.1 26.5 %collective-permute-start.10 = (bf16[640,512]{1,0:T(8,128)(2,1)}, bf16[640,512]{1,0:T(8,128)(2,1)S(1)}, u32[]{:S(2)}, u32[]{:S(2)}) collective-permute-start(bf16[640,512]{1,0:T(8,128)(2,1)} %get-tuple-element.24), channel_id=1, source_target_pairs={{0,4},{1,5},{2,6},{3,7},{4,8},{5,9},{6,10},{7,11},{8,12},{9,13},{1... | collective-permute-start | bytes 1966088 | tf_op jit(solution)/shard_map/ppermute | solution.py:152
  80.9 18.2 %collective-permute-start.12 = (bf16[640,512]{1,0:T(8,128)(2,1)}, bf16[640,512]{1,0:T(8,128)(2,1)S(1)}, u32[]{:S(2)}, u32[]{:S(2)}) collective-permute-start(bf16[640,512]{1,0:T(8,128)(2,1)} %add_convert_fusion.2), channel_id=1, source_target_pairs={{0,12},{1,13},{2,14},{3,15},{4,0},{5,1},{6,2},{7,3},{8,4},{9,5},{1... | collective-permute-start | bytes 1966088 | tf_op jit(solution)/shard_map/ppermute | solution.py:152
  83.6 36.0 %collective-permute-start.9 = (bf16[640,512]{1,0:T(8,128)(2,1)}, bf16[640,512]{1,0:T(8,128)(2,1)S(1)}, u32[]{:S(2)}, u32[]{:S(2)}) collective-permute-start(bf16[640,512]{1,0:T(8,128)(2,1)} %get-tuple-element.22), channel_id=1, source_target_pairs={{0,12},{1,13},{2,14},{3,15},{4,0},{5,1},{6,2},{7,3},{8,4},{9,5},{1... | collective-permute-start | bytes 1966088 | tf_op jit(solution)/shard_map/ppermute | solution.py:152
  92.1 7.0 %copy-start.2 = (bf16[640,512]{1,0:T(8,128)(2,1)S(1)}, bf16[640,512]{1,0:T(8,128)(2,1)}, u32[]{:S(2)}) copy-start(bf16[640,512]{1,0:T(8,128)(2,1)} %get-tuple-element.23) | copy-start | bytes 1966084
  93.6 5.8 %copy-start.1 = (bf16[4,384,512]{2,1,0:T(8,128)(2,1)S(1)}, bf16[4,384,512]{2,1,0:T(8,128)(2,1)}, u32[]{:S(2)}) copy-start(bf16[4,384,512]{2,1,0:T(8,128)(2,1)} %project.8) | copy-start | bytes 4718596
  93.6 25.9 %collective-permute-start.8 = (bf16[640,512]{1,0:T(8,128)(2,1)S(1)}, bf16[640,512]{1,0:T(8,128)(2,1)S(1)}, u32[]{:S(2)}, u32[]{:S(2)}) collective-permute-start(bf16[640,512]{1,0:T(8,128)(2,1)S(1)} %add_convert_fusion.3), channel_id=1, source_target_pairs={{0,4},{1,5},{2,6},{3,7},{4,8},{5,9},{6,10},{7,11},{8,12},{9,13},{1... | collective-permute-start | bytes 1966088 | tf_op jit(solution)/shard_map/ppermute | solution.py:152
  99.3 20.2 %collective-permute-start.13 = (bf16[640,512]{1,0:T(8,128)(2,1)S(1)}, bf16[640,512]{1,0:T(8,128)(2,1)S(1)}, u32[]{:S(2)}, u32[]{:S(2)}) collective-permute-start(bf16[640,512]{1,0:T(8,128)(2,1)S(1)} %add_convert_fusion.1), channel_id=1, source_target_pairs={{0,2},{1,3},{2,0},{3,1},{4,6},{5,7},{6,4},{7,5},{8,10},{9,11},{10,... | collective-permute-start | bytes 1966088 | tf_op jit(solution)/shard_map/ppermute | solution.py:152
  99.6 15.0 %collective-permute-start.15 = (bf16[192,512]{1,0:T(8,128)(2,1)S(1)}, bf16[192,512]{1,0:T(8,128)(2,1)S(1)}, u32[]{:S(2)}, u32[]{:S(2)}) collective-permute-start(bf16[192,512]{1,0:T(8,128)(2,1)S(1)} %get-tuple-element.31), channel_id=1, source_target_pairs={{0,4},{1,5},{2,6},{3,7},{4,8},{5,9},{6,10},{7,11},{8,12},{9,13},{1... | collective-permute-start | bytes 589832 | tf_op jit(solution)/shard_map/ppermute | solution.py:152
  101.4 14.1 %collective-permute-start.17 = (bf16[192,512]{1,0:T(8,128)(2,1)S(1)}, bf16[192,512]{1,0:T(8,128)(2,1)S(1)}, u32[]{:S(2)}, u32[]{:S(2)}) collective-permute-start(bf16[192,512]{1,0:T(8,128)(2,1)S(1)} %get-tuple-element.32), channel_id=1, source_target_pairs={{0,12},{1,13},{2,14},{3,15},{4,0},{5,1},{6,2},{7,3},{8,4},{9,5},{1... | collective-permute-start | bytes 589832 | tf_op jit(solution)/shard_map/ppermute | solution.py:152
  103.4 16.1 %copy-start.3 = (bf16[640,512]{1,0:T(8,128)(2,1)S(1)}, bf16[640,512]{1,0:T(8,128)(2,1)}, u32[]{:S(2)}) copy-start(bf16[640,512]{1,0:T(8,128)(2,1)} %get-tuple-element.19) | copy-start | bytes 1966084
  115.7 11.4 %collective-permute-start.16 = (bf16[384,512]{1,0:T(8,128)(2,1)S(1)}, bf16[384,512]{1,0:T(8,128)(2,1)S(1)}, u32[]{:S(2)}, u32[]{:S(2)}) collective-permute-start(bf16[384,512]{1,0:T(8,128)(2,1)S(1)} %pad_maximum_fusion.1), channel_id=1, source_target_pairs={{0,4},{1,5},{2,6},{3,7},{4,8},{5,9},{6,10},{7,11},{8,12},{9,13},{1... | collective-permute-start | bytes 1179656 | tf_op jit(solution)/shard_map/ppermute | solution.py:152
  117.6 9.4 %collective-permute-start.18 = (bf16[384,512]{1,0:T(8,128)(2,1)S(1)}, bf16[384,512]{1,0:T(8,128)(2,1)S(1)}, u32[]{:S(2)}, u32[]{:S(2)}) collective-permute-start(bf16[384,512]{1,0:T(8,128)(2,1)S(1)} %pad_maximum_fusion.2), channel_id=1, source_target_pairs={{0,12},{1,13},{2,14},{3,15},{4,0},{5,1},{6,2},{7,3},{8,4},{9,5},{1... | collective-permute-start | bytes 1179656 | tf_op jit(solution)/shard_map/ppermute | solution.py:152

commit v3 on v1

--- a/solution.py
+++ b/solution.py
@@ -1,3 +1,5 @@
+import functools
+
 import jax
 import jax.numpy as jnp
 from jax import lax
@@ -8,6 +10,7 @@
 f32, bf16 = jnp.float32, jnp.bfloat16
 LANES = 128
 SUBS = 8
+PAD = 8
 
 
 def row_scan(values, factor, rows):
@@ -20,18 +23,25 @@
     return values
 
 
+def fill(rows_ref, x_ref, halo, steps):
+    for s in range(SUBS):
+        at = s * (steps + PAD) + PAD
+        rows_ref[pl.ds(at, steps), :] = x_ref[pl.ds(s * steps, steps), :].astype(f32)
+        before = x_ref[pl.ds(s * steps - 16, 16), :].astype(f32)[14:] if s else halo.astype(f32)
+        rows_ref[pl.ds(at - 2, 2), :] = before
+
+
 def state_kernel(key_ref, val_ref, halo_ref, sf_ref, rate_ref, p_ref, own_ref, start_ref, xs):
     n_modes = rate_ref.shape[0]
     steps = p_ref.shape[0]
     rows = lax.broadcasted_iota(jnp.int32, (SUBS, LANES), 0)
     for j in range(2):
-        xs[j, pl.ds(8, SUBS * steps), :] = (key_ref, val_ref)[j][0].astype(f32)
-        xs[j, pl.ds(6, 2), :] = halo_ref[j + 1].astype(f32)
+        fill(xs.at[j], (key_ref, val_ref)[j].at[0], halo_ref[j + 1], steps)
     w = [[jnp.broadcast_to(sf_ref[k, j + 1][None], (SUBS, LANES)) for k in range(3)] for j in range(2)]
     decay = [jnp.exp(-jnp.broadcast_to(rate_ref[pl.ds(r, 1), :], (SUBS, LANES))) for r in range(n_modes)]
 
     def tap(j, at):
-        return xs[j, pl.ds(8 + at, SUBS, stride=steps), :]
+        return xs[j, pl.ds(8 + at, SUBS, stride=steps + PAD), :]
 
     def body(t, carry):
         k1, k2, v1, v2, state = carry
@@ -45,7 +55,7 @@
 
     zero = jnp.zeros((SUBS, LANES), f32)
     init = (tap(0, -1), tap(0, -2), tap(1, -1), tap(1, -2), (zero,) * n_modes)
-    state = lax.fori_loop(0, steps, body, init, unroll=4)[4]
+    state = lax.fori_loop(0, steps, body, init, unroll=8)[4]
     for r in range(n_modes):
         rate = jnp.broadcast_to(rate_ref[pl.ds(r, 1), :], (SUBS, LANES))
         scanned = row_scan(state[r], jnp.exp(-rate * steps), rows)
@@ -57,8 +67,7 @@
     n_modes = rate_ref.shape[0]
     steps = p_ref.shape[0]
     rows = lax.broadcasted_iota(jnp.int32, (SUBS, LANES), 0).astype(f32)
-    xs[pl.ds(8, SUBS * steps), :] = x_ref[0].astype(f32)
-    xs[pl.ds(6, 2), :] = halo_ref[0].astype(f32)
+    fill(xs, x_ref.at[0], halo_ref[0], steps)
     w = [jnp.broadcast_to(sf_ref[k, 0][None], (SUBS, LANES)) for k in range(3)]
     decay, gain, state0 = [], [], []
     for r in range(n_modes):
@@ -69,7 +78,7 @@
         state0.append(start_ref[r] + jnp.exp(-rate * steps * rows) * enter)
 
     def tap(at):
-        return xs[pl.ds(8 + at, SUBS, stride=steps), :]
+        return xs[pl.ds(8 + at, SUBS, stride=steps + PAD), :]
 
     def body(t, carry):
         x1, x2, state = carry
@@ -80,11 +89,12 @@
         parts = [c * s for c, s in zip(gain, state)]
         while len(parts) > 1:
             parts = [a + b for a, b in zip(parts[::2], parts[1::2])]
-        ys[pl.ds(t, SUBS, stride=steps), :] = gate * parts[0]
+        ys[pl.ds(t, SUBS, stride=steps + PAD), :] = gate * parts[0]
         return (x0, x1, state)
 
     lax.fori_loop(0, steps, body, (tap(-1), tap(-2), tuple(state0)), unroll=4)
-    out_ref[...] = ys[...].astype(bf16)
+    for s in range(SUBS):
+        out_ref[pl.ds(s * steps, steps), :] = ys[pl.ds(s * (steps + PAD), steps), :].astype(bf16)
 
 
 def states(x, halo, sf, rate):
@@ -112,8 +122,8 @@
             jax.ShapeDtypeStruct((modes, width), f32),
             jax.ShapeDtypeStruct((modes, SUBS, width), f32),
         ],
-        scratch_shapes=[pltpu.VMEM((2, n_tok + 8, LANES), f32)],
-        compiler_params=pltpu.CompilerParams(vmem_limit_bytes=32 << 20),
+        scratch_shapes=[pltpu.VMEM((2, n_tok + SUBS * PAD, LANES), f32)],
+        compiler_params=pltpu.CompilerParams(vmem_limit_bytes=60 << 20),
         name="states",
     )(x, x, halo, sf, rate)
 
@@ -139,35 +149,143 @@
         ],
         out_specs=pl.BlockSpec((n_tok, LANES), col),
         out_shape=jax.ShapeDtypeStruct((n_tok, width), bf16),
-        scratch_shapes=[pltpu.VMEM((n_tok + 8, LANES), f32), pltpu.VMEM((n_tok, LANES), f32)],
-        compiler_params=pltpu.CompilerParams(vmem_limit_bytes=32 << 20),
+        scratch_shapes=[pltpu.VMEM((n_tok + SUBS * PAD, LANES), f32), pltpu.VMEM((n_tok + SUBS * PAD, LANES), f32)],
+        compiler_params=pltpu.CompilerParams(vmem_limit_bytes=60 << 20),
         name="gated",
     )(x, halo, sf, rate, res, p, start, enter)
 
 
-def passed_along(x, axis, by):
-    length = lax.axis_size(axis)
-    pairs = [(i, i + by) for i in range(length) if 0 <= i + by < length]
-    return lax.ppermute(x, axis, pairs)
+def spread(x, axis, target):
+    pairs = [(i, target(i)) for i in range(lax.axis_size(axis))]
+    return lax.ppermute(x, axis, [(i, j) for i, j in pairs if j is not None])
+
+
+def to_core(x):
+    return spread(x, "ch", lambda i: i ^ 1)
+
+
+def to_far_z(x):
+    return spread(x, "ch", lambda i: i ^ 2)
+
+
+def to_y(x, by):
+    return spread(x, "ch", lambda i: (i + 4 * by) % 16)
+
+
+def to_x(x, by):
+    return spread(x, "ctx", lambda i: i // 4 * 4 + (i + by) % 4)
 
 
 def entering_state(own, rate, n_tok):
-    block = jnp.exp(-rate * n_tok)
-    one, two, three = (passed_along(own, "ctx", k) for k in (1, 2, 3))
-    last = one + block * (two + block * three)
-    four = own + block * last
-    return last + block * block * block * passed_along(four, "ctx", 4)
+    at = lax.axis_index("ctx") % 4
+    behind = [own] + [to_x(own, k) for k in (1, 2, 3)]
+    near = jnp.zeros_like(own)
+    whole = jnp.zeros_like(own)
+    for k, state in enumerate(behind):
+        if k:
+            near = near + jnp.where(at >= k, jnp.exp(-rate * (n_tok * (k - 1))) * state, 0.0)
+        ahead = ((3 - (at - k)) % 4).astype(f32)
+        whole = whole + jnp.exp(-rate * (n_tok * ahead)) * state
+    before = spread(whole, "ctx", lambda i: i + 4 if i < 4 else None)
+    return near + jnp.exp(-rate * (n_tok * at.astype(f32))) * before
+
+
+def project_kernel(plan, cols_ref, g_ref, gp_ref, w_ref, wp_ref, *refs):
+    out_refs, (weights, sems) = refs[:-2], refs[-2:]
+    depth = g_ref.shape[1]
+    copies = []
+    for k, (col, _) in enumerate(plan):
+        at = pl.ds(pl.multiple_of(cols_ref[col] * depth, depth), depth)
+        pair = []
+        for j, source in enumerate((w_ref, wp_ref)):
+            copy = pltpu.make_async_copy(source.at[:, at], weights.at[k, j], sems.at[k, j])
+            copy.start()
+            pair.append(copy)
+        copies.append(pair)
+    for k, (_, pieces) in enumerate(plan):
+        for copy in copies[k]:
+            copy.wait()
+        for first, count, out, slot in pieces:
+            rows = pl.ds(first, count)
+            acc = jnp.dot(g_ref[rows, :], weights[k, 0], preferred_element_type=f32)
+            acc = acc + jnp.dot(gp_ref[rows, :], weights[k, 1], preferred_element_type=f32)
+            out_refs[out][slot] = acc.astype(bf16)
+
+
+def project(operands, plan, counts):
+    cols, g, gp, w, wp = operands
+    depth = g.shape[1]
+    slots = [0] * len(counts)
+    laid = []
+    for (dy, dz), pieces in plan:
+        mine = []
+        for first, out in pieces:
+            mine.append((first, counts[out], out, slots[out]))
+            slots[out] += 1
+        laid.append((2 * dy + dz, mine))
+    vmem = pl.BlockSpec(memory_space=pltpu.VMEM)
+    hbm = pl.BlockSpec(memory_space=pltpu.HBM)
+    return pl.pallas_call(
+        functools.partial(project_kernel, laid),
+        in_specs=[pl.BlockSpec(memory_space=pltpu.SMEM), vmem, vmem, hbm, hbm],
+        out_specs=[vmem] * len(counts),
+        out_shape=[jax.ShapeDtypeStruct((n, count, depth), bf16) for n, count in zip(slots, counts)],
+        scratch_shapes=[
+            pltpu.VMEM((len(plan), 2, depth, depth), bf16),
+            pltpu.SemaphoreType.DMA((len(plan), 2)),
+        ],
+        compiler_params=pltpu.CompilerParams(vmem_limit_bytes=50 << 20),
+        name="project",
+    )(cols, g, gp, w, wp)
+
+
+def total(*parts):
+    return sum(p.astype(f32) for p in parts).astype(bf16)
+
+
+Z_TOK = 384
 
 
 def per_device(features, short_filter, decay_rate, residues, out_weight):
     n_tok = features.shape[0]
-    halo = passed_along(features[n_tok - 2 :], "ctx", 1).transpose(1, 0, 2)
+    halo = spread(features[n_tok - 2 :], "ctx", lambda i: i + 1 if i < 7 else None).transpose(1, 0, 2)
     x = features.transpose(1, 0, 2)
+    weight_pair = to_core(out_weight)
+    me = lax.axis_index("ch")
+    steps = jnp.arange(8, dtype=jnp.int32)
+    cols = (me // 4 + steps // 2) % 4 * 4 + (me // 2 + steps) % 2 * 2 + me % 2
     product, own, start = states(x, halo, short_filter, decay_rate)
     enter = entering_state(own, decay_rate, float(n_tok))
-    gated_out = gated(x, halo, short_filter, decay_rate, residues, product, start, enter)
-    partial_value = jnp.dot(gated_out, out_weight, preferred_element_type=f32)
-    return lax.psum_scatter(partial_value.astype(bf16), "ch", scatter_dimension=1, tiled=True)
+    mine = gated(x, halo, short_filter, decay_rate, residues, product, start, enter)
+    operands = (cols, mine, to_core(mine), out_weight, weight_pair)
+    n_y = n_tok - Z_TOK
+    a, b, z = 0, n_y // 2, n_y
+
+    up2, down2, far = project(
+        operands,
+        [((2, 0), [(a, 0), (b, 1)]), ((2, 1), [(a, 0), (b, 1), (z, 2)]), ((3, 1), [(z, 2)]), ((1, 1), [(z, 2)]), ((0, 1), [(z, 2)])],
+        [b, b, Z_TOK],
+    )
+    up2, down2, far = to_y(up2, 1), to_y(down2, -1), to_far_z(far)
+    up, down, up_more, down_more, keep_a, keep_b, near = project(
+        operands,
+        [((1, 0), [(b, 0), (a, 2)]), ((1, 1), [(b, 0), (a, 2)]), ((3, 0), [(a, 1), (b, 3)]), ((3, 1), [(a, 1), (b, 3)])]
+        + [((0, 0), [(a, 4), (b, 5)]), ((0, 1), [(a, 4), (b, 5)])],
+        [b, b, b, b, b, b],
+    ) + project(operands, [((2, 0), [(z, 0)]), ((3, 0), [(z, 0)]), ((1, 0), [(z, 0)]), ((0, 0), [(z, 0)])], [Z_TOK])
+    up, down = to_y(up, 1), to_y(down, -1)
+    up_more, down_more = to_y(total(up_more, up2), 1), to_y(total(down_more, down2), -1)
+    up, down, up_more, down_more = lax.optimization_barrier((up, down, up_more, down_more))
+    over = to_far_z(jnp.stack([total(keep_a[1], up_more[1], down[1]), total(keep_b[1], up[1], down_more[1])]))
+    done_a = total(keep_a[0], up_more[0], down[0], over[0])
+    done_b = total(keep_b[0], up[0], down_more[0], over[1])
+
+    half = Z_TOK // 2
+    s2a, s2b = to_y(total(near[0, :half], far[0, :half]), 1), to_y(total(near[0, half:], far[0, half:]), -1)
+    s3 = jnp.concatenate([total(near[1, :half], far[1, :half]), total(near[1, half:], far[1, half:], s2b)])
+    s1 = jnp.concatenate([total(near[2, :half], far[2, :half], s2a), total(near[2, half:], far[2, half:])])
+    s1, s3 = to_y(s1, 1), to_y(s3, -1)
+    return jnp.concatenate([done_a, done_b, total(near[3], far[3], s1, s3)])
 
 
 def solution(mesh):

time: 223 us -> 118 us (0.53)
  waiting for transfers between devices: 152 us -> 40.9 us
  Pallas kernels: 15.4 us -> 33.2 us
  starting transfers between devices: 21 us -> 36.2 us
  matrix products: 15.1 us -> 0 us
  between operations: 13.5 us -> 0.2 us
  other arithmetic: 0.04 us -> 4.15 us
    reduce_scatter x1 -> x0, waiting for transfers between devices: 148 us -> none  [per_device(): lax.psum_scatter(partial_value.astype(bf16), 'ch', scatter_dimension=1, t...]
    ppermute x5 -> x19, waiting for transfers between devices: 4.47 us -> 40.9 us  [spread(): return lax.ppermute(x, axis, [(i, j) for i, j in pairs if j is not None])]
    pallas_call x0 -> x3, Pallas kernels: none -> 18.9 us  [project(): pl.pallas_call(functools.partial(project_kernel, laid), in_specs=[pl.Bloc...]
    ppermute x5 -> x19, starting transfers between devices: 21 us -> 36.2 us  [spread(): return lax.ppermute(x, axis, [(i, j) for i, j in pairs if j is not None])]
    dot_general x1 -> x0, matrix products: 15.1 us -> none  [per_device(): partial_value = jnp.dot(gated_out, out_weight, preferred_element_type=f32)]
  transfers between devices with their start and end apart: 6 -> 19, of which waited for: 4 -> 9; matrix products, arithmetic and copies ran while one was open for 0% -> 3% of each run, Pallas kernels for 0% -> 22%
where the time goes in v3:
time: 118 us
  waiting for transfers between devices  40.9 us (35%)
  starting transfers between devices  36.2 us (31%)
  Pallas kernels  33.2 us (28%)
  other arithmetic  4.15 us (4%)
  local copies, waits for them, and re-layouts  2.96 us (3%)
    ppermute x19, waiting for transfers between devices, spread(): return lax.ppermute(x, axis, [(i, j) for i, j in pairs if j is not None])  40.9 us
    ppermute x19, starting transfers between devices, spread(): return lax.ppermute(x, axis, [(i, j) for i, j in pairs if j is not None])  36.2 us
    pallas_call x3, Pallas kernels, project(): pl.pallas_call(functools.partial(project_kernel, laid), in_specs=[pl.Bloc...  18.9 us
    pallas_call x1, Pallas kernels, gated(): pl.pallas_call(gate_kernel, grid=(width // LANES,), in_specs=[pl.BlockSpe...  7.95 us
    pallas_call x1, Pallas kernels, states(): pl.pallas_call(state_kernel, grid=(width // LANES,), in_specs=[pl.BlockSp...  6.35 us
  transfers between devices with their start and end apart: 19, of which 9 were waited for; matrix products, arithmetic and copies ran while one was open for 3% of the time, Pallas kernels for 22%

profile of v3, /device:TPU:0, one launch (start us, length us, event | category | flops | bytes accessed | tf_op | source)
XLA Modules:
  0.0 117.6 jit_solution(7559860257599549640)
XLA Ops:
  0.0 0.0 collective-permute-start.6
  0.0 0.7 slice.87
  0.8 3.5 %collective-permute-start = (bf16[2,3,512]{2,0,1:T(2,128)(2,1)S(1)}, bf16[2,3,512]{2,0,1:T(2,128)(2,1)S(1)}, u32[]{:S(2)}, u32[]{:S(2)}) collective-permute-start(bf16[2,3,512]{2,0,1:T(2,128)(2,1)S(1)} %slice.87), channel_id=1, source_target_pairs={{0,16},{16,32},{32,48},{48,64},{64,80},{80,96},{96,112},{1,17},{17... | collective-permute-start | bytes 18440 | tf_op jit(solution)/shard_map/ppermute | solution.py:160
  4.2 1.3 %collective-permute-done = bf16[2,3,512]{2,0,1:T(2,128)(2,1)S(1)} collective-permute-done((bf16[2,3,512]{2,0,1:T(2,128)(2,1)S(1)}, bf16[2,3,512]{2,0,1:T(2,128)(2,1)S(1)}, u32[]{:S(2)}, u32[]{:S(2)}) %collective-permute-start) | collective-permute-done | bytes 6176 | tf_op jit(solution)/shard_map/ppermute | solution.py:160
  5.6 0.0 copy-start.5
  5.6 0.6 copy-done.5
  6.2 0.0 copy-start.4
  6.2 6.3 %states.1 = (f32[128,8,512]{2,1,0:T(8,128)}, f32[16,512]{1,0:T(8,128)}, f32[16,8,512]{2,1,0:T(8,128)}) custom-call(bf16[3,1024,512]{2,1,0:T(8,128)(2,1)} %bitcast.28, bf16[3,1024,512]{2,1,0:T(8,128)(2,1)} %bitcast.29, bf16[3,2,512]{2,1,0:T(2,128)(2,1)} %bitcast.31, f32[3,3,512]{2,1,0:T(4,128)} %sf_ref.3, f32[16,512]{1,0:T(8,128)} %rate_ref.3), custom_call_target="tpu_custom_call" | custom-call | tf_op jit(solution)/shard_map/states/pallas_call | solution.py:105
  12.5 3.5 %collective-permute-start.3 = (f32[16,512]{1,0:T(8,128)}, f32[16,512]{1,0:T(8,128)S(1)}, u32[]{:S(2)}, u32[]{:S(2)}) collective-permute-start(f32[16,512]{1,0:T(8,128)} %get-tuple-element.23), channel_id=1, source_target_pairs={{0,48},{16,0},{32,16},{48,32},{64,112},{80,64},{96,80},{112,96},{1... | collective-permute-start | bytes 98312 | tf_op jit(solution)/shard_map/ppermute | solution.py:160
  16.1 0.8 collective-permute-start.2
  16.9 0.9 collective-permute-start.1
  17.8 0.2 collective-permute-done.3
  18.0 3.7 %collective-permute-done.2 = f32[16,512]{1,0:T(8,128)S(1)} collective-permute-done((f32[16,512]{1,0:T(8,128)}, f32[16,512]{1,0:T(8,128)S(1)}, u32[]{:S(2)}, u32[]{:S(2)}) %collective-permute-start.2) | collective-permute-done | bytes 32800 | tf_op jit(solution)/shard_map/ppermute | solution.py:160
  21.7 0.5 collective-permute-done.1
  22.2 0.0 copy-done.4
  22.2 0.8 multiply_add_fusion.1
  23.0 3.9 %collective-permute-start.4 = (f32[16,512]{1,0:T(8,128)S(1)}, f32[16,512]{1,0:T(8,128)S(1)}, u32[]{:S(2)}, u32[]{:S(2)}) collective-permute-start(f32[16,512]{1,0:T(8,128)S(1)} %multiply_add_fusion.1), channel_id=1, source_target_pairs={{0,64},{16,80},{32,96},{48,112},{1,65},{17,81},{33,97},{49,113},{2... | collective-permute-start | bytes 98312 | tf_op jit(solution)/shard_map/ppermute | solution.py:160
  26.9 1.6 %collective-permute-done.4 = f32[16,512]{1,0:T(8,128)S(1)} collective-permute-done((f32[16,512]{1,0:T(8,128)S(1)}, f32[16,512]{1,0:T(8,128)S(1)}, u32[]{:S(2)}, u32[]{:S(2)}) %collective-permute-start.4) | collective-permute-done | bytes 32800 | tf_op jit(solution)/shard_map/ppermute | solution.py:160
  28.5 0.6 multiply_add_fusion.enter_ref
  29.1 8.0 %gated.1.g_ref = bf16[1024,512]{1,0:T(8,128)(2,1)} custom-call(bf16[3,1024,512]{2,1,0:T(8,128)(2,1)} %bitcast.30, bf16[3,2,512]{2,1,0:T(2,128)(2,1)} %bitcast.32, f32[3,3,512]{2,1,0:T(4,128)} %sf_ref.3, f32[16,512]{1,0:T(8,128)} %rate_ref.3, f32[16,512]{1,0:T(8,128)} %res_ref.1, f32[128,8,512]{2,1,0:T(8,128)} %get-tuple-element.21.p_ref, ...), custom_call_target="tpu_custom_call" | custom-call | tf_op jit(solution)/shard_map/gated/pallas_call | solution.py:137
  37.0 0.0 collective-permute-start.5
  37.1 2.8 %collective-permute-done.5.gp_ref = bf16[1024,512]{1,0:T(8,128)(2,1)S(1)} collective-permute-done((bf16[1024,512]{1,0:T(8,128)(2,1)}, bf16[1024,512]{1,0:T(8,128)(2,1)S(1)}, u32[]{:S(2)}, u32[]{:S(2)}) %collective-permute-start.5) | collective-permute-done | bytes 1048608 | tf_op jit(solution)/shard_map/ppermute | solution.py:160
  39.9 0.0 copy-start.2
  39.9 0.0 collective-permute-done.6.wp_ref
  39.9 1.6 %copy-done = bf16[1024,512]{1,0:T(8,128)(2,1)S(1)} copy-done((bf16[1024,512]{1,0:T(8,128)(2,1)S(1)}, bf16[1024,512]{1,0:T(8,128)(2,1)}, u32[]{:S(2)}) %copy-start) | copy-done | bytes 1048600
  41.5 6.8 %project.4 = (bf16[2,320,512]{2,1,0:T(8,128)(2,1)S(1)}, bf16[2,320,512]{2,1,0:T(8,128)(2,1)S(1)}, bf16[4,384,512]{2,1,0:T(8,128)(2,1)}) custom-call(s32[8]{0:T(128)S(1)} %fusion.15.cols_ref, bf16[1024,512]{1,0:T(8,128)(2,1)S(1)} %copy-done, bf16[1024,512]{1,0:T(8,128)(2,1)S(1)} %collective-permute-done.5.gp_ref, bf16[512,8192]{1,0:T(8,128)(2,1)} %w_ref.5, ...), custom_call_target="tpu_custom_call" | custom-call | tf_op jit(solution)/shard_map/project/pallas_call | solution.py:228
  48.4 0.0 copy-done.2
  48.4 1.6 %collective-permute-start.9 = (bf16[2,320,512]{2,1,0:T(8,128)(2,1)S(1)}, bf16[2,320,512]{2,1,0:T(8,128)(2,1)S(1)}, u32[]{:S(2)}, u32[]{:S(2)}) collective-permute-start(bf16[2,320,512]{2,1,0:T(8,128)(2,1)S(1)} %get-tuple-element.28), channel_id=1, source_target_pairs={{0,4},{1,5},{2,6},{3,7},{4,8},{5,9},{6,10},{7,11},{8,12},{9,13},{1... | collective-permute-start | bytes 1966088 | tf_op jit(solution)/shard_map/ppermute | solution.py:160
  50.0 1.7 %collective-permute-start.11 = (bf16[2,320,512]{2,1,0:T(8,128)(2,1)S(1)}, bf16[2,320,512]{2,1,0:T(8,128)(2,1)S(1)}, u32[]{:S(2)}, u32[]{:S(2)}) collective-permute-start(bf16[2,320,512]{2,1,0:T(8,128)(2,1)S(1)} %get-tuple-element.30), channel_id=1, source_target_pairs={{0,12},{1,13},{2,14},{3,15},{4,0},{5,1},{6,2},{7,3},{8,4},{9,5},{1... | collective-permute-start | bytes 1966088 | tf_op jit(solution)/shard_map/ppermute | solution.py:160
  51.7 3.6 %collective-permute-start.14 = (bf16[4,384,512]{2,1,0:T(8,128)(2,1)}, bf16[4,384,512]{2,1,0:T(8,128)(2,1)S(1)}, u32[]{:S(2)}, u32[]{:S(2)}) collective-permute-start(bf16[4,384,512]{2,1,0:T(8,128)(2,1)} %get-tuple-element.36), channel_id=1, source_target_pairs={{0,2},{1,3},{2,0},{3,1},{4,6},{5,7},{6,4},{7,5},{8,10},{9,11},{10,... | collective-permute-start | bytes 4718600 | tf_op jit(solution)/shard_map/ppermute | solution.py:160
  55.3 7.9 %project.3 = (bf16[2,320,512]{2,1,0:T(8,128)(2,1)S(1)}, bf16[2,320,512]{2,1,0:T(8,128)(2,1)S(1)}, bf16[2,320,512]{2,1,0:T(8,128)(2,1)S(1)}, bf16[2,320,512]{2,1,...) custom-call(s32[8]{0:T(128)S(1)} %fusion.15.cols_ref, ...), custom_call_target="tpu_custom_call" | custom-call | tf_op jit(solution)/shard_map/project/pallas_call | solution.py:228
  63.2 0.4 collective-permute-start.7
  63.6 2.9 %collective-permute-start.8 = (bf16[2,320,512]{2,1,0:T(8,128)(2,1)S(1)}, bf16[2,320,512]{2,1,0:T(8,128)(2,1)S(1)}, u32[]{:S(2)}, u32[]{:S(2)}) collective-permute-start(bf16[2,320,512]{2,1,0:T(8,128)(2,1)S(1)} %get-tuple-element.26), channel_id=1, source_target_pairs={{0,12},{1,13},{2,14},{3,15},{4,0},{5,1},{6,2},{7,3},{8,4},{9,5},{1... | collective-permute-start | bytes 1966088 | tf_op jit(solution)/shard_map/ppermute | solution.py:160
  66.5 0.0 collective-permute-done.9
  66.5 0.2 add_convert_fusion.1
  66.7 1.2 collective-permute-start.10
  67.9 0.0 collective-permute-done.11
  67.9 0.2 add_convert_fusion
  68.0 2.2 %collective-permute-start.12 = (bf16[2,320,512]{2,1,0:T(8,128)(2,1)S(1)}, bf16[2,320,512]{2,1,0:T(8,128)(2,1)S(1)}, u32[]{:S(2)}, u32[]{:S(2)}) collective-permute-start(bf16[2,320,512]{2,1,0:T(8,128)(2,1)S(1)} %add_convert_fusion), channel_id=1, source_target_pairs={{0,12},{1,13},{2,14},{3,15},{4,0},{5,1},{6,2},{7,3},{8,4},{9,5},{1... | collective-permute-start | bytes 1966088 | tf_op jit(solution)/shard_map/ppermute | solution.py:160
  70.3 0.0 copy-done.1
  70.3 0.0 copy-done.3
  70.3 4.1 %project.5 = bf16[4,384,512]{2,1,0:T(8,128)(2,1)S(1)} custom-call(s32[8]{0:T(128)S(1)} %fusion.15.cols_ref, bf16[1024,512]{1,0:T(8,128)(2,1)S(1)} %copy-done.1, bf16[1024,512]{1,0:T(8,128)(2,1)S(1)} %copy-done.3, bf16[512,8192]{1,0:T(8,128)(2,1)} %w_ref.5, bf16[512,8192]{1,0:T(8,128)(2,1)} %collective-permute-done.6.wp_ref), custom_call_target="tpu_custom_call" | custom-call | tf_op jit(solution)/shard_map/project/pallas_call | solution.py:228
  74.4 7.8 %collective-permute-done.7 = bf16[2,320,512]{2,1,0:T(8,128)(2,1)S(1)} collective-permute-done((bf16[2,320,512]{2,1,0:T(8,128)(2,1)S(1)}, bf16[2,320,512]{2,1,0:T(8,128)(2,1)S(1)}, u32[]{:S(2)}, u32[]{:S(2)}) %collective-permute-start.7) | collective-permute-done | bytes 655392 | tf_op jit(solution)/shard_map/ppermute | solution.py:160
  82.2 0.0 collective-permute-done.8
  82.2 12.4 %collective-permute-done.10 = bf16[2,320,512]{2,1,0:T(8,128)(2,1)S(1)} collective-permute-done((bf16[2,320,512]{2,1,0:T(8,128)(2,1)S(1)}, bf16[2,320,512]{2,1,0:T(8,128)(2,1)S(1)}, u32[]{:S(2)}, u32[]{:S(2)}) %collective-permute-start.10) | collective-permute-done | bytes 655392 | tf_op jit(solution)/shard_map/ppermute | solution.py:160
  94.6 0.0 collective-permute-done.12
  94.6 0.0 collective-permute-done.14
  94.6 0.2 fusion.6
  94.8 1.6 %collective-permute-start.15 = (bf16[192,512]{1,0:T(8,128)(2,1)S(1)}, bf16[192,512]{1,0:T(8,128)(2,1)S(1)}, u32[]{:S(2)}, u32[]{:S(2)}) collective-permute-start(bf16[192,512]{1,0:T(8,128)(2,1)S(1)} %get-tuple-element.39), channel_id=1, source_target_pairs={{0,4},{1,5},{2,6},{3,7},{4,8},{5,9},{6,10},{7,11},{8,12},{9,13},{1... | collective-permute-start | bytes 589832 | tf_op jit(solution)/shard_map/ppermute | solution.py:160
  96.5 1.7 %collective-permute-start.17 = (bf16[192,512]{1,0:T(8,128)(2,1)S(1)}, bf16[192,512]{1,0:T(8,128)(2,1)S(1)}, u32[]{:S(2)}, u32[]{:S(2)}) collective-permute-start(bf16[192,512]{1,0:T(8,128)(2,1)S(1)} %get-tuple-element.40), channel_id=1, source_target_pairs={{0,12},{1,13},{2,14},{3,15},{4,0},{5,1},{6,2},{7,3},{8,4},{9,5},{1... | collective-permute-start | bytes 589832 | tf_op jit(solution)/shard_map/ppermute | solution.py:160
  98.2 0.3 add_convert_fusion.4
  98.5 0.1 pad_maximum_fusion.1
  98.5 3.7 %collective-permute-start.13 = (bf16[2,320,512]{2,1,0:T(8,128)(2,1)S(1)}, bf16[2,320,512]{2,1,0:T(8,128)(2,1)S(1)}, u32[]{:S(2)}, u32[]{:S(2)}) collective-permute-start(bf16[2,320,512]{2,1,0:T(8,128)(2,1)S(1)} %pad_maximum_fusion.1), channel_id=1, source_target_pairs={{0,2},{1,3},{2,0},{3,1},{4,6},{5,7},{6,4},{7,5},{8,10},{9,11},{10,... | collective-permute-start | bytes 1966088 | tf_op jit(solution)/shard_map/ppermute | solution.py:160
  102.2 0.0 collective-permute-done.15
  102.2 0.0 collective-permute-done.17
  102.2 0.1 fusion.3
  102.4 2.9 %collective-permute-start.18 = (bf16[384,512]{1,0:T(8,128)(2,1)S(1)}, bf16[384,512]{1,0:T(8,128)(2,1)S(1)}, u32[]{:S(2)}, u32[]{:S(2)}) collective-permute-start(bf16[384,512]{1,0:T(8,128)(2,1)S(1)} %pad_maximum_fusion.3), channel_id=1, source_target_pairs={{0,12},{1,13},{2,14},{3,15},{4,0},{5,1},{6,2},{7,3},{8,4},{9,5},{1... | collective-permute-start | bytes 1179656 | tf_op jit(solution)/shard_map/ppermute | solution.py:160
  105.3 0.1 collective-permute-start.16
  105.4 10.5 %collective-permute-done.13 = bf16[2,320,512]{2,1,0:T(8,128)(2,1)S(1)} collective-permute-done((bf16[2,320,512]{2,1,0:T(8,128)(2,1)S(1)}, bf16[2,320,512]{2,1,0:T(8,128)(2,1)S(1)}, u32[]{:S(2)}, u32[]{:S(2)}) %collective-permute-start.13) | collective-permute-done | bytes 655392 | tf_op jit(solution)/shard_map/ppermute | solution.py:160
  115.9 0.4 fusion.4
  116.3 0.0 collective-permute-done.18
  116.3 0.0 collective-permute-done.16
  116.3 0.2 fusion.1
  116.5 1.0 pad_maximum_fusion
  (6 shorter events, 0.1 us)
Async XLA Ops:
  0.0 39.9 %collective-permute-start.6 = (bf16[512,8192]{1,0:T(8,128)(2,1)}, bf16[512,8192]{1,0:T(8,128)(2,1)}, u32[]{:S(2)}, u32[]{:S(2)}) collective-permute-start(bf16[512,8192]{1,0:T(8,128)(2,1)} %w_ref.5), channel_id=1, source_target_pairs={{0,1},{1,0},{2,3},{3,2},{4,5},{5,4},{6,7},{7,6},{8,9},{9,8},{10,11... | collective-permute-start | bytes 25165832 | tf_op jit(solution)/shard_map/ppermute | solution.py:160
  0.8 4.8 %collective-permute-start = (bf16[2,3,512]{2,0,1:T(2,128)(2,1)S(1)}, bf16[2,3,512]{2,0,1:T(2,128)(2,1)S(1)}, u32[]{:S(2)}, u32[]{:S(2)}) collective-permute-start(bf16[2,3,512]{2,0,1:T(2,128)(2,1)S(1)} %slice.87), channel_id=1, source_target_pairs={{0,16},{16,32},{32,48},{48,64},{64,80},{80,96},{96,112},{1,17},{17... | collective-permute-start | bytes 18440 | tf_op jit(solution)/shard_map/ppermute | solution.py:160
  5.6 0.6 copy-start.5
  6.2 16.0 %copy-start.4 = (f32[16,512]{1,0:T(8,128)S(1)}, f32[16,512]{1,0:T(8,128)}, u32[]{:S(2)}) copy-start(f32[16,512]{1,0:T(8,128)} %rate_ref.3) | copy-start | bytes 98308
  12.5 5.5 %collective-permute-start.3 = (f32[16,512]{1,0:T(8,128)}, f32[16,512]{1,0:T(8,128)S(1)}, u32[]{:S(2)}, u32[]{:S(2)}) collective-permute-start(f32[16,512]{1,0:T(8,128)} %get-tuple-element.23), channel_id=1, source_target_pairs={{0,48},{16,0},{32,16},{48,32},{64,112},{80,64},{96,80},{112,96},{1... | collective-permute-start | bytes 98312 | tf_op jit(solution)/shard_map/ppermute | solution.py:160
  16.1 5.6 %collective-permute-start.2 = (f32[16,512]{1,0:T(8,128)}, f32[16,512]{1,0:T(8,128)S(1)}, u32[]{:S(2)}, u32[]{:S(2)}) collective-permute-start(f32[16,512]{1,0:T(8,128)} %get-tuple-element.23), channel_id=1, source_target_pairs={{0,32},{16,48},{32,0},{48,16},{64,96},{80,112},{96,64},{112,80},{1... | collective-permute-start | bytes 98312 | tf_op jit(solution)/shard_map/ppermute | solution.py:160
  16.9 5.3 %collective-permute-start.1 = (f32[16,512]{1,0:T(8,128)}, f32[16,512]{1,0:T(8,128)S(1)}, u32[]{:S(2)}, u32[]{:S(2)}) collective-permute-start(f32[16,512]{1,0:T(8,128)} %get-tuple-element.23), channel_id=1, source_target_pairs={{0,16},{16,32},{32,48},{48,0},{64,80},{80,96},{96,112},{112,64},{1... | collective-permute-start | bytes 98312 | tf_op jit(solution)/shard_map/ppermute | solution.py:160
  23.0 5.5 %collective-permute-start.4 = (f32[16,512]{1,0:T(8,128)S(1)}, f32[16,512]{1,0:T(8,128)S(1)}, u32[]{:S(2)}, u32[]{:S(2)}) collective-permute-start(f32[16,512]{1,0:T(8,128)S(1)} %multiply_add_fusion.1), channel_id=1, source_target_pairs={{0,64},{16,80},{32,96},{48,112},{1,65},{17,81},{33,97},{49,113},{2... | collective-permute-start | bytes 98312 | tf_op jit(solution)/shard_map/ppermute | solution.py:160
  37.0 2.9 %collective-permute-start.5 = (bf16[1024,512]{1,0:T(8,128)(2,1)}, bf16[1024,512]{1,0:T(8,128)(2,1)S(1)}, u32[]{:S(2)}, u32[]{:S(2)}) collective-permute-start(bf16[1024,512]{1,0:T(8,128)(2,1)} %gated.1.g_ref), channel_id=1, source_target_pairs={{0,1},{1,0},{2,3},{3,2},{4,5},{5,4},{6,7},{7,6},{8,9},{9,8},{10,11... | collective-permute-start | bytes 3145736 | tf_op jit(solution)/shard_map/ppermute | solution.py:160
  39.9 8.5 %copy-start.2 = (bf16[1024,512]{1,0:T(8,128)(2,1)}, bf16[1024,512]{1,0:T(8,128)(2,1)S(1)}, u32[]{:S(2)}) copy-start(bf16[1024,512]{1,0:T(8,128)(2,1)S(1)} %collective-permute-done.5.gp_ref) | copy-start | bytes 3145732
  39.9 1.6 %copy-start = (bf16[1024,512]{1,0:T(8,128)(2,1)S(1)}, bf16[1024,512]{1,0:T(8,128)(2,1)}, u32[]{:S(2)}) copy-start(bf16[1024,512]{1,0:T(8,128)(2,1)} %gated.1.g_ref) | copy-start | bytes 3145732
  48.4 18.1 %collective-permute-start.9 = (bf16[2,320,512]{2,1,0:T(8,128)(2,1)S(1)}, bf16[2,320,512]{2,1,0:T(8,128)(2,1)S(1)}, u32[]{:S(2)}, u32[]{:S(2)}) collective-permute-start(bf16[2,320,512]{2,1,0:T(8,128)(2,1)S(1)} %get-tuple-element.28), channel_id=1, source_target_pairs={{0,4},{1,5},{2,6},{3,7},{4,8},{5,9},{6,10},{7,11},{8,12},{9,13},{1... | collective-permute-start | bytes 1966088 | tf_op jit(solution)/shard_map/ppermute | solution.py:160
  50.0 17.8 %collective-permute-start.11 = (bf16[2,320,512]{2,1,0:T(8,128)(2,1)S(1)}, bf16[2,320,512]{2,1,0:T(8,128)(2,1)S(1)}, u32[]{:S(2)}, u32[]{:S(2)}) collective-permute-start(bf16[2,320,512]{2,1,0:T(8,128)(2,1)S(1)} %get-tuple-element.30), channel_id=1, source_target_pairs={{0,12},{1,13},{2,14},{3,15},{4,0},{5,1},{6,2},{7,3},{8,4},{9,5},{1... | collective-permute-start | bytes 1966088 | tf_op jit(solution)/shard_map/ppermute | solution.py:160
  51.7 42.9 %collective-permute-start.14 = (bf16[4,384,512]{2,1,0:T(8,128)(2,1)}, bf16[4,384,512]{2,1,0:T(8,128)(2,1)S(1)}, u32[]{:S(2)}, u32[]{:S(2)}) collective-permute-start(bf16[4,384,512]{2,1,0:T(8,128)(2,1)} %get-tuple-element.36), channel_id=1, source_target_pairs={{0,2},{1,3},{2,0},{3,1},{4,6},{5,7},{6,4},{7,5},{8,10},{9,11},{10,... | collective-permute-start | bytes 4718600 | tf_op jit(solution)/shard_map/ppermute | solution.py:160
  63.2 18.9 %collective-permute-start.7 = (bf16[2,320,512]{2,1,0:T(8,128)(2,1)S(1)}, bf16[2,320,512]{2,1,0:T(8,128)(2,1)S(1)}, u32[]{:S(2)}, u32[]{:S(2)}) collective-permute-start(bf16[2,320,512]{2,1,0:T(8,128)(2,1)S(1)} %get-tuple-element.25), channel_id=1, source_target_pairs={{0,4},{1,5},{2,6},{3,7},{4,8},{5,9},{6,10},{7,11},{8,12},{9,13},{1... | collective-permute-start | bytes 1966088 | tf_op jit(solution)/shard_map/ppermute | solution.py:160
  63.6 18.5 %collective-permute-start.8 = (bf16[2,320,512]{2,1,0:T(8,128)(2,1)S(1)}, bf16[2,320,512]{2,1,0:T(8,128)(2,1)S(1)}, u32[]{:S(2)}, u32[]{:S(2)}) collective-permute-start(bf16[2,320,512]{2,1,0:T(8,128)(2,1)S(1)} %get-tuple-element.26), channel_id=1, source_target_pairs={{0,12},{1,13},{2,14},{3,15},{4,0},{5,1},{6,2},{7,3},{8,4},{9,5},{1... | collective-permute-start | bytes 1966088 | tf_op jit(solution)/shard_map/ppermute | solution.py:160
  66.5 3.8 %copy-start.1 = (bf16[1024,512]{1,0:T(8,128)(2,1)S(1)}, bf16[1024,512]{1,0:T(8,128)(2,1)}, u32[]{:S(2)}) copy-start(bf16[1024,512]{1,0:T(8,128)(2,1)} %gated.1.g_ref) | copy-start | bytes 3145732
  66.5 3.8 %copy-start.3 = (bf16[1024,512]{1,0:T(8,128)(2,1)S(1)}, bf16[1024,512]{1,0:T(8,128)(2,1)}, u32[]{:S(2)}) copy-start(bf16[1024,512]{1,0:T(8,128)(2,1)} %copy-done.2) | copy-start | bytes 3145732
  66.7 27.9 %collective-permute-start.10 = (bf16[2,320,512]{2,1,0:T(8,128)(2,1)S(1)}, bf16[2,320,512]{2,1,0:T(8,128)(2,1)S(1)}, u32[]{:S(2)}, u32[]{:S(2)}) collective-permute-start(bf16[2,320,512]{2,1,0:T(8,128)(2,1)S(1)} %add_convert_fusion.1), channel_id=1, source_target_pairs={{0,4},{1,5},{2,6},{3,7},{4,8},{5,9},{6,10},{7,11},{8,12},{9,13},{1... | collective-permute-start | bytes 1966088 | tf_op jit(solution)/shard_map/ppermute | solution.py:160
  68.0 26.6 %collective-permute-start.12 = (bf16[2,320,512]{2,1,0:T(8,128)(2,1)S(1)}, bf16[2,320,512]{2,1,0:T(8,128)(2,1)S(1)}, u32[]{:S(2)}, u32[]{:S(2)}) collective-permute-start(bf16[2,320,512]{2,1,0:T(8,128)(2,1)S(1)} %add_convert_fusion), channel_id=1, source_target_pairs={{0,12},{1,13},{2,14},{3,15},{4,0},{5,1},{6,2},{7,3},{8,4},{9,5},{1... | collective-permute-start | bytes 1966088 | tf_op jit(solution)/shard_map/ppermute | solution.py:160
  94.8 7.3 %collective-permute-start.15 = (bf16[192,512]{1,0:T(8,128)(2,1)S(1)}, bf16[192,512]{1,0:T(8,128)(2,1)S(1)}, u32[]{:S(2)}, u32[]{:S(2)}) collective-permute-start(bf16[192,512]{1,0:T(8,128)(2,1)S(1)} %get-tuple-element.39), channel_id=1, source_target_pairs={{0,4},{1,5},{2,6},{3,7},{4,8},{5,9},{6,10},{7,11},{8,12},{9,13},{1... | collective-permute-start | bytes 589832 | tf_op jit(solution)/shard_map/ppermute | solution.py:160
  96.5 5.7 %collective-permute-start.17 = (bf16[192,512]{1,0:T(8,128)(2,1)S(1)}, bf16[192,512]{1,0:T(8,128)(2,1)S(1)}, u32[]{:S(2)}, u32[]{:S(2)}) collective-permute-start(bf16[192,512]{1,0:T(8,128)(2,1)S(1)} %get-tuple-element.40), channel_id=1, source_target_pairs={{0,12},{1,13},{2,14},{3,15},{4,0},{5,1},{6,2},{7,3},{8,4},{9,5},{1... | collective-permute-start | bytes 589832 | tf_op jit(solution)/shard_map/ppermute | solution.py:160
  98.5 17.4 %collective-permute-start.13 = (bf16[2,320,512]{2,1,0:T(8,128)(2,1)S(1)}, bf16[2,320,512]{2,1,0:T(8,128)(2,1)S(1)}, u32[]{:S(2)}, u32[]{:S(2)}) collective-permute-start(bf16[2,320,512]{2,1,0:T(8,128)(2,1)S(1)} %pad_maximum_fusion.1), channel_id=1, source_target_pairs={{0,2},{1,3},{2,0},{3,1},{4,6},{5,7},{6,4},{7,5},{8,10},{9,11},{10,... | collective-permute-start | bytes 1966088 | tf_op jit(solution)/shard_map/ppermute | solution.py:160
  102.4 13.9 %collective-permute-start.18 = (bf16[384,512]{1,0:T(8,128)(2,1)S(1)}, bf16[384,512]{1,0:T(8,128)(2,1)S(1)}, u32[]{:S(2)}, u32[]{:S(2)}) collective-permute-start(bf16[384,512]{1,0:T(8,128)(2,1)S(1)} %pad_maximum_fusion.3), channel_id=1, source_target_pairs={{0,12},{1,13},{2,14},{3,15},{4,0},{5,1},{6,2},{7,3},{8,4},{9,5},{1... | collective-permute-start | bytes 1179656 | tf_op jit(solution)/shard_map/ppermute | solution.py:160
  105.3 11.0 %collective-permute-start.16 = (bf16[384,512]{1,0:T(8,128)(2,1)S(1)}, bf16[384,512]{1,0:T(8,128)(2,1)S(1)}, u32[]{:S(2)}, u32[]{:S(2)}) collective-permute-start(bf16[384,512]{1,0:T(8,128)(2,1)S(1)} %pad_maximum_fusion.2), channel_id=1, source_target_pairs={{0,4},{1,5},{2,6},{3,7},{4,8},{5,9},{6,10},{7,11},{8,12},{9,13},{1... | collective-permute-start | bytes 1179656 | tf_op jit(solution)/shard_map/ppermute | solution.py:160

commit v4 on v3

--- a/solution.py
+++ b/solution.py
@@ -123,7 +123,7 @@
             jax.ShapeDtypeStruct((modes, SUBS, width), f32),
         ],
         scratch_shapes=[pltpu.VMEM((2, n_tok + SUBS * PAD, LANES), f32)],
-        compiler_params=pltpu.CompilerParams(vmem_limit_bytes=60 << 20),
+        compiler_params=pltpu.CompilerParams(vmem_limit_bytes=59 << 20),
         name="states",
     )(x, x, halo, sf, rate)
 
@@ -150,7 +150,7 @@
         out_specs=pl.BlockSpec((n_tok, LANES), col),
         out_shape=jax.ShapeDtypeStruct((n_tok, width), bf16),
         scratch_shapes=[pltpu.VMEM((n_tok + SUBS * PAD, LANES), f32), pltpu.VMEM((n_tok + SUBS * PAD, LANES), f32)],
-        compiler_params=pltpu.CompilerParams(vmem_limit_bytes=60 << 20),
+        compiler_params=pltpu.CompilerParams(vmem_limit_bytes=59 << 20),
         name="gated",
     )(x, halo, sf, rate, res, p, start, enter)
 
@@ -190,60 +190,67 @@
     return near + jnp.exp(-rate * (n_tok * at.astype(f32))) * before
 
 
-def project_kernel(plan, cols_ref, g_ref, gp_ref, w_ref, wp_ref, *refs):
-    out_refs, (weights, sems) = refs[:-2], refs[-2:]
+def project_kernel(plan, n_added, cols_ref, g_ref, gp_ref, w_ref, wp_ref, *refs):
+    added, refs = refs[:n_added], refs[n_added:]
+    out_refs, (acts, weights, act_sems, weight_sems) = refs[:-4], refs[-4:]
     depth = g_ref.shape[1]
+    act_copies = [pltpu.make_async_copy(r, acts.at[j], act_sems.at[j]) for j, r in enumerate((g_ref, gp_ref))]
     copies = []
     for k, (col, _) in enumerate(plan):
         at = pl.ds(pl.multiple_of(cols_ref[col] * depth, depth), depth)
-        pair = []
-        for j, source in enumerate((w_ref, wp_ref)):
-            copy = pltpu.make_async_copy(source.at[:, at], weights.at[k, j], sems.at[k, j])
+        pair = [
+            pltpu.make_async_copy(source.at[:, at], weights.at[k, j], weight_sems.at[k, j])
+            for j, source in enumerate((w_ref, wp_ref))
+        ]
+        for copy in act_copies + pair if k == 0 else pair:
             copy.start()
-            pair.append(copy)
         copies.append(pair)
     for k, (_, pieces) in enumerate(plan):
-        for copy in copies[k]:
+        for copy in act_copies + copies[k] if k == 0 else copies[k]:
             copy.wait()
-        for first, count, out, slot in pieces:
+        for first, count, out, slot, extra in pieces:
             rows = pl.ds(first, count)
-            acc = jnp.dot(g_ref[rows, :], weights[k, 0], preferred_element_type=f32)
-            acc = acc + jnp.dot(gp_ref[rows, :], weights[k, 1], preferred_element_type=f32)
+            acc = jnp.dot(acts[0, rows, :], weights[k, 0], preferred_element_type=f32)
+            acc = acc + jnp.dot(acts[1, rows, :], weights[k, 1], preferred_element_type=f32)
+            if extra is not None:
+                acc = acc + added[extra[0]][extra[1]].astype(f32)
             out_refs[out][slot] = acc.astype(bf16)
 
 
-def project(operands, plan, counts):
+def project(operands, plan, counts, added=()):
     cols, g, gp, w, wp = operands
-    depth = g.shape[1]
+    n_tok, depth = g.shape
     slots = [0] * len(counts)
     laid = []
     for (dy, dz), pieces in plan:
         mine = []
-        for first, out in pieces:
-            mine.append((first, counts[out], out, slots[out]))
+        for first, out, *extra in pieces:
+            mine.append((first, counts[out], out, slots[out], extra[0] if extra else None))
             slots[out] += 1
         laid.append((2 * dy + dz, mine))
     vmem = pl.BlockSpec(memory_space=pltpu.VMEM)
-    hbm = pl.BlockSpec(memory_space=pltpu.HBM)
+    anywhere = pl.BlockSpec(memory_space=pl.ANY)
     return pl.pallas_call(
-        functools.partial(project_kernel, laid),
-        in_specs=[pl.BlockSpec(memory_space=pltpu.SMEM), vmem, vmem, hbm, hbm],
+        functools.partial(project_kernel, laid, len(added)),
+        in_specs=[pl.BlockSpec(memory_space=pltpu.SMEM)] + [anywhere] * 4 + [vmem] * len(added),
         out_specs=[vmem] * len(counts),
         out_shape=[jax.ShapeDtypeStruct((n, count, depth), bf16) for n, count in zip(slots, counts)],
         scratch_shapes=[
+            pltpu.VMEM((2, n_tok, depth), bf16),
             pltpu.VMEM((len(plan), 2, depth, depth), bf16),
+            pltpu.SemaphoreType.DMA((2,)),
             pltpu.SemaphoreType.DMA((len(plan), 2)),
         ],
         compiler_params=pltpu.CompilerParams(vmem_limit_bytes=50 << 20),
         name="project",
-    )(cols, g, gp, w, wp)
+    )(cols, g, gp, w, wp, *added)
 
 
 def total(*parts):
     return sum(p.astype(f32) for p in parts).astype(bf16)
 
 
-Z_TOK = 384
+Z_TOK = 320
 
 
 def per_device(features, short_filter, decay_rate, residues, out_weight):
@@ -261,31 +268,38 @@
     n_y = n_tok - Z_TOK
     a, b, z = 0, n_y // 2, n_y
 
-    up2, down2, far = project(
+    up2, down2 = project(operands, [((2, dz), [(a, 0), (b, 1)]) for dz in (1, 0)], [b, b])
+    up2, down2 = to_y(up2, 1), to_y(down2, -1)
+    (far,) = project(operands, [((dy, 1), [(z, 0)]) for dy in range(4)], [Z_TOK])
+    far = to_far_z(far)
+
+    up, down, up_more, down_more, keep_a, keep_b = project(
         operands,
-        [((2, 0), [(a, 0), (b, 1)]), ((2, 1), [(a, 0), (b, 1), (z, 2)]), ((3, 1), [(z, 2)]), ((1, 1), [(z, 2)]), ((0, 1), [(z, 2)])],
-        [b, b, Z_TOK],
+        [((1, 1), [(b, 0), (a, 2)]), ((3, 1), [(a, 1), (b, 3)]), ((0, 1), [(a, 4), (b, 5)])],
+        [b] * 6,
     )
-    up2, down2, far = to_y(up2, 1), to_y(down2, -1), to_far_z(far)
-    up, down, up_more, down_more, keep_a, keep_b, near = project(
+    up, down = to_y(up[0], 1), to_y(down[0], -1)
+    up_more, down_more = to_y(total(up_more[0], up2[0]), 1), to_y(total(down_more[0], down2[0]), -1)
+    rise, fall, stay_a, stay_b = project(
         operands,
-        [((1, 0), [(b, 0), (a, 2)]), ((1, 1), [(b, 0), (a, 2)]), ((3, 0), [(a, 1), (b, 3)]), ((3, 1), [(a, 1), (b, 3)])]
-        + [((0, 0), [(a, 4), (b, 5)]), ((0, 1), [(a, 4), (b, 5)])],
-        [b, b, b, b, b, b],
-    ) + project(operands, [((2, 0), [(z, 0)]), ((3, 0), [(z, 0)]), ((1, 0), [(z, 0)]), ((0, 0), [(z, 0)])], [Z_TOK])
-    up, down = to_y(up, 1), to_y(down, -1)
-    up_more, down_more = to_y(total(up_more, up2), 1), to_y(total(down_more, down2), -1)
+        [((1, 0), [(b, 0), (a, 0, (0, 1))]), ((3, 0), [(a, 1), (b, 1, (1, 1))]), ((0, 0), [(a, 2), (b, 3)])],
+        [b] * 4,
+        [up2, down2],
+    )
+    rise, fall = to_y(rise, 1), to_y(fall, -1)
+    (near,) = project(operands, [((dy, 0), [(z, 0)]) for dy in range(4)], [Z_TOK])
     up, down, up_more, down_more = lax.optimization_barrier((up, down, up_more, down_more))
-    over = to_far_z(jnp.stack([total(keep_a[1], up_more[1], down[1]), total(keep_b[1], up[1], down_more[1])]))
-    done_a = total(keep_a[0], up_more[0], down[0], over[0])
-    done_b = total(keep_b[0], up[0], down_more[0], over[1])
+    over = to_far_z(jnp.stack([total(keep_a[0], up_more, down), total(keep_b[0], up, down_more)]))
+    rise, fall = lax.optimization_barrier((rise, fall))
+    done_a = total(stay_a[0], rise[1], fall[0], over[0])
+    done_b = total(stay_b[0], rise[0], fall[1], over[1])
 
     half = Z_TOK // 2
-    s2a, s2b = to_y(total(near[0, :half], far[0, :half]), 1), to_y(total(near[0, half:], far[0, half:]), -1)
-    s3 = jnp.concatenate([total(near[1, :half], far[1, :half]), total(near[1, half:], far[1, half:], s2b)])
-    s1 = jnp.concatenate([total(near[2, :half], far[2, :half], s2a), total(near[2, half:], far[2, half:])])
+    s2a, s2b = to_y(total(near[2, :half], far[2, :half]), 1), to_y(total(near[2, half:], far[2, half:]), -1)
+    s3 = jnp.concatenate([total(near[3, :half], far[3, :half]), total(near[3, half:], far[3, half:], s2b)])
+    s1 = jnp.concatenate([total(near[1, :half], far[1, :half], s2a), total(near[1, half:], far[1, half:])])
     s1, s3 = to_y(s1, 1), to_y(s3, -1)
-    return jnp.concatenate([done_a, done_b, total(near[3], far[3], s1, s3)])
+    return jnp.concatenate([done_a, done_b, total(near[0], far[0], s1, s3)])
 
 
 def solution(mesh):

time: 118 us -> 114 us (0.966)
  waiting for transfers between devices: 40.9 us -> 29.3 us
  Pallas kernels: 33.2 us -> 37.1 us
  starting transfers between devices: 36.2 us -> 39.3 us
    ppermute x19 -> x21, waiting for transfers between devices: 40.9 us -> 29.3 us  [spread(): return lax.ppermute(x, axis, [(i, j) for i, j in pairs if j is not None])]
    pallas_call x3 -> x5, Pallas kernels: 18.9 us -> 22.8 us  [project(): pl.pallas_call(functools.partial(project_kernel, laid, len(added)), in_sp...]
    ppermute x19 -> x21, starting transfers between devices: 36.2 us -> 39.3 us  [spread(): return lax.ppermute(x, axis, [(i, j) for i, j in pairs if j is not None])]
  transfers between devices with their start and end apart: 19 -> 21, of which waited for: 9 -> 10; matrix products, arithmetic and copies ran while one was open for 3% -> 3% of each run, Pallas kernels for 22% -> 30%
where the time goes in v4:
time: 114 us; the launch traced here: 113 us
  starting transfers between devices  39.3 us (34%)
  Pallas kernels  37.1 us (33%)
  waiting for transfers between devices  29.3 us (26%)
  other arithmetic  3.95 us (3%)
  local copies, waits for them, and re-layouts  2.96 us (3%)
    ppermute x21, starting transfers between devices, spread(): return lax.ppermute(x, axis, [(i, j) for i, j in pairs if j is not None])  39.3 us
    ppermute x21, waiting for transfers between devices, spread(): return lax.ppermute(x, axis, [(i, j) for i, j in pairs if j is not None])  29.3 us
    pallas_call x5, Pallas kernels, project(): pl.pallas_call(functools.partial(project_kernel, laid, len(added)), in_sp...  22.8 us
    pallas_call x1, Pallas kernels, gated(): pl.pallas_call(gate_kernel, grid=(width // LANES,), in_specs=[pl.BlockSpe...  7.95 us
    pallas_call x1, Pallas kernels, states(): pl.pallas_call(state_kernel, grid=(width // LANES,), in_specs=[pl.BlockSp...  6.34 us
  transfers between devices with their start and end apart: 21, of which 10 were waited for; matrix products, arithmetic and copies ran while one was open for 3% of the time, Pallas kernels for 30%

profile of v4, /device:TPU:0, one launch (start us, length us, event | category | flops | bytes accessed | tf_op | source)
XLA Modules:
  0.0 112.8 jit_solution(4221858264249302366)
XLA Ops:
  0.0 0.0 collective-permute-start.6
  0.0 0.7 slice.69
  0.8 3.5 %collective-permute-start = (bf16[2,3,512]{2,0,1:T(2,128)(2,1)S(1)}, bf16[2,3,512]{2,0,1:T(2,128)(2,1)S(1)}, u32[]{:S(2)}, u32[]{:S(2)}) collective-permute-start(bf16[2,3,512]{2,0,1:T(2,128)(2,1)S(1)} %slice.69), channel_id=1, source_target_pairs={{0,16},{16,32},{32,48},{48,64},{64,80},{80,96},{96,112},{1,17},{17... | collective-permute-start | bytes 18440 | tf_op jit(solution)/shard_map/ppermute | solution.py:160
  4.2 1.3 %collective-permute-done = bf16[2,3,512]{2,0,1:T(2,128)(2,1)S(1)} collective-permute-done((bf16[2,3,512]{2,0,1:T(2,128)(2,1)S(1)}, bf16[2,3,512]{2,0,1:T(2,128)(2,1)S(1)}, u32[]{:S(2)}, u32[]{:S(2)}) %collective-permute-start) | collective-permute-done | bytes 6176 | tf_op jit(solution)/shard_map/ppermute | solution.py:160
  5.6 0.6 copy-done.5
  6.2 6.3 %states.1 = (f32[128,8,512]{2,1,0:T(8,128)}, f32[16,512]{1,0:T(8,128)}, f32[16,8,512]{2,1,0:T(8,128)}) custom-call(bf16[3,1024,512]{2,1,0:T(8,128)(2,1)} %bitcast.46, bf16[3,1024,512]{2,1,0:T(8,128)(2,1)} %bitcast.47, bf16[3,2,512]{2,1,0:T(2,128)(2,1)} %bitcast.49, f32[3,3,512]{2,1,0:T(4,128)} %sf_ref.3, f32[16,512]{1,0:T(8,128)} %rate_ref.3), custom_call_target="tpu_custom_call" | custom-call | tf_op jit(solution)/shard_map/states/pallas_call | solution.py:105
  12.5 3.5 %collective-permute-start.3 = (f32[16,512]{1,0:T(8,128)}, f32[16,512]{1,0:T(8,128)S(1)}, u32[]{:S(2)}, u32[]{:S(2)}) collective-permute-start(f32[16,512]{1,0:T(8,128)} %get-tuple-element.28), channel_id=1, source_target_pairs={{0,48},{16,0},{32,16},{48,32},{64,112},{80,64},{96,80},{112,96},{1... | collective-permute-start | bytes 98312 | tf_op jit(solution)/shard_map/ppermute | solution.py:160
  16.1 0.8 collective-permute-start.2
  16.9 0.9 collective-permute-start.1
  17.7 0.2 collective-permute-done.3
  18.0 3.7 %collective-permute-done.2 = f32[16,512]{1,0:T(8,128)S(1)} collective-permute-done((f32[16,512]{1,0:T(8,128)}, f32[16,512]{1,0:T(8,128)S(1)}, u32[]{:S(2)}, u32[]{:S(2)}) %collective-permute-start.2) | collective-permute-done | bytes 32800 | tf_op jit(solution)/shard_map/ppermute | solution.py:160
  21.7 0.5 collective-permute-done.1
  22.2 0.8 multiply_add_fusion.1
  23.0 3.9 %collective-permute-start.4 = (f32[16,512]{1,0:T(8,128)S(1)}, f32[16,512]{1,0:T(8,128)S(1)}, u32[]{:S(2)}, u32[]{:S(2)}) collective-permute-start(f32[16,512]{1,0:T(8,128)S(1)} %multiply_add_fusion.1), channel_id=1, source_target_pairs={{0,64},{16,80},{32,96},{48,112},{1,65},{17,81},{33,97},{49,113},{2... | collective-permute-start | bytes 98312 | tf_op jit(solution)/shard_map/ppermute | solution.py:160
  26.9 1.6 %collective-permute-done.4 = f32[16,512]{1,0:T(8,128)S(1)} collective-permute-done((f32[16,512]{1,0:T(8,128)S(1)}, f32[16,512]{1,0:T(8,128)S(1)}, u32[]{:S(2)}, u32[]{:S(2)}) %collective-permute-start.4) | collective-permute-done | bytes 32800 | tf_op jit(solution)/shard_map/ppermute | solution.py:160
  28.4 0.6 multiply_add_fusion.enter_ref
  29.1 8.0 %gated.1.g_ref = bf16[1024,512]{1,0:T(8,128)(2,1)} custom-call(bf16[3,1024,512]{2,1,0:T(8,128)(2,1)} %bitcast.48, bf16[3,2,512]{2,1,0:T(2,128)(2,1)} %bitcast.50, f32[3,3,512]{2,1,0:T(4,128)} %sf_ref.3, f32[16,512]{1,0:T(8,128)} %rate_ref.3, f32[16,512]{1,0:T(8,128)} %res_ref.1, f32[128,8,512]{2,1,0:T(8,128)} %get-tuple-element.26.p_ref, ...), custom_call_target="tpu_custom_call" | custom-call | tf_op jit(solution)/shard_map/gated/pallas_call | solution.py:137
  37.0 0.0 collective-permute-start.5
  37.1 2.8 %collective-permute-done.5.gp_ref = bf16[1024,512]{1,0:T(8,128)(2,1)S(1)} collective-permute-done((bf16[1024,512]{1,0:T(8,128)(2,1)}, bf16[1024,512]{1,0:T(8,128)(2,1)S(1)}, u32[]{:S(2)}, u32[]{:S(2)}) %collective-permute-start.5) | collective-permute-done | bytes 1048608 | tf_op jit(solution)/shard_map/ppermute | solution.py:160
  39.9 0.0 collective-permute-done.6.wp_ref
  39.9 1.6 %copy-done = bf16[1024,512]{1,0:T(8,128)(2,1)S(1)} copy-done((bf16[1024,512]{1,0:T(8,128)(2,1)S(1)}, bf16[1024,512]{1,0:T(8,128)(2,1)}, u32[]{:S(2)}) %copy-start) | copy-done | bytes 1048600
  41.5 3.8 %project.5 = (bf16[2,352,512]{2,1,0:T(8,128)(2,1)S(1)}, bf16[2,352,512]{2,1,0:T(8,128)(2,1)S(1)}) custom-call(s32[8]{0:T(128)S(1)} %fusion.23.cols_ref, bf16[1024,512]{1,0:T(8,128)(2,1)S(1)} %copy-done, bf16[1024,512]{1,0:T(8,128)(2,1)S(1)} %collective-permute-done.5.gp_ref, bf16[512,8192]{1,0:T(8,128)(2,1)} %w_ref.9, ...), custom_call_target="tpu_custom_call" | custom-call | tf_op jit(solution)/shard_map/project/pallas_call | solution.py:233
  45.3 1.6 %collective-permute-start.7 = (bf16[2,352,512]{2,1,0:T(8,128)(2,1)S(1)}, bf16[2,352,512]{2,1,0:T(8,128)(2,1)S(1)}, u32[]{:S(2)}, u32[]{:S(2)}) collective-permute-start(bf16[2,352,512]{2,1,0:T(8,128)(2,1)S(1)} %get-tuple-element.29), channel_id=1, source_target_pairs={{0,4},{1,5},{2,6},{3,7},{4,8},{5,9},{6,10},{7,11},{8,12},{9,13},{1... | collective-permute-start | bytes 2162696 | tf_op jit(solution)/shard_map/ppermute | solution.py:160
  46.9 1.7 %collective-permute-start.8 = (bf16[2,352,512]{2,1,0:T(8,128)(2,1)S(1)}, bf16[2,352,512]{2,1,0:T(8,128)(2,1)S(1)}, u32[]{:S(2)}, u32[]{:S(2)}) collective-permute-start(bf16[2,352,512]{2,1,0:T(8,128)(2,1)S(1)} %get-tuple-element.30), channel_id=1, source_target_pairs={{0,12},{1,13},{2,14},{3,15},{4,0},{5,1},{6,2},{7,3},{8,4},{9,5},{1... | collective-permute-start | bytes 2162696 | tf_op jit(solution)/shard_map/ppermute | solution.py:160
  48.6 0.0 copy-done.1
  48.6 4.0 %project.9 = bf16[4,320,512]{2,1,0:T(8,128)(2,1)S(1)} custom-call(s32[8]{0:T(128)S(1)} %fusion.23.cols_ref, bf16[1024,512]{1,0:T(8,128)(2,1)S(1)} %copy-done.1, bf16[1024,512]{1,0:T(8,128)(2,1)S(1)} %collective-permute-done.5.gp_ref, bf16[512,8192]{1,0:T(8,128)(2,1)} %w_ref.9, bf16[512,8192]{1,0:T(8,128)(2,1)} %collective-permute-done.6.wp_ref), custom_call_target="tpu_custom_call" | custom-call | tf_op jit(solution)/shard_map/project/pallas_call | solution.py:233
  52.6 3.7 %collective-permute-start.16 = (bf16[4,320,512]{2,1,0:T(8,128)(2,1)S(1)}, bf16[4,320,512]{2,1,0:T(8,128)(2,1)S(1)}, u32[]{:S(2)}, u32[]{:S(2)}) collective-permute-start(bf16[4,320,512]{2,1,0:T(8,128)(2,1)S(1)} %project.9), channel_id=1, source_target_pairs={{0,2},{1,3},{2,0},{3,1},{4,6},{5,7},{6,4},{7,5},{8,10},{9,11},{10,... | collective-permute-start | bytes 3932168 | tf_op jit(solution)/shard_map/ppermute | solution.py:160
  56.3 5.5 %project.7 = (bf16[1,352,512]{2,1,0:T(8,128)(2,1)S(1)}, bf16[1,352,512]{2,1,0:T(8,128)(2,1)S(1)}, bf16[1,352,512]{2,1,0:T(8,128)(2,1)S(1)}, bf16[1,352,512]{2,1,...) custom-call(s32[8]{0:T(128)S(1)} %fusion.23.cols_ref, ...), custom_call_target="tpu_custom_call" | custom-call | tf_op jit(solution)/shard_map/project/pallas_call | solution.py:233
  61.8 0.4 collective-permute-start.11
  62.2 2.9 %collective-permute-start.12 = (bf16[352,512]{1,0:T(8,128)(2,1)S(1)}, bf16[352,512]{1,0:T(8,128)(2,1)S(1)}, u32[]{:S(2)}, u32[]{:S(2)}) collective-permute-start(bf16[352,512]{1,0:T(8,128)(2,1)S(1)} %bitcast.44), channel_id=1, source_target_pairs={{0,12},{1,13},{2,14},{3,15},{4,0},{5,1},{6,2},{7,3},{8,4},{9,5},{1... | collective-permute-start | bytes 1081352 | tf_op jit(solution)/shard_map/ppermute | solution.py:160
  65.1 0.0 collective-permute-done.7.refs_0_
  65.1 0.1 fusion.6
  65.2 0.9 collective-permute-start.13
  66.1 0.0 collective-permute-done.8.refs_1_
  66.1 0.1 fusion.7
  66.2 2.5 %collective-permute-start.14 = (bf16[352,512]{1,0:T(8,128)(2,1)S(1)}, bf16[352,512]{1,0:T(8,128)(2,1)S(1)}, u32[]{:S(2)}, u32[]{:S(2)}) collective-permute-start(bf16[352,512]{1,0:T(8,128)(2,1)S(1)} %fusion.7), channel_id=1, source_target_pairs={{0,12},{1,13},{2,14},{3,15},{4,0},{5,1},{6,2},{7,3},{8,4},{9,5},{1... | collective-permute-start | bytes 1081352 | tf_op jit(solution)/shard_map/ppermute | solution.py:160
  68.6 4.0 %project.8 = bf16[4,320,512]{2,1,0:T(8,128)(2,1)S(1)} custom-call(s32[8]{0:T(128)S(1)} %fusion.23.cols_ref, bf16[1024,512]{1,0:T(8,128)(2,1)S(1)} %copy-done.1, bf16[1024,512]{1,0:T(8,128)(2,1)S(1)} %copy-done.3, bf16[512,8192]{1,0:T(8,128)(2,1)} %w_ref.9, bf16[512,8192]{1,0:T(8,128)(2,1)} %collective-permute-done.6.wp_ref), custom_call_target="tpu_custom_call" | custom-call | tf_op jit(solution)/shard_map/project/pallas_call | solution.py:233
  72.7 5.6 %project.6 = (bf16[2,352,512]{2,1,0:T(8,128)(2,1)S(1)}, bf16[2,352,512]{2,1,0:T(8,128)(2,1)S(1)}, bf16[1,352,512]{2,1,0:T(8,128)(2,1)S(1)}, bf16[1,352,512]{2,1,0:T(8,128)(2,1)S(1)}) custom-call(s32[8]{0:T(128)S(1)} %fusion.23.cols_ref, bf16[1024,512]{1,0:T(8,128)(2,1)} %gated.1.g_ref, bf16[1024,512]{1,0:T(8,128)(2,1)} %copy-done.2, ...), custom_call_target="tpu_custom_call" | custom-call | tf_op jit(solution)/shard_map/project/pallas_call | solution.py:233
  78.2 0.0 collective-permute-done.11
  78.2 0.1 collective-permute-start.9
  78.3 0.0 collective-permute-done.12
  78.3 3.2 %collective-permute-start.10 = (bf16[2,352,512]{2,1,0:T(8,128)(2,1)S(1)}, bf16[2,352,512]{2,1,0:T(8,128)(2,1)S(1)}, u32[]{:S(2)}, u32[]{:S(2)}) collective-permute-start(bf16[2,352,512]{2,1,0:T(8,128)(2,1)S(1)} %get-tuple-element.33), channel_id=1, source_target_pairs={{0,12},{1,13},{2,14},{3,15},{4,0},{5,1},{6,2},{7,3},{8,4},{9,5},{1... | collective-permute-start | bytes 2162696 | tf_op jit(solution)/shard_map/ppermute | solution.py:160
  81.5 0.0 collective-permute-done.13
  81.5 0.0 collective-permute-done.14
  81.5 3.4 %collective-permute-done.16 = bf16[4,320,512]{2,1,0:T(8,128)(2,1)S(1)} collective-permute-done((bf16[4,320,512]{2,1,0:T(8,128)(2,1)S(1)}, bf16[4,320,512]{2,1,0:T(8,128)(2,1)S(1)}, u32[]{:S(2)}, u32[]{:S(2)}) %collective-permute-start.16) | collective-permute-done | bytes 1310752 | tf_op jit(solution)/shard_map/ppermute | solution.py:160
  84.9 0.2 fusion.14
  85.1 0.3 collective-permute-start.17
  85.4 3.0 %collective-permute-start.19 = (bf16[160,512]{1,0:T(8,128)(2,1)S(1)}, bf16[160,512]{1,0:T(8,128)(2,1)S(1)}, u32[]{:S(2)}, u32[]{:S(2)}) collective-permute-start(bf16[160,512]{1,0:T(8,128)(2,1)S(1)} %get-tuple-element.50), channel_id=1, source_target_pairs={{0,12},{1,13},{2,14},{3,15},{4,0},{5,1},{6,2},{7,3},{8,4},{9,5},{1... | collective-permute-start | bytes 491528 | tf_op jit(solution)/shard_map/ppermute | solution.py:160
  88.4 0.3 fusion.10
  88.7 0.1 pad_maximum_fusion.1
  88.8 3.3 %collective-permute-start.15 = (bf16[2,352,512]{2,1,0:T(8,128)(2,1)S(1)}, bf16[2,352,512]{2,1,0:T(8,128)(2,1)S(1)}, u32[]{:S(2)}, u32[]{:S(2)}) collective-permute-start(bf16[2,352,512]{2,1,0:T(8,128)(2,1)S(1)} %pad_maximum_fusion.1), channel_id=1, source_target_pairs={{0,2},{1,3},{2,0},{3,1},{4,6},{5,7},{6,4},{7,5},{8,10},{9,11},{10,... | collective-permute-start | bytes 2162696 | tf_op jit(solution)/shard_map/ppermute | solution.py:160
  92.1 7.5 %collective-permute-done.17 = bf16[160,512]{1,0:T(8,128)(2,1)S(1)} collective-permute-done((bf16[160,512]{1,0:T(8,128)(2,1)S(1)}, bf16[160,512]{1,0:T(8,128)(2,1)S(1)}, u32[]{:S(2)}, u32[]{:S(2)}) %collective-permute-start.17) | collective-permute-done | bytes 163872 | tf_op jit(solution)/shard_map/ppermute | solution.py:160
  99.6 0.0 collective-permute-done.19
  99.6 0.1 fusion.13
  99.8 3.0 %collective-permute-start.20 = (bf16[320,512]{1,0:T(8,128)(2,1)S(1)}, bf16[320,512]{1,0:T(8,128)(2,1)S(1)}, u32[]{:S(2)}, u32[]{:S(2)}) collective-permute-start(bf16[320,512]{1,0:T(8,128)(2,1)S(1)} %pad_maximum_fusion.3), channel_id=1, source_target_pairs={{0,12},{1,13},{2,14},{3,15},{4,0},{5,1},{6,2},{7,3},{8,4},{9,5},{1... | collective-permute-start | bytes 983048 | tf_op jit(solution)/shard_map/ppermute | solution.py:160
  102.8 0.1 collective-permute-start.18
  102.9 0.0 collective-permute-done.9
  102.9 0.0 collective-permute-done.10
  102.9 4.8 %collective-permute-done.20 = bf16[320,512]{1,0:T(8,128)(2,1)S(1)} collective-permute-done((bf16[320,512]{1,0:T(8,128)(2,1)S(1)}, bf16[320,512]{1,0:T(8,128)(2,1)S(1)}, u32[]{:S(2)}, u32[]{:S(2)}) %collective-permute-start.20) | collective-permute-done | bytes 327712 | tf_op jit(solution)/shard_map/ppermute | solution.py:160
  107.8 3.4 %collective-permute-done.18 = bf16[320,512]{1,0:T(8,128)(2,1)S(1)} collective-permute-done((bf16[320,512]{1,0:T(8,128)(2,1)S(1)}, bf16[320,512]{1,0:T(8,128)(2,1)S(1)}, u32[]{:S(2)}, u32[]{:S(2)}) %collective-permute-start.18) | collective-permute-done | bytes 327712 | tf_op jit(solution)/shard_map/ppermute | solution.py:160
  111.2 0.2 fusion.5
  111.4 0.0 collective-permute-done.15
  111.4 0.4 fusion.8
  111.8 1.0 pad_maximum_fusion
  (12 shorter events, 0.1 us)
Async XLA Ops:
  0.0 39.9 %collective-permute-start.6 = (bf16[512,8192]{1,0:T(8,128)(2,1)}, bf16[512,8192]{1,0:T(8,128)(2,1)}, u32[]{:S(2)}, u32[]{:S(2)}) collective-permute-start(bf16[512,8192]{1,0:T(8,128)(2,1)} %w_ref.9), channel_id=1, source_target_pairs={{0,1},{1,0},{2,3},{3,2},{4,5},{5,4},{6,7},{7,6},{8,9},{9,8},{10,11... | collective-permute-start | bytes 25165832 | tf_op jit(solution)/shard_map/ppermute | solution.py:160
  0.8 4.8 %collective-permute-start = (bf16[2,3,512]{2,0,1:T(2,128)(2,1)S(1)}, bf16[2,3,512]{2,0,1:T(2,128)(2,1)S(1)}, u32[]{:S(2)}, u32[]{:S(2)}) collective-permute-start(bf16[2,3,512]{2,0,1:T(2,128)(2,1)S(1)} %slice.69), channel_id=1, source_target_pairs={{0,16},{16,32},{32,48},{48,64},{64,80},{80,96},{96,112},{1,17},{17... | collective-permute-start | bytes 18440 | tf_op jit(solution)/shard_map/ppermute | solution.py:160
  5.6 0.6 copy-start.5
  6.2 16.0 %copy-start.4 = (f32[16,512]{1,0:T(8,128)S(1)}, f32[16,512]{1,0:T(8,128)}, u32[]{:S(2)}) copy-start(f32[16,512]{1,0:T(8,128)} %rate_ref.3) | copy-start | bytes 98308
  12.5 5.5 %collective-permute-start.3 = (f32[16,512]{1,0:T(8,128)}, f32[16,512]{1,0:T(8,128)S(1)}, u32[]{:S(2)}, u32[]{:S(2)}) collective-permute-start(f32[16,512]{1,0:T(8,128)} %get-tuple-element.28), channel_id=1, source_target_pairs={{0,48},{16,0},{32,16},{48,32},{64,112},{80,64},{96,80},{112,96},{1... | collective-permute-start | bytes 98312 | tf_op jit(solution)/shard_map/ppermute | solution.py:160
  16.1 5.6 %collective-permute-start.2 = (f32[16,512]{1,0:T(8,128)}, f32[16,512]{1,0:T(8,128)S(1)}, u32[]{:S(2)}, u32[]{:S(2)}) collective-permute-start(f32[16,512]{1,0:T(8,128)} %get-tuple-element.28), channel_id=1, source_target_pairs={{0,32},{16,48},{32,0},{48,16},{64,96},{80,112},{96,64},{112,80},{1... | collective-permute-start | bytes 98312 | tf_op jit(solution)/shard_map/ppermute | solution.py:160
  16.9 5.3 %collective-permute-start.1 = (f32[16,512]{1,0:T(8,128)}, f32[16,512]{1,0:T(8,128)S(1)}, u32[]{:S(2)}, u32[]{:S(2)}) collective-permute-start(f32[16,512]{1,0:T(8,128)} %get-tuple-element.28), channel_id=1, source_target_pairs={{0,16},{16,32},{32,48},{48,0},{64,80},{80,96},{96,112},{112,64},{1... | collective-permute-start | bytes 98312 | tf_op jit(solution)/shard_map/ppermute | solution.py:160
  23.0 5.5 %collective-permute-start.4 = (f32[16,512]{1,0:T(8,128)S(1)}, f32[16,512]{1,0:T(8,128)S(1)}, u32[]{:S(2)}, u32[]{:S(2)}) collective-permute-start(f32[16,512]{1,0:T(8,128)S(1)} %multiply_add_fusion.1), channel_id=1, source_target_pairs={{0,64},{16,80},{32,96},{48,112},{1,65},{17,81},{33,97},{49,113},{2... | collective-permute-start | bytes 98312 | tf_op jit(solution)/shard_map/ppermute | solution.py:160
  37.0 2.9 %collective-permute-start.5 = (bf16[1024,512]{1,0:T(8,128)(2,1)}, bf16[1024,512]{1,0:T(8,128)(2,1)S(1)}, u32[]{:S(2)}, u32[]{:S(2)}) collective-permute-start(bf16[1024,512]{1,0:T(8,128)(2,1)} %gated.1.g_ref), channel_id=1, source_target_pairs={{0,1},{1,0},{2,3},{3,2},{4,5},{5,4},{6,7},{7,6},{8,9},{9,8},{10,11... | collective-permute-start | bytes 3145736 | tf_op jit(solution)/shard_map/ppermute | solution.py:160
  39.9 8.7 %copy-start.2 = (bf16[1024,512]{1,0:T(8,128)(2,1)}, bf16[1024,512]{1,0:T(8,128)(2,1)S(1)}, u32[]{:S(2)}) copy-start(bf16[1024,512]{1,0:T(8,128)(2,1)S(1)} %collective-permute-done.5.gp_ref) | copy-start | bytes 3145732
  39.9 1.6 %copy-start = (bf16[1024,512]{1,0:T(8,128)(2,1)S(1)}, bf16[1024,512]{1,0:T(8,128)(2,1)}, u32[]{:S(2)}) copy-start(bf16[1024,512]{1,0:T(8,128)(2,1)} %gated.1.g_ref) | copy-start | bytes 3145732
  41.5 7.1 %copy-start.1 = (bf16[1024,512]{1,0:T(8,128)(2,1)S(1)}, bf16[1024,512]{1,0:T(8,128)(2,1)}, u32[]{:S(2)}) copy-start(bf16[1024,512]{1,0:T(8,128)(2,1)} %gated.1.g_ref) | copy-start | bytes 3145732
  45.3 19.8 %collective-permute-start.7 = (bf16[2,352,512]{2,1,0:T(8,128)(2,1)S(1)}, bf16[2,352,512]{2,1,0:T(8,128)(2,1)S(1)}, u32[]{:S(2)}, u32[]{:S(2)}) collective-permute-start(bf16[2,352,512]{2,1,0:T(8,128)(2,1)S(1)} %get-tuple-element.29), channel_id=1, source_target_pairs={{0,4},{1,5},{2,6},{3,7},{4,8},{5,9},{6,10},{7,11},{8,12},{9,13},{1... | collective-permute-start | bytes 2162696 | tf_op jit(solution)/shard_map/ppermute | solution.py:160
  46.9 19.2 %collective-permute-start.8 = (bf16[2,352,512]{2,1,0:T(8,128)(2,1)S(1)}, bf16[2,352,512]{2,1,0:T(8,128)(2,1)S(1)}, u32[]{:S(2)}, u32[]{:S(2)}) collective-permute-start(bf16[2,352,512]{2,1,0:T(8,128)(2,1)S(1)} %get-tuple-element.30), channel_id=1, source_target_pairs={{0,12},{1,13},{2,14},{3,15},{4,0},{5,1},{6,2},{7,3},{8,4},{9,5},{1... | collective-permute-start | bytes 2162696 | tf_op jit(solution)/shard_map/ppermute | solution.py:160
  52.6 32.3 %collective-permute-start.16 = (bf16[4,320,512]{2,1,0:T(8,128)(2,1)S(1)}, bf16[4,320,512]{2,1,0:T(8,128)(2,1)S(1)}, u32[]{:S(2)}, u32[]{:S(2)}) collective-permute-start(bf16[4,320,512]{2,1,0:T(8,128)(2,1)S(1)} %project.9), channel_id=1, source_target_pairs={{0,2},{1,3},{2,0},{3,1},{4,6},{5,7},{6,4},{7,5},{8,10},{9,11},{10,... | collective-permute-start | bytes 3932168 | tf_op jit(solution)/shard_map/ppermute | solution.py:160
  61.8 6.9 %copy-start.3 = (bf16[1024,512]{1,0:T(8,128)(2,1)S(1)}, bf16[1024,512]{1,0:T(8,128)(2,1)}, u32[]{:S(2)}) copy-start(bf16[1024,512]{1,0:T(8,128)(2,1)} %copy-done.2) | copy-start | bytes 3145732
  61.8 16.5 %collective-permute-start.11 = (bf16[352,512]{1,0:T(8,128)(2,1)S(1)}, bf16[352,512]{1,0:T(8,128)(2,1)S(1)}, u32[]{:S(2)}, u32[]{:S(2)}) collective-permute-start(bf16[352,512]{1,0:T(8,128)(2,1)S(1)} %bitcast.45), channel_id=1, source_target_pairs={{0,4},{1,5},{2,6},{3,7},{4,8},{5,9},{6,10},{7,11},{8,12},{9,13},{1... | collective-permute-start | bytes 1081352 | tf_op jit(solution)/shard_map/ppermute | solution.py:160
  62.2 16.1 %collective-permute-start.12 = (bf16[352,512]{1,0:T(8,128)(2,1)S(1)}, bf16[352,512]{1,0:T(8,128)(2,1)S(1)}, u32[]{:S(2)}, u32[]{:S(2)}) collective-permute-start(bf16[352,512]{1,0:T(8,128)(2,1)S(1)} %bitcast.44), channel_id=1, source_target_pairs={{0,12},{1,13},{2,14},{3,15},{4,0},{5,1},{6,2},{7,3},{8,4},{9,5},{1... | collective-permute-start | bytes 1081352 | tf_op jit(solution)/shard_map/ppermute | solution.py:160
  65.2 16.4 %collective-permute-start.13 = (bf16[352,512]{1,0:T(8,128)(2,1)S(1)}, bf16[352,512]{1,0:T(8,128)(2,1)S(1)}, u32[]{:S(2)}, u32[]{:S(2)}) collective-permute-start(bf16[352,512]{1,0:T(8,128)(2,1)S(1)} %fusion.6), channel_id=1, source_target_pairs={{0,4},{1,5},{2,6},{3,7},{4,8},{5,9},{6,10},{7,11},{8,12},{9,13},{1... | collective-permute-start | bytes 1081352 | tf_op jit(solution)/shard_map/ppermute | solution.py:160
  66.2 15.4 %collective-permute-start.14 = (bf16[352,512]{1,0:T(8,128)(2,1)S(1)}, bf16[352,512]{1,0:T(8,128)(2,1)S(1)}, u32[]{:S(2)}, u32[]{:S(2)}) collective-permute-start(bf16[352,512]{1,0:T(8,128)(2,1)S(1)} %fusion.7), channel_id=1, source_target_pairs={{0,12},{1,13},{2,14},{3,15},{4,0},{5,1},{6,2},{7,3},{8,4},{9,5},{1... | collective-permute-start | bytes 1081352 | tf_op jit(solution)/shard_map/ppermute | solution.py:160
  78.2 24.7 %collective-permute-start.9 = (bf16[2,352,512]{2,1,0:T(8,128)(2,1)S(1)}, bf16[2,352,512]{2,1,0:T(8,128)(2,1)S(1)}, u32[]{:S(2)}, u32[]{:S(2)}) collective-permute-start(bf16[2,352,512]{2,1,0:T(8,128)(2,1)S(1)} %get-tuple-element.32), channel_id=1, source_target_pairs={{0,4},{1,5},{2,6},{3,7},{4,8},{5,9},{6,10},{7,11},{8,12},{9,13},{1... | collective-permute-start | bytes 2162696 | tf_op jit(solution)/shard_map/ppermute | solution.py:160
  78.3 24.6 %collective-permute-start.10 = (bf16[2,352,512]{2,1,0:T(8,128)(2,1)S(1)}, bf16[2,352,512]{2,1,0:T(8,128)(2,1)S(1)}, u32[]{:S(2)}, u32[]{:S(2)}) collective-permute-start(bf16[2,352,512]{2,1,0:T(8,128)(2,1)S(1)} %get-tuple-element.33), channel_id=1, source_target_pairs={{0,12},{1,13},{2,14},{3,15},{4,0},{5,1},{6,2},{7,3},{8,4},{9,5},{1... | collective-permute-start | bytes 2162696 | tf_op jit(solution)/shard_map/ppermute | solution.py:160
  85.1 14.5 %collective-permute-start.17 = (bf16[160,512]{1,0:T(8,128)(2,1)S(1)}, bf16[160,512]{1,0:T(8,128)(2,1)S(1)}, u32[]{:S(2)}, u32[]{:S(2)}) collective-permute-start(bf16[160,512]{1,0:T(8,128)(2,1)S(1)} %get-tuple-element.49), channel_id=1, source_target_pairs={{0,4},{1,5},{2,6},{3,7},{4,8},{5,9},{6,10},{7,11},{8,12},{9,13},{1... | collective-permute-start | bytes 491528 | tf_op jit(solution)/shard_map/ppermute | solution.py:160
  85.4 14.2 %collective-permute-start.19 = (bf16[160,512]{1,0:T(8,128)(2,1)S(1)}, bf16[160,512]{1,0:T(8,128)(2,1)S(1)}, u32[]{:S(2)}, u32[]{:S(2)}) collective-permute-start(bf16[160,512]{1,0:T(8,128)(2,1)S(1)} %get-tuple-element.50), channel_id=1, source_target_pairs={{0,12},{1,13},{2,14},{3,15},{4,0},{5,1},{6,2},{7,3},{8,4},{9,5},{1... | collective-permute-start | bytes 491528 | tf_op jit(solution)/shard_map/ppermute | solution.py:160
  88.8 22.6 %collective-permute-start.15 = (bf16[2,352,512]{2,1,0:T(8,128)(2,1)S(1)}, bf16[2,352,512]{2,1,0:T(8,128)(2,1)S(1)}, u32[]{:S(2)}, u32[]{:S(2)}) collective-permute-start(bf16[2,352,512]{2,1,0:T(8,128)(2,1)S(1)} %pad_maximum_fusion.1), channel_id=1, source_target_pairs={{0,2},{1,3},{2,0},{3,1},{4,6},{5,7},{6,4},{7,5},{8,10},{9,11},{10,... | collective-permute-start | bytes 2162696 | tf_op jit(solution)/shard_map/ppermute | solution.py:160
  99.8 8.0 %collective-permute-start.20 = (bf16[320,512]{1,0:T(8,128)(2,1)S(1)}, bf16[320,512]{1,0:T(8,128)(2,1)S(1)}, u32[]{:S(2)}, u32[]{:S(2)}) collective-permute-start(bf16[320,512]{1,0:T(8,128)(2,1)S(1)} %pad_maximum_fusion.3), channel_id=1, source_target_pairs={{0,12},{1,13},{2,14},{3,15},{4,0},{5,1},{6,2},{7,3},{8,4},{9,5},{1... | collective-permute-start | bytes 983048 | tf_op jit(solution)/shard_map/ppermute | solution.py:160
  102.8 8.4 %collective-permute-start.18 = (bf16[320,512]{1,0:T(8,128)(2,1)S(1)}, bf16[320,512]{1,0:T(8,128)(2,1)S(1)}, u32[]{:S(2)}, u32[]{:S(2)}) collective-permute-start(bf16[320,512]{1,0:T(8,128)(2,1)S(1)} %pad_maximum_fusion.2), channel_id=1, source_target_pairs={{0,4},{1,5},{2,6},{3,7},{4,8},{5,9},{6,10},{7,11},{8,12},{9,13},{1... | collective-permute-start | bytes 983048 | tf_op jit(solution)/shard_map/ppermute | solution.py:160

commit v5 on v4

--- a/solution.py
+++ b/solution.py
@@ -11,6 +11,7 @@
 LANES = 128
 SUBS = 8
 PAD = 8
+STATE_ROWS, FIRST, LAST, PAYLOAD = 16, 16, 20, 32
 
 
 def row_scan(values, factor, rows):
@@ -27,64 +28,107 @@
     for s in range(SUBS):
         at = s * (steps + PAD) + PAD
         rows_ref[pl.ds(at, steps), :] = x_ref[pl.ds(s * steps, steps), :].astype(f32)
-        before = x_ref[pl.ds(s * steps - 16, 16), :].astype(f32)[14:] if s else halo.astype(f32)
+        before = x_ref[pl.ds(s * steps - 16, 16), :].astype(f32)[14:] if s else halo
         rows_ref[pl.ds(at - 2, 2), :] = before
 
 
-def state_kernel(key_ref, val_ref, halo_ref, sf_ref, rate_ref, p_ref, own_ref, start_ref, xs):
+def state_kernel(key_ref, val_ref, query_ref, sf_ref, rate_ref, p_ref, told_ref, start_ref, xs, told):
     n_modes = rate_ref.shape[0]
     steps = p_ref.shape[0]
     rows = lax.broadcasted_iota(jnp.int32, (SUBS, LANES), 0)
+    none = jnp.zeros((2, LANES), f32)
     for j in range(2):
-        fill(xs.at[j], (key_ref, val_ref)[j].at[0], halo_ref[j + 1], steps)
+        fill(xs.at[j], (key_ref, val_ref)[j].at[0], none, steps)
     w = [[jnp.broadcast_to(sf_ref[k, j + 1][None], (SUBS, LANES)) for k in range(3)] for j in range(2)]
     decay = [jnp.exp(-jnp.broadcast_to(rate_ref[pl.ds(r, 1), :], (SUBS, LANES))) for r in range(n_modes)]
 
     def tap(j, at):
-        return xs[j, pl.ds(8 + at, SUBS, stride=steps + PAD), :]
-
-    def body(t, carry):
+        return xs[j, pl.ds(PAD + at, SUBS, stride=steps + PAD), :]
+
+    def body(t, carry, first=False):
         k1, k2, v1, v2, state = carry
         k0, v0 = tap(0, t), tap(1, t)
         key = w[0][0] * k0 + w[0][1] * k1 + w[0][2] * k2
         val = w[1][0] * v0 + w[1][1] * v1 + w[1][2] * v2
         p = (key * val).astype(bf16).astype(f32)
+        if first:
+            p = jnp.where(rows >= 1, p, 0.0)
         p_ref[t] = p
         state = tuple(a * s + p for a, s in zip(decay, state))
         return (k0, k1, v0, v1, state)
 
     zero = jnp.zeros((SUBS, LANES), f32)
-    init = (tap(0, -1), tap(0, -2), tap(1, -1), tap(1, -2), (zero,) * n_modes)
-    state = lax.fori_loop(0, steps, body, init, unroll=8)[4]
+    carry = (tap(0, -1), tap(0, -2), tap(1, -1), tap(1, -2), (zero,) * n_modes)
+    carry = body(1, body(0, carry, True), True)
+    state = lax.fori_loop(2, steps, body, carry, unroll=7)[4]
     for r in range(n_modes):
         rate = jnp.broadcast_to(rate_ref[pl.ds(r, 1), :], (SUBS, LANES))
         scanned = row_scan(state[r], jnp.exp(-rate * steps), rows)
-        own_ref[pl.ds(r, 1), :] = scanned[SUBS - 1 :]
+        told[pl.ds(r, 1), :] = scanned[SUBS - 1 :]
         start_ref[r] = jnp.where(rows >= 1, pltpu.roll(scanned, 1, axis=0), 0.0)
-
-
-def gate_kernel(x_ref, halo_ref, sf_ref, rate_ref, res_ref, p_ref, start_ref, enter_ref, out_ref, xs, ys):
+    end = (SUBS - 1) * (steps + PAD) + PAD + steps
+    told[pl.ds(LAST, PAYLOAD - LAST), :] = jnp.zeros((PAYLOAD - LAST, LANES), f32)
+    told[pl.ds(LAST, 2), :] = query_ref[0].astype(f32)[14:]
+    for j in range(2):
+        told[pl.ds(FIRST + 2 * j, 2), :] = xs[j, pl.ds(PAD, 2), :]
+        told[pl.ds(LAST + 2 + 2 * j, 2), :] = xs[j, pl.ds(end - 2, 2), :]
+    told_ref[...] = told[...].astype(bf16)
+
+
+def gate_kernel(at_ref, x_ref, sf_ref, rate_ref, res_ref, p_ref, start_ref, *refs):
+    told_refs, (out_ref, xs, ys, told) = refs[:-4], refs[-4:]
     n_modes = rate_ref.shape[0]
     steps = p_ref.shape[0]
-    rows = lax.broadcasted_iota(jnp.int32, (SUBS, LANES), 0).astype(f32)
-    fill(xs, x_ref.at[0], halo_ref[0], steps)
+    n_tok = SUBS * steps
+    me = at_ref[0]
+    rows = lax.broadcasted_iota(jnp.int32, (SUBS, LANES), 0)
+
+    told[0] = jnp.zeros((PAYLOAD, LANES), f32)
+    for n, ref in enumerate(told_refs):
+        told[1 + neighbour(me, n)] = ref[...].astype(f32)
+
+    def first_products(j):
+        taps = []
+        for i in range(2):
+            row = lambda slot, at: told[slot, pl.ds(at, 1), :]
+            x = [row(j, LAST + 2 + 2 * i), row(j, LAST + 3 + 2 * i), row(1 + j, FIRST + 2 * i), row(1 + j, FIRST + 1 + 2 * i)]
+            w = [sf_ref[k, i + 1][None] for k in range(3)]
+            taps.append([w[0] * x[t + 2] + w[1] * x[t + 1] + w[2] * x[t] for t in range(2)])
+        return [(taps[0][t] * taps[1][t]).astype(bf16).astype(f32) for t in range(2)]
+
+    rates = rate_ref[...]
+    late = [jnp.exp(-rates * (n_tok - 1 - t)) for t in range(2)]
+    enter_all = jnp.zeros_like(rates)
+    for j in range(len(told_refs) - 1):
+        p0, p1 = first_products(j)
+        ended = told[1 + j, :n_modes, :] + late[0] * p0 + late[1] * p1
+        gap = (jnp.maximum(me - 1 - j, 0) * n_tok).astype(f32)
+        enter_all = enter_all + jnp.where(j < me, jnp.exp(-rates * gap), 0.0) * ended
+    told[0, pl.ds(0, n_modes), :] = enter_all
+    p_first = [jnp.broadcast_to(p, (SUBS, LANES)) for p in first_products(me)]
+
+    fill(xs, x_ref.at[0], told[me, pl.ds(LAST, 2), :], steps)
     w = [jnp.broadcast_to(sf_ref[k, 0][None], (SUBS, LANES)) for k in range(3)]
     decay, gain, state0 = [], [], []
     for r in range(n_modes):
         rate = jnp.broadcast_to(rate_ref[pl.ds(r, 1), :], (SUBS, LANES))
-        enter = jnp.broadcast_to(enter_ref[pl.ds(r, 1), :], (SUBS, LANES))
+        enter = jnp.broadcast_to(told[0, pl.ds(r, 1), :], (SUBS, LANES))
         decay.append(jnp.exp(-rate))
         gain.append(jnp.broadcast_to(res_ref[pl.ds(r, 1), :], (SUBS, LANES)))
-        state0.append(start_ref[r] + jnp.exp(-rate * steps * rows) * enter)
+        passed = (rows * steps).astype(f32)
+        mine = jnp.exp(-rate * (passed - 1.0)) * p_first[0] + jnp.exp(-rate * (passed - 2.0)) * p_first[1]
+        state0.append(start_ref[r] + jnp.exp(-rate * passed) * enter + jnp.where(rows >= 1, mine, 0.0))
 
     def tap(at):
-        return xs[pl.ds(8 + at, SUBS, stride=steps + PAD), :]
-
-    def body(t, carry):
+        return xs[pl.ds(PAD + at, SUBS, stride=steps + PAD), :]
+
+    def body(t, carry, first=None):
         x1, x2, state = carry
         x0 = tap(t)
         gate = w[0] * x0 + w[1] * x1 + w[2] * x2
         p = p_ref[t]
+        if first is not None:
+            p = jnp.where(rows >= 1, p, first)
         state = tuple(a * s + p for a, s in zip(decay, state))
         parts = [c * s for c, s in zip(gain, state)]
         while len(parts) > 1:
@@ -92,43 +136,50 @@
         ys[pl.ds(t, SUBS, stride=steps + PAD), :] = gate * parts[0]
         return (x0, x1, state)
 
-    lax.fori_loop(0, steps, body, (tap(-1), tap(-2), tuple(state0)), unroll=4)
+    carry = (tap(-1), tap(-2), tuple(state0))
+    carry = body(1, body(0, carry, p_first[0]), p_first[1])
+    lax.fori_loop(2, steps, body, carry, unroll=6)
     for s in range(SUBS):
         out_ref[pl.ds(s * steps, steps), :] = ys[pl.ds(s * (steps + PAD), steps), :].astype(bf16)
 
 
-def states(x, halo, sf, rate):
+def neighbour(me, n):
+    return (me // 4 + n // 4) % 2 * 4 + (me + 8 - n) % 4
+
+
+def states(x, sf, rate):
     _, n_tok, width = x.shape
     modes = rate.shape[0]
     steps = n_tok // SUBS
     col = lambda g: (0, g)
+    three = lambda g: (0, 0, g)
     return pl.pallas_call(
         state_kernel,
         grid=(width // LANES,),
         in_specs=[
             pl.BlockSpec((1, n_tok, LANES), lambda g: (1, 0, g)),
             pl.BlockSpec((1, n_tok, LANES), lambda g: (2, 0, g)),
-            pl.BlockSpec((3, 2, LANES), lambda g: (0, 0, g)),
-            pl.BlockSpec((3, 3, LANES), lambda g: (0, 0, g)),
+            pl.BlockSpec((1, 16, LANES), lambda g: (0, n_tok // 16 - 1, g)),
+            pl.BlockSpec((3, 3, LANES), three),
             pl.BlockSpec((modes, LANES), col),
         ],
         out_specs=[
-            pl.BlockSpec((steps, SUBS, LANES), lambda g: (0, 0, g)),
-            pl.BlockSpec((modes, LANES), col),
-            pl.BlockSpec((modes, SUBS, LANES), lambda g: (0, 0, g)),
+            pl.BlockSpec((steps, SUBS, LANES), three),
+            pl.BlockSpec((PAYLOAD, LANES), col),
+            pl.BlockSpec((modes, SUBS, LANES), three),
         ],
         out_shape=[
             jax.ShapeDtypeStruct((steps, SUBS, width), f32),
-            jax.ShapeDtypeStruct((modes, width), f32),
+            jax.ShapeDtypeStruct((PAYLOAD, width), bf16),
             jax.ShapeDtypeStruct((modes, SUBS, width), f32),
         ],
-        scratch_shapes=[pltpu.VMEM((2, n_tok + SUBS * PAD, LANES), f32)],
-        compiler_params=pltpu.CompilerParams(vmem_limit_bytes=59 << 20),
+        scratch_shapes=[pltpu.VMEM((2, n_tok + SUBS * PAD, LANES), f32), pltpu.VMEM((PAYLOAD, LANES), f32)],
+        compiler_params=pltpu.CompilerParams(vmem_limit_bytes=60 << 20),
         name="states",
-    )(x, x, halo, sf, rate)
-
-
-def gated(x, halo, sf, rate, res, p, start, enter):
+    )(x, x, x, sf, rate)
+
+
+def gated(at, x, sf, rate, res, p, start, told):
     _, n_tok, width = x.shape
     modes = rate.shape[0]
     steps = n_tok // SUBS
@@ -138,21 +189,25 @@
         gate_kernel,
         grid=(width // LANES,),
         in_specs=[
+            pl.BlockSpec(memory_space=pltpu.SMEM),
             pl.BlockSpec((1, n_tok, LANES), three),
-            pl.BlockSpec((1, 2, LANES), three),
             pl.BlockSpec((3, 3, LANES), three),
             pl.BlockSpec((modes, LANES), col),
             pl.BlockSpec((modes, LANES), col),
             pl.BlockSpec((steps, SUBS, LANES), three),
             pl.BlockSpec((modes, SUBS, LANES), three),
-            pl.BlockSpec((modes, LANES), col),
-        ],
+        ]
+        + [pl.BlockSpec((PAYLOAD, LANES), col)] * len(told),
         out_specs=pl.BlockSpec((n_tok, LANES), col),
         out_shape=jax.ShapeDtypeStruct((n_tok, width), bf16),
-        scratch_shapes=[pltpu.VMEM((n_tok + SUBS * PAD, LANES), f32), pltpu.VMEM((n_tok + SUBS * PAD, LANES), f32)],
-        compiler_params=pltpu.CompilerParams(vmem_limit_bytes=59 << 20),
+        scratch_shapes=[
+            pltpu.VMEM((n_tok + SUBS * PAD, LANES), f32),
+            pltpu.VMEM((n_tok + SUBS * PAD, LANES), f32),
+            pltpu.VMEM((len(told) + 1, PAYLOAD, LANES), f32),
+        ],
+        compiler_params=pltpu.CompilerParams(vmem_limit_bytes=60 << 20),
         name="gated",
-    )(x, halo, sf, rate, res, p, start, enter)
+    )(at, x, sf, rate, res, p, start, *told)
 
 
 def spread(x, axis, target):
@@ -172,22 +227,8 @@
     return spread(x, "ch", lambda i: (i + 4 * by) % 16)
 
 
-def to_x(x, by):
-    return spread(x, "ctx", lambda i: i // 4 * 4 + (i + by) % 4)
-
-
-def entering_state(own, rate, n_tok):
-    at = lax.axis_index("ctx") % 4
-    behind = [own] + [to_x(own, k) for k in (1, 2, 3)]
-    near = jnp.zeros_like(own)
-    whole = jnp.zeros_like(own)
-    for k, state in enumerate(behind):
-        if k:
-            near = near + jnp.where(at >= k, jnp.exp(-rate * (n_tok * (k - 1))) * state, 0.0)
-        ahead = ((3 - (at - k)) % 4).astype(f32)
-        whole = whole + jnp.exp(-rate * (n_tok * ahead)) * state
-    before = spread(whole, "ctx", lambda i: i + 4 if i < 4 else None)
-    return near + jnp.exp(-rate * (n_tok * at.astype(f32))) * before
+def to_block(x, n):
+    return spread(x, "ctx", lambda i: (i // 4 + n // 4) % 2 * 4 + (i + n) % 4)
 
 
 def project_kernel(plan, n_added, cols_ref, g_ref, gp_ref, w_ref, wp_ref, *refs):
@@ -217,7 +258,7 @@
             out_refs[out][slot] = acc.astype(bf16)
 
 
-def project(operands, plan, counts, added=()):
+def project(operands, plan, counts, added=(), limit=50):
     cols, g, gp, w, wp = operands
     n_tok, depth = g.shape
     slots = [0] * len(counts)
@@ -241,7 +282,7 @@
             pltpu.SemaphoreType.DMA((2,)),
             pltpu.SemaphoreType.DMA((len(plan), 2)),
         ],
-        compiler_params=pltpu.CompilerParams(vmem_limit_bytes=50 << 20),
+        compiler_params=pltpu.CompilerParams(vmem_limit_bytes=limit << 20),
         name="project",
     )(cols, g, gp, w, wp, *added)
 
@@ -255,20 +296,20 @@
 
 def per_device(features, short_filter, decay_rate, residues, out_weight):
     n_tok = features.shape[0]
-    halo = spread(features[n_tok - 2 :], "ctx", lambda i: i + 1 if i < 7 else None).transpose(1, 0, 2)
     x = features.transpose(1, 0, 2)
     weight_pair = to_core(out_weight)
     me = lax.axis_index("ch")
     steps = jnp.arange(8, dtype=jnp.int32)
     cols = (me // 4 + steps // 2) % 4 * 4 + (me // 2 + steps) % 2 * 2 + me % 2
-    product, own, start = states(x, halo, short_filter, decay_rate)
-    enter = entering_state(own, decay_rate, float(n_tok))
-    mine = gated(x, halo, short_filter, decay_rate, residues, product, start, enter)
+    product, told, start = states(x, short_filter, decay_rate)
+    heard = [told] + [to_block(told, n) for n in range(1, 8)]
+    at = lax.axis_index("ctx").astype(jnp.int32)[None]
+    mine = gated(at, x, short_filter, decay_rate, residues, product, start, heard)
     operands = (cols, mine, to_core(mine), out_weight, weight_pair)
     n_y = n_tok - Z_TOK
     a, b, z = 0, n_y // 2, n_y
 
-    up2, down2 = project(operands, [((2, dz), [(a, 0), (b, 1)]) for dz in (1, 0)], [b, b])
+    up2, down2 = project(operands, [((2, dz), [(a, 0), (b, 1)]) for dz in (1, 0)], [b, b], limit=59)
     up2, down2 = to_y(up2, 1), to_y(down2, -1)
     (far,) = project(operands, [((dy, 1), [(z, 0)]) for dy in range(4)], [Z_TOK])
     far = to_far_z(far)
@@ -287,7 +328,8 @@
         [up2, down2],
     )
     rise, fall = to_y(rise, 1), to_y(fall, -1)
-    (near,) = project(operands, [((dy, 0), [(z, 0)]) for dy in range(4)], [Z_TOK])
+    last = (cols, lax.optimization_barrier((mine, stay_a))[0]) + operands[2:]
+    (near,) = project(last, [((dy, 0), [(z, 0)]) for dy in range(4)], [Z_TOK])
     up, down, up_more, down_more = lax.optimization_barrier((up, down, up_more, down_more))
     over = to_far_z(jnp.stack([total(keep_a[0], up_more, down), total(keep_b[0], up, down_more)]))
     rise, fall = lax.optimization_barrier((rise, fall))

time: 114 us -> 111 us (0.974)
  starting transfers between devices: 39.3 us -> 35.8 us
  Pallas kernels: 37.1 us -> 39.7 us
    ppermute x21 -> x23, starting transfers between devices: 39.3 us -> 35.8 us  [spread(): return lax.ppermute(x, axis, [(i, j) for i, j in pairs if j is not None])]
    pallas_call x5, Pallas kernels: 22.8 us -> 24.7 us  [project(): pl.pallas_call(functools.partial(project_kernel, laid, len(added)), in_sp...]
    add x2 -> x0, other arithmetic: 1.43 us -> none  [the longest x1 0.79 us: entering_state(): whole = whole + jnp.exp(-rate * (n_tok * ahead)) * state]
    unnamed x12 -> x26, local copies, waits for them, and re-layouts: 2.21 us -> 2.78 us
    ppermute x21 -> x23, waiting for transfers between devices: 29.3 us -> 29.2 us  [spread(): return lax.ppermute(x, axis, [(i, j) for i, j in pairs if j is not None])]
  transfers between devices with their start and end apart: 21 -> 23, of which waited for: 10 -> 10; matrix products, arithmetic and copies ran while one was open for 3% -> 1% of each run, Pallas kernels for 30% -> 31%
where the time goes in v5:
time: 111 us
  Pallas kernels  39.7 us (36%)
  starting transfers between devices  35.8 us (32%)
  waiting for transfers between devices  29.2 us (26%)
  other arithmetic  3.03 us (3%)
  local copies, waits for them, and re-layouts  2.78 us (3%)
    ppermute x23, starting transfers between devices, spread(): return lax.ppermute(x, axis, [(i, j) for i, j in pairs if j is not None])  35.8 us
    ppermute x23, waiting for transfers between devices, spread(): return lax.ppermute(x, axis, [(i, j) for i, j in pairs if j is not None])  29.2 us
    pallas_call x5, Pallas kernels, project(): pl.pallas_call(functools.partial(project_kernel, laid, len(added)), in_sp...  24.7 us
    pallas_call x1, Pallas kernels, gated(): pl.pallas_call(gate_kernel, grid=(width // LANES,), in_specs=[pl.BlockSpe...  8.66 us
    pallas_call x1, Pallas kernels, states(): pl.pallas_call(state_kernel, grid=(width // LANES,), in_specs=[pl.BlockSp...  6.38 us
    unnamed x26, local copies, waits for them, and re-layouts  2.78 us
  transfers between devices with their start and end apart: 23, of which 10 were waited for; matrix products, arithmetic and copies ran while one was open for 1% of the time, Pallas kernels for 31%

profile of v5, /device:TPU:0, one launch (start us, length us, event | category | flops | bytes accessed | tf_op | source)
XLA Modules:
  0.0 110.8 jit_solution(4086282935224329222)
XLA Ops:
  0.0 0.0 collective-permute-start.8
  0.0 6.4 %states.1 = (f32[128,8,512]{2,1,0:T(8,128)}, bf16[32,512]{1,0:T(8,128)(2,1)}, f32[16,8,512]{2,1,0:T(8,128)}) custom-call(bf16[3,1024,512]{2,1,0:T(8,128)(2,1)} %bitcast.46, bf16[3,1024,512]{2,1,0:T(8,128)(2,1)} %bitcast.47, bf16[3,1024,512]{2,1,0:T(8,128)(2,1)} %bitcast.48, f32[3,3,512]{2,1,0:T(4,128)} %sf_ref.3, f32[16,512]{1,0:T(8,128)} %rate_ref.3), custom_call_target="tpu_custom_call" | custom-call | tf_op jit(solution)/shard_map/states/pallas_call | solution.py:156
  6.4 4.2 %collective-permute-start.6 = (bf16[32,512]{1,0:T(8,128)(2,1)}, bf16[32,512]{1,0:T(8,128)(2,1)S(1)}, u32[]{:S(2)}, u32[]{:S(2)}) collective-permute-start(bf16[32,512]{1,0:T(8,128)(2,1)} %get-tuple-element.29.refs_0_), channel_id=1, source_target_pairs={{0,112},{16,64},{32,80},{48,96},{64,48},{80,0},{96,16},{112,32},{1... | collective-permute-start | bytes 98312 | tf_op jit(solution)/shard_map/ppermute | solution.py:215
  10.6 0.3 collective-permute-start.5
  10.9 2.2 %collective-permute-start.4 = (bf16[32,512]{1,0:T(8,128)(2,1)}, bf16[32,512]{1,0:T(8,128)(2,1)S(1)}, u32[]{:S(2)}, u32[]{:S(2)}) collective-permute-start(bf16[32,512]{1,0:T(8,128)(2,1)} %get-tuple-element.29.refs_0_), channel_id=1, source_target_pairs={{0,80},{16,96},{32,112},{48,64},{64,16},{80,32},{96,48},{112,0},{1... | collective-permute-start | bytes 98312 | tf_op jit(solution)/shard_map/ppermute | solution.py:215
  13.2 0.1 collective-permute-start.3
  13.3 0.0 collective-permute-done.6.refs_7_
  13.3 2.4 %collective-permute-start.2 = (bf16[32,512]{1,0:T(8,128)(2,1)}, bf16[32,512]{1,0:T(8,128)(2,1)S(1)}, u32[]{:S(2)}, u32[]{:S(2)}) collective-permute-start(bf16[32,512]{1,0:T(8,128)(2,1)} %get-tuple-element.29.refs_0_), channel_id=1, source_target_pairs={{0,48},{16,0},{32,16},{48,32},{64,112},{80,64},{96,80},{112,96},{1... | collective-permute-start | bytes 98312 | tf_op jit(solution)/shard_map/ppermute | solution.py:215
  15.6 1.5 %collective-permute-done.5.refs_6_ = bf16[32,512]{1,0:T(8,128)(2,1)S(1)} collective-permute-done((bf16[32,512]{1,0:T(8,128)(2,1)}, bf16[32,512]{1,0:T(8,128)(2,1)S(1)}, u32[]{:S(2)}, u32[]{:S(2)}) %collective-permute-start.5) | collective-permute-done | bytes 32800 | tf_op jit(solution)/shard_map/ppermute | solution.py:215
  17.1 0.9 collective-permute-start.1
  18.1 0.0 collective-permute-done.4.refs_5_
  18.1 1.0 collective-permute-start
  19.1 0.0 collective-permute-done.3.refs_4_
  19.1 0.0 collective-permute-done.2.refs_3_
  19.1 3.6 %collective-permute-done.1.refs_2_ = bf16[32,512]{1,0:T(8,128)(2,1)S(1)} collective-permute-done((bf16[32,512]{1,0:T(8,128)(2,1)}, bf16[32,512]{1,0:T(8,128)(2,1)S(1)}, u32[]{:S(2)}, u32[]{:S(2)}) %collective-permute-start.1) | collective-permute-done | bytes 32800 | tf_op jit(solution)/shard_map/ppermute | solution.py:215
  22.8 0.7 collective-permute-done.refs_1_
  23.5 0.6 copy-done.12
  24.0 8.7 %gated.1.g_ref = bf16[1024,512]{1,0:T(8,128)(2,1)} custom-call(s32[1]{0:T(128)} %bitcast.at_ref, bf16[3,1024,512]{2,1,0:T(8,128)(2,1)} %bitcast.49, f32[3,3,512]{2,1,0:T(4,128)} %sf_ref.3, f32[16,512]{1,0:T(8,128)} %rate_ref.3, f32[16,512]{1,0:T(8,128)} %res_ref.1, f32[128,8,512]{2,1,0:T(8,128)} %get-tuple-element.27.p_ref, ...), custom_call_target="tpu_custom_call" | custom-call | tf_op jit(solution)/shard_map/gated/pallas_call | solution.py:188
  32.7 0.1 collective-permute-start.7
  32.8 0.5 fusion.23.cols_ref
  33.3 2.3 %collective-permute-done.7.gp_ref = bf16[1024,512]{1,0:T(8,128)(2,1)S(1)} collective-permute-done((bf16[1024,512]{1,0:T(8,128)(2,1)}, bf16[1024,512]{1,0:T(8,128)(2,1)S(1)}, u32[]{:S(2)}, u32[]{:S(2)}) %collective-permute-start.7) | collective-permute-done | bytes 1048608 | tf_op jit(solution)/shard_map/ppermute | solution.py:215
  35.6 0.0 collective-permute-done.8.wp_ref
  35.6 1.0 copy-done.2
  36.6 5.5 %project.5 = (bf16[2,352,512]{2,1,0:T(8,128)(2,1)}, bf16[2,352,512]{2,1,0:T(8,128)(2,1)}) custom-call(s32[8]{0:T(128)} %fusion.23.cols_ref, bf16[1024,512]{1,0:T(8,128)(2,1)} %gated.1.g_ref, bf16[1024,512]{1,0:T(8,128)(2,1)} %copy-done.2, bf16[512,8192]{1,0:T(8,128)(2,1)} %w_ref.9, bf16[512,8192]{1,0:T(8,128)(2,1)} %collective-permute-done.8.wp_ref), custom_call_target="tpu_custom_call" | custom-call | tf_op jit(solution)/shard_map/project/pallas_call | solution.py:274
  42.1 3.0 %collective-permute-start.10 = (bf16[2,352,512]{2,1,0:T(8,128)(2,1)}, bf16[2,352,512]{2,1,0:T(8,128)(2,1)S(1)}, u32[]{:S(2)}, u32[]{:S(2)}) collective-permute-start(bf16[2,352,512]{2,1,0:T(8,128)(2,1)} %get-tuple-element.31), channel_id=1, source_target_pairs={{0,12},{1,13},{2,14},{3,15},{4,0},{5,1},{6,2},{7,3},{8,4},{9,5},{1... | collective-permute-start | bytes 2162696 | tf_op jit(solution)/shard_map/ppermute | solution.py:215
  45.1 0.0 collective-permute-start.9
  45.2 1.2 %copy-done.3 = bf16[1024,512]{1,0:T(8,128)(2,1)S(1)} copy-done((bf16[1024,512]{1,0:T(8,128)(2,1)S(1)}, bf16[1024,512]{1,0:T(8,128)(2,1)}, u32[]{:S(2)}) %copy-start.3) | copy-done | bytes 1048600
  46.4 4.0 %project.9 = bf16[4,320,512]{2,1,0:T(8,128)(2,1)S(1)} custom-call(s32[8]{0:T(128)S(1)} %copy-done.5, bf16[1024,512]{1,0:T(8,128)(2,1)S(1)} %copy-done, bf16[1024,512]{1,0:T(8,128)(2,1)S(1)} %copy-done.3, bf16[512,8192]{1,0:T(8,128)(2,1)} %w_ref.9, bf16[512,8192]{1,0:T(8,128)(2,1)} %collective-permute-done.8.wp_ref), custom_call_target="tpu_custom_call" | custom-call | tf_op jit(solution)/shard_map/project/pallas_call | solution.py:274
  50.4 3.7 %collective-permute-start.18 = (bf16[4,320,512]{2,1,0:T(8,128)(2,1)S(1)}, bf16[4,320,512]{2,1,0:T(8,128)(2,1)S(1)}, u32[]{:S(2)}, u32[]{:S(2)}) collective-permute-start(bf16[4,320,512]{2,1,0:T(8,128)(2,1)S(1)} %project.9), channel_id=1, source_target_pairs={{0,2},{1,3},{2,0},{3,1},{4,6},{5,7},{6,4},{7,5},{8,10},{9,11},{10,... | collective-permute-start | bytes 3932168 | tf_op jit(solution)/shard_map/ppermute | solution.py:215
  54.1 5.5 %project.7 = (bf16[1,352,512]{2,1,0:T(8,128)(2,1)S(1)}, bf16[1,352,512]{2,1,0:T(8,128)(2,1)S(1)}, bf16[1,352,512]{2,1,0:T(8,128)(2,1)S(1)}, bf16[1,352,512]{2,1,...) custom-call(s32[8]{0:T(128)S(1)} %copy-done.5, bf16[1024,512]{1,0:T(8,128)(2,1)S(1)} %copy-done, ...), custom_call_target="tpu_custom_call" | custom-call | tf_op jit(solution)/shard_map/project/pallas_call | solution.py:274
  59.6 0.7 collective-permute-start.13
  60.3 2.7 %collective-permute-start.14 = (bf16[352,512]{1,0:T(8,128)(2,1)S(1)}, bf16[352,512]{1,0:T(8,128)(2,1)S(1)}, u32[]{:S(2)}, u32[]{:S(2)}) collective-permute-start(bf16[352,512]{1,0:T(8,128)(2,1)S(1)} %bitcast.44), channel_id=1, source_target_pairs={{0,12},{1,13},{2,14},{3,15},{4,0},{5,1},{6,2},{7,3},{8,4},{9,5},{1... | collective-permute-start | bytes 1081352 | tf_op jit(solution)/shard_map/ppermute | solution.py:215
  63.0 0.0 collective-permute-done.10.refs_1_
  63.0 0.1 fusion.7
  63.1 2.0 %collective-permute-start.16 = (bf16[352,512]{1,0:T(8,128)(2,1)S(1)}, bf16[352,512]{1,0:T(8,128)(2,1)S(1)}, u32[]{:S(2)}, u32[]{:S(2)}) collective-permute-start(bf16[352,512]{1,0:T(8,128)(2,1)S(1)} %fusion.7), channel_id=1, source_target_pairs={{0,12},{1,13},{2,14},{3,15},{4,0},{5,1},{6,2},{7,3},{8,4},{9,5},{1... | collective-permute-start | bytes 1081352 | tf_op jit(solution)/shard_map/ppermute | solution.py:215
  65.1 0.5 collective-permute-done.9.refs_0_
  65.6 0.1 fusion.6
  65.7 0.0 copy-start.1
  65.7 0.3 collective-permute-start.15
  66.0 5.7 %project.6 = (bf16[2,352,512]{2,1,0:T(8,128)(2,1)S(1)}, bf16[2,352,512]{2,1,0:T(8,128)(2,1)S(1)}, bf16[1,352,512]{2,1,0:T(8,128)(2,1)S(1)}, bf16[1,352,512]{2,1,0:T(8,128)(2,1)S(1)}) custom-call(s32[8]{0:T(128)S(1)} %copy-done.5, bf16[1024,512]{1,0:T(8,128)(2,1)} %gated.1.g_ref, bf16[1024,512]{1,0:T(8,128)(2,1)} %copy-done.2, bf16[512,8192]{1,0:T(8,128)(2,1)} %w_ref.9, ...), custom_call_target="tpu_custom_call" | custom-call | tf_op jit(solution)/shard_map/project/pallas_call | solution.py:274
  71.7 4.0 %project.8 = bf16[4,320,512]{2,1,0:T(8,128)(2,1)S(1)} custom-call(s32[8]{0:T(128)S(1)} %copy-done.5, bf16[1024,512]{1,0:T(8,128)(2,1)S(1)} %copy-done.1, bf16[1024,512]{1,0:T(8,128)(2,1)S(1)} %copy-done.4, bf16[512,8192]{1,0:T(8,128)(2,1)} %w_ref.9, bf16[512,8192]{1,0:T(8,128)(2,1)} %collective-permute-done.8.wp_ref), custom_call_target="tpu_custom_call" | custom-call | tf_op jit(solution)/shard_map/project/pallas_call | solution.py:274
  75.7 0.1 collective-permute-start.11
  75.8 0.0 collective-permute-done.14
  75.8 3.2 %collective-permute-start.12 = (bf16[2,352,512]{2,1,0:T(8,128)(2,1)S(1)}, bf16[2,352,512]{2,1,0:T(8,128)(2,1)S(1)}, u32[]{:S(2)}, u32[]{:S(2)}) collective-permute-start(bf16[2,352,512]{2,1,0:T(8,128)(2,1)S(1)} %get-tuple-element.34), channel_id=1, source_target_pairs={{0,12},{1,13},{2,14},{3,15},{4,0},{5,1},{6,2},{7,3},{8,4},{9,5},{1... | collective-permute-start | bytes 2162696 | tf_op jit(solution)/shard_map/ppermute | solution.py:215
  79.0 2.0 %collective-permute-done.15 = bf16[352,512]{1,0:T(8,128)(2,1)S(1)} collective-permute-done((bf16[352,512]{1,0:T(8,128)(2,1)S(1)}, bf16[352,512]{1,0:T(8,128)(2,1)S(1)}, u32[]{:S(2)}, u32[]{:S(2)}) %collective-permute-start.15) | collective-permute-done | bytes 360480 | tf_op jit(solution)/shard_map/ppermute | solution.py:215
  81.0 1.9 %collective-permute-done.18 = bf16[4,320,512]{2,1,0:T(8,128)(2,1)S(1)} collective-permute-done((bf16[4,320,512]{2,1,0:T(8,128)(2,1)S(1)}, bf16[4,320,512]{2,1,0:T(8,128)(2,1)S(1)}, u32[]{:S(2)}, u32[]{:S(2)}) %collective-permute-start.18) | collective-permute-done | bytes 1310752 | tf_op jit(solution)/shard_map/ppermute | solution.py:215
  82.9 0.2 fusion.14
  83.1 0.4 collective-permute-start.19
  83.5 2.9 %collective-permute-start.21 = (bf16[160,512]{1,0:T(8,128)(2,1)S(1)}, bf16[160,512]{1,0:T(8,128)(2,1)S(1)}, u32[]{:S(2)}, u32[]{:S(2)}) collective-permute-start(bf16[160,512]{1,0:T(8,128)(2,1)S(1)} %get-tuple-element.52), channel_id=1, source_target_pairs={{0,12},{1,13},{2,14},{3,15},{4,0},{5,1},{6,2},{7,3},{8,4},{9,5},{1... | collective-permute-start | bytes 491528 | tf_op jit(solution)/shard_map/ppermute | solution.py:215
  86.4 0.3 fusion.10
  86.7 0.1 pad_maximum_fusion.1
  86.8 3.3 %collective-permute-start.17 = (bf16[2,352,512]{2,1,0:T(8,128)(2,1)S(1)}, bf16[2,352,512]{2,1,0:T(8,128)(2,1)S(1)}, u32[]{:S(2)}, u32[]{:S(2)}) collective-permute-start(bf16[2,352,512]{2,1,0:T(8,128)(2,1)S(1)} %pad_maximum_fusion.1), channel_id=1, source_target_pairs={{0,2},{1,3},{2,0},{3,1},{4,6},{5,7},{6,4},{7,5},{8,10},{9,11},{10,... | collective-permute-start | bytes 2162696 | tf_op jit(solution)/shard_map/ppermute | solution.py:215
  90.1 8.7 %collective-permute-done.19 = bf16[160,512]{1,0:T(8,128)(2,1)S(1)} collective-permute-done((bf16[160,512]{1,0:T(8,128)(2,1)S(1)}, bf16[160,512]{1,0:T(8,128)(2,1)S(1)}, u32[]{:S(2)}, u32[]{:S(2)}) %collective-permute-start.19) | collective-permute-done | bytes 163872 | tf_op jit(solution)/shard_map/ppermute | solution.py:215
  98.9 0.0 collective-permute-done.21
  98.9 0.1 fusion.13
  99.0 1.7 %collective-permute-start.22 = (bf16[320,512]{1,0:T(8,128)(2,1)S(1)}, bf16[320,512]{1,0:T(8,128)(2,1)S(1)}, u32[]{:S(2)}, u32[]{:S(2)}) collective-permute-start(bf16[320,512]{1,0:T(8,128)(2,1)S(1)} %pad_maximum_fusion.3), channel_id=1, source_target_pairs={{0,12},{1,13},{2,14},{3,15},{4,0},{5,1},{6,2},{7,3},{8,4},{9,5},{1... | collective-permute-start | bytes 983048 | tf_op jit(solution)/shard_map/ppermute | solution.py:215
  100.8 0.5 collective-permute-start.20
  101.2 0.0 collective-permute-done.11
  101.2 0.0 collective-permute-done.12
  101.2 6.5 %collective-permute-done.22 = bf16[320,512]{1,0:T(8,128)(2,1)S(1)} collective-permute-done((bf16[320,512]{1,0:T(8,128)(2,1)S(1)}, bf16[320,512]{1,0:T(8,128)(2,1)S(1)}, u32[]{:S(2)}, u32[]{:S(2)}) %collective-permute-start.22) | collective-permute-done | bytes 327712 | tf_op jit(solution)/shard_map/ppermute | solution.py:215
  107.7 1.5 %collective-permute-done.20 = bf16[320,512]{1,0:T(8,128)(2,1)S(1)} collective-permute-done((bf16[320,512]{1,0:T(8,128)(2,1)S(1)}, bf16[320,512]{1,0:T(8,128)(2,1)S(1)}, u32[]{:S(2)}, u32[]{:S(2)}) %collective-permute-start.20) | collective-permute-done | bytes 327712 | tf_op jit(solution)/shard_map/ppermute | solution.py:215
  109.2 0.2 fusion.5
  109.4 0.4 fusion.8
  109.8 1.0 pad_maximum_fusion
  (27 shorter events, 0.1 us)
Async XLA Ops:
  0.0 35.6 %collective-permute-start.8 = (bf16[512,8192]{1,0:T(8,128)(2,1)}, bf16[512,8192]{1,0:T(8,128)(2,1)}, u32[]{:S(2)}, u32[]{:S(2)}) collective-permute-start(bf16[512,8192]{1,0:T(8,128)(2,1)} %w_ref.9), channel_id=1, source_target_pairs={{0,1},{1,0},{2,3},{3,2},{4,5},{5,4},{6,7},{7,6},{8,9},{9,8},{10,11... | collective-permute-start | bytes 25165832 | tf_op jit(solution)/shard_map/ppermute | solution.py:215
  6.4 6.9 %collective-permute-start.6 = (bf16[32,512]{1,0:T(8,128)(2,1)}, bf16[32,512]{1,0:T(8,128)(2,1)S(1)}, u32[]{:S(2)}, u32[]{:S(2)}) collective-permute-start(bf16[32,512]{1,0:T(8,128)(2,1)} %get-tuple-element.29.refs_0_), channel_id=1, source_target_pairs={{0,112},{16,64},{32,80},{48,96},{64,48},{80,0},{96,16},{112,32},{1... | collective-permute-start | bytes 98312 | tf_op jit(solution)/shard_map/ppermute | solution.py:215
  10.6 6.5 %collective-permute-start.5 = (bf16[32,512]{1,0:T(8,128)(2,1)}, bf16[32,512]{1,0:T(8,128)(2,1)S(1)}, u32[]{:S(2)}, u32[]{:S(2)}) collective-permute-start(bf16[32,512]{1,0:T(8,128)(2,1)} %get-tuple-element.29.refs_0_), channel_id=1, source_target_pairs={{0,96},{16,112},{32,64},{48,80},{64,32},{80,48},{96,0},{112,16},{1... | collective-permute-start | bytes 98312 | tf_op jit(solution)/shard_map/ppermute | solution.py:215
  10.9 7.2 %collective-permute-start.4 = (bf16[32,512]{1,0:T(8,128)(2,1)}, bf16[32,512]{1,0:T(8,128)(2,1)S(1)}, u32[]{:S(2)}, u32[]{:S(2)}) collective-permute-start(bf16[32,512]{1,0:T(8,128)(2,1)} %get-tuple-element.29.refs_0_), channel_id=1, source_target_pairs={{0,80},{16,96},{32,112},{48,64},{64,16},{80,32},{96,48},{112,0},{1... | collective-permute-start | bytes 98312 | tf_op jit(solution)/shard_map/ppermute | solution.py:215
  13.2 5.9 %collective-permute-start.3 = (bf16[32,512]{1,0:T(8,128)(2,1)}, bf16[32,512]{1,0:T(8,128)(2,1)S(1)}, u32[]{:S(2)}, u32[]{:S(2)}) collective-permute-start(bf16[32,512]{1,0:T(8,128)(2,1)} %get-tuple-element.29.refs_0_), channel_id=1, source_target_pairs={{0,64},{16,80},{32,96},{48,112},{64,0},{80,16},{96,32},{112,48},{1... | collective-permute-start | bytes 98312 | tf_op jit(solution)/shard_map/ppermute | solution.py:215
  13.3 10.1 %copy-start.6 = (bf16[32,512]{1,0:T(8,128)(2,1)}, bf16[32,512]{1,0:T(8,128)(2,1)S(1)}, u32[]{:S(2)}) copy-start(bf16[32,512]{1,0:T(8,128)(2,1)S(1)} %collective-permute-done.6.refs_7_) | copy-start | bytes 98308
  13.3 5.8 %collective-permute-start.2 = (bf16[32,512]{1,0:T(8,128)(2,1)}, bf16[32,512]{1,0:T(8,128)(2,1)S(1)}, u32[]{:S(2)}, u32[]{:S(2)}) collective-permute-start(bf16[32,512]{1,0:T(8,128)(2,1)} %get-tuple-element.29.refs_0_), channel_id=1, source_target_pairs={{0,48},{16,0},{32,16},{48,32},{64,112},{80,64},{96,80},{112,96},{1... | collective-permute-start | bytes 98312 | tf_op jit(solution)/shard_map/ppermute | solution.py:215
  17.1 6.3 %copy-start.7 = (bf16[32,512]{1,0:T(8,128)(2,1)}, bf16[32,512]{1,0:T(8,128)(2,1)S(1)}, u32[]{:S(2)}) copy-start(bf16[32,512]{1,0:T(8,128)(2,1)S(1)} %collective-permute-done.5.refs_6_) | copy-start | bytes 98308
  17.1 5.6 %collective-permute-start.1 = (bf16[32,512]{1,0:T(8,128)(2,1)}, bf16[32,512]{1,0:T(8,128)(2,1)S(1)}, u32[]{:S(2)}, u32[]{:S(2)}) collective-permute-start(bf16[32,512]{1,0:T(8,128)(2,1)} %get-tuple-element.29.refs_0_), channel_id=1, source_target_pairs={{0,32},{16,48},{32,0},{48,16},{64,96},{80,112},{96,64},{112,80},{1... | collective-permute-start | bytes 98312 | tf_op jit(solution)/shard_map/ppermute | solution.py:215
  18.1 5.3 %copy-start.8 = (bf16[32,512]{1,0:T(8,128)(2,1)}, bf16[32,512]{1,0:T(8,128)(2,1)S(1)}, u32[]{:S(2)}) copy-start(bf16[32,512]{1,0:T(8,128)(2,1)S(1)} %collective-permute-done.4.refs_5_) | copy-start | bytes 98308
  18.1 5.3 %collective-permute-start = (bf16[32,512]{1,0:T(8,128)(2,1)}, bf16[32,512]{1,0:T(8,128)(2,1)S(1)}, u32[]{:S(2)}, u32[]{:S(2)}) collective-permute-start(bf16[32,512]{1,0:T(8,128)(2,1)} %get-tuple-element.29.refs_0_), channel_id=1, source_target_pairs={{0,16},{16,32},{32,48},{48,0},{64,80},{80,96},{96,112},{112,64},{1... | collective-permute-start | bytes 98312 | tf_op jit(solution)/shard_map/ppermute | solution.py:215
  19.1 4.3 %copy-start.9 = (bf16[32,512]{1,0:T(8,128)(2,1)}, bf16[32,512]{1,0:T(8,128)(2,1)S(1)}, u32[]{:S(2)}) copy-start(bf16[32,512]{1,0:T(8,128)(2,1)S(1)} %collective-permute-done.3.refs_4_) | copy-start | bytes 98308
  19.1 4.3 %copy-start.10 = (bf16[32,512]{1,0:T(8,128)(2,1)}, bf16[32,512]{1,0:T(8,128)(2,1)S(1)}, u32[]{:S(2)}) copy-start(bf16[32,512]{1,0:T(8,128)(2,1)S(1)} %collective-permute-done.2.refs_3_) | copy-start | bytes 98308
  22.8 0.7 copy-start.11
  23.4 0.6 copy-start.12
  32.7 3.0 %collective-permute-start.7 = (bf16[1024,512]{1,0:T(8,128)(2,1)}, bf16[1024,512]{1,0:T(8,128)(2,1)S(1)}, u32[]{:S(2)}, u32[]{:S(2)}) collective-permute-start(bf16[1024,512]{1,0:T(8,128)(2,1)} %gated.1.g_ref), channel_id=1, source_target_pairs={{0,1},{1,0},{2,3},{3,2},{4,5},{5,4},{6,7},{7,6},{8,9},{9,8},{10,11... | collective-permute-start | bytes 3145736 | tf_op jit(solution)/shard_map/ppermute | solution.py:215
  33.3 11.8 %copy-start = (bf16[1024,512]{1,0:T(8,128)(2,1)S(1)}, bf16[1024,512]{1,0:T(8,128)(2,1)}, u32[]{:S(2)}) copy-start(bf16[1024,512]{1,0:T(8,128)(2,1)} %gated.1.g_ref) | copy-start | bytes 3145732
  33.3 11.8 %copy-start.5 = (s32[8]{0:T(128)S(1)}, s32[8]{0:T(128)}, u32[]{:S(2)}) copy-start(s32[8]{0:T(128)} %fusion.23.cols_ref) | copy-start | bytes 100
  35.6 1.0 copy-start.2
  42.1 20.9 %collective-permute-start.10 = (bf16[2,352,512]{2,1,0:T(8,128)(2,1)}, bf16[2,352,512]{2,1,0:T(8,128)(2,1)S(1)}, u32[]{:S(2)}, u32[]{:S(2)}) collective-permute-start(bf16[2,352,512]{2,1,0:T(8,128)(2,1)} %get-tuple-element.31), channel_id=1, source_target_pairs={{0,12},{1,13},{2,14},{3,15},{4,0},{5,1},{6,2},{7,3},{8,4},{9,5},{1... | collective-permute-start | bytes 2162696 | tf_op jit(solution)/shard_map/ppermute | solution.py:215
  45.1 20.4 %collective-permute-start.9 = (bf16[2,352,512]{2,1,0:T(8,128)(2,1)}, bf16[2,352,512]{2,1,0:T(8,128)(2,1)S(1)}, u32[]{:S(2)}, u32[]{:S(2)}) collective-permute-start(bf16[2,352,512]{2,1,0:T(8,128)(2,1)} %get-tuple-element.30), channel_id=1, source_target_pairs={{0,4},{1,5},{2,6},{3,7},{4,8},{5,9},{6,10},{7,11},{8,12},{9,13},{1... | collective-permute-start | bytes 2162696 | tf_op jit(solution)/shard_map/ppermute | solution.py:215
  45.1 1.2 %copy-start.3 = (bf16[1024,512]{1,0:T(8,128)(2,1)S(1)}, bf16[1024,512]{1,0:T(8,128)(2,1)}, u32[]{:S(2)}) copy-start(bf16[1024,512]{1,0:T(8,128)(2,1)} %copy-done.2) | copy-start | bytes 3145732
  50.4 32.5 %collective-permute-start.18 = (bf16[4,320,512]{2,1,0:T(8,128)(2,1)S(1)}, bf16[4,320,512]{2,1,0:T(8,128)(2,1)S(1)}, u32[]{:S(2)}, u32[]{:S(2)}) collective-permute-start(bf16[4,320,512]{2,1,0:T(8,128)(2,1)S(1)} %project.9), channel_id=1, source_target_pairs={{0,2},{1,3},{2,0},{3,1},{4,6},{5,7},{6,4},{7,5},{8,10},{9,11},{10,... | collective-permute-start | bytes 3932168 | tf_op jit(solution)/shard_map/ppermute | solution.py:215
  59.6 16.1 %collective-permute-start.13 = (bf16[352,512]{1,0:T(8,128)(2,1)S(1)}, bf16[352,512]{1,0:T(8,128)(2,1)S(1)}, u32[]{:S(2)}, u32[]{:S(2)}) collective-permute-start(bf16[352,512]{1,0:T(8,128)(2,1)S(1)} %bitcast.45), channel_id=1, source_target_pairs={{0,4},{1,5},{2,6},{3,7},{4,8},{5,9},{6,10},{7,11},{8,12},{9,13},{1... | collective-permute-start | bytes 1081352 | tf_op jit(solution)/shard_map/ppermute | solution.py:215
  60.3 15.5 %collective-permute-start.14 = (bf16[352,512]{1,0:T(8,128)(2,1)S(1)}, bf16[352,512]{1,0:T(8,128)(2,1)S(1)}, u32[]{:S(2)}, u32[]{:S(2)}) collective-permute-start(bf16[352,512]{1,0:T(8,128)(2,1)S(1)} %bitcast.44), channel_id=1, source_target_pairs={{0,12},{1,13},{2,14},{3,15},{4,0},{5,1},{6,2},{7,3},{8,4},{9,5},{1... | collective-permute-start | bytes 1081352 | tf_op jit(solution)/shard_map/ppermute | solution.py:215
  63.1 15.9 %collective-permute-start.16 = (bf16[352,512]{1,0:T(8,128)(2,1)S(1)}, bf16[352,512]{1,0:T(8,128)(2,1)S(1)}, u32[]{:S(2)}, u32[]{:S(2)}) collective-permute-start(bf16[352,512]{1,0:T(8,128)(2,1)S(1)} %fusion.7), channel_id=1, source_target_pairs={{0,12},{1,13},{2,14},{3,15},{4,0},{5,1},{6,2},{7,3},{8,4},{9,5},{1... | collective-permute-start | bytes 1081352 | tf_op jit(solution)/shard_map/ppermute | solution.py:215
  65.7 6.0 %copy-start.1 = (bf16[1024,512]{1,0:T(8,128)(2,1)S(1)}, bf16[1024,512]{1,0:T(8,128)(2,1)}, u32[]{:S(2)}) copy-start(bf16[1024,512]{1,0:T(8,128)(2,1)} %gated.1.g_ref) | copy-start | bytes 3145732
  65.7 6.0 %copy-start.4 = (bf16[1024,512]{1,0:T(8,128)(2,1)S(1)}, bf16[1024,512]{1,0:T(8,128)(2,1)}, u32[]{:S(2)}) copy-start(bf16[1024,512]{1,0:T(8,128)(2,1)} %copy-done.2) | copy-start | bytes 3145732
  65.7 15.3 %collective-permute-start.15 = (bf16[352,512]{1,0:T(8,128)(2,1)S(1)}, bf16[352,512]{1,0:T(8,128)(2,1)S(1)}, u32[]{:S(2)}, u32[]{:S(2)}) collective-permute-start(bf16[352,512]{1,0:T(8,128)(2,1)S(1)} %fusion.6), channel_id=1, source_target_pairs={{0,4},{1,5},{2,6},{3,7},{4,8},{5,9},{6,10},{7,11},{8,12},{9,13},{1... | collective-permute-start | bytes 1081352 | tf_op jit(solution)/shard_map/ppermute | solution.py:215
  75.7 25.5 %collective-permute-start.11 = (bf16[2,352,512]{2,1,0:T(8,128)(2,1)S(1)}, bf16[2,352,512]{2,1,0:T(8,128)(2,1)S(1)}, u32[]{:S(2)}, u32[]{:S(2)}) collective-permute-start(bf16[2,352,512]{2,1,0:T(8,128)(2,1)S(1)} %get-tuple-element.33), channel_id=1, source_target_pairs={{0,4},{1,5},{2,6},{3,7},{4,8},{5,9},{6,10},{7,11},{8,12},{9,13},{1... | collective-permute-start | bytes 2162696 | tf_op jit(solution)/shard_map/ppermute | solution.py:215
  75.8 25.4 %collective-permute-start.12 = (bf16[2,352,512]{2,1,0:T(8,128)(2,1)S(1)}, bf16[2,352,512]{2,1,0:T(8,128)(2,1)S(1)}, u32[]{:S(2)}, u32[]{:S(2)}) collective-permute-start(bf16[2,352,512]{2,1,0:T(8,128)(2,1)S(1)} %get-tuple-element.34), channel_id=1, source_target_pairs={{0,12},{1,13},{2,14},{3,15},{4,0},{5,1},{6,2},{7,3},{8,4},{9,5},{1... | collective-permute-start | bytes 2162696 | tf_op jit(solution)/shard_map/ppermute | solution.py:215
  83.1 15.7 %collective-permute-start.19 = (bf16[160,512]{1,0:T(8,128)(2,1)S(1)}, bf16[160,512]{1,0:T(8,128)(2,1)S(1)}, u32[]{:S(2)}, u32[]{:S(2)}) collective-permute-start(bf16[160,512]{1,0:T(8,128)(2,1)S(1)} %get-tuple-element.51), channel_id=1, source_target_pairs={{0,4},{1,5},{2,6},{3,7},{4,8},{5,9},{6,10},{7,11},{8,12},{9,13},{1... | collective-permute-start | bytes 491528 | tf_op jit(solution)/shard_map/ppermute | solution.py:215
  83.5 15.4 %collective-permute-start.21 = (bf16[160,512]{1,0:T(8,128)(2,1)S(1)}, bf16[160,512]{1,0:T(8,128)(2,1)S(1)}, u32[]{:S(2)}, u32[]{:S(2)}) collective-permute-start(bf16[160,512]{1,0:T(8,128)(2,1)S(1)} %get-tuple-element.52), channel_id=1, source_target_pairs={{0,12},{1,13},{2,14},{3,15},{4,0},{5,1},{6,2},{7,3},{8,4},{9,5},{1... | collective-permute-start | bytes 491528 | tf_op jit(solution)/shard_map/ppermute | solution.py:215
  86.8 22.6 %collective-permute-start.17 = (bf16[2,352,512]{2,1,0:T(8,128)(2,1)S(1)}, bf16[2,352,512]{2,1,0:T(8,128)(2,1)S(1)}, u32[]{:S(2)}, u32[]{:S(2)}) collective-permute-start(bf16[2,352,512]{2,1,0:T(8,128)(2,1)S(1)} %pad_maximum_fusion.1), channel_id=1, source_target_pairs={{0,2},{1,3},{2,0},{3,1},{4,6},{5,7},{6,4},{7,5},{8,10},{9,11},{10,... | collective-permute-start | bytes 2162696 | tf_op jit(solution)/shard_map/ppermute | solution.py:215
  99.0 8.7 %collective-permute-start.22 = (bf16[320,512]{1,0:T(8,128)(2,1)S(1)}, bf16[320,512]{1,0:T(8,128)(2,1)S(1)}, u32[]{:S(2)}, u32[]{:S(2)}) collective-permute-start(bf16[320,512]{1,0:T(8,128)(2,1)S(1)} %pad_maximum_fusion.3), channel_id=1, source_target_pairs={{0,12},{1,13},{2,14},{3,15},{4,0},{5,1},{6,2},{7,3},{8,4},{9,5},{1... | collective-permute-start | bytes 983048 | tf_op jit(solution)/shard_map/ppermute | solution.py:215
  100.8 8.4 %collective-permute-start.20 = (bf16[320,512]{1,0:T(8,128)(2,1)S(1)}, bf16[320,512]{1,0:T(8,128)(2,1)S(1)}, u32[]{:S(2)}, u32[]{:S(2)}) collective-permute-start(bf16[320,512]{1,0:T(8,128)(2,1)S(1)} %pad_maximum_fusion.2), channel_id=1, source_target_pairs={{0,4},{1,5},{2,6},{3,7},{4,8},{5,9},{6,10},{7,11},{8,12},{9,13},{1... | collective-permute-start | bytes 983048 | tf_op jit(solution)/shard_map/ppermute | solution.py:215

commit v6 on v5

--- a/solution.py
+++ b/solution.py
@@ -85,7 +85,8 @@
 
     told[0] = jnp.zeros((PAYLOAD, LANES), f32)
     for n, ref in enumerate(told_refs):
-        told[1 + neighbour(me, n)] = ref[...].astype(f32)
+        for k in range(2):
+            told[1 + neighbour(me, n, k)] = ref[k].astype(f32)
 
     def first_products(j):
         taps = []
@@ -99,7 +100,7 @@
     rates = rate_ref[...]
     late = [jnp.exp(-rates * (n_tok - 1 - t)) for t in range(2)]
     enter_all = jnp.zeros_like(rates)
-    for j in range(len(told_refs) - 1):
+    for j in range(2 * len(told_refs) - 1):
         p0, p1 = first_products(j)
         ended = told[1 + j, :n_modes, :] + late[0] * p0 + late[1] * p1
         gap = (jnp.maximum(me - 1 - j, 0) * n_tok).astype(f32)
@@ -143,8 +144,8 @@
         out_ref[pl.ds(s * steps, steps), :] = ys[pl.ds(s * (steps + PAD), steps), :].astype(bf16)
 
 
-def neighbour(me, n):
-    return (me // 4 + n // 4) % 2 * 4 + (me + 8 - n) % 4
+def neighbour(me, n, k):
+    return (me // 4 + k) % 2 * 4 + (me + 4 - n) % 4
 
 
 def states(x, sf, rate):
@@ -197,13 +198,13 @@
             pl.BlockSpec((steps, SUBS, LANES), three),
             pl.BlockSpec((modes, SUBS, LANES), three),
         ]
-        + [pl.BlockSpec((PAYLOAD, LANES), col)] * len(told),
+        + [pl.BlockSpec((2, PAYLOAD, LANES), three)] * len(told),
         out_specs=pl.BlockSpec((n_tok, LANES), col),
         out_shape=jax.ShapeDtypeStruct((n_tok, width), bf16),
         scratch_shapes=[
             pltpu.VMEM((n_tok + SUBS * PAD, LANES), f32),
             pltpu.VMEM((n_tok + SUBS * PAD, LANES), f32),
-            pltpu.VMEM((len(told) + 1, PAYLOAD, LANES), f32),
+            pltpu.VMEM((2 * len(told) + 1, PAYLOAD, LANES), f32),
         ],
         compiler_params=pltpu.CompilerParams(vmem_limit_bytes=60 << 20),
         name="gated",
@@ -227,8 +228,12 @@
     return spread(x, "ch", lambda i: (i + 4 * by) % 16)
 
 
-def to_block(x, n):
-    return spread(x, "ctx", lambda i: (i // 4 + n // 4) % 2 * 4 + (i + n) % 4)
+def to_x(x, by):
+    return spread(x, "ctx", lambda i: i // 4 * 4 + (i + by) % 4)
+
+
+def to_near_z(x):
+    return spread(x, "ctx", lambda i: (i + 4) % 8)
 
 
 def project_kernel(plan, n_added, cols_ref, g_ref, gp_ref, w_ref, wp_ref, *refs):
@@ -258,7 +263,7 @@
             out_refs[out][slot] = acc.astype(bf16)
 
 
-def project(operands, plan, counts, added=(), limit=50):
+def project(operands, plan, counts, added=()):
     cols, g, gp, w, wp = operands
     n_tok, depth = g.shape
     slots = [0] * len(counts)
@@ -282,7 +287,7 @@
             pltpu.SemaphoreType.DMA((2,)),
             pltpu.SemaphoreType.DMA((len(plan), 2)),
         ],
-        compiler_params=pltpu.CompilerParams(vmem_limit_bytes=limit << 20),
+        compiler_params=pltpu.CompilerParams(vmem_limit_bytes=50 << 20),
         name="project",
     )(cols, g, gp, w, wp, *added)
 
@@ -302,18 +307,20 @@
     steps = jnp.arange(8, dtype=jnp.int32)
     cols = (me // 4 + steps // 2) % 4 * 4 + (me // 2 + steps) % 2 * 2 + me % 2
     product, told, start = states(x, short_filter, decay_rate)
-    heard = [told] + [to_block(told, n) for n in range(1, 8)]
+    told = jnp.stack([told, to_near_z(told)])
+    heard = [told] + [to_x(told, n) for n in (1, 2, 3)]
     at = lax.axis_index("ctx").astype(jnp.int32)[None]
     mine = gated(at, x, short_filter, decay_rate, residues, product, start, heard)
     operands = (cols, mine, to_core(mine), out_weight, weight_pair)
     n_y = n_tok - Z_TOK
     a, b, z = 0, n_y // 2, n_y
 
-    up2, down2 = project(operands, [((2, dz), [(a, 0), (b, 1)]) for dz in (1, 0)], [b, b], limit=59)
-    up2, down2 = to_y(up2, 1), to_y(down2, -1)
-    (far,) = project(operands, [((dy, 1), [(z, 0)]) for dy in range(4)], [Z_TOK])
-    far = to_far_z(far)
-
+    up2, down2, far = project(
+        operands,
+        [((2, 1), [(a, 0), (b, 1), (z, 2)]), ((2, 0), [(a, 0), (b, 1)])] + [((dy, 1), [(z, 2)]) for dy in (3, 1, 0)],
+        [b, b, Z_TOK],
+    )
+    up2, down2, far = to_y(up2, 1), to_y(down2, -1), to_far_z(far)
     up, down, up_more, down_more, keep_a, keep_b = project(
         operands,
         [((1, 1), [(b, 0), (a, 2)]), ((3, 1), [(a, 1), (b, 3)]), ((0, 1), [(a, 4), (b, 5)])],
@@ -321,27 +328,30 @@
     )
     up, down = to_y(up[0], 1), to_y(down[0], -1)
     up_more, down_more = to_y(total(up_more[0], up2[0]), 1), to_y(total(down_more[0], down2[0]), -1)
-    rise, fall, stay_a, stay_b = project(
+    rise, fall, rise_more, fall_more, stay_a, stay_b = project(
         operands,
-        [((1, 0), [(b, 0), (a, 0, (0, 1))]), ((3, 0), [(a, 1), (b, 1, (1, 1))]), ((0, 0), [(a, 2), (b, 3)])],
-        [b] * 4,
+        [((1, 0), [(b, 0), (a, 2, (0, 1))]), ((3, 0), [(a, 1), (b, 3, (1, 1))]), ((0, 0), [(a, 4), (b, 5)])],
+        [b] * 6,
         [up2, down2],
     )
-    rise, fall = to_y(rise, 1), to_y(fall, -1)
     last = (cols, lax.optimization_barrier((mine, stay_a))[0]) + operands[2:]
-    (near,) = project(last, [((dy, 0), [(z, 0)]) for dy in range(4)], [Z_TOK])
+    (near,) = project(last, [((dy, 0), [(z, 0)]) for dy in (2, 3, 1, 0)], [Z_TOK])
+    half = Z_TOK // 2
+    s2a, s2b = total(near[0, :half], far[0, :half]), total(near[0, half:], far[0, half:])
+    rise, fall = to_y(rise[0], 1), to_y(fall[0], -1)
+    rise_more, fall_more, _, _ = lax.optimization_barrier((rise_more[0], fall_more[0], s2a, s2b))
+    s2a, s2b = to_y(s2a, 1), to_y(s2b, -1)
+    rise_more, fall_more = to_y(rise_more, 1), to_y(fall_more, -1)
     up, down, up_more, down_more = lax.optimization_barrier((up, down, up_more, down_more))
     over = to_far_z(jnp.stack([total(keep_a[0], up_more, down), total(keep_b[0], up, down_more)]))
-    rise, fall = lax.optimization_barrier((rise, fall))
-    done_a = total(stay_a[0], rise[1], fall[0], over[0])
-    done_b = total(stay_b[0], rise[0], fall[1], over[1])
-
-    half = Z_TOK // 2
-    s2a, s2b = to_y(total(near[2, :half], far[2, :half]), 1), to_y(total(near[2, half:], far[2, half:]), -1)
-    s3 = jnp.concatenate([total(near[3, :half], far[3, :half]), total(near[3, half:], far[3, half:], s2b)])
-    s1 = jnp.concatenate([total(near[1, :half], far[1, :half], s2a), total(near[1, half:], far[1, half:])])
+    rise, fall, rise_more, fall_more = lax.optimization_barrier((rise, fall, rise_more, fall_more))
+    done_a = total(stay_a[0], rise_more, fall, over[0])
+    done_b = total(stay_b[0], rise, fall_more, over[1])
+
+    s3 = jnp.concatenate([total(near[1, :half], far[1, :half]), total(near[1, half:], far[1, half:], s2b)])
+    s1 = jnp.concatenate([total(near[2, :half], far[2, :half], s2a), total(near[2, half:], far[2, half:])])
     s1, s3 = to_y(s1, 1), to_y(s3, -1)
-    return jnp.concatenate([done_a, done_b, total(near[0], far[0], s1, s3)])
+    return jnp.concatenate([done_a, done_b, total(near[3], far[3], s1, s3)])
 
 
 def solution(mesh):

time: 111 us -> 107 us (0.964)
  Pallas kernels: 39.7 us -> 36.6 us
    pallas_call x5 -> x4, Pallas kernels: 24.7 us -> 21.8 us  [project(): pl.pallas_call(functools.partial(project_kernel, laid, len(added)), in_sp...]
    ppermute x23 -> x22, starting transfers between devices: 35.8 us -> 34.8 us  [spread(): return lax.ppermute(x, axis, [(i, j) for i, j in pairs if j is not None])]
    ppermute x23 -> x22, waiting for transfers between devices: 29.2 us -> 28.6 us  [spread(): return lax.ppermute(x, axis, [(i, j) for i, j in pairs if j is not None])]
    unnamed x26 -> x18, local copies, waits for them, and re-layouts: 2.78 us -> 2.23 us
  transfers between devices with their start and end apart: 23 -> 22, of which waited for: 10 -> 11; matrix products, arithmetic and copies ran while one was open for 1% -> 2% of each run, Pallas kernels for 31% -> 28%
where the time goes in v6:
time: 107 us; the launch traced here: 106 us
  Pallas kernels  36.6 us (34%)
  starting transfers between devices  34.8 us (33%)
  waiting for transfers between devices  28.6 us (27%)
  other arithmetic  3.27 us (3%)
  local copies, waits for them, and re-layouts  2.23 us (2%)
    ppermute x22, starting transfers between devices, spread(): return lax.ppermute(x, axis, [(i, j) for i, j in pairs if j is not None])  34.8 us
    ppermute x22, waiting for transfers between devices, spread(): return lax.ppermute(x, axis, [(i, j) for i, j in pairs if j is not None])  28.6 us
    pallas_call x4, Pallas kernels, project(): pl.pallas_call(functools.partial(project_kernel, laid, len(added)), in_sp...  21.8 us
    pallas_call x1, Pallas kernels, gated(): pl.pallas_call(gate_kernel, grid=(width // LANES,), in_specs=[pl.BlockSpe...  8.5 us
    pallas_call x1, Pallas kernels, states(): pl.pallas_call(state_kernel, grid=(width // LANES,), in_specs=[pl.BlockSp...  6.38 us
    unnamed x18, local copies, waits for them, and re-layouts  2.23 us
  transfers between devices with their start and end apart: 22, of which 11 were waited for; matrix products, arithmetic and copies ran while one was open for 2% of the time, Pallas kernels for 28%

profile of v6, /device:TPU:0, one launch (start us, length us, event | category | flops | bytes accessed | tf_op | source)
XLA Modules:
  0.0 105.8 jit_solution(11104110243681823842)
XLA Ops:
  0.0 0.0 collective-permute-start.5
  0.0 6.4 %states.1 = (f32[128,8,512]{2,1,0:T(8,128)}, bf16[32,512]{1,0:T(8,128)(2,1)}, f32[16,8,512]{2,1,0:T(8,128)}) custom-call(bf16[3,1024,512]{2,1,0:T(8,128)(2,1)} %bitcast.68, bf16[3,1024,512]{2,1,0:T(8,128)(2,1)} %bitcast.69, bf16[3,1024,512]{2,1,0:T(8,128)(2,1)} %bitcast.70, f32[3,3,512]{2,1,0:T(4,128)} %sf_ref.3, f32[16,512]{1,0:T(8,128)} %rate_ref.3), custom_call_target="tpu_custom_call" | custom-call | tf_op jit(solution)/shard_map/states/pallas_call | solution.py:157
  6.4 2.0 %collective-permute-start = (bf16[32,512]{1,0:T(8,128)(2,1)}, bf16[32,512]{1,0:T(8,128)(2,1)S(1)}, u32[]{:S(2)}, u32[]{:S(2)}) collective-permute-start(bf16[32,512]{1,0:T(8,128)(2,1)} %get-tuple-element.36), channel_id=1, source_target_pairs={{0,64},{16,80},{32,96},{48,112},{64,0},{80,16},{96,32},{112,48},{1... | collective-permute-start | bytes 98312 | tf_op jit(solution)/shard_map/ppermute | solution.py:216
  8.4 2.3 %collective-permute-done = bf16[32,512]{1,0:T(8,128)(2,1)S(1)} collective-permute-done((bf16[32,512]{1,0:T(8,128)(2,1)}, bf16[32,512]{1,0:T(8,128)(2,1)S(1)}, u32[]{:S(2)}, u32[]{:S(2)}) %collective-permute-start) | collective-permute-done | bytes 32800 | tf_op jit(solution)/shard_map/ppermute | solution.py:216
  10.6 0.8 pad_maximum_fusion.4.refs_0_
  11.4 2.8 %collective-permute-start.3 = (bf16[2,32,512]{2,1,0:T(8,128)(2,1)S(1)}, bf16[2,32,512]{2,1,0:T(8,128)(2,1)S(1)}, u32[]{:S(2)}, u32[]{:S(2)}) collective-permute-start(bf16[2,32,512]{2,1,0:T(8,128)(2,1)S(1)} %pad_maximum_fusion.4.refs_0_), channel_id=1, source_target_pairs={{0,48},{16,0},{32,16},{48,32},{64,112},{80,64},{96,80},{112,96},{1... | collective-permute-start | bytes 196616 | tf_op jit(solution)/shard_map/ppermute | solution.py:216
  14.2 0.8 collective-permute-start.2
  15.0 0.9 collective-permute-start.1
  15.9 0.5 collective-permute-done.3.refs_3_
  16.5 3.6 %collective-permute-done.2.refs_2_ = bf16[2,32,512]{2,1,0:T(8,128)(2,1)S(1)} collective-permute-done((bf16[2,32,512]{2,1,0:T(8,128)(2,1)S(1)}, bf16[2,32,512]{2,1,0:T(8,128)(2,1)S(1)}, u32[]{:S(2)}, u32[]{:S(2)}) %collective-permute-start.2) | collective-permute-done | bytes 65568 | tf_op jit(solution)/shard_map/ppermute | solution.py:216
  20.0 0.7 collective-permute-done.1.refs_1_
  20.7 0.0 copy-done.7
  20.7 0.6 copy-done.8
  21.3 8.5 %gated.1.g_ref = bf16[1024,512]{1,0:T(8,128)(2,1)} custom-call(s32[1]{0:T(128)} %bitcast.at_ref, bf16[3,1024,512]{2,1,0:T(8,128)(2,1)} %bitcast.71, f32[3,3,512]{2,1,0:T(4,128)} %sf_ref.3, f32[16,512]{1,0:T(8,128)} %rate_ref.3, f32[16,512]{1,0:T(8,128)} %res_ref.1, f32[128,8,512]{2,1,0:T(8,128)} %get-tuple-element.34.p_ref, ...), custom_call_target="tpu_custom_call" | custom-call | tf_op jit(solution)/shard_map/gated/pallas_call | solution.py:189
  29.8 0.0 collective-permute-start.4
  29.9 2.8 %collective-permute-done.4.gp_ref = bf16[1024,512]{1,0:T(8,128)(2,1)S(1)} collective-permute-done((bf16[1024,512]{1,0:T(8,128)(2,1)}, bf16[1024,512]{1,0:T(8,128)(2,1)S(1)}, u32[]{:S(2)}, u32[]{:S(2)}) %collective-permute-start.4) | collective-permute-done | bytes 1048608 | tf_op jit(solution)/shard_map/ppermute | solution.py:216
  32.7 0.0 collective-permute-done.5.wp_ref
  32.7 1.6 %copy-done = bf16[1024,512]{1,0:T(8,128)(2,1)S(1)} copy-done((bf16[1024,512]{1,0:T(8,128)(2,1)S(1)}, bf16[1024,512]{1,0:T(8,128)(2,1)}, u32[]{:S(2)}) %copy-start) | copy-done | bytes 1048600
  34.3 6.8 %project.4 = (bf16[2,352,512]{2,1,0:T(8,128)(2,1)S(1)}, bf16[2,352,512]{2,1,0:T(8,128)(2,1)S(1)}, bf16[4,320,512]{2,1,0:T(8,128)(2,1)}) custom-call(s32[8]{0:T(128)S(1)} %fusion.25.cols_ref, bf16[1024,512]{1,0:T(8,128)(2,1)S(1)} %copy-done, bf16[1024,512]{1,0:T(8,128)(2,1)S(1)} %collective-permute-done.4.gp_ref, bf16[512,8192]{1,0:T(8,128)(2,1)} %w_ref.7, ...), custom_call_target="tpu_custom_call" | custom-call | tf_op jit(solution)/shard_map/project/pallas_call | solution.py:279
  41.1 1.6 %collective-permute-start.6 = (bf16[2,352,512]{2,1,0:T(8,128)(2,1)S(1)}, bf16[2,352,512]{2,1,0:T(8,128)(2,1)S(1)}, u32[]{:S(2)}, u32[]{:S(2)}) collective-permute-start(bf16[2,352,512]{2,1,0:T(8,128)(2,1)S(1)} %get-tuple-element.37), channel_id=1, source_target_pairs={{0,4},{1,5},{2,6},{3,7},{4,8},{5,9},{6,10},{7,11},{8,12},{9,13},{1... | collective-permute-start | bytes 2162696 | tf_op jit(solution)/shard_map/ppermute | solution.py:216
  42.7 1.7 %collective-permute-start.7 = (bf16[2,352,512]{2,1,0:T(8,128)(2,1)S(1)}, bf16[2,352,512]{2,1,0:T(8,128)(2,1)S(1)}, u32[]{:S(2)}, u32[]{:S(2)}) collective-permute-start(bf16[2,352,512]{2,1,0:T(8,128)(2,1)S(1)} %get-tuple-element.38), channel_id=1, source_target_pairs={{0,12},{1,13},{2,14},{3,15},{4,0},{5,1},{6,2},{7,3},{8,4},{9,5},{1... | collective-permute-start | bytes 2162696 | tf_op jit(solution)/shard_map/ppermute | solution.py:216
  44.4 3.8 %collective-permute-start.10 = (bf16[4,320,512]{2,1,0:T(8,128)(2,1)}, bf16[4,320,512]{2,1,0:T(8,128)(2,1)S(1)}, u32[]{:S(2)}, u32[]{:S(2)}) collective-permute-start(bf16[4,320,512]{2,1,0:T(8,128)(2,1)} %get-tuple-element.45), channel_id=1, source_target_pairs={{0,2},{1,3},{2,0},{3,1},{4,6},{5,7},{6,4},{7,5},{8,10},{9,11},{10,... | collective-permute-start | bytes 3932168 | tf_op jit(solution)/shard_map/ppermute | solution.py:216
  48.2 5.5 %project.7 = (bf16[1,352,512]{2,1,0:T(8,128)(2,1)S(1)}, bf16[1,352,512]{2,1,0:T(8,128)(2,1)S(1)}, bf16[1,352,512]{2,1,0:T(8,128)(2,1)S(1)}, bf16[1,352,512]{2,1,...) custom-call(s32[8]{0:T(128)S(1)} %fusion.25.cols_ref, ...), custom_call_target="tpu_custom_call" | custom-call | tf_op jit(solution)/shard_map/project/pallas_call | solution.py:279
  53.7 0.4 collective-permute-start.13
  54.1 2.9 %collective-permute-start.14 = (bf16[352,512]{1,0:T(8,128)(2,1)S(1)}, bf16[352,512]{1,0:T(8,128)(2,1)S(1)}, u32[]{:S(2)}, u32[]{:S(2)}) collective-permute-start(bf16[352,512]{1,0:T(8,128)(2,1)S(1)} %bitcast.66), channel_id=1, source_target_pairs={{0,12},{1,13},{2,14},{3,15},{4,0},{5,1},{6,2},{7,3},{8,4},{9,5},{1... | collective-permute-start | bytes 1081352 | tf_op jit(solution)/shard_map/ppermute | solution.py:216
  57.0 4.3 %collective-permute-done.6.refs_0_ = bf16[2,352,512]{2,1,0:T(8,128)(2,1)S(1)} collective-permute-done((bf16[2,352,512]{2,1,0:T(8,128)(2,1)S(1)}, bf16[2,352,512]{2,1,0:T(8,128)(2,1)S(1)}, u32[]{:S(2)}, u32[]{:S(2)}) %collective-permute-start.6) | collective-permute-done | bytes 720928 | tf_op jit(solution)/shard_map/ppermute | solution.py:216
  61.3 0.1 fusion.10
  61.4 0.4 collective-permute-start.15
  61.9 0.0 collective-permute-done.7.refs_1_
  61.9 0.1 fusion.11
  62.0 0.0 copy-start.2
  62.0 2.9 %collective-permute-start.16 = (bf16[352,512]{1,0:T(8,128)(2,1)S(1)}, bf16[352,512]{1,0:T(8,128)(2,1)S(1)}, u32[]{:S(2)}, u32[]{:S(2)}) collective-permute-start(bf16[352,512]{1,0:T(8,128)(2,1)S(1)} %fusion.11), channel_id=1, source_target_pairs={{0,12},{1,13},{2,14},{3,15},{4,0},{5,1},{6,2},{7,3},{8,4},{9,5},{1... | collective-permute-start | bytes 1081352 | tf_op jit(solution)/shard_map/ppermute | solution.py:216
  64.9 5.5 %project.5 = (bf16[1,352,512]{2,1,0:T(8,128)(2,1)S(1)}, bf16[1,352,512]{2,1,0:T(8,128)(2,1)S(1)}, bf16[1,352,512]{2,1,0:T(8,128)(2,1)S(1)}, bf16[1,352,512]{2,1,...) custom-call(s32[8]{0:T(128)S(1)} %fusion.25.cols_ref, ...), custom_call_target="tpu_custom_call" | custom-call | tf_op jit(solution)/shard_map/project/pallas_call | solution.py:279
  70.5 4.0 %project.6 = bf16[4,320,512]{2,1,0:T(8,128)(2,1)S(1)} custom-call(s32[8]{0:T(128)S(1)} %fusion.25.cols_ref, bf16[1024,512]{1,0:T(8,128)(2,1)S(1)} %copy-done.2, bf16[1024,512]{1,0:T(8,128)(2,1)S(1)} %copy-done.4, bf16[512,8192]{1,0:T(8,128)(2,1)} %w_ref.7, bf16[512,8192]{1,0:T(8,128)(2,1)} %collective-permute-done.5.wp_ref), custom_call_target="tpu_custom_call" | custom-call | tf_op jit(solution)/shard_map/project/pallas_call | solution.py:279
  74.5 0.0 collective-permute-done.13
  74.5 0.9 collective-permute-start.9
  75.4 0.0 collective-permute-done.14
  75.4 1.2 %collective-permute-start.8 = (bf16[352,512]{1,0:T(8,128)(2,1)S(1)}, bf16[352,512]{1,0:T(8,128)(2,1)S(1)}, u32[]{:S(2)}, u32[]{:S(2)}) collective-permute-start(bf16[352,512]{1,0:T(8,128)(2,1)S(1)} %bitcast.64), channel_id=1, source_target_pairs={{0,4},{1,5},{2,6},{3,7},{4,8},{5,9},{6,10},{7,11},{8,12},{9,13},{1... | collective-permute-start | bytes 1081352 | tf_op jit(solution)/shard_map/ppermute | solution.py:216
  76.6 0.0 collective-permute-done.15
  76.6 0.2 collective-permute-done.16
  76.8 0.3 collective-permute-done.10
  77.1 0.2 fusion.16
  77.3 1.8 %collective-permute-start.18 = (bf16[160,512]{1,0:T(8,128)(2,1)S(1)}, bf16[160,512]{1,0:T(8,128)(2,1)S(1)}, u32[]{:S(2)}, u32[]{:S(2)}) collective-permute-start(bf16[160,512]{1,0:T(8,128)(2,1)S(1)} %get-tuple-element.65), channel_id=1, source_target_pairs={{0,4},{1,5},{2,6},{3,7},{4,8},{5,9},{6,10},{7,11},{8,12},{9,13},{1... | collective-permute-start | bytes 491528 | tf_op jit(solution)/shard_map/ppermute | solution.py:216
  79.0 1.5 %collective-permute-start.20 = (bf16[160,512]{1,0:T(8,128)(2,1)S(1)}, bf16[160,512]{1,0:T(8,128)(2,1)S(1)}, u32[]{:S(2)}, u32[]{:S(2)}) collective-permute-start(bf16[160,512]{1,0:T(8,128)(2,1)S(1)} %get-tuple-element.68), channel_id=1, source_target_pairs={{0,12},{1,13},{2,14},{3,15},{4,0},{5,1},{6,2},{7,3},{8,4},{9,5},{1... | collective-permute-start | bytes 491528 | tf_op jit(solution)/shard_map/ppermute | solution.py:216
  80.6 0.3 fusion.12
  80.9 0.1 pad_maximum_fusion.1
  80.9 3.7 %collective-permute-start.17 = (bf16[2,352,512]{2,1,0:T(8,128)(2,1)S(1)}, bf16[2,352,512]{2,1,0:T(8,128)(2,1)S(1)}, u32[]{:S(2)}, u32[]{:S(2)}) collective-permute-start(bf16[2,352,512]{2,1,0:T(8,128)(2,1)S(1)} %pad_maximum_fusion.1), channel_id=1, source_target_pairs={{0,2},{1,3},{2,0},{3,1},{4,6},{5,7},{6,4},{7,5},{8,10},{9,11},{10,... | collective-permute-start | bytes 2162696 | tf_op jit(solution)/shard_map/ppermute | solution.py:216
  84.7 3.4 %collective-permute-done.18 = bf16[160,512]{1,0:T(8,128)(2,1)S(1)} collective-permute-done((bf16[160,512]{1,0:T(8,128)(2,1)S(1)}, bf16[160,512]{1,0:T(8,128)(2,1)S(1)}, u32[]{:S(2)}, u32[]{:S(2)}) %collective-permute-start.18) | collective-permute-done | bytes 163872 | tf_op jit(solution)/shard_map/ppermute | solution.py:216
  88.1 0.6 collective-permute-start.11
  88.7 0.0 collective-permute-done.20
  88.7 2.6 %collective-permute-start.12 = (bf16[352,512]{1,0:T(8,128)(2,1)S(1)}, bf16[352,512]{1,0:T(8,128)(2,1)S(1)}, u32[]{:S(2)}, u32[]{:S(2)}) collective-permute-start(bf16[352,512]{1,0:T(8,128)(2,1)S(1)} %bitcast.62), channel_id=1, source_target_pairs={{0,12},{1,13},{2,14},{3,15},{4,0},{5,1},{6,2},{7,3},{8,4},{9,5},{1... | collective-permute-start | bytes 1081352 | tf_op jit(solution)/shard_map/ppermute | solution.py:216
  91.3 0.1 fusion.15
  91.5 0.0 collective-permute-done.9
  91.5 0.1 collective-permute-start.21
  91.6 0.0 collective-permute-done.8
  91.6 2.0 %collective-permute-start.19 = (bf16[320,512]{1,0:T(8,128)(2,1)S(1)}, bf16[320,512]{1,0:T(8,128)(2,1)S(1)}, u32[]{:S(2)}, u32[]{:S(2)}) collective-permute-start(bf16[320,512]{1,0:T(8,128)(2,1)S(1)} %pad_maximum_fusion.2), channel_id=1, source_target_pairs={{0,4},{1,5},{2,6},{3,7},{4,8},{5,9},{6,10},{7,11},{8,12},{9,13},{1... | collective-permute-start | bytes 983048 | tf_op jit(solution)/shard_map/ppermute | solution.py:216
  93.6 6.6 %collective-permute-done.11 = bf16[352,512]{1,0:T(8,128)(2,1)S(1)} collective-permute-done((bf16[352,512]{1,0:T(8,128)(2,1)S(1)}, bf16[352,512]{1,0:T(8,128)(2,1)S(1)}, u32[]{:S(2)}, u32[]{:S(2)}) %collective-permute-start.11) | collective-permute-done | bytes 360480 | tf_op jit(solution)/shard_map/ppermute | solution.py:216
  100.2 0.0 collective-permute-done.12
  100.2 3.9 %collective-permute-done.21 = bf16[320,512]{1,0:T(8,128)(2,1)S(1)} collective-permute-done((bf16[320,512]{1,0:T(8,128)(2,1)S(1)}, bf16[320,512]{1,0:T(8,128)(2,1)S(1)}, u32[]{:S(2)}, u32[]{:S(2)}) %collective-permute-start.21) | collective-permute-done | bytes 327712 | tf_op jit(solution)/shard_map/ppermute | solution.py:216
  104.2 0.0 collective-permute-done.19
  104.2 0.2 fusion.9
  104.3 0.0 collective-permute-done.17
  104.3 0.4 fusion.2
  104.7 1.0 pad_maximum_fusion
  (17 shorter events, 0.1 us)
Async XLA Ops:
  0.0 32.7 %collective-permute-start.5 = (bf16[512,8192]{1,0:T(8,128)(2,1)}, bf16[512,8192]{1,0:T(8,128)(2,1)}, u32[]{:S(2)}, u32[]{:S(2)}) collective-permute-start(bf16[512,8192]{1,0:T(8,128)(2,1)} %w_ref.7), channel_id=1, source_target_pairs={{0,1},{1,0},{2,3},{3,2},{4,5},{5,4},{6,7},{7,6},{8,9},{9,8},{10,11... | collective-permute-start | bytes 25165832 | tf_op jit(solution)/shard_map/ppermute | solution.py:216
  6.4 4.3 %collective-permute-start = (bf16[32,512]{1,0:T(8,128)(2,1)}, bf16[32,512]{1,0:T(8,128)(2,1)S(1)}, u32[]{:S(2)}, u32[]{:S(2)}) collective-permute-start(bf16[32,512]{1,0:T(8,128)(2,1)} %get-tuple-element.36), channel_id=1, source_target_pairs={{0,64},{16,80},{32,96},{48,112},{64,0},{80,16},{96,32},{112,48},{1... | collective-permute-start | bytes 98312 | tf_op jit(solution)/shard_map/ppermute | solution.py:216
  11.4 9.3 %copy-start.5 = (bf16[2,32,512]{2,1,0:T(8,128)(2,1)}, bf16[2,32,512]{2,1,0:T(8,128)(2,1)S(1)}, u32[]{:S(2)}) copy-start(bf16[2,32,512]{2,1,0:T(8,128)(2,1)S(1)} %pad_maximum_fusion.4.refs_0_) | copy-start | bytes 196612
  11.4 5.0 %collective-permute-start.3 = (bf16[2,32,512]{2,1,0:T(8,128)(2,1)S(1)}, bf16[2,32,512]{2,1,0:T(8,128)(2,1)S(1)}, u32[]{:S(2)}, u32[]{:S(2)}) collective-permute-start(bf16[2,32,512]{2,1,0:T(8,128)(2,1)S(1)} %pad_maximum_fusion.4.refs_0_), channel_id=1, source_target_pairs={{0,48},{16,0},{32,16},{48,32},{64,112},{80,64},{96,80},{112,96},{1... | collective-permute-start | bytes 196616 | tf_op jit(solution)/shard_map/ppermute | solution.py:216
  14.2 5.8 %collective-permute-start.2 = (bf16[2,32,512]{2,1,0:T(8,128)(2,1)S(1)}, bf16[2,32,512]{2,1,0:T(8,128)(2,1)S(1)}, u32[]{:S(2)}, u32[]{:S(2)}) collective-permute-start(bf16[2,32,512]{2,1,0:T(8,128)(2,1)S(1)} %pad_maximum_fusion.4.refs_0_), channel_id=1, source_target_pairs={{0,32},{16,48},{32,0},{48,16},{64,96},{80,112},{96,64},{112,80},{1... | collective-permute-start | bytes 196616 | tf_op jit(solution)/shard_map/ppermute | solution.py:216
  15.0 5.7 %collective-permute-start.1 = (bf16[2,32,512]{2,1,0:T(8,128)(2,1)S(1)}, bf16[2,32,512]{2,1,0:T(8,128)(2,1)S(1)}, u32[]{:S(2)}, u32[]{:S(2)}) collective-permute-start(bf16[2,32,512]{2,1,0:T(8,128)(2,1)S(1)} %pad_maximum_fusion.4.refs_0_), channel_id=1, source_target_pairs={{0,16},{16,32},{32,48},{48,0},{64,80},{80,96},{96,112},{112,64},{1... | collective-permute-start | bytes 196616 | tf_op jit(solution)/shard_map/ppermute | solution.py:216
  16.5 4.3 %copy-start.6 = (bf16[2,32,512]{2,1,0:T(8,128)(2,1)}, bf16[2,32,512]{2,1,0:T(8,128)(2,1)S(1)}, u32[]{:S(2)}) copy-start(bf16[2,32,512]{2,1,0:T(8,128)(2,1)S(1)} %collective-permute-done.3.refs_3_) | copy-start | bytes 196612
  20.0 0.7 copy-start.7
  20.7 0.6 copy-start.8
  29.8 2.9 %collective-permute-start.4 = (bf16[1024,512]{1,0:T(8,128)(2,1)}, bf16[1024,512]{1,0:T(8,128)(2,1)S(1)}, u32[]{:S(2)}, u32[]{:S(2)}) collective-permute-start(bf16[1024,512]{1,0:T(8,128)(2,1)} %gated.1.g_ref), channel_id=1, source_target_pairs={{0,1},{1,0},{2,3},{3,2},{4,5},{5,4},{6,7},{7,6},{8,9},{9,8},{10,11... | collective-permute-start | bytes 3145736 | tf_op jit(solution)/shard_map/ppermute | solution.py:216
  32.7 8.4 %copy-start.3 = (bf16[1024,512]{1,0:T(8,128)(2,1)}, bf16[1024,512]{1,0:T(8,128)(2,1)S(1)}, u32[]{:S(2)}) copy-start(bf16[1024,512]{1,0:T(8,128)(2,1)S(1)} %collective-permute-done.4.gp_ref) | copy-start | bytes 3145732
  32.7 1.6 %copy-start = (bf16[1024,512]{1,0:T(8,128)(2,1)S(1)}, bf16[1024,512]{1,0:T(8,128)(2,1)}, u32[]{:S(2)}) copy-start(bf16[1024,512]{1,0:T(8,128)(2,1)} %gated.1.g_ref) | copy-start | bytes 3145732
  34.3 13.9 %copy-start.1 = (bf16[1024,512]{1,0:T(8,128)(2,1)S(1)}, bf16[1024,512]{1,0:T(8,128)(2,1)}, u32[]{:S(2)}) copy-start(bf16[1024,512]{1,0:T(8,128)(2,1)} %gated.1.g_ref) | copy-start | bytes 3145732
  41.1 20.3 %collective-permute-start.6 = (bf16[2,352,512]{2,1,0:T(8,128)(2,1)S(1)}, bf16[2,352,512]{2,1,0:T(8,128)(2,1)S(1)}, u32[]{:S(2)}, u32[]{:S(2)}) collective-permute-start(bf16[2,352,512]{2,1,0:T(8,128)(2,1)S(1)} %get-tuple-element.37), channel_id=1, source_target_pairs={{0,4},{1,5},{2,6},{3,7},{4,8},{5,9},{6,10},{7,11},{8,12},{9,13},{1... | collective-permute-start | bytes 2162696 | tf_op jit(solution)/shard_map/ppermute | solution.py:216
  42.7 19.1 %collective-permute-start.7 = (bf16[2,352,512]{2,1,0:T(8,128)(2,1)S(1)}, bf16[2,352,512]{2,1,0:T(8,128)(2,1)S(1)}, u32[]{:S(2)}, u32[]{:S(2)}) collective-permute-start(bf16[2,352,512]{2,1,0:T(8,128)(2,1)S(1)} %get-tuple-element.38), channel_id=1, source_target_pairs={{0,12},{1,13},{2,14},{3,15},{4,0},{5,1},{6,2},{7,3},{8,4},{9,5},{1... | collective-permute-start | bytes 2162696 | tf_op jit(solution)/shard_map/ppermute | solution.py:216
  44.4 32.7 %collective-permute-start.10 = (bf16[4,320,512]{2,1,0:T(8,128)(2,1)}, bf16[4,320,512]{2,1,0:T(8,128)(2,1)S(1)}, u32[]{:S(2)}, u32[]{:S(2)}) collective-permute-start(bf16[4,320,512]{2,1,0:T(8,128)(2,1)} %get-tuple-element.45), channel_id=1, source_target_pairs={{0,2},{1,3},{2,0},{3,1},{4,6},{5,7},{6,4},{7,5},{8,10},{9,11},{10,... | collective-permute-start | bytes 3932168 | tf_op jit(solution)/shard_map/ppermute | solution.py:216
  53.7 20.8 %collective-permute-start.13 = (bf16[352,512]{1,0:T(8,128)(2,1)S(1)}, bf16[352,512]{1,0:T(8,128)(2,1)S(1)}, u32[]{:S(2)}, u32[]{:S(2)}) collective-permute-start(bf16[352,512]{1,0:T(8,128)(2,1)S(1)} %bitcast.67), channel_id=1, source_target_pairs={{0,4},{1,5},{2,6},{3,7},{4,8},{5,9},{6,10},{7,11},{8,12},{9,13},{1... | collective-permute-start | bytes 1081352 | tf_op jit(solution)/shard_map/ppermute | solution.py:216
  54.1 21.3 %collective-permute-start.14 = (bf16[352,512]{1,0:T(8,128)(2,1)S(1)}, bf16[352,512]{1,0:T(8,128)(2,1)S(1)}, u32[]{:S(2)}, u32[]{:S(2)}) collective-permute-start(bf16[352,512]{1,0:T(8,128)(2,1)S(1)} %bitcast.66), channel_id=1, source_target_pairs={{0,12},{1,13},{2,14},{3,15},{4,0},{5,1},{6,2},{7,3},{8,4},{9,5},{1... | collective-permute-start | bytes 1081352 | tf_op jit(solution)/shard_map/ppermute | solution.py:216
  61.4 15.2 %collective-permute-start.15 = (bf16[352,512]{1,0:T(8,128)(2,1)S(1)}, bf16[352,512]{1,0:T(8,128)(2,1)S(1)}, u32[]{:S(2)}, u32[]{:S(2)}) collective-permute-start(bf16[352,512]{1,0:T(8,128)(2,1)S(1)} %fusion.10), channel_id=1, source_target_pairs={{0,4},{1,5},{2,6},{3,7},{4,8},{5,9},{6,10},{7,11},{8,12},{9,13},{1... | collective-permute-start | bytes 1081352 | tf_op jit(solution)/shard_map/ppermute | solution.py:216
  62.0 8.5 %copy-start.2 = (bf16[1024,512]{1,0:T(8,128)(2,1)S(1)}, bf16[1024,512]{1,0:T(8,128)(2,1)}, u32[]{:S(2)}) copy-start(bf16[1024,512]{1,0:T(8,128)(2,1)} %gated.1.g_ref) | copy-start | bytes 3145732
  62.0 8.5 %copy-start.4 = (bf16[1024,512]{1,0:T(8,128)(2,1)S(1)}, bf16[1024,512]{1,0:T(8,128)(2,1)}, u32[]{:S(2)}) copy-start(bf16[1024,512]{1,0:T(8,128)(2,1)} %copy-done.3) | copy-start | bytes 3145732
  62.0 14.8 %collective-permute-start.16 = (bf16[352,512]{1,0:T(8,128)(2,1)S(1)}, bf16[352,512]{1,0:T(8,128)(2,1)S(1)}, u32[]{:S(2)}, u32[]{:S(2)}) collective-permute-start(bf16[352,512]{1,0:T(8,128)(2,1)S(1)} %fusion.11), channel_id=1, source_target_pairs={{0,12},{1,13},{2,14},{3,15},{4,0},{5,1},{6,2},{7,3},{8,4},{9,5},{1... | collective-permute-start | bytes 1081352 | tf_op jit(solution)/shard_map/ppermute | solution.py:216
  74.5 17.0 %collective-permute-start.9 = (bf16[352,512]{1,0:T(8,128)(2,1)S(1)}, bf16[352,512]{1,0:T(8,128)(2,1)S(1)}, u32[]{:S(2)}, u32[]{:S(2)}) collective-permute-start(bf16[352,512]{1,0:T(8,128)(2,1)S(1)} %bitcast.65), channel_id=1, source_target_pairs={{0,12},{1,13},{2,14},{3,15},{4,0},{5,1},{6,2},{7,3},{8,4},{9,5},{1... | collective-permute-start | bytes 1081352 | tf_op jit(solution)/shard_map/ppermute | solution.py:216
  75.4 16.2 %collective-permute-start.8 = (bf16[352,512]{1,0:T(8,128)(2,1)S(1)}, bf16[352,512]{1,0:T(8,128)(2,1)S(1)}, u32[]{:S(2)}, u32[]{:S(2)}) collective-permute-start(bf16[352,512]{1,0:T(8,128)(2,1)S(1)} %bitcast.64), channel_id=1, source_target_pairs={{0,4},{1,5},{2,6},{3,7},{4,8},{5,9},{6,10},{7,11},{8,12},{9,13},{1... | collective-permute-start | bytes 1081352 | tf_op jit(solution)/shard_map/ppermute | solution.py:216
  77.3 10.8 %collective-permute-start.18 = (bf16[160,512]{1,0:T(8,128)(2,1)S(1)}, bf16[160,512]{1,0:T(8,128)(2,1)S(1)}, u32[]{:S(2)}, u32[]{:S(2)}) collective-permute-start(bf16[160,512]{1,0:T(8,128)(2,1)S(1)} %get-tuple-element.65), channel_id=1, source_target_pairs={{0,4},{1,5},{2,6},{3,7},{4,8},{5,9},{6,10},{7,11},{8,12},{9,13},{1... | collective-permute-start | bytes 491528 | tf_op jit(solution)/shard_map/ppermute | solution.py:216
  79.0 9.7 %collective-permute-start.20 = (bf16[160,512]{1,0:T(8,128)(2,1)S(1)}, bf16[160,512]{1,0:T(8,128)(2,1)S(1)}, u32[]{:S(2)}, u32[]{:S(2)}) collective-permute-start(bf16[160,512]{1,0:T(8,128)(2,1)S(1)} %get-tuple-element.68), channel_id=1, source_target_pairs={{0,12},{1,13},{2,14},{3,15},{4,0},{5,1},{6,2},{7,3},{8,4},{9,5},{1... | collective-permute-start | bytes 491528 | tf_op jit(solution)/shard_map/ppermute | solution.py:216
  80.9 23.4 %collective-permute-start.17 = (bf16[2,352,512]{2,1,0:T(8,128)(2,1)S(1)}, bf16[2,352,512]{2,1,0:T(8,128)(2,1)S(1)}, u32[]{:S(2)}, u32[]{:S(2)}) collective-permute-start(bf16[2,352,512]{2,1,0:T(8,128)(2,1)S(1)} %pad_maximum_fusion.1), channel_id=1, source_target_pairs={{0,2},{1,3},{2,0},{3,1},{4,6},{5,7},{6,4},{7,5},{8,10},{9,11},{10,... | collective-permute-start | bytes 2162696 | tf_op jit(solution)/shard_map/ppermute | solution.py:216
  88.1 12.1 %collective-permute-start.11 = (bf16[352,512]{1,0:T(8,128)(2,1)S(1)}, bf16[352,512]{1,0:T(8,128)(2,1)S(1)}, u32[]{:S(2)}, u32[]{:S(2)}) collective-permute-start(bf16[352,512]{1,0:T(8,128)(2,1)S(1)} %bitcast.63), channel_id=1, source_target_pairs={{0,4},{1,5},{2,6},{3,7},{4,8},{5,9},{6,10},{7,11},{8,12},{9,13},{1... | collective-permute-start | bytes 1081352 | tf_op jit(solution)/shard_map/ppermute | solution.py:216
  88.7 11.5 %collective-permute-start.12 = (bf16[352,512]{1,0:T(8,128)(2,1)S(1)}, bf16[352,512]{1,0:T(8,128)(2,1)S(1)}, u32[]{:S(2)}, u32[]{:S(2)}) collective-permute-start(bf16[352,512]{1,0:T(8,128)(2,1)S(1)} %bitcast.62), channel_id=1, source_target_pairs={{0,12},{1,13},{2,14},{3,15},{4,0},{5,1},{6,2},{7,3},{8,4},{9,5},{1... | collective-permute-start | bytes 1081352 | tf_op jit(solution)/shard_map/ppermute | solution.py:216
  91.5 12.6 %collective-permute-start.21 = (bf16[320,512]{1,0:T(8,128)(2,1)S(1)}, bf16[320,512]{1,0:T(8,128)(2,1)S(1)}, u32[]{:S(2)}, u32[]{:S(2)}) collective-permute-start(bf16[320,512]{1,0:T(8,128)(2,1)S(1)} %pad_maximum_fusion.3), channel_id=1, source_target_pairs={{0,12},{1,13},{2,14},{3,15},{4,0},{5,1},{6,2},{7,3},{8,4},{9,5},{1... | collective-permute-start | bytes 983048 | tf_op jit(solution)/shard_map/ppermute | solution.py:216
  91.6 12.5 %collective-permute-start.19 = (bf16[320,512]{1,0:T(8,128)(2,1)S(1)}, bf16[320,512]{1,0:T(8,128)(2,1)S(1)}, u32[]{:S(2)}, u32[]{:S(2)}) collective-permute-start(bf16[320,512]{1,0:T(8,128)(2,1)S(1)} %pad_maximum_fusion.2), channel_id=1, source_target_pairs={{0,4},{1,5},{2,6},{3,7},{4,8},{5,9},{6,10},{7,11},{8,12},{9,13},{1... | collective-permute-start | bytes 983048 | tf_op jit(solution)/shard_map/ppermute | solution.py:216

commit v7 on v6

--- a/solution.py
+++ b/solution.py
@@ -206,7 +206,7 @@
             pltpu.VMEM((n_tok + SUBS * PAD, LANES), f32),
             pltpu.VMEM((2 * len(told) + 1, PAYLOAD, LANES), f32),
         ],
-        compiler_params=pltpu.CompilerParams(vmem_limit_bytes=60 << 20),
+        compiler_params=pltpu.CompilerParams(vmem_limit_bytes=48 << 20),
         name="gated",
     )(at, x, sf, rate, res, p, start, *told)
 
@@ -315,12 +315,10 @@
     n_y = n_tok - Z_TOK
     a, b, z = 0, n_y // 2, n_y
 
-    up2, down2, far = project(
-        operands,
-        [((2, 1), [(a, 0), (b, 1), (z, 2)]), ((2, 0), [(a, 0), (b, 1)])] + [((dy, 1), [(z, 2)]) for dy in (3, 1, 0)],
-        [b, b, Z_TOK],
-    )
-    up2, down2, far = to_y(up2, 1), to_y(down2, -1), to_far_z(far)
+    up2, down2 = project(operands, [((2, dz), [(a, 0), (b, 1)]) for dz in (1, 0)], [b, b])
+    up2, down2 = to_y(up2, 1), to_y(down2, -1)
+    (far,) = project(operands, [((dy, 1), [(z, 0)]) for dy in (0, 1, 2, 3)], [Z_TOK])
+    far = to_far_z(far)
     up, down, up_more, down_more, keep_a, keep_b = project(
         operands,
         [((1, 1), [(b, 0), (a, 2)]), ((3, 1), [(a, 1), (b, 3)]), ((0, 1), [(a, 4), (b, 5)])],
@@ -337,7 +335,7 @@
     last = (cols, lax.optimization_barrier((mine, stay_a))[0]) + operands[2:]
     (near,) = project(last, [((dy, 0), [(z, 0)]) for dy in (2, 3, 1, 0)], [Z_TOK])
     half = Z_TOK // 2
-    s2a, s2b = total(near[0, :half], far[0, :half]), total(near[0, half:], far[0, half:])
+    s2a, s2b = total(near[0, :half], far[2, :half]), total(near[0, half:], far[2, half:])
     rise, fall = to_y(rise[0], 1), to_y(fall[0], -1)
     rise_more, fall_more, _, _ = lax.optimization_barrier((rise_more[0], fall_more[0], s2a, s2b))
     s2a, s2b = to_y(s2a, 1), to_y(s2b, -1)
@@ -348,10 +346,10 @@
     done_a = total(stay_a[0], rise_more, fall, over[0])
     done_b = total(stay_b[0], rise, fall_more, over[1])
 
-    s3 = jnp.concatenate([total(near[1, :half], far[1, :half]), total(near[1, half:], far[1, half:], s2b)])
-    s1 = jnp.concatenate([total(near[2, :half], far[2, :half], s2a), total(near[2, half:], far[2, half:])])
+    s3 = jnp.concatenate([total(near[1, :half], far[3, :half]), total(near[1, half:], far[3, half:], s2b)])
+    s1 = jnp.concatenate([total(near[2, :half], far[1, :half], s2a), total(near[2, half:], far[1, half:])])
     s1, s3 = to_y(s1, 1), to_y(s3, -1)
-    return jnp.concatenate([done_a, done_b, total(near[3], far[3], s1, s3)])
+    return jnp.concatenate([done_a, done_b, total(near[3], far[0], s1, s3)])
 
 
 def solution(mesh):

time: 107 us -> 105 us (0.981); the launches traced: 106 us -> 105 us
  waiting for transfers between devices: 28.6 us -> 24 us
  starting transfers between devices: 34.8 us -> 37.5 us
    ppermute x22, waiting for transfers between devices: 28.6 us -> 24 us  [spread(): return lax.ppermute(x, axis, [(i, j) for i, j in pairs if j is not None])]
    ppermute x22, starting transfers between devices: 34.8 us -> 37.5 us  [spread(): return lax.ppermute(x, axis, [(i, j) for i, j in pairs if j is not None])]
    pallas_call x4 -> x5, Pallas kernels: 21.8 us -> 23.1 us  [project(): pl.pallas_call(functools.partial(project_kernel, laid, len(added)), in_sp...]
  transfers between devices with their start and end apart: 22 -> 22, of which waited for: 11 -> 11; matrix products, arithmetic and copies ran while one was open for 2% -> 2% of each run, Pallas kernels for 28% -> 32%
where the time goes in v7:
time: 105 us
  starting transfers between devices  37.5 us (36%)
  Pallas kernels  37.3 us (36%)
  waiting for transfers between devices  24 us (23%)
  other arithmetic  3.29 us (3%)
  local copies, waits for them, and re-layouts  2.57 us (2%)
    ppermute x22, starting transfers between devices, spread(): return lax.ppermute(x, axis, [(i, j) for i, j in pairs if j is not None])  37.5 us
    ppermute x22, waiting for transfers between devices, spread(): return lax.ppermute(x, axis, [(i, j) for i, j in pairs if j is not None])  24 us
    pallas_call x5, Pallas kernels, project(): pl.pallas_call(functools.partial(project_kernel, laid, len(added)), in_sp...  23.1 us
    pallas_call x1, Pallas kernels, gated(): pl.pallas_call(gate_kernel, grid=(width // LANES,), in_specs=[pl.BlockSpe...  7.8 us
    pallas_call x1, Pallas kernels, states(): pl.pallas_call(state_kernel, grid=(width // LANES,), in_specs=[pl.BlockSp...  6.4 us
    unnamed x18, local copies, waits for them, and re-layouts  2.57 us
  transfers between devices with their start and end apart: 22, of which 11 were waited for; matrix products, arithmetic and copies ran while one was open for 2% of the time, Pallas kernels for 32%

profile of v7, /device:TPU:0, one launch (start us, length us, event | category | flops | bytes accessed | tf_op | source)
XLA Modules:
  0.0 104.9 jit_solution(6629875937021465573)
XLA Ops:
  0.0 0.0 collective-permute-start.5
  0.0 6.4 %states.1 = (f32[128,8,512]{2,1,0:T(8,128)}, bf16[32,512]{1,0:T(8,128)(2,1)}, f32[16,8,512]{2,1,0:T(8,128)}) custom-call(bf16[3,1024,512]{2,1,0:T(8,128)(2,1)} %bitcast.68, bf16[3,1024,512]{2,1,0:T(8,128)(2,1)} %bitcast.69, bf16[3,1024,512]{2,1,0:T(8,128)(2,1)} %bitcast.70, f32[3,3,512]{2,1,0:T(4,128)} %sf_ref.3, f32[16,512]{1,0:T(8,128)} %rate_ref.3), custom_call_target="tpu_custom_call" | custom-call | tf_op jit(solution)/shard_map/states/pallas_call | solution.py:157
  6.4 2.0 %collective-permute-start = (bf16[32,512]{1,0:T(8,128)(2,1)}, bf16[32,512]{1,0:T(8,128)(2,1)S(1)}, u32[]{:S(2)}, u32[]{:S(2)}) collective-permute-start(bf16[32,512]{1,0:T(8,128)(2,1)} %get-tuple-element.35), channel_id=1, source_target_pairs={{0,64},{16,80},{32,96},{48,112},{64,0},{80,16},{96,32},{112,48},{1... | collective-permute-start | bytes 98312 | tf_op jit(solution)/shard_map/ppermute | solution.py:216
  8.4 2.3 %collective-permute-done = bf16[32,512]{1,0:T(8,128)(2,1)S(1)} collective-permute-done((bf16[32,512]{1,0:T(8,128)(2,1)}, bf16[32,512]{1,0:T(8,128)(2,1)S(1)}, u32[]{:S(2)}, u32[]{:S(2)}) %collective-permute-start) | collective-permute-done | bytes 32800 | tf_op jit(solution)/shard_map/ppermute | solution.py:216
  10.7 0.8 pad_maximum_fusion.4.refs_0_
  11.5 1.5 %collective-permute-start.1 = (bf16[2,32,512]{2,1,0:T(8,128)(2,1)S(1)}, bf16[2,32,512]{2,1,0:T(8,128)(2,1)S(1)}, u32[]{:S(2)}, u32[]{:S(2)}) collective-permute-start(bf16[2,32,512]{2,1,0:T(8,128)(2,1)S(1)} %pad_maximum_fusion.4.refs_0_), channel_id=1, source_target_pairs={{0,16},{16,32},{32,48},{48,0},{64,80},{80,96},{96,112},{112,64},{1... | collective-permute-start | bytes 196616 | tf_op jit(solution)/shard_map/ppermute | solution.py:216
  12.9 2.7 %collective-permute-start.2 = (bf16[2,32,512]{2,1,0:T(8,128)(2,1)S(1)}, bf16[2,32,512]{2,1,0:T(8,128)(2,1)S(1)}, u32[]{:S(2)}, u32[]{:S(2)}) collective-permute-start(bf16[2,32,512]{2,1,0:T(8,128)(2,1)S(1)} %pad_maximum_fusion.4.refs_0_), channel_id=1, source_target_pairs={{0,32},{16,48},{32,0},{48,16},{64,96},{80,112},{96,64},{112,80},{1... | collective-permute-start | bytes 196616 | tf_op jit(solution)/shard_map/ppermute | solution.py:216
  15.7 1.4 %collective-permute-start.3 = (bf16[2,32,512]{2,1,0:T(8,128)(2,1)S(1)}, bf16[2,32,512]{2,1,0:T(8,128)(2,1)S(1)}, u32[]{:S(2)}, u32[]{:S(2)}) collective-permute-start(bf16[2,32,512]{2,1,0:T(8,128)(2,1)S(1)} %pad_maximum_fusion.4.refs_0_), channel_id=1, source_target_pairs={{0,48},{16,0},{32,16},{48,32},{64,112},{80,64},{96,80},{112,96},{1... | collective-permute-start | bytes 196616 | tf_op jit(solution)/shard_map/ppermute | solution.py:216
  17.1 0.4 collective-permute-done.1.refs_1_
  17.5 1.3 %collective-permute-done.2.refs_2_ = bf16[2,32,512]{2,1,0:T(8,128)(2,1)S(1)} collective-permute-done((bf16[2,32,512]{2,1,0:T(8,128)(2,1)S(1)}, bf16[2,32,512]{2,1,0:T(8,128)(2,1)S(1)}, u32[]{:S(2)}, u32[]{:S(2)}) %collective-permute-start.2) | collective-permute-done | bytes 65568 | tf_op jit(solution)/shard_map/ppermute | solution.py:216
  18.9 1.1 %collective-permute-done.3.refs_3_ = bf16[2,32,512]{2,1,0:T(8,128)(2,1)S(1)} collective-permute-done((bf16[2,32,512]{2,1,0:T(8,128)(2,1)S(1)}, bf16[2,32,512]{2,1,0:T(8,128)(2,1)S(1)}, u32[]{:S(2)}, u32[]{:S(2)}) %collective-permute-start.3) | collective-permute-done | bytes 65568 | tf_op jit(solution)/shard_map/ppermute | solution.py:216
  20.0 1.6 %copy-done.4 = f32[128,8,512]{2,1,0:T(8,128)S(1)} copy-done((f32[128,8,512]{2,1,0:T(8,128)S(1)}, f32[128,8,512]{2,1,0:T(8,128)}, u32[]{:S(2)}) %copy-start.4) | copy-done | bytes 2097176
  21.5 0.9 copy-done.5
  22.5 7.8 %gated.1.g_ref = bf16[1024,512]{1,0:T(8,128)(2,1)S(1)} custom-call(s32[1]{0:T(128)} %bitcast.at_ref, bf16[3,1024,512]{2,1,0:T(8,128)(2,1)} %bitcast.71, f32[3,3,512]{2,1,0:T(4,128)S(1)} %copy-done.7, f32[16,512]{1,0:T(8,128)S(1)} %copy-done.6, f32[16,512]{1,0:T(8,128)S(1)} %copy-done.8, f32[128,8,512]{2,1,0:T(8,128)S(1)} %copy-done.4, ...), custom_call_target="tpu_custom_call" | custom-call | tf_op jit(solution)/shard_map/gated/pallas_call | solution.py:189
  30.3 0.0 copy-start
  30.3 0.1 collective-permute-start.4
  30.5 2.6 %collective-permute-done.4.gp_ref = bf16[1024,512]{1,0:T(8,128)(2,1)S(1)} collective-permute-done((bf16[1024,512]{1,0:T(8,128)(2,1)S(1)}, bf16[1024,512]{1,0:T(8,128)(2,1)S(1)}, u32[]{:S(2)}, u32[]{:S(2)}) %collective-permute-start.4) | collective-permute-done | bytes 1048608 | tf_op jit(solution)/shard_map/ppermute | solution.py:216
  33.1 0.0 collective-permute-done.5.wp_ref
  33.1 3.8 %project.5 = (bf16[2,352,512]{2,1,0:T(8,128)(2,1)S(1)}, bf16[2,352,512]{2,1,0:T(8,128)(2,1)S(1)}) custom-call(s32[8]{0:T(128)S(1)} %fusion.25.cols_ref, bf16[1024,512]{1,0:T(8,128)(2,1)S(1)} %gated.1.g_ref, bf16[1024,512]{1,0:T(8,128)(2,1)S(1)} %collective-permute-done.4.gp_ref, bf16[512,8192]{1,0:T(8,128)(2,1)} %w_ref.9, ...), custom_call_target="tpu_custom_call" | custom-call | tf_op jit(solution)/shard_map/project/pallas_call | solution.py:279
  36.8 3.1 %collective-permute-start.7 = (bf16[2,352,512]{2,1,0:T(8,128)(2,1)S(1)}, bf16[2,352,512]{2,1,0:T(8,128)(2,1)S(1)}, u32[]{:S(2)}, u32[]{:S(2)}) collective-permute-start(bf16[2,352,512]{2,1,0:T(8,128)(2,1)S(1)} %get-tuple-element.37), channel_id=1, source_target_pairs={{0,12},{1,13},{2,14},{3,15},{4,0},{5,1},{6,2},{7,3},{8,4},{9,5},{1... | collective-permute-start | bytes 2162696 | tf_op jit(solution)/shard_map/ppermute | solution.py:216
  39.9 0.0 collective-permute-start.6
  39.9 4.0 %project.8 = bf16[4,320,512]{2,1,0:T(8,128)(2,1)S(1)} custom-call(s32[8]{0:T(128)S(1)} %fusion.25.cols_ref, bf16[1024,512]{1,0:T(8,128)(2,1)S(1)} %gated.1.g_ref, bf16[1024,512]{1,0:T(8,128)(2,1)S(1)} %collective-permute-done.4.gp_ref, bf16[512,8192]{1,0:T(8,128)(2,1)} %w_ref.9, bf16[512,8192]{1,0:T(8,128)(2,1)} %collective-permute-done.5.wp_ref), custom_call_target="tpu_custom_call" | custom-call | tf_op jit(solution)/shard_map/project/pallas_call | solution.py:279
  43.9 3.9 %collective-permute-start.10 = (bf16[4,320,512]{2,1,0:T(8,128)(2,1)S(1)}, bf16[4,320,512]{2,1,0:T(8,128)(2,1)S(1)}, u32[]{:S(2)}, u32[]{:S(2)}) collective-permute-start(bf16[4,320,512]{2,1,0:T(8,128)(2,1)S(1)} %project.8), channel_id=1, source_target_pairs={{0,2},{1,3},{2,0},{3,1},{4,6},{5,7},{6,4},{7,5},{8,10},{9,11},{10,... | collective-permute-start | bytes 3932168 | tf_op jit(solution)/shard_map/ppermute | solution.py:216
  47.8 5.5 %project.9 = (bf16[1,352,512]{2,1,0:T(8,128)(2,1)S(1)}, bf16[1,352,512]{2,1,0:T(8,128)(2,1)S(1)}, bf16[1,352,512]{2,1,0:T(8,128)(2,1)S(1)}, bf16[1,352,512]{2,1,...) custom-call(s32[8]{0:T(128)S(1)} %fusion.25.cols_ref, ...), custom_call_target="tpu_custom_call" | custom-call | tf_op jit(solution)/shard_map/project/pallas_call | solution.py:279
  53.3 0.7 collective-permute-start.13
  54.0 2.7 %collective-permute-start.14 = (bf16[352,512]{1,0:T(8,128)(2,1)S(1)}, bf16[352,512]{1,0:T(8,128)(2,1)S(1)}, u32[]{:S(2)}, u32[]{:S(2)}) collective-permute-start(bf16[352,512]{1,0:T(8,128)(2,1)S(1)} %bitcast.66), channel_id=1, source_target_pairs={{0,12},{1,13},{2,14},{3,15},{4,0},{5,1},{6,2},{7,3},{8,4},{9,5},{1... | collective-permute-start | bytes 1081352 | tf_op jit(solution)/shard_map/ppermute | solution.py:216
  56.7 0.0 collective-permute-done.7.refs_1_
  56.7 0.1 fusion.11
  56.8 2.7 %collective-permute-start.16 = (bf16[352,512]{1,0:T(8,128)(2,1)S(1)}, bf16[352,512]{1,0:T(8,128)(2,1)S(1)}, u32[]{:S(2)}, u32[]{:S(2)}) collective-permute-start(bf16[352,512]{1,0:T(8,128)(2,1)S(1)} %fusion.11), channel_id=1, source_target_pairs={{0,12},{1,13},{2,14},{3,15},{4,0},{5,1},{6,2},{7,3},{8,4},{9,5},{1... | collective-permute-start | bytes 1081352 | tf_op jit(solution)/shard_map/ppermute | solution.py:216
  59.5 0.7 collective-permute-done.6.refs_0_
  60.2 0.1 fusion.10
  60.2 0.0 copy-start.1
  60.3 0.1 collective-permute-start.15
  60.4 5.9 %project.6 = (bf16[1,352,512]{2,1,0:T(8,128)(2,1)S(1)}, bf16[1,352,512]{2,1,0:T(8,128)(2,1)S(1)}, bf16[1,352,512]{2,1,0:T(8,128)(2,1)S(1)}, bf16[1,352,512]{2,1,...) custom-call(s32[8]{0:T(128)S(1)} %fusion.25.cols_ref, bf16[1024,512]{1,0:T(8,128)(2,1)} %copy-done, ...), custom_call_target="tpu_custom_call" | custom-call | tf_op jit(solution)/shard_map/project/pallas_call | solution.py:279
  66.2 4.0 %project.7 = bf16[4,320,512]{2,1,0:T(8,128)(2,1)S(1)} custom-call(s32[8]{0:T(128)S(1)} %fusion.25.cols_ref, bf16[1024,512]{1,0:T(8,128)(2,1)S(1)} %copy-done.1, bf16[1024,512]{1,0:T(8,128)(2,1)S(1)} %copy-done.3, bf16[512,8192]{1,0:T(8,128)(2,1)} %w_ref.9, bf16[512,8192]{1,0:T(8,128)(2,1)} %collective-permute-done.5.wp_ref), custom_call_target="tpu_custom_call" | custom-call | tf_op jit(solution)/shard_map/project/pallas_call | solution.py:279
  70.3 0.0 collective-permute-done.13
  70.3 0.3 collective-permute-start.8
  70.5 0.0 collective-permute-done.14
  70.5 3.2 %collective-permute-start.9 = (bf16[352,512]{1,0:T(8,128)(2,1)S(1)}, bf16[352,512]{1,0:T(8,128)(2,1)S(1)}, u32[]{:S(2)}, u32[]{:S(2)}) collective-permute-start(bf16[352,512]{1,0:T(8,128)(2,1)S(1)} %bitcast.64), channel_id=1, source_target_pairs={{0,12},{1,13},{2,14},{3,15},{4,0},{5,1},{6,2},{7,3},{8,4},{9,5},{1... | collective-permute-start | bytes 1081352 | tf_op jit(solution)/shard_map/ppermute | solution.py:216
  73.8 0.0 collective-permute-done.16
  73.8 1.8 %collective-permute-done.15 = bf16[352,512]{1,0:T(8,128)(2,1)S(1)} collective-permute-done((bf16[352,512]{1,0:T(8,128)(2,1)S(1)}, bf16[352,512]{1,0:T(8,128)(2,1)S(1)}, u32[]{:S(2)}, u32[]{:S(2)}) %collective-permute-start.15) | collective-permute-done | bytes 360480 | tf_op jit(solution)/shard_map/ppermute | solution.py:216
  75.6 1.0 collective-permute-done.10
  76.6 0.2 fusion.16
  76.8 0.4 collective-permute-start.18
  77.2 2.9 %collective-permute-start.20 = (bf16[160,512]{1,0:T(8,128)(2,1)S(1)}, bf16[160,512]{1,0:T(8,128)(2,1)S(1)}, u32[]{:S(2)}, u32[]{:S(2)}) collective-permute-start(bf16[160,512]{1,0:T(8,128)(2,1)S(1)} %get-tuple-element.66), channel_id=1, source_target_pairs={{0,12},{1,13},{2,14},{3,15},{4,0},{5,1},{6,2},{7,3},{8,4},{9,5},{1... | collective-permute-start | bytes 491528 | tf_op jit(solution)/shard_map/ppermute | solution.py:216
  80.1 0.3 fusion.12
  80.4 0.1 pad_maximum_fusion.1
  80.5 3.3 %collective-permute-start.17 = (bf16[2,352,512]{2,1,0:T(8,128)(2,1)S(1)}, bf16[2,352,512]{2,1,0:T(8,128)(2,1)S(1)}, u32[]{:S(2)}, u32[]{:S(2)}) collective-permute-start(bf16[2,352,512]{2,1,0:T(8,128)(2,1)S(1)} %pad_maximum_fusion.1), channel_id=1, source_target_pairs={{0,2},{1,3},{2,0},{3,1},{4,6},{5,7},{6,4},{7,5},{8,10},{9,11},{10,... | collective-permute-start | bytes 2162696 | tf_op jit(solution)/shard_map/ppermute | solution.py:216
  83.8 1.9 %collective-permute-done.18 = bf16[160,512]{1,0:T(8,128)(2,1)S(1)} collective-permute-done((bf16[160,512]{1,0:T(8,128)(2,1)S(1)}, bf16[160,512]{1,0:T(8,128)(2,1)S(1)}, u32[]{:S(2)}, u32[]{:S(2)}) %collective-permute-start.18) | collective-permute-done | bytes 163872 | tf_op jit(solution)/shard_map/ppermute | solution.py:216
  85.7 0.0 collective-permute-start.11
  85.7 0.0 collective-permute-done.20
  85.7 3.2 %collective-permute-start.12 = (bf16[352,512]{1,0:T(8,128)(2,1)S(1)}, bf16[352,512]{1,0:T(8,128)(2,1)S(1)}, u32[]{:S(2)}, u32[]{:S(2)}) collective-permute-start(bf16[352,512]{1,0:T(8,128)(2,1)S(1)} %bitcast.62), channel_id=1, source_target_pairs={{0,12},{1,13},{2,14},{3,15},{4,0},{5,1},{6,2},{7,3},{8,4},{9,5},{1... | collective-permute-start | bytes 1081352 | tf_op jit(solution)/shard_map/ppermute | solution.py:216
  89.0 0.1 fusion.15
  89.1 0.0 collective-permute-done.8
  89.2 0.1 collective-permute-start.19
  89.2 0.0 collective-permute-done.9
  89.2 3.2 %collective-permute-start.21 = (bf16[320,512]{1,0:T(8,128)(2,1)S(1)}, bf16[320,512]{1,0:T(8,128)(2,1)S(1)}, u32[]{:S(2)}, u32[]{:S(2)}) collective-permute-start(bf16[320,512]{1,0:T(8,128)(2,1)S(1)} %pad_maximum_fusion.3), channel_id=1, source_target_pairs={{0,12},{1,13},{2,14},{3,15},{4,0},{5,1},{6,2},{7,3},{8,4},{9,5},{1... | collective-permute-start | bytes 983048 | tf_op jit(solution)/shard_map/ppermute | solution.py:216
  92.5 5.8 %collective-permute-done.11 = bf16[352,512]{1,0:T(8,128)(2,1)S(1)} collective-permute-done((bf16[352,512]{1,0:T(8,128)(2,1)S(1)}, bf16[352,512]{1,0:T(8,128)(2,1)S(1)}, u32[]{:S(2)}, u32[]{:S(2)}) %collective-permute-start.11) | collective-permute-done | bytes 360480 | tf_op jit(solution)/shard_map/ppermute | solution.py:216
  98.3 0.0 collective-permute-done.12
  98.3 5.0 %collective-permute-done.19 = bf16[320,512]{1,0:T(8,128)(2,1)S(1)} collective-permute-done((bf16[320,512]{1,0:T(8,128)(2,1)S(1)}, bf16[320,512]{1,0:T(8,128)(2,1)S(1)}, u32[]{:S(2)}, u32[]{:S(2)}) %collective-permute-start.19) | collective-permute-done | bytes 327712 | tf_op jit(solution)/shard_map/ppermute | solution.py:216
  103.3 0.2 fusion.9
  103.4 0.0 collective-permute-done.17
  103.4 0.4 fusion.2
  103.8 1.0 pad_maximum_fusion
  (18 shorter events, 0.1 us)
Async XLA Ops:
  0.0 33.1 %collective-permute-start.5 = (bf16[512,8192]{1,0:T(8,128)(2,1)}, bf16[512,8192]{1,0:T(8,128)(2,1)}, u32[]{:S(2)}, u32[]{:S(2)}) collective-permute-start(bf16[512,8192]{1,0:T(8,128)(2,1)} %w_ref.9), channel_id=1, source_target_pairs={{0,1},{1,0},{2,3},{3,2},{4,5},{5,4},{6,7},{7,6},{8,9},{9,8},{10,11... | collective-permute-start | bytes 25165832 | tf_op jit(solution)/shard_map/ppermute | solution.py:216
  0.0 19.9 %copy-start.6 = (f32[16,512]{1,0:T(8,128)S(1)}, f32[16,512]{1,0:T(8,128)}, u32[]{:S(2)}) copy-start(f32[16,512]{1,0:T(8,128)} %rate_ref.3) | copy-start | bytes 98308
  0.0 19.9 %copy-start.7 = (f32[3,3,512]{2,1,0:T(4,128)S(1)}, f32[3,3,512]{2,1,0:T(4,128)}, u32[]{:S(2)}) copy-start(f32[3,3,512]{2,1,0:T(4,128)} %sf_ref.3) | copy-start | bytes 55300
  0.0 19.9 %copy-start.8 = (f32[16,512]{1,0:T(8,128)S(1)}, f32[16,512]{1,0:T(8,128)}, u32[]{:S(2)}) copy-start(f32[16,512]{1,0:T(8,128)} %res_ref.1) | copy-start | bytes 98308
  6.4 4.3 %collective-permute-start = (bf16[32,512]{1,0:T(8,128)(2,1)}, bf16[32,512]{1,0:T(8,128)(2,1)S(1)}, u32[]{:S(2)}, u32[]{:S(2)}) collective-permute-start(bf16[32,512]{1,0:T(8,128)(2,1)} %get-tuple-element.35), channel_id=1, source_target_pairs={{0,64},{16,80},{32,96},{48,112},{64,0},{80,16},{96,32},{112,48},{1... | collective-permute-start | bytes 98312 | tf_op jit(solution)/shard_map/ppermute | solution.py:216
  11.5 6.1 %collective-permute-start.1 = (bf16[2,32,512]{2,1,0:T(8,128)(2,1)S(1)}, bf16[2,32,512]{2,1,0:T(8,128)(2,1)S(1)}, u32[]{:S(2)}, u32[]{:S(2)}) collective-permute-start(bf16[2,32,512]{2,1,0:T(8,128)(2,1)S(1)} %pad_maximum_fusion.4.refs_0_), channel_id=1, source_target_pairs={{0,16},{16,32},{32,48},{48,0},{64,80},{80,96},{96,112},{112,64},{1... | collective-permute-start | bytes 196616 | tf_op jit(solution)/shard_map/ppermute | solution.py:216
  12.9 5.9 %collective-permute-start.2 = (bf16[2,32,512]{2,1,0:T(8,128)(2,1)S(1)}, bf16[2,32,512]{2,1,0:T(8,128)(2,1)S(1)}, u32[]{:S(2)}, u32[]{:S(2)}) collective-permute-start(bf16[2,32,512]{2,1,0:T(8,128)(2,1)S(1)} %pad_maximum_fusion.4.refs_0_), channel_id=1, source_target_pairs={{0,32},{16,48},{32,0},{48,16},{64,96},{80,112},{96,64},{112,80},{1... | collective-permute-start | bytes 196616 | tf_op jit(solution)/shard_map/ppermute | solution.py:216
  15.7 4.3 %collective-permute-start.3 = (bf16[2,32,512]{2,1,0:T(8,128)(2,1)S(1)}, bf16[2,32,512]{2,1,0:T(8,128)(2,1)S(1)}, u32[]{:S(2)}, u32[]{:S(2)}) collective-permute-start(bf16[2,32,512]{2,1,0:T(8,128)(2,1)S(1)} %pad_maximum_fusion.4.refs_0_), channel_id=1, source_target_pairs={{0,48},{16,0},{32,16},{48,32},{64,112},{80,64},{96,80},{112,96},{1... | collective-permute-start | bytes 196616 | tf_op jit(solution)/shard_map/ppermute | solution.py:216
  20.0 1.6 %copy-start.4 = (f32[128,8,512]{2,1,0:T(8,128)S(1)}, f32[128,8,512]{2,1,0:T(8,128)}, u32[]{:S(2)}) copy-start(f32[128,8,512]{2,1,0:T(8,128)} %get-tuple-element.33.p_ref) | copy-start | bytes 6291460
  21.5 0.9 copy-start.5
  30.3 17.5 %copy-start = (bf16[1024,512]{1,0:T(8,128)(2,1)}, bf16[1024,512]{1,0:T(8,128)(2,1)S(1)}, u32[]{:S(2)}) copy-start(bf16[1024,512]{1,0:T(8,128)(2,1)S(1)} %gated.1.g_ref) | copy-start | bytes 3145732
  30.3 2.7 %collective-permute-start.4 = (bf16[1024,512]{1,0:T(8,128)(2,1)S(1)}, bf16[1024,512]{1,0:T(8,128)(2,1)S(1)}, u32[]{:S(2)}, u32[]{:S(2)}) collective-permute-start(bf16[1024,512]{1,0:T(8,128)(2,1)S(1)} %gated.1.g_ref), channel_id=1, source_target_pairs={{0,1},{1,0},{2,3},{3,2},{4,5},{5,4},{6,7},{7,6},{8,9},{9,8},{10,11... | collective-permute-start | bytes 3145736 | tf_op jit(solution)/shard_map/ppermute | solution.py:216
  33.1 6.9 %copy-start.2 = (bf16[1024,512]{1,0:T(8,128)(2,1)}, bf16[1024,512]{1,0:T(8,128)(2,1)S(1)}, u32[]{:S(2)}) copy-start(bf16[1024,512]{1,0:T(8,128)(2,1)S(1)} %collective-permute-done.4.gp_ref) | copy-start | bytes 3145732
  36.8 19.9 %collective-permute-start.7 = (bf16[2,352,512]{2,1,0:T(8,128)(2,1)S(1)}, bf16[2,352,512]{2,1,0:T(8,128)(2,1)S(1)}, u32[]{:S(2)}, u32[]{:S(2)}) collective-permute-start(bf16[2,352,512]{2,1,0:T(8,128)(2,1)S(1)} %get-tuple-element.37), channel_id=1, source_target_pairs={{0,12},{1,13},{2,14},{3,15},{4,0},{5,1},{6,2},{7,3},{8,4},{9,5},{1... | collective-permute-start | bytes 2162696 | tf_op jit(solution)/shard_map/ppermute | solution.py:216
  39.9 20.2 %collective-permute-start.6 = (bf16[2,352,512]{2,1,0:T(8,128)(2,1)S(1)}, bf16[2,352,512]{2,1,0:T(8,128)(2,1)S(1)}, u32[]{:S(2)}, u32[]{:S(2)}) collective-permute-start(bf16[2,352,512]{2,1,0:T(8,128)(2,1)S(1)} %get-tuple-element.36), channel_id=1, source_target_pairs={{0,4},{1,5},{2,6},{3,7},{4,8},{5,9},{6,10},{7,11},{8,12},{9,13},{1... | collective-permute-start | bytes 2162696 | tf_op jit(solution)/shard_map/ppermute | solution.py:216
  43.9 32.7 %collective-permute-start.10 = (bf16[4,320,512]{2,1,0:T(8,128)(2,1)S(1)}, bf16[4,320,512]{2,1,0:T(8,128)(2,1)S(1)}, u32[]{:S(2)}, u32[]{:S(2)}) collective-permute-start(bf16[4,320,512]{2,1,0:T(8,128)(2,1)S(1)} %project.8), channel_id=1, source_target_pairs={{0,2},{1,3},{2,0},{3,1},{4,6},{5,7},{6,4},{7,5},{8,10},{9,11},{10,... | collective-permute-start | bytes 3932168 | tf_op jit(solution)/shard_map/ppermute | solution.py:216
  53.3 16.9 %collective-permute-start.13 = (bf16[352,512]{1,0:T(8,128)(2,1)S(1)}, bf16[352,512]{1,0:T(8,128)(2,1)S(1)}, u32[]{:S(2)}, u32[]{:S(2)}) collective-permute-start(bf16[352,512]{1,0:T(8,128)(2,1)S(1)} %bitcast.67), channel_id=1, source_target_pairs={{0,4},{1,5},{2,6},{3,7},{4,8},{5,9},{6,10},{7,11},{8,12},{9,13},{1... | collective-permute-start | bytes 1081352 | tf_op jit(solution)/shard_map/ppermute | solution.py:216
  54.0 16.6 %collective-permute-start.14 = (bf16[352,512]{1,0:T(8,128)(2,1)S(1)}, bf16[352,512]{1,0:T(8,128)(2,1)S(1)}, u32[]{:S(2)}, u32[]{:S(2)}) collective-permute-start(bf16[352,512]{1,0:T(8,128)(2,1)S(1)} %bitcast.66), channel_id=1, source_target_pairs={{0,12},{1,13},{2,14},{3,15},{4,0},{5,1},{6,2},{7,3},{8,4},{9,5},{1... | collective-permute-start | bytes 1081352 | tf_op jit(solution)/shard_map/ppermute | solution.py:216
  56.8 17.0 %collective-permute-start.16 = (bf16[352,512]{1,0:T(8,128)(2,1)S(1)}, bf16[352,512]{1,0:T(8,128)(2,1)S(1)}, u32[]{:S(2)}, u32[]{:S(2)}) collective-permute-start(bf16[352,512]{1,0:T(8,128)(2,1)S(1)} %fusion.11), channel_id=1, source_target_pairs={{0,12},{1,13},{2,14},{3,15},{4,0},{5,1},{6,2},{7,3},{8,4},{9,5},{1... | collective-permute-start | bytes 1081352 | tf_op jit(solution)/shard_map/ppermute | solution.py:216
  60.2 6.0 %copy-start.1 = (bf16[1024,512]{1,0:T(8,128)(2,1)S(1)}, bf16[1024,512]{1,0:T(8,128)(2,1)}, u32[]{:S(2)}) copy-start(bf16[1024,512]{1,0:T(8,128)(2,1)} %copy-done) | copy-start | bytes 3145732
  60.3 6.0 %copy-start.3 = (bf16[1024,512]{1,0:T(8,128)(2,1)S(1)}, bf16[1024,512]{1,0:T(8,128)(2,1)}, u32[]{:S(2)}) copy-start(bf16[1024,512]{1,0:T(8,128)(2,1)} %copy-done.2) | copy-start | bytes 3145732
  60.3 15.3 %collective-permute-start.15 = (bf16[352,512]{1,0:T(8,128)(2,1)S(1)}, bf16[352,512]{1,0:T(8,128)(2,1)S(1)}, u32[]{:S(2)}, u32[]{:S(2)}) collective-permute-start(bf16[352,512]{1,0:T(8,128)(2,1)S(1)} %fusion.10), channel_id=1, source_target_pairs={{0,4},{1,5},{2,6},{3,7},{4,8},{5,9},{6,10},{7,11},{8,12},{9,13},{1... | collective-permute-start | bytes 1081352 | tf_op jit(solution)/shard_map/ppermute | solution.py:216
  70.3 18.9 %collective-permute-start.8 = (bf16[352,512]{1,0:T(8,128)(2,1)S(1)}, bf16[352,512]{1,0:T(8,128)(2,1)S(1)}, u32[]{:S(2)}, u32[]{:S(2)}) collective-permute-start(bf16[352,512]{1,0:T(8,128)(2,1)S(1)} %bitcast.65), channel_id=1, source_target_pairs={{0,4},{1,5},{2,6},{3,7},{4,8},{5,9},{6,10},{7,11},{8,12},{9,13},{1... | collective-permute-start | bytes 1081352 | tf_op jit(solution)/shard_map/ppermute | solution.py:216
  70.5 18.7 %collective-permute-start.9 = (bf16[352,512]{1,0:T(8,128)(2,1)S(1)}, bf16[352,512]{1,0:T(8,128)(2,1)S(1)}, u32[]{:S(2)}, u32[]{:S(2)}) collective-permute-start(bf16[352,512]{1,0:T(8,128)(2,1)S(1)} %bitcast.64), channel_id=1, source_target_pairs={{0,12},{1,13},{2,14},{3,15},{4,0},{5,1},{6,2},{7,3},{8,4},{9,5},{1... | collective-permute-start | bytes 1081352 | tf_op jit(solution)/shard_map/ppermute | solution.py:216
  76.8 8.9 %collective-permute-start.18 = (bf16[160,512]{1,0:T(8,128)(2,1)S(1)}, bf16[160,512]{1,0:T(8,128)(2,1)S(1)}, u32[]{:S(2)}, u32[]{:S(2)}) collective-permute-start(bf16[160,512]{1,0:T(8,128)(2,1)S(1)} %get-tuple-element.63), channel_id=1, source_target_pairs={{0,4},{1,5},{2,6},{3,7},{4,8},{5,9},{6,10},{7,11},{8,12},{9,13},{1... | collective-permute-start | bytes 491528 | tf_op jit(solution)/shard_map/ppermute | solution.py:216
  77.2 8.5 %collective-permute-start.20 = (bf16[160,512]{1,0:T(8,128)(2,1)S(1)}, bf16[160,512]{1,0:T(8,128)(2,1)S(1)}, u32[]{:S(2)}, u32[]{:S(2)}) collective-permute-start(bf16[160,512]{1,0:T(8,128)(2,1)S(1)} %get-tuple-element.66), channel_id=1, source_target_pairs={{0,12},{1,13},{2,14},{3,15},{4,0},{5,1},{6,2},{7,3},{8,4},{9,5},{1... | collective-permute-start | bytes 491528 | tf_op jit(solution)/shard_map/ppermute | solution.py:216
  80.5 22.9 %collective-permute-start.17 = (bf16[2,352,512]{2,1,0:T(8,128)(2,1)S(1)}, bf16[2,352,512]{2,1,0:T(8,128)(2,1)S(1)}, u32[]{:S(2)}, u32[]{:S(2)}) collective-permute-start(bf16[2,352,512]{2,1,0:T(8,128)(2,1)S(1)} %pad_maximum_fusion.1), channel_id=1, source_target_pairs={{0,2},{1,3},{2,0},{3,1},{4,6},{5,7},{6,4},{7,5},{8,10},{9,11},{10,... | collective-permute-start | bytes 2162696 | tf_op jit(solution)/shard_map/ppermute | solution.py:216
  85.7 12.6 %collective-permute-start.11 = (bf16[352,512]{1,0:T(8,128)(2,1)S(1)}, bf16[352,512]{1,0:T(8,128)(2,1)S(1)}, u32[]{:S(2)}, u32[]{:S(2)}) collective-permute-start(bf16[352,512]{1,0:T(8,128)(2,1)S(1)} %bitcast.63), channel_id=1, source_target_pairs={{0,4},{1,5},{2,6},{3,7},{4,8},{5,9},{6,10},{7,11},{8,12},{9,13},{1... | collective-permute-start | bytes 1081352 | tf_op jit(solution)/shard_map/ppermute | solution.py:216
  85.7 12.6 %collective-permute-start.12 = (bf16[352,512]{1,0:T(8,128)(2,1)S(1)}, bf16[352,512]{1,0:T(8,128)(2,1)S(1)}, u32[]{:S(2)}, u32[]{:S(2)}) collective-permute-start(bf16[352,512]{1,0:T(8,128)(2,1)S(1)} %bitcast.62), channel_id=1, source_target_pairs={{0,12},{1,13},{2,14},{3,15},{4,0},{5,1},{6,2},{7,3},{8,4},{9,5},{1... | collective-permute-start | bytes 1081352 | tf_op jit(solution)/shard_map/ppermute | solution.py:216
  89.2 14.1 %collective-permute-start.19 = (bf16[320,512]{1,0:T(8,128)(2,1)S(1)}, bf16[320,512]{1,0:T(8,128)(2,1)S(1)}, u32[]{:S(2)}, u32[]{:S(2)}) collective-permute-start(bf16[320,512]{1,0:T(8,128)(2,1)S(1)} %pad_maximum_fusion.2), channel_id=1, source_target_pairs={{0,4},{1,5},{2,6},{3,7},{4,8},{5,9},{6,10},{7,11},{8,12},{9,13},{1... | collective-permute-start | bytes 983048 | tf_op jit(solution)/shard_map/ppermute | solution.py:216
  89.2 14.0 %collective-permute-start.21 = (bf16[320,512]{1,0:T(8,128)(2,1)S(1)}, bf16[320,512]{1,0:T(8,128)(2,1)S(1)}, u32[]{:S(2)}, u32[]{:S(2)}) collective-permute-start(bf16[320,512]{1,0:T(8,128)(2,1)S(1)} %pad_maximum_fusion.3), channel_id=1, source_target_pairs={{0,12},{1,13},{2,14},{3,15},{4,0},{5,1},{6,2},{7,3},{8,4},{9,5},{1... | collective-permute-start | bytes 983048 | tf_op jit(solution)/shard_map/ppermute | solution.py:216

commit v8 on v7

--- a/solution.py
+++ b/solution.py
@@ -263,7 +263,7 @@
             out_refs[out][slot] = acc.astype(bf16)
 
 
-def project(operands, plan, counts, added=()):
+def project(operands, plan, counts, added=(), limit=50):
     cols, g, gp, w, wp = operands
     n_tok, depth = g.shape
     slots = [0] * len(counts)
@@ -287,7 +287,7 @@
             pltpu.SemaphoreType.DMA((2,)),
             pltpu.SemaphoreType.DMA((len(plan), 2)),
         ],
-        compiler_params=pltpu.CompilerParams(vmem_limit_bytes=50 << 20),
+        compiler_params=pltpu.CompilerParams(vmem_limit_bytes=limit << 20),
         name="project",
     )(cols, g, gp, w, wp, *added)
 
@@ -296,7 +296,7 @@
     return sum(p.astype(f32) for p in parts).astype(bf16)
 
 
-Z_TOK = 320
+Z_TOK = 352
 
 
 def per_device(features, short_filter, decay_rate, residues, out_weight):
@@ -315,7 +315,7 @@
     n_y = n_tok - Z_TOK
     a, b, z = 0, n_y // 2, n_y
 
-    up2, down2 = project(operands, [((2, dz), [(a, 0), (b, 1)]) for dz in (1, 0)], [b, b])
+    up2, down2 = project(operands, [((2, dz), [(a, 0), (b, 1)]) for dz in (1, 0)], [b, b], limit=50)
     up2, down2 = to_y(up2, 1), to_y(down2, -1)
     (far,) = project(operands, [((dy, 1), [(z, 0)]) for dy in (0, 1, 2, 3)], [Z_TOK])
     far = to_far_z(far)
@@ -326,30 +326,24 @@
     )
     up, down = to_y(up[0], 1), to_y(down[0], -1)
     up_more, down_more = to_y(total(up_more[0], up2[0]), 1), to_y(total(down_more[0], down2[0]), -1)
-    rise, fall, rise_more, fall_more, stay_a, stay_b = project(
+    rise, fall, stay_a, stay_b = project(
         operands,
-        [((1, 0), [(b, 0), (a, 2, (0, 1))]), ((3, 0), [(a, 1), (b, 3, (1, 1))]), ((0, 0), [(a, 4), (b, 5)])],
-        [b] * 6,
+        [((1, 0), [(b, 0), (a, 0, (0, 1))]), ((3, 0), [(a, 1), (b, 1, (1, 1))]), ((0, 0), [(a, 2), (b, 3)])],
+        [b] * 4,
         [up2, down2],
     )
     last = (cols, lax.optimization_barrier((mine, stay_a))[0]) + operands[2:]
     (near,) = project(last, [((dy, 0), [(z, 0)]) for dy in (2, 3, 1, 0)], [Z_TOK])
-    half = Z_TOK // 2
-    s2a, s2b = total(near[0, :half], far[2, :half]), total(near[0, half:], far[2, half:])
-    rise, fall = to_y(rise[0], 1), to_y(fall[0], -1)
-    rise_more, fall_more, _, _ = lax.optimization_barrier((rise_more[0], fall_more[0], s2a, s2b))
-    s2a, s2b = to_y(s2a, 1), to_y(s2b, -1)
-    rise_more, fall_more = to_y(rise_more, 1), to_y(fall_more, -1)
+    one, two, three = (total(near[i], far[dy]) for i, dy in ((2, 1), (0, 2), (1, 3)))
+    rise, fall = to_y(rise, 1), to_y(fall, -1)
+    one, two, three = to_y(one, 1), to_y(two, 2), to_y(three, -1)
     up, down, up_more, down_more = lax.optimization_barrier((up, down, up_more, down_more))
     over = to_far_z(jnp.stack([total(keep_a[0], up_more, down), total(keep_b[0], up, down_more)]))
-    rise, fall, rise_more, fall_more = lax.optimization_barrier((rise, fall, rise_more, fall_more))
-    done_a = total(stay_a[0], rise_more, fall, over[0])
-    done_b = total(stay_b[0], rise, fall_more, over[1])
-
-    s3 = jnp.concatenate([total(near[1, :half], far[3, :half]), total(near[1, half:], far[3, half:], s2b)])
-    s1 = jnp.concatenate([total(near[2, :half], far[1, :half], s2a), total(near[2, half:], far[1, half:])])
-    s1, s3 = to_y(s1, 1), to_y(s3, -1)
-    return jnp.concatenate([done_a, done_b, total(near[3], far[0], s1, s3)])
+    rise, fall = lax.optimization_barrier((rise, fall))
+    done_a = total(stay_a[0], rise[1], fall[0], over[0])
+    done_b = total(stay_b[0], rise[0], fall[1], over[1])
+
+    return jnp.concatenate([done_a, done_b, total(near[3], far[0], one, two, three)])
 
 
 def solution(mesh):

time: 105 us -> 106 us (level)
  waiting for transfers between devices: 24 us -> 32.6 us
  starting transfers between devices: 37.5 us -> 29.6 us
    ppermute x22 -> x19, waiting for transfers between devices: 24 us -> 32.6 us  [spread(): return lax.ppermute(x, axis, [(i, j) for i, j in pairs if j is not None])]
    ppermute x22 -> x19, starting transfers between devices: 37.5 us -> 29.6 us  [spread(): return lax.ppermute(x, axis, [(i, j) for i, j in pairs if j is not None])]
  transfers between devices with their start and end apart: 22 -> 19, of which waited for: 11 -> 12; matrix products, arithmetic and copies ran while one was open for 2% -> 2% of each run, Pallas kernels for 32% -> 32%
where the time goes in v8:
time: 106 us; the launch traced here: 105 us
  Pallas kernels  37 us (35%)
  waiting for transfers between devices  32.6 us (31%)
  starting transfers between devices  29.6 us (28%)
  other arithmetic  3.26 us (3%)
  local copies, waits for them, and re-layouts  2.57 us (2%)
    ppermute x19, waiting for transfers between devices, spread(): return lax.ppermute(x, axis, [(i, j) for i, j in pairs if j is not None])  32.6 us
    ppermute x19, starting transfers between devices, spread(): return lax.ppermute(x, axis, [(i, j) for i, j in pairs if j is not None])  29.6 us
    pallas_call x5, Pallas kernels, project(): pl.pallas_call(functools.partial(project_kernel, laid, len(added)), in_sp...  22.8 us
    pallas_call x1, Pallas kernels, gated(): pl.pallas_call(gate_kernel, grid=(width // LANES,), in_specs=[pl.BlockSpe...  7.8 us
    pallas_call x1, Pallas kernels, states(): pl.pallas_call(state_kernel, grid=(width // LANES,), in_specs=[pl.BlockSp...  6.4 us
    unnamed x18, local copies, waits for them, and re-layouts  2.57 us
  transfers between devices with their start and end apart: 19, of which 12 were waited for; matrix products, arithmetic and copies ran while one was open for 2% of the time, Pallas kernels for 32%

profile of v8, /device:TPU:0, one launch (start us, length us, event | category | flops | bytes accessed | tf_op | source)
XLA Modules:
  0.0 105.2 jit_solution(9817058718500752614)
XLA Ops:
  0.0 0.0 collective-permute-start.5
  0.0 6.4 %states.1 = (f32[128,8,512]{2,1,0:T(8,128)}, bf16[32,512]{1,0:T(8,128)(2,1)}, f32[16,8,512]{2,1,0:T(8,128)}) custom-call(bf16[3,1024,512]{2,1,0:T(8,128)(2,1)} %bitcast.40, bf16[3,1024,512]{2,1,0:T(8,128)(2,1)} %bitcast.41, bf16[3,1024,512]{2,1,0:T(8,128)(2,1)} %bitcast.42, f32[3,3,512]{2,1,0:T(4,128)} %sf_ref.3, f32[16,512]{1,0:T(8,128)} %rate_ref.3), custom_call_target="tpu_custom_call" | custom-call | tf_op jit(solution)/shard_map/states/pallas_call | solution.py:157
  6.4 2.0 %collective-permute-start = (bf16[32,512]{1,0:T(8,128)(2,1)}, bf16[32,512]{1,0:T(8,128)(2,1)S(1)}, u32[]{:S(2)}, u32[]{:S(2)}) collective-permute-start(bf16[32,512]{1,0:T(8,128)(2,1)} %get-tuple-element.29), channel_id=1, source_target_pairs={{0,64},{16,80},{32,96},{48,112},{64,0},{80,16},{96,32},{112,48},{1... | collective-permute-start | bytes 98312 | tf_op jit(solution)/shard_map/ppermute | solution.py:216
  8.4 2.3 %collective-permute-done = bf16[32,512]{1,0:T(8,128)(2,1)S(1)} collective-permute-done((bf16[32,512]{1,0:T(8,128)(2,1)}, bf16[32,512]{1,0:T(8,128)(2,1)S(1)}, u32[]{:S(2)}, u32[]{:S(2)}) %collective-permute-start) | collective-permute-done | bytes 32800 | tf_op jit(solution)/shard_map/ppermute | solution.py:216
  10.7 0.8 pad_maximum_fusion.2.refs_0_
  11.5 2.8 %collective-permute-start.3 = (bf16[2,32,512]{2,1,0:T(8,128)(2,1)S(1)}, bf16[2,32,512]{2,1,0:T(8,128)(2,1)S(1)}, u32[]{:S(2)}, u32[]{:S(2)}) collective-permute-start(bf16[2,32,512]{2,1,0:T(8,128)(2,1)S(1)} %pad_maximum_fusion.2.refs_0_), channel_id=1, source_target_pairs={{0,48},{16,0},{32,16},{48,32},{64,112},{80,64},{96,80},{112,96},{1... | collective-permute-start | bytes 196616 | tf_op jit(solution)/shard_map/ppermute | solution.py:216
  14.2 0.8 collective-permute-start.2
  15.0 0.9 collective-permute-start.1
  15.9 0.5 collective-permute-done.3.refs_3_
  16.4 3.6 %collective-permute-done.2.refs_2_ = bf16[2,32,512]{2,1,0:T(8,128)(2,1)S(1)} collective-permute-done((bf16[2,32,512]{2,1,0:T(8,128)(2,1)S(1)}, bf16[2,32,512]{2,1,0:T(8,128)(2,1)S(1)}, u32[]{:S(2)}, u32[]{:S(2)}) %collective-permute-start.2) | collective-permute-done | bytes 65568 | tf_op jit(solution)/shard_map/ppermute | solution.py:216
  20.0 0.7 collective-permute-done.1.refs_1_
  20.7 0.0 copy-done.6
  20.7 0.0 copy-done.7
  20.7 0.0 copy-done.8
  20.7 0.0 copy-start.4
  20.7 1.6 %copy-done.4 = f32[128,8,512]{2,1,0:T(8,128)S(1)} copy-done((f32[128,8,512]{2,1,0:T(8,128)S(1)}, f32[128,8,512]{2,1,0:T(8,128)}, u32[]{:S(2)}) %copy-start.4) | copy-done | bytes 2097176
  22.3 0.9 copy-done.5
  23.2 7.8 %gated.1.g_ref = bf16[1024,512]{1,0:T(8,128)(2,1)S(1)} custom-call(s32[1]{0:T(128)} %bitcast.at_ref, bf16[3,1024,512]{2,1,0:T(8,128)(2,1)} %bitcast.43, f32[3,3,512]{2,1,0:T(4,128)S(1)} %copy-done.7, f32[16,512]{1,0:T(8,128)S(1)} %copy-done.6, f32[16,512]{1,0:T(8,128)S(1)} %copy-done.8, f32[128,8,512]{2,1,0:T(8,128)S(1)} %copy-done.4, ...), custom_call_target="tpu_custom_call" | custom-call | tf_op jit(solution)/shard_map/gated/pallas_call | solution.py:189
  31.0 0.0 copy-start
  31.1 0.1 collective-permute-start.4
  31.2 2.6 %collective-permute-done.4.gp_ref = bf16[1024,512]{1,0:T(8,128)(2,1)S(1)} collective-permute-done((bf16[1024,512]{1,0:T(8,128)(2,1)S(1)}, bf16[1024,512]{1,0:T(8,128)(2,1)S(1)}, u32[]{:S(2)}, u32[]{:S(2)}) %collective-permute-start.4) | collective-permute-done | bytes 1048608 | tf_op jit(solution)/shard_map/ppermute | solution.py:216
  33.8 0.0 collective-permute-done.5.wp_ref
  33.8 3.7 %project.5 = (bf16[2,336,512]{2,1,0:T(8,128)(2,1)S(1)}, bf16[2,336,512]{2,1,0:T(8,128)(2,1)S(1)}) custom-call(s32[8]{0:T(128)S(1)} %fusion.21.cols_ref, bf16[1024,512]{1,0:T(8,128)(2,1)S(1)} %gated.1.g_ref, bf16[1024,512]{1,0:T(8,128)(2,1)S(1)} %collective-permute-done.4.gp_ref, bf16[512,8192]{1,0:T(8,128)(2,1)} %w_ref.9, ...), custom_call_target="tpu_custom_call" | custom-call | tf_op jit(solution)/shard_map/project/pallas_call | solution.py:279
  37.5 3.1 %collective-permute-start.7 = (bf16[2,336,512]{2,1,0:T(8,128)(2,1)S(1)}, bf16[2,336,512]{2,1,0:T(8,128)(2,1)S(1)}, u32[]{:S(2)}, u32[]{:S(2)}) collective-permute-start(bf16[2,336,512]{2,1,0:T(8,128)(2,1)S(1)} %get-tuple-element.31), channel_id=1, source_target_pairs={{0,12},{1,13},{2,14},{3,15},{4,0},{5,1},{6,2},{7,3},{8,4},{9,5},{1... | collective-permute-start | bytes 2064392 | tf_op jit(solution)/shard_map/ppermute | solution.py:216
  40.6 0.0 collective-permute-start.6
  40.6 0.0 copy-done.2
  40.6 4.1 %project.9 = bf16[4,352,512]{2,1,0:T(8,128)(2,1)S(1)} custom-call(s32[8]{0:T(128)S(1)} %fusion.21.cols_ref, bf16[1024,512]{1,0:T(8,128)(2,1)S(1)} %gated.1.g_ref, bf16[1024,512]{1,0:T(8,128)(2,1)S(1)} %collective-permute-done.4.gp_ref, bf16[512,8192]{1,0:T(8,128)(2,1)} %w_ref.9, bf16[512,8192]{1,0:T(8,128)(2,1)} %collective-permute-done.5.wp_ref), custom_call_target="tpu_custom_call" | custom-call | tf_op jit(solution)/shard_map/project/pallas_call | solution.py:279
  44.7 3.9 %collective-permute-start.15 = (bf16[4,352,512]{2,1,0:T(8,128)(2,1)S(1)}, bf16[4,352,512]{2,1,0:T(8,128)(2,1)S(1)}, u32[]{:S(2)}, u32[]{:S(2)}) collective-permute-start(bf16[4,352,512]{2,1,0:T(8,128)(2,1)S(1)} %project.9), channel_id=1, source_target_pairs={{0,2},{1,3},{2,0},{3,1},{4,6},{5,7},{6,4},{7,5},{8,10},{9,11},{10,... | collective-permute-start | bytes 4325384 | tf_op jit(solution)/shard_map/ppermute | solution.py:216
  48.6 0.0 copy-done
  48.6 5.4 %project.7 = (bf16[1,336,512]{2,1,0:T(8,128)(2,1)S(1)}, bf16[1,336,512]{2,1,0:T(8,128)(2,1)S(1)}, bf16[1,336,512]{2,1,0:T(8,128)(2,1)S(1)}, bf16[1,336,512]{2,1,...) custom-call(s32[8]{0:T(128)S(1)} %fusion.21.cols_ref, ...), custom_call_target="tpu_custom_call" | custom-call | tf_op jit(solution)/shard_map/project/pallas_call | solution.py:279
  54.0 0.7 collective-permute-start.10
  54.7 2.7 %collective-permute-start.11 = (bf16[336,512]{1,0:T(8,128)(2,1)S(1)}, bf16[336,512]{1,0:T(8,128)(2,1)S(1)}, u32[]{:S(2)}, u32[]{:S(2)}) collective-permute-start(bf16[336,512]{1,0:T(8,128)(2,1)S(1)} %bitcast.38), channel_id=1, source_target_pairs={{0,12},{1,13},{2,14},{3,15},{4,0},{5,1},{6,2},{7,3},{8,4},{9,5},{1... | collective-permute-start | bytes 1032200 | tf_op jit(solution)/shard_map/ppermute | solution.py:216
  57.4 0.0 collective-permute-done.7.refs_1_
  57.4 0.1 fusion.11
  57.5 2.0 %collective-permute-start.13 = (bf16[336,512]{1,0:T(8,128)(2,1)S(1)}, bf16[336,512]{1,0:T(8,128)(2,1)S(1)}, u32[]{:S(2)}, u32[]{:S(2)}) collective-permute-start(bf16[336,512]{1,0:T(8,128)(2,1)S(1)} %fusion.11), channel_id=1, source_target_pairs={{0,12},{1,13},{2,14},{3,15},{4,0},{5,1},{6,2},{7,3},{8,4},{9,5},{1... | collective-permute-start | bytes 1032200 | tf_op jit(solution)/shard_map/ppermute | solution.py:216
  59.5 0.6 collective-permute-done.6.refs_0_
  60.1 0.1 fusion.10
  60.2 0.1 collective-permute-start.12
  60.3 5.5 %project.6 = (bf16[2,336,512]{2,1,0:T(8,128)(2,1)S(1)}, bf16[2,336,512]{2,1,0:T(8,128)(2,1)S(1)}, bf16[1,336,512]{2,1,0:T(8,128)(2,1)S(1)}, bf16[1,336,512]{2,1,0:T(8,128)(2,1)S(1)}) custom-call(s32[8]{0:T(128)S(1)} %fusion.21.cols_ref, bf16[1024,512]{1,0:T(8,128)(2,1)} %copy-done, bf16[1024,512]{1,0:T(8,128)(2,1)} %copy-done.2, bf16[512,8192]{1,0:T(8,128)(2,1)} %w_ref.9, ...), custom_call_target="tpu_custom_call" | custom-call | tf_op jit(solution)/shard_map/project/pallas_call | solution.py:279
  65.8 0.0 copy-start.1
  65.8 1.7 %collective-permute-done.10 = bf16[336,512]{1,0:T(8,128)(2,1)S(1)} collective-permute-done((bf16[336,512]{1,0:T(8,128)(2,1)S(1)}, bf16[336,512]{1,0:T(8,128)(2,1)S(1)}, u32[]{:S(2)}, u32[]{:S(2)}) %collective-permute-start.10) | collective-permute-done | bytes 344096 | tf_op jit(solution)/shard_map/ppermute | solution.py:216
  67.5 0.0 collective-permute-start.8
  67.5 0.0 collective-permute-done.11
  67.5 3.2 %collective-permute-start.9 = (bf16[2,336,512]{2,1,0:T(8,128)(2,1)S(1)}, bf16[2,336,512]{2,1,0:T(8,128)(2,1)S(1)}, u32[]{:S(2)}, u32[]{:S(2)}) collective-permute-start(bf16[2,336,512]{2,1,0:T(8,128)(2,1)S(1)} %get-tuple-element.34), channel_id=1, source_target_pairs={{0,12},{1,13},{2,14},{3,15},{4,0},{5,1},{6,2},{7,3},{8,4},{9,5},{1... | collective-permute-start | bytes 2064392 | tf_op jit(solution)/shard_map/ppermute | solution.py:216
  70.7 2.6 %collective-permute-done.13 = bf16[336,512]{1,0:T(8,128)(2,1)S(1)} collective-permute-done((bf16[336,512]{1,0:T(8,128)(2,1)S(1)}, bf16[336,512]{1,0:T(8,128)(2,1)S(1)}, u32[]{:S(2)}, u32[]{:S(2)}) %collective-permute-start.13) | collective-permute-done | bytes 344096 | tf_op jit(solution)/shard_map/ppermute | solution.py:216
  73.3 1.6 %collective-permute-done.12 = bf16[336,512]{1,0:T(8,128)(2,1)S(1)} collective-permute-done((bf16[336,512]{1,0:T(8,128)(2,1)S(1)}, bf16[336,512]{1,0:T(8,128)(2,1)S(1)}, u32[]{:S(2)}, u32[]{:S(2)}) %collective-permute-start.12) | collective-permute-done | bytes 344096 | tf_op jit(solution)/shard_map/ppermute | solution.py:216
  74.9 0.3 fusion.14
  75.2 0.1 pad_maximum_fusion.1
  75.2 4.1 %collective-permute-start.14 = (bf16[2,336,512]{2,1,0:T(8,128)(2,1)S(1)}, bf16[2,336,512]{2,1,0:T(8,128)(2,1)S(1)}, u32[]{:S(2)}, u32[]{:S(2)}) collective-permute-start(bf16[2,336,512]{2,1,0:T(8,128)(2,1)S(1)} %pad_maximum_fusion.1), channel_id=1, source_target_pairs={{0,2},{1,3},{2,0},{3,1},{4,6},{5,7},{6,4},{7,5},{8,10},{9,11},{10,... | collective-permute-start | bytes 2064392 | tf_op jit(solution)/shard_map/ppermute | solution.py:216
  79.3 4.1 %project.8 = bf16[4,352,512]{2,1,0:T(8,128)(2,1)S(1)} custom-call(s32[8]{0:T(128)S(1)} %fusion.21.cols_ref, bf16[1024,512]{1,0:T(8,128)(2,1)S(1)} %copy-done.1, bf16[1024,512]{1,0:T(8,128)(2,1)S(1)} %copy-done.3, bf16[512,8192]{1,0:T(8,128)(2,1)} %w_ref.9, bf16[512,8192]{1,0:T(8,128)(2,1)} %collective-permute-done.5.wp_ref), custom_call_target="tpu_custom_call" | custom-call | tf_op jit(solution)/shard_map/project/pallas_call | solution.py:279
  83.5 0.0 collective-permute-done.15
  83.5 0.3 fusion.7
  83.8 0.1 collective-permute-start.16
  83.9 3.2 %collective-permute-start.18 = (bf16[352,512]{1,0:T(8,128)(2,1)S(1)}, bf16[352,512]{1,0:T(8,128)(2,1)S(1)}, u32[]{:S(2)}, u32[]{:S(2)}) collective-permute-start(bf16[352,512]{1,0:T(8,128)(2,1)S(1)} %get-tuple-element.50), channel_id=1, source_target_pairs={{0,12},{1,13},{2,14},{3,15},{4,0},{5,1},{6,2},{7,3},{8,4},{9,5},{1... | collective-permute-start | bytes 1081352 | tf_op jit(solution)/shard_map/ppermute | solution.py:216
  87.1 2.5 %collective-permute-done.8 = bf16[2,336,512]{2,1,0:T(8,128)(2,1)S(1)} collective-permute-done((bf16[2,336,512]{2,1,0:T(8,128)(2,1)S(1)}, bf16[2,336,512]{2,1,0:T(8,128)(2,1)S(1)}, u32[]{:S(2)}, u32[]{:S(2)}) %collective-permute-start.8) | collective-permute-done | bytes 688160 | tf_op jit(solution)/shard_map/ppermute | solution.py:216
  89.6 0.0 collective-permute-start.17
  89.6 0.0 collective-permute-done.9
  89.6 5.4 %collective-permute-done.14 = bf16[2,336,512]{2,1,0:T(8,128)(2,1)S(1)} collective-permute-done((bf16[2,336,512]{2,1,0:T(8,128)(2,1)S(1)}, bf16[2,336,512]{2,1,0:T(8,128)(2,1)S(1)}, u32[]{:S(2)}, u32[]{:S(2)}) %collective-permute-start.14) | collective-permute-done | bytes 688160 | tf_op jit(solution)/shard_map/ppermute | solution.py:216
  95.0 0.4 fusion.12
  95.4 8.6 %collective-permute-done.16 = bf16[352,512]{1,0:T(8,128)(2,1)S(1)} collective-permute-done((bf16[352,512]{1,0:T(8,128)(2,1)S(1)}, bf16[352,512]{1,0:T(8,128)(2,1)S(1)}, u32[]{:S(2)}, u32[]{:S(2)}) %collective-permute-start.16) | collective-permute-done | bytes 360480 | tf_op jit(solution)/shard_map/ppermute | solution.py:216
  103.9 0.0 collective-permute-done.18
  103.9 0.0 collective-permute-done.17
  104.0 0.2 fusion.2
  104.2 1.0 pad_maximum_fusion
  (9 shorter events, 0.0 us)
Async XLA Ops:
  0.0 33.8 %collective-permute-start.5 = (bf16[512,8192]{1,0:T(8,128)(2,1)}, bf16[512,8192]{1,0:T(8,128)(2,1)}, u32[]{:S(2)}, u32[]{:S(2)}) collective-permute-start(bf16[512,8192]{1,0:T(8,128)(2,1)} %w_ref.9), channel_id=1, source_target_pairs={{0,1},{1,0},{2,3},{3,2},{4,5},{5,4},{6,7},{7,6},{8,9},{9,8},{10,11... | collective-permute-start | bytes 25165832 | tf_op jit(solution)/shard_map/ppermute | solution.py:216
  0.0 20.7 %copy-start.6 = (f32[16,512]{1,0:T(8,128)S(1)}, f32[16,512]{1,0:T(8,128)}, u32[]{:S(2)}) copy-start(f32[16,512]{1,0:T(8,128)} %rate_ref.3) | copy-start | bytes 98308
  0.0 20.7 %copy-start.7 = (f32[3,3,512]{2,1,0:T(4,128)S(1)}, f32[3,3,512]{2,1,0:T(4,128)}, u32[]{:S(2)}) copy-start(f32[3,3,512]{2,1,0:T(4,128)} %sf_ref.3) | copy-start | bytes 55300
  0.0 20.7 %copy-start.8 = (f32[16,512]{1,0:T(8,128)S(1)}, f32[16,512]{1,0:T(8,128)}, u32[]{:S(2)}) copy-start(f32[16,512]{1,0:T(8,128)} %res_ref.1) | copy-start | bytes 98308
  6.4 4.3 %collective-permute-start = (bf16[32,512]{1,0:T(8,128)(2,1)}, bf16[32,512]{1,0:T(8,128)(2,1)S(1)}, u32[]{:S(2)}, u32[]{:S(2)}) collective-permute-start(bf16[32,512]{1,0:T(8,128)(2,1)} %get-tuple-element.29), channel_id=1, source_target_pairs={{0,64},{16,80},{32,96},{48,112},{64,0},{80,16},{96,32},{112,48},{1... | collective-permute-start | bytes 98312 | tf_op jit(solution)/shard_map/ppermute | solution.py:216
  11.5 5.0 %collective-permute-start.3 = (bf16[2,32,512]{2,1,0:T(8,128)(2,1)S(1)}, bf16[2,32,512]{2,1,0:T(8,128)(2,1)S(1)}, u32[]{:S(2)}, u32[]{:S(2)}) collective-permute-start(bf16[2,32,512]{2,1,0:T(8,128)(2,1)S(1)} %pad_maximum_fusion.2.refs_0_), channel_id=1, source_target_pairs={{0,48},{16,0},{32,16},{48,32},{64,112},{80,64},{96,80},{112,96},{1... | collective-permute-start | bytes 196616 | tf_op jit(solution)/shard_map/ppermute | solution.py:216
  14.2 5.8 %collective-permute-start.2 = (bf16[2,32,512]{2,1,0:T(8,128)(2,1)S(1)}, bf16[2,32,512]{2,1,0:T(8,128)(2,1)S(1)}, u32[]{:S(2)}, u32[]{:S(2)}) collective-permute-start(bf16[2,32,512]{2,1,0:T(8,128)(2,1)S(1)} %pad_maximum_fusion.2.refs_0_), channel_id=1, source_target_pairs={{0,32},{16,48},{32,0},{48,16},{64,96},{80,112},{96,64},{112,80},{1... | collective-permute-start | bytes 196616 | tf_op jit(solution)/shard_map/ppermute | solution.py:216
  15.0 5.7 %collective-permute-start.1 = (bf16[2,32,512]{2,1,0:T(8,128)(2,1)S(1)}, bf16[2,32,512]{2,1,0:T(8,128)(2,1)S(1)}, u32[]{:S(2)}, u32[]{:S(2)}) collective-permute-start(bf16[2,32,512]{2,1,0:T(8,128)(2,1)S(1)} %pad_maximum_fusion.2.refs_0_), channel_id=1, source_target_pairs={{0,16},{16,32},{32,48},{48,0},{64,80},{80,96},{96,112},{112,64},{1... | collective-permute-start | bytes 196616 | tf_op jit(solution)/shard_map/ppermute | solution.py:216
  20.7 1.6 %copy-start.4 = (f32[128,8,512]{2,1,0:T(8,128)S(1)}, f32[128,8,512]{2,1,0:T(8,128)}, u32[]{:S(2)}) copy-start(f32[128,8,512]{2,1,0:T(8,128)} %get-tuple-element.27.p_ref) | copy-start | bytes 6291460
  22.3 0.9 copy-start.5
  31.0 17.6 %copy-start = (bf16[1024,512]{1,0:T(8,128)(2,1)}, bf16[1024,512]{1,0:T(8,128)(2,1)S(1)}, u32[]{:S(2)}) copy-start(bf16[1024,512]{1,0:T(8,128)(2,1)S(1)} %gated.1.g_ref) | copy-start | bytes 3145732
  31.1 2.7 %collective-permute-start.4 = (bf16[1024,512]{1,0:T(8,128)(2,1)S(1)}, bf16[1024,512]{1,0:T(8,128)(2,1)S(1)}, u32[]{:S(2)}, u32[]{:S(2)}) collective-permute-start(bf16[1024,512]{1,0:T(8,128)(2,1)S(1)} %gated.1.g_ref), channel_id=1, source_target_pairs={{0,1},{1,0},{2,3},{3,2},{4,5},{5,4},{6,7},{7,6},{8,9},{9,8},{10,11... | collective-permute-start | bytes 3145736 | tf_op jit(solution)/shard_map/ppermute | solution.py:216
  33.8 6.8 %copy-start.2 = (bf16[1024,512]{1,0:T(8,128)(2,1)}, bf16[1024,512]{1,0:T(8,128)(2,1)S(1)}, u32[]{:S(2)}) copy-start(bf16[1024,512]{1,0:T(8,128)(2,1)S(1)} %collective-permute-done.4.gp_ref) | copy-start | bytes 3145732
  37.5 19.9 %collective-permute-start.7 = (bf16[2,336,512]{2,1,0:T(8,128)(2,1)S(1)}, bf16[2,336,512]{2,1,0:T(8,128)(2,1)S(1)}, u32[]{:S(2)}, u32[]{:S(2)}) collective-permute-start(bf16[2,336,512]{2,1,0:T(8,128)(2,1)S(1)} %get-tuple-element.31), channel_id=1, source_target_pairs={{0,12},{1,13},{2,14},{3,15},{4,0},{5,1},{6,2},{7,3},{8,4},{9,5},{1... | collective-permute-start | bytes 2064392 | tf_op jit(solution)/shard_map/ppermute | solution.py:216
  40.6 19.5 %collective-permute-start.6 = (bf16[2,336,512]{2,1,0:T(8,128)(2,1)S(1)}, bf16[2,336,512]{2,1,0:T(8,128)(2,1)S(1)}, u32[]{:S(2)}, u32[]{:S(2)}) collective-permute-start(bf16[2,336,512]{2,1,0:T(8,128)(2,1)S(1)} %get-tuple-element.30), channel_id=1, source_target_pairs={{0,4},{1,5},{2,6},{3,7},{4,8},{5,9},{6,10},{7,11},{8,12},{9,13},{1... | collective-permute-start | bytes 2064392 | tf_op jit(solution)/shard_map/ppermute | solution.py:216
  44.7 38.7 %collective-permute-start.15 = (bf16[4,352,512]{2,1,0:T(8,128)(2,1)S(1)}, bf16[4,352,512]{2,1,0:T(8,128)(2,1)S(1)}, u32[]{:S(2)}, u32[]{:S(2)}) collective-permute-start(bf16[4,352,512]{2,1,0:T(8,128)(2,1)S(1)} %project.9), channel_id=1, source_target_pairs={{0,2},{1,3},{2,0},{3,1},{4,6},{5,7},{6,4},{7,5},{8,10},{9,11},{10,... | collective-permute-start | bytes 4325384 | tf_op jit(solution)/shard_map/ppermute | solution.py:216
  54.0 13.5 %collective-permute-start.10 = (bf16[336,512]{1,0:T(8,128)(2,1)S(1)}, bf16[336,512]{1,0:T(8,128)(2,1)S(1)}, u32[]{:S(2)}, u32[]{:S(2)}) collective-permute-start(bf16[336,512]{1,0:T(8,128)(2,1)S(1)} %bitcast.39), channel_id=1, source_target_pairs={{0,4},{1,5},{2,6},{3,7},{4,8},{5,9},{6,10},{7,11},{8,12},{9,13},{1... | collective-permute-start | bytes 1032200 | tf_op jit(solution)/shard_map/ppermute | solution.py:216
  54.7 12.8 %collective-permute-start.11 = (bf16[336,512]{1,0:T(8,128)(2,1)S(1)}, bf16[336,512]{1,0:T(8,128)(2,1)S(1)}, u32[]{:S(2)}, u32[]{:S(2)}) collective-permute-start(bf16[336,512]{1,0:T(8,128)(2,1)S(1)} %bitcast.38), channel_id=1, source_target_pairs={{0,12},{1,13},{2,14},{3,15},{4,0},{5,1},{6,2},{7,3},{8,4},{9,5},{1... | collective-permute-start | bytes 1032200 | tf_op jit(solution)/shard_map/ppermute | solution.py:216
  57.5 15.8 %collective-permute-start.13 = (bf16[336,512]{1,0:T(8,128)(2,1)S(1)}, bf16[336,512]{1,0:T(8,128)(2,1)S(1)}, u32[]{:S(2)}, u32[]{:S(2)}) collective-permute-start(bf16[336,512]{1,0:T(8,128)(2,1)S(1)} %fusion.11), channel_id=1, source_target_pairs={{0,12},{1,13},{2,14},{3,15},{4,0},{5,1},{6,2},{7,3},{8,4},{9,5},{1... | collective-permute-start | bytes 1032200 | tf_op jit(solution)/shard_map/ppermute | solution.py:216
  60.2 14.7 %collective-permute-start.12 = (bf16[336,512]{1,0:T(8,128)(2,1)S(1)}, bf16[336,512]{1,0:T(8,128)(2,1)S(1)}, u32[]{:S(2)}, u32[]{:S(2)}) collective-permute-start(bf16[336,512]{1,0:T(8,128)(2,1)S(1)} %fusion.10), channel_id=1, source_target_pairs={{0,4},{1,5},{2,6},{3,7},{4,8},{5,9},{6,10},{7,11},{8,12},{9,13},{1... | collective-permute-start | bytes 1032200 | tf_op jit(solution)/shard_map/ppermute | solution.py:216
  65.8 13.5 %copy-start.1 = (bf16[1024,512]{1,0:T(8,128)(2,1)S(1)}, bf16[1024,512]{1,0:T(8,128)(2,1)}, u32[]{:S(2)}) copy-start(bf16[1024,512]{1,0:T(8,128)(2,1)} %copy-done) | copy-start | bytes 3145732
  65.8 13.5 %copy-start.3 = (bf16[1024,512]{1,0:T(8,128)(2,1)S(1)}, bf16[1024,512]{1,0:T(8,128)(2,1)}, u32[]{:S(2)}) copy-start(bf16[1024,512]{1,0:T(8,128)(2,1)} %copy-done.2) | copy-start | bytes 3145732
  67.5 22.1 %collective-permute-start.8 = (bf16[2,336,512]{2,1,0:T(8,128)(2,1)S(1)}, bf16[2,336,512]{2,1,0:T(8,128)(2,1)S(1)}, u32[]{:S(2)}, u32[]{:S(2)}) collective-permute-start(bf16[2,336,512]{2,1,0:T(8,128)(2,1)S(1)} %get-tuple-element.33), channel_id=1, source_target_pairs={{0,4},{1,5},{2,6},{3,7},{4,8},{5,9},{6,10},{7,11},{8,12},{9,13},{1... | collective-permute-start | bytes 2064392 | tf_op jit(solution)/shard_map/ppermute | solution.py:216
  67.5 22.1 %collective-permute-start.9 = (bf16[2,336,512]{2,1,0:T(8,128)(2,1)S(1)}, bf16[2,336,512]{2,1,0:T(8,128)(2,1)S(1)}, u32[]{:S(2)}, u32[]{:S(2)}) collective-permute-start(bf16[2,336,512]{2,1,0:T(8,128)(2,1)S(1)} %get-tuple-element.34), channel_id=1, source_target_pairs={{0,12},{1,13},{2,14},{3,15},{4,0},{5,1},{6,2},{7,3},{8,4},{9,5},{1... | collective-permute-start | bytes 2064392 | tf_op jit(solution)/shard_map/ppermute | solution.py:216
  75.2 19.8 %collective-permute-start.14 = (bf16[2,336,512]{2,1,0:T(8,128)(2,1)S(1)}, bf16[2,336,512]{2,1,0:T(8,128)(2,1)S(1)}, u32[]{:S(2)}, u32[]{:S(2)}) collective-permute-start(bf16[2,336,512]{2,1,0:T(8,128)(2,1)S(1)} %pad_maximum_fusion.1), channel_id=1, source_target_pairs={{0,2},{1,3},{2,0},{3,1},{4,6},{5,7},{6,4},{7,5},{8,10},{9,11},{10,... | collective-permute-start | bytes 2064392 | tf_op jit(solution)/shard_map/ppermute | solution.py:216
  83.8 20.2 %collective-permute-start.16 = (bf16[352,512]{1,0:T(8,128)(2,1)S(1)}, bf16[352,512]{1,0:T(8,128)(2,1)S(1)}, u32[]{:S(2)}, u32[]{:S(2)}) collective-permute-start(bf16[352,512]{1,0:T(8,128)(2,1)S(1)} %get-tuple-element.49), channel_id=1, source_target_pairs={{0,4},{1,5},{2,6},{3,7},{4,8},{5,9},{6,10},{7,11},{8,12},{9,13},{1... | collective-permute-start | bytes 1081352 | tf_op jit(solution)/shard_map/ppermute | solution.py:216
  83.9 20.1 %collective-permute-start.18 = (bf16[352,512]{1,0:T(8,128)(2,1)S(1)}, bf16[352,512]{1,0:T(8,128)(2,1)S(1)}, u32[]{:S(2)}, u32[]{:S(2)}) collective-permute-start(bf16[352,512]{1,0:T(8,128)(2,1)S(1)} %get-tuple-element.50), channel_id=1, source_target_pairs={{0,12},{1,13},{2,14},{3,15},{4,0},{5,1},{6,2},{7,3},{8,4},{9,5},{1... | collective-permute-start | bytes 1081352 | tf_op jit(solution)/shard_map/ppermute | solution.py:216
  89.6 14.3 %collective-permute-start.17 = (bf16[352,512]{1,0:T(8,128)(2,1)S(1)}, bf16[352,512]{1,0:T(8,128)(2,1)S(1)}, u32[]{:S(2)}, u32[]{:S(2)}) collective-permute-start(bf16[352,512]{1,0:T(8,128)(2,1)S(1)} %get-tuple-element.51), channel_id=1, source_target_pairs={{0,8},{1,9},{2,10},{3,11},{4,12},{5,13},{6,14},{7,15},{8,0},{9,1},... | collective-permute-start | bytes 1081352 | tf_op jit(solution)/shard_map/ppermute | solution.py:216

commit v9 on v8

--- a/solution.py
+++ b/solution.py
@@ -296,7 +296,7 @@
     return sum(p.astype(f32) for p in parts).astype(bf16)
 
 
-Z_TOK = 352
+Z_TOK = 320
 
 
 def per_device(features, short_filter, decay_rate, residues, out_weight):
@@ -334,16 +334,20 @@
     )
     last = (cols, lax.optimization_barrier((mine, stay_a))[0]) + operands[2:]
     (near,) = project(last, [((dy, 0), [(z, 0)]) for dy in (2, 3, 1, 0)], [Z_TOK])
-    one, two, three = (total(near[i], far[dy]) for i, dy in ((2, 1), (0, 2), (1, 3)))
+    half = Z_TOK // 2
+    s2a, s2b = total(near[0, :half], far[2, :half]), total(near[0, half:], far[2, half:])
     rise, fall = to_y(rise, 1), to_y(fall, -1)
-    one, two, three = to_y(one, 1), to_y(two, 2), to_y(three, -1)
+    s2a, s2b = to_y(s2a, 1), to_y(s2b, -1)
     up, down, up_more, down_more = lax.optimization_barrier((up, down, up_more, down_more))
     over = to_far_z(jnp.stack([total(keep_a[0], up_more, down), total(keep_b[0], up, down_more)]))
     rise, fall = lax.optimization_barrier((rise, fall))
     done_a = total(stay_a[0], rise[1], fall[0], over[0])
     done_b = total(stay_b[0], rise[0], fall[1], over[1])
 
-    return jnp.concatenate([done_a, done_b, total(near[3], far[0], one, two, three)])
+    s1 = total(near[2], far[1], jnp.pad(s2a, ((0, half), (0, 0))))
+    s3 = total(near[1], far[3], jnp.pad(s2b, ((half, 0), (0, 0))))
+    s1, s3 = to_y(s1, 1), to_y(s3, -1)
+    return jnp.concatenate([done_a, done_b, total(near[3], far[0], s1, s3)])
 
 
 def solution(mesh):

time: 106 us -> 106 us (level)
  starting transfers between devices: 29.6 us -> 33 us
  waiting for transfers between devices: 32.6 us -> 29.6 us
    ppermute x19 -> x20, starting transfers between devices: 29.6 us -> 33 us  [spread(): return lax.ppermute(x, axis, [(i, j) for i, j in pairs if j is not None])]
    ppermute x19 -> x20, waiting for transfers between devices: 32.6 us -> 29.6 us  [spread(): return lax.ppermute(x, axis, [(i, j) for i, j in pairs if j is not None])]
  transfers between devices with their start and end apart: 19 -> 20, of which waited for: 12 -> 10; matrix products, arithmetic and copies ran while one was open for 2% -> 2% of each run, Pallas kernels for 32% -> 32%
where the time goes in v9:
time: 106 us
  Pallas kernels  37.2 us (35%)
  starting transfers between devices  33 us (31%)
  waiting for transfers between devices  29.6 us (28%)
  other arithmetic  3.24 us (3%)
  local copies, waits for them, and re-layouts  2.57 us (2%)
    ppermute x20, starting transfers between devices, spread(): return lax.ppermute(x, axis, [(i, j) for i, j in pairs if j is not None])  33 us
    ppermute x20, waiting for transfers between devices, spread(): return lax.ppermute(x, axis, [(i, j) for i, j in pairs if j is not None])  29.6 us
    pallas_call x5, Pallas kernels, project(): pl.pallas_call(functools.partial(project_kernel, laid, len(added)), in_sp...  23 us
    pallas_call x1, Pallas kernels, gated(): pl.pallas_call(gate_kernel, grid=(width // LANES,), in_specs=[pl.BlockSpe...  7.8 us
    pallas_call x1, Pallas kernels, states(): pl.pallas_call(state_kernel, grid=(width // LANES,), in_specs=[pl.BlockSp...  6.41 us
    unnamed x18, local copies, waits for them, and re-layouts  2.57 us
  transfers between devices with their start and end apart: 20, of which 10 were waited for; matrix products, arithmetic and copies ran while one was open for 2% of the time, Pallas kernels for 32%

profile of v9, /device:TPU:0, one launch (start us, length us, event | category | flops | bytes accessed | tf_op | source)
XLA Modules:
  0.0 105.9 jit_solution(846012940817953144)
XLA Ops:
  0.0 0.0 collective-permute-start.5
  0.0 6.4 %states.1 = (f32[128,8,512]{2,1,0:T(8,128)}, bf16[32,512]{1,0:T(8,128)(2,1)}, f32[16,8,512]{2,1,0:T(8,128)}) custom-call(bf16[3,1024,512]{2,1,0:T(8,128)(2,1)} %bitcast.44, bf16[3,1024,512]{2,1,0:T(8,128)(2,1)} %bitcast.45, bf16[3,1024,512]{2,1,0:T(8,128)(2,1)} %bitcast.46, f32[3,3,512]{2,1,0:T(4,128)} %sf_ref.3, f32[16,512]{1,0:T(8,128)} %rate_ref.3), custom_call_target="tpu_custom_call" | custom-call | tf_op jit(solution)/shard_map/states/pallas_call | solution.py:157
  6.4 2.0 %collective-permute-start = (bf16[32,512]{1,0:T(8,128)(2,1)}, bf16[32,512]{1,0:T(8,128)(2,1)S(1)}, u32[]{:S(2)}, u32[]{:S(2)}) collective-permute-start(bf16[32,512]{1,0:T(8,128)(2,1)} %get-tuple-element.29), channel_id=1, source_target_pairs={{0,64},{16,80},{32,96},{48,112},{64,0},{80,16},{96,32},{112,48},{1... | collective-permute-start | bytes 98312 | tf_op jit(solution)/shard_map/ppermute | solution.py:216
  8.4 2.3 %collective-permute-done = bf16[32,512]{1,0:T(8,128)(2,1)S(1)} collective-permute-done((bf16[32,512]{1,0:T(8,128)(2,1)}, bf16[32,512]{1,0:T(8,128)(2,1)S(1)}, u32[]{:S(2)}, u32[]{:S(2)}) %collective-permute-start) | collective-permute-done | bytes 32800 | tf_op jit(solution)/shard_map/ppermute | solution.py:216
  10.7 0.8 pad_maximum_fusion.2.refs_0_
  11.5 2.8 %collective-permute-start.3 = (bf16[2,32,512]{2,1,0:T(8,128)(2,1)S(1)}, bf16[2,32,512]{2,1,0:T(8,128)(2,1)S(1)}, u32[]{:S(2)}, u32[]{:S(2)}) collective-permute-start(bf16[2,32,512]{2,1,0:T(8,128)(2,1)S(1)} %pad_maximum_fusion.2.refs_0_), channel_id=1, source_target_pairs={{0,48},{16,0},{32,16},{48,32},{64,112},{80,64},{96,80},{112,96},{1... | collective-permute-start | bytes 196616 | tf_op jit(solution)/shard_map/ppermute | solution.py:216
  14.2 0.8 collective-permute-start.2
  15.0 0.9 collective-permute-start.1
  15.9 0.5 collective-permute-done.3.refs_3_
  16.4 3.6 %collective-permute-done.2.refs_2_ = bf16[2,32,512]{2,1,0:T(8,128)(2,1)S(1)} collective-permute-done((bf16[2,32,512]{2,1,0:T(8,128)(2,1)S(1)}, bf16[2,32,512]{2,1,0:T(8,128)(2,1)S(1)}, u32[]{:S(2)}, u32[]{:S(2)}) %collective-permute-start.2) | collective-permute-done | bytes 65568 | tf_op jit(solution)/shard_map/ppermute | solution.py:216
  20.0 0.7 collective-permute-done.1.refs_1_
  20.7 0.0 copy-done.6
  20.7 0.0 copy-done.7
  20.7 0.0 copy-done.8
  20.7 1.6 %copy-done.4 = f32[128,8,512]{2,1,0:T(8,128)S(1)} copy-done((f32[128,8,512]{2,1,0:T(8,128)S(1)}, f32[128,8,512]{2,1,0:T(8,128)}, u32[]{:S(2)}) %copy-start.4) | copy-done | bytes 2097176
  22.3 0.9 copy-done.5
  23.2 7.8 %gated.1.g_ref = bf16[1024,512]{1,0:T(8,128)(2,1)S(1)} custom-call(s32[1]{0:T(128)} %bitcast.at_ref, bf16[3,1024,512]{2,1,0:T(8,128)(2,1)} %bitcast.47, f32[3,3,512]{2,1,0:T(4,128)S(1)} %copy-done.7, f32[16,512]{1,0:T(8,128)S(1)} %copy-done.6, f32[16,512]{1,0:T(8,128)S(1)} %copy-done.8, f32[128,8,512]{2,1,0:T(8,128)S(1)} %copy-done.4, ...), custom_call_target="tpu_custom_call" | custom-call | tf_op jit(solution)/shard_map/gated/pallas_call | solution.py:189
  31.1 0.0 copy-start
  31.1 0.1 collective-permute-start.4
  31.2 2.6 %collective-permute-done.4.gp_ref = bf16[1024,512]{1,0:T(8,128)(2,1)S(1)} collective-permute-done((bf16[1024,512]{1,0:T(8,128)(2,1)S(1)}, bf16[1024,512]{1,0:T(8,128)(2,1)S(1)}, u32[]{:S(2)}, u32[]{:S(2)}) %collective-permute-start.4) | collective-permute-done | bytes 1048608 | tf_op jit(solution)/shard_map/ppermute | solution.py:216
  33.8 0.0 collective-permute-done.5.wp_ref
  33.8 3.8 %project.5 = (bf16[2,352,512]{2,1,0:T(8,128)(2,1)S(1)}, bf16[2,352,512]{2,1,0:T(8,128)(2,1)S(1)}) custom-call(s32[8]{0:T(128)S(1)} %fusion.21.cols_ref, bf16[1024,512]{1,0:T(8,128)(2,1)S(1)} %gated.1.g_ref, bf16[1024,512]{1,0:T(8,128)(2,1)S(1)} %collective-permute-done.4.gp_ref, bf16[512,8192]{1,0:T(8,128)(2,1)} %w_ref.9, ...), custom_call_target="tpu_custom_call" | custom-call | tf_op jit(solution)/shard_map/project/pallas_call | solution.py:279
  37.6 3.1 %collective-permute-start.7 = (bf16[2,352,512]{2,1,0:T(8,128)(2,1)S(1)}, bf16[2,352,512]{2,1,0:T(8,128)(2,1)S(1)}, u32[]{:S(2)}, u32[]{:S(2)}) collective-permute-start(bf16[2,352,512]{2,1,0:T(8,128)(2,1)S(1)} %get-tuple-element.31), channel_id=1, source_target_pairs={{0,12},{1,13},{2,14},{3,15},{4,0},{5,1},{6,2},{7,3},{8,4},{9,5},{1... | collective-permute-start | bytes 2162696 | tf_op jit(solution)/shard_map/ppermute | solution.py:216
  40.7 0.0 collective-permute-start.6
  40.7 4.0 %project.9 = bf16[4,320,512]{2,1,0:T(8,128)(2,1)S(1)} custom-call(s32[8]{0:T(128)S(1)} %fusion.21.cols_ref, bf16[1024,512]{1,0:T(8,128)(2,1)S(1)} %gated.1.g_ref, bf16[1024,512]{1,0:T(8,128)(2,1)S(1)} %collective-permute-done.4.gp_ref, bf16[512,8192]{1,0:T(8,128)(2,1)} %w_ref.9, bf16[512,8192]{1,0:T(8,128)(2,1)} %collective-permute-done.5.wp_ref), custom_call_target="tpu_custom_call" | custom-call | tf_op jit(solution)/shard_map/project/pallas_call | solution.py:279
  44.7 3.9 %collective-permute-start.15 = (bf16[4,320,512]{2,1,0:T(8,128)(2,1)S(1)}, bf16[4,320,512]{2,1,0:T(8,128)(2,1)S(1)}, u32[]{:S(2)}, u32[]{:S(2)}) collective-permute-start(bf16[4,320,512]{2,1,0:T(8,128)(2,1)S(1)} %project.9), channel_id=1, source_target_pairs={{0,2},{1,3},{2,0},{3,1},{4,6},{5,7},{6,4},{7,5},{8,10},{9,11},{10,... | collective-permute-start | bytes 3932168 | tf_op jit(solution)/shard_map/ppermute | solution.py:216
  48.6 5.5 %project.7 = (bf16[1,352,512]{2,1,0:T(8,128)(2,1)S(1)}, bf16[1,352,512]{2,1,0:T(8,128)(2,1)S(1)}, bf16[1,352,512]{2,1,0:T(8,128)(2,1)S(1)}, bf16[1,352,512]{2,1,...) custom-call(s32[8]{0:T(128)S(1)} %fusion.21.cols_ref, ...), custom_call_target="tpu_custom_call" | custom-call | tf_op jit(solution)/shard_map/project/pallas_call | solution.py:279
  54.1 0.7 collective-permute-start.10
  54.7 2.7 %collective-permute-start.11 = (bf16[352,512]{1,0:T(8,128)(2,1)S(1)}, bf16[352,512]{1,0:T(8,128)(2,1)S(1)}, u32[]{:S(2)}, u32[]{:S(2)}) collective-permute-start(bf16[352,512]{1,0:T(8,128)(2,1)S(1)} %bitcast.42), channel_id=1, source_target_pairs={{0,12},{1,13},{2,14},{3,15},{4,0},{5,1},{6,2},{7,3},{8,4},{9,5},{1... | collective-permute-start | bytes 1081352 | tf_op jit(solution)/shard_map/ppermute | solution.py:216
  57.4 0.0 collective-permute-done.7.refs_1_
  57.5 0.1 fusion.9
  57.5 2.7 %collective-permute-start.13 = (bf16[352,512]{1,0:T(8,128)(2,1)S(1)}, bf16[352,512]{1,0:T(8,128)(2,1)S(1)}, u32[]{:S(2)}, u32[]{:S(2)}) collective-permute-start(bf16[352,512]{1,0:T(8,128)(2,1)S(1)} %fusion.9), channel_id=1, source_target_pairs={{0,12},{1,13},{2,14},{3,15},{4,0},{5,1},{6,2},{7,3},{8,4},{9,5},{1... | collective-permute-start | bytes 1081352 | tf_op jit(solution)/shard_map/ppermute | solution.py:216
  60.2 0.7 collective-permute-done.6.refs_0_
  60.9 0.1 fusion.8
  61.0 0.0 copy-start.1
  61.1 0.1 collective-permute-start.12
  61.1 5.8 %project.6 = (bf16[2,352,512]{2,1,0:T(8,128)(2,1)S(1)}, bf16[2,352,512]{2,1,0:T(8,128)(2,1)S(1)}, bf16[1,352,512]{2,1,0:T(8,128)(2,1)S(1)}, bf16[1,352,512]{2,1,0:T(8,128)(2,1)S(1)}) custom-call(s32[8]{0:T(128)S(1)} %fusion.21.cols_ref, bf16[1024,512]{1,0:T(8,128)(2,1)} %copy-done, bf16[1024,512]{1,0:T(8,128)(2,1)} %copy-done.2, bf16[512,8192]{1,0:T(8,128)(2,1)} %w_ref.9, ...), custom_call_target="tpu_custom_call" | custom-call | tf_op jit(solution)/shard_map/project/pallas_call | solution.py:279
  66.9 4.0 %project.8 = bf16[4,320,512]{2,1,0:T(8,128)(2,1)S(1)} custom-call(s32[8]{0:T(128)S(1)} %fusion.21.cols_ref, bf16[1024,512]{1,0:T(8,128)(2,1)S(1)} %copy-done.1, bf16[1024,512]{1,0:T(8,128)(2,1)S(1)} %copy-done.3, bf16[512,8192]{1,0:T(8,128)(2,1)} %w_ref.9, bf16[512,8192]{1,0:T(8,128)(2,1)} %collective-permute-done.5.wp_ref), custom_call_target="tpu_custom_call" | custom-call | tf_op jit(solution)/shard_map/project/pallas_call | solution.py:279
  71.0 0.0 collective-permute-done.10
  71.0 0.3 collective-permute-start.8
  71.2 0.0 collective-permute-done.11
  71.2 3.2 %collective-permute-start.9 = (bf16[2,352,512]{2,1,0:T(8,128)(2,1)S(1)}, bf16[2,352,512]{2,1,0:T(8,128)(2,1)S(1)}, u32[]{:S(2)}, u32[]{:S(2)}) collective-permute-start(bf16[2,352,512]{2,1,0:T(8,128)(2,1)S(1)} %get-tuple-element.34), channel_id=1, source_target_pairs={{0,12},{1,13},{2,14},{3,15},{4,0},{5,1},{6,2},{7,3},{8,4},{9,5},{1... | collective-permute-start | bytes 2162696 | tf_op jit(solution)/shard_map/ppermute | solution.py:216
  74.5 0.0 collective-permute-done.13
  74.5 1.9 %collective-permute-done.12 = bf16[352,512]{1,0:T(8,128)(2,1)S(1)} collective-permute-done((bf16[352,512]{1,0:T(8,128)(2,1)S(1)}, bf16[352,512]{1,0:T(8,128)(2,1)S(1)}, u32[]{:S(2)}, u32[]{:S(2)}) %collective-permute-start.12) | collective-permute-done | bytes 360480 | tf_op jit(solution)/shard_map/ppermute | solution.py:216
  76.4 1.0 collective-permute-done.15
  77.4 0.1 fusion.14
  77.5 0.4 collective-permute-start.16
  77.8 2.9 %collective-permute-start.18 = (bf16[160,512]{1,0:T(8,128)(2,1)S(1)}, bf16[160,512]{1,0:T(8,128)(2,1)S(1)}, u32[]{:S(2)}, u32[]{:S(2)}) collective-permute-start(bf16[160,512]{1,0:T(8,128)(2,1)S(1)} %get-tuple-element.52), channel_id=1, source_target_pairs={{0,12},{1,13},{2,14},{3,15},{4,0},{5,1},{6,2},{7,3},{8,4},{9,5},{1... | collective-permute-start | bytes 491528 | tf_op jit(solution)/shard_map/ppermute | solution.py:216
  80.8 0.3 fusion.12
  81.1 0.1 pad_maximum_fusion.1
  81.1 3.3 %collective-permute-start.14 = (bf16[2,352,512]{2,1,0:T(8,128)(2,1)S(1)}, bf16[2,352,512]{2,1,0:T(8,128)(2,1)S(1)}, u32[]{:S(2)}, u32[]{:S(2)}) collective-permute-start(bf16[2,352,512]{2,1,0:T(8,128)(2,1)S(1)} %pad_maximum_fusion.1), channel_id=1, source_target_pairs={{0,2},{1,3},{2,0},{3,1},{4,6},{5,7},{6,4},{7,5},{8,10},{9,11},{10,... | collective-permute-start | bytes 2162696 | tf_op jit(solution)/shard_map/ppermute | solution.py:216
  84.5 9.7 %collective-permute-done.16 = bf16[160,512]{1,0:T(8,128)(2,1)S(1)} collective-permute-done((bf16[160,512]{1,0:T(8,128)(2,1)S(1)}, bf16[160,512]{1,0:T(8,128)(2,1)S(1)}, u32[]{:S(2)}, u32[]{:S(2)}) %collective-permute-start.16) | collective-permute-done | bytes 163872 | tf_op jit(solution)/shard_map/ppermute | solution.py:216
  94.2 0.0 collective-permute-done.18
  94.2 0.2 fusion.5
  94.4 0.1 collective-permute-start.17
  94.5 3.2 %collective-permute-start.19 = (bf16[320,512]{1,0:T(8,128)(2,1)S(1)}, bf16[320,512]{1,0:T(8,128)(2,1)S(1)}, u32[]{:S(2)}, u32[]{:S(2)}) collective-permute-start(bf16[320,512]{1,0:T(8,128)(2,1)S(1)} %get-tuple-element.50), channel_id=1, source_target_pairs={{0,12},{1,13},{2,14},{3,15},{4,0},{5,1},{6,2},{7,3},{8,4},{9,5},{1... | collective-permute-start | bytes 983048 | tf_op jit(solution)/shard_map/ppermute | solution.py:216
  97.7 0.0 collective-permute-done.8
  97.7 0.0 collective-permute-done.9
  97.7 6.5 %collective-permute-done.17 = bf16[320,512]{1,0:T(8,128)(2,1)S(1)} collective-permute-done((bf16[320,512]{1,0:T(8,128)(2,1)S(1)}, bf16[320,512]{1,0:T(8,128)(2,1)S(1)}, u32[]{:S(2)}, u32[]{:S(2)}) %collective-permute-start.17) | collective-permute-done | bytes 327712 | tf_op jit(solution)/shard_map/ppermute | solution.py:216
  104.3 0.0 collective-permute-done.19
  104.3 0.2 fusion.7
  104.4 0.0 collective-permute-done.14
  104.4 0.4 fusion.10
  104.8 1.0 pad_maximum_fusion
  (12 shorter events, 0.0 us)
Async XLA Ops:
  0.0 33.8 %collective-permute-start.5 = (bf16[512,8192]{1,0:T(8,128)(2,1)}, bf16[512,8192]{1,0:T(8,128)(2,1)}, u32[]{:S(2)}, u32[]{:S(2)}) collective-permute-start(bf16[512,8192]{1,0:T(8,128)(2,1)} %w_ref.9), channel_id=1, source_target_pairs={{0,1},{1,0},{2,3},{3,2},{4,5},{5,4},{6,7},{7,6},{8,9},{9,8},{10,11... | collective-permute-start | bytes 25165832 | tf_op jit(solution)/shard_map/ppermute | solution.py:216
  0.0 20.7 %copy-start.6 = (f32[16,512]{1,0:T(8,128)S(1)}, f32[16,512]{1,0:T(8,128)}, u32[]{:S(2)}) copy-start(f32[16,512]{1,0:T(8,128)} %rate_ref.3) | copy-start | bytes 98308
  0.0 20.7 %copy-start.7 = (f32[3,3,512]{2,1,0:T(4,128)S(1)}, f32[3,3,512]{2,1,0:T(4,128)}, u32[]{:S(2)}) copy-start(f32[3,3,512]{2,1,0:T(4,128)} %sf_ref.3) | copy-start | bytes 55300
  0.0 20.7 %copy-start.8 = (f32[16,512]{1,0:T(8,128)S(1)}, f32[16,512]{1,0:T(8,128)}, u32[]{:S(2)}) copy-start(f32[16,512]{1,0:T(8,128)} %res_ref.1) | copy-start | bytes 98308
  6.4 4.3 %collective-permute-start = (bf16[32,512]{1,0:T(8,128)(2,1)}, bf16[32,512]{1,0:T(8,128)(2,1)S(1)}, u32[]{:S(2)}, u32[]{:S(2)}) collective-permute-start(bf16[32,512]{1,0:T(8,128)(2,1)} %get-tuple-element.29), channel_id=1, source_target_pairs={{0,64},{16,80},{32,96},{48,112},{64,0},{80,16},{96,32},{112,48},{1... | collective-permute-start | bytes 98312 | tf_op jit(solution)/shard_map/ppermute | solution.py:216
  11.5 5.0 %collective-permute-start.3 = (bf16[2,32,512]{2,1,0:T(8,128)(2,1)S(1)}, bf16[2,32,512]{2,1,0:T(8,128)(2,1)S(1)}, u32[]{:S(2)}, u32[]{:S(2)}) collective-permute-start(bf16[2,32,512]{2,1,0:T(8,128)(2,1)S(1)} %pad_maximum_fusion.2.refs_0_), channel_id=1, source_target_pairs={{0,48},{16,0},{32,16},{48,32},{64,112},{80,64},{96,80},{112,96},{1... | collective-permute-start | bytes 196616 | tf_op jit(solution)/shard_map/ppermute | solution.py:216
  14.2 5.8 %collective-permute-start.2 = (bf16[2,32,512]{2,1,0:T(8,128)(2,1)S(1)}, bf16[2,32,512]{2,1,0:T(8,128)(2,1)S(1)}, u32[]{:S(2)}, u32[]{:S(2)}) collective-permute-start(bf16[2,32,512]{2,1,0:T(8,128)(2,1)S(1)} %pad_maximum_fusion.2.refs_0_), channel_id=1, source_target_pairs={{0,32},{16,48},{32,0},{48,16},{64,96},{80,112},{96,64},{112,80},{1... | collective-permute-start | bytes 196616 | tf_op jit(solution)/shard_map/ppermute | solution.py:216
  15.0 5.7 %collective-permute-start.1 = (bf16[2,32,512]{2,1,0:T(8,128)(2,1)S(1)}, bf16[2,32,512]{2,1,0:T(8,128)(2,1)S(1)}, u32[]{:S(2)}, u32[]{:S(2)}) collective-permute-start(bf16[2,32,512]{2,1,0:T(8,128)(2,1)S(1)} %pad_maximum_fusion.2.refs_0_), channel_id=1, source_target_pairs={{0,16},{16,32},{32,48},{48,0},{64,80},{80,96},{96,112},{112,64},{1... | collective-permute-start | bytes 196616 | tf_op jit(solution)/shard_map/ppermute | solution.py:216
  20.7 1.6 %copy-start.4 = (f32[128,8,512]{2,1,0:T(8,128)S(1)}, f32[128,8,512]{2,1,0:T(8,128)}, u32[]{:S(2)}) copy-start(f32[128,8,512]{2,1,0:T(8,128)} %get-tuple-element.27.p_ref) | copy-start | bytes 6291460
  22.3 0.9 copy-start.5
  31.1 17.5 %copy-start = (bf16[1024,512]{1,0:T(8,128)(2,1)}, bf16[1024,512]{1,0:T(8,128)(2,1)S(1)}, u32[]{:S(2)}) copy-start(bf16[1024,512]{1,0:T(8,128)(2,1)S(1)} %gated.1.g_ref) | copy-start | bytes 3145732
  31.1 2.7 %collective-permute-start.4 = (bf16[1024,512]{1,0:T(8,128)(2,1)S(1)}, bf16[1024,512]{1,0:T(8,128)(2,1)S(1)}, u32[]{:S(2)}, u32[]{:S(2)}) collective-permute-start(bf16[1024,512]{1,0:T(8,128)(2,1)S(1)} %gated.1.g_ref), channel_id=1, source_target_pairs={{0,1},{1,0},{2,3},{3,2},{4,5},{5,4},{6,7},{7,6},{8,9},{9,8},{10,11... | collective-permute-start | bytes 3145736 | tf_op jit(solution)/shard_map/ppermute | solution.py:216
  33.8 6.9 %copy-start.2 = (bf16[1024,512]{1,0:T(8,128)(2,1)}, bf16[1024,512]{1,0:T(8,128)(2,1)S(1)}, u32[]{:S(2)}) copy-start(bf16[1024,512]{1,0:T(8,128)(2,1)S(1)} %collective-permute-done.4.gp_ref) | copy-start | bytes 3145732
  37.6 19.9 %collective-permute-start.7 = (bf16[2,352,512]{2,1,0:T(8,128)(2,1)S(1)}, bf16[2,352,512]{2,1,0:T(8,128)(2,1)S(1)}, u32[]{:S(2)}, u32[]{:S(2)}) collective-permute-start(bf16[2,352,512]{2,1,0:T(8,128)(2,1)S(1)} %get-tuple-element.31), channel_id=1, source_target_pairs={{0,12},{1,13},{2,14},{3,15},{4,0},{5,1},{6,2},{7,3},{8,4},{9,5},{1... | collective-permute-start | bytes 2162696 | tf_op jit(solution)/shard_map/ppermute | solution.py:216
  40.7 20.2 %collective-permute-start.6 = (bf16[2,352,512]{2,1,0:T(8,128)(2,1)S(1)}, bf16[2,352,512]{2,1,0:T(8,128)(2,1)S(1)}, u32[]{:S(2)}, u32[]{:S(2)}) collective-permute-start(bf16[2,352,512]{2,1,0:T(8,128)(2,1)S(1)} %get-tuple-element.30), channel_id=1, source_target_pairs={{0,4},{1,5},{2,6},{3,7},{4,8},{5,9},{6,10},{7,11},{8,12},{9,13},{1... | collective-permute-start | bytes 2162696 | tf_op jit(solution)/shard_map/ppermute | solution.py:216
  44.7 32.7 %collective-permute-start.15 = (bf16[4,320,512]{2,1,0:T(8,128)(2,1)S(1)}, bf16[4,320,512]{2,1,0:T(8,128)(2,1)S(1)}, u32[]{:S(2)}, u32[]{:S(2)}) collective-permute-start(bf16[4,320,512]{2,1,0:T(8,128)(2,1)S(1)} %project.9), channel_id=1, source_target_pairs={{0,2},{1,3},{2,0},{3,1},{4,6},{5,7},{6,4},{7,5},{8,10},{9,11},{10,... | collective-permute-start | bytes 3932168 | tf_op jit(solution)/shard_map/ppermute | solution.py:216
  54.1 16.9 %collective-permute-start.10 = (bf16[352,512]{1,0:T(8,128)(2,1)S(1)}, bf16[352,512]{1,0:T(8,128)(2,1)S(1)}, u32[]{:S(2)}, u32[]{:S(2)}) collective-permute-start(bf16[352,512]{1,0:T(8,128)(2,1)S(1)} %bitcast.43), channel_id=1, source_target_pairs={{0,4},{1,5},{2,6},{3,7},{4,8},{5,9},{6,10},{7,11},{8,12},{9,13},{1... | collective-permute-start | bytes 1081352 | tf_op jit(solution)/shard_map/ppermute | solution.py:216
  54.7 16.5 %collective-permute-start.11 = (bf16[352,512]{1,0:T(8,128)(2,1)S(1)}, bf16[352,512]{1,0:T(8,128)(2,1)S(1)}, u32[]{:S(2)}, u32[]{:S(2)}) collective-permute-start(bf16[352,512]{1,0:T(8,128)(2,1)S(1)} %bitcast.42), channel_id=1, source_target_pairs={{0,12},{1,13},{2,14},{3,15},{4,0},{5,1},{6,2},{7,3},{8,4},{9,5},{1... | collective-permute-start | bytes 1081352 | tf_op jit(solution)/shard_map/ppermute | solution.py:216
  57.5 16.9 %collective-permute-start.13 = (bf16[352,512]{1,0:T(8,128)(2,1)S(1)}, bf16[352,512]{1,0:T(8,128)(2,1)S(1)}, u32[]{:S(2)}, u32[]{:S(2)}) collective-permute-start(bf16[352,512]{1,0:T(8,128)(2,1)S(1)} %fusion.9), channel_id=1, source_target_pairs={{0,12},{1,13},{2,14},{3,15},{4,0},{5,1},{6,2},{7,3},{8,4},{9,5},{1... | collective-permute-start | bytes 1081352 | tf_op jit(solution)/shard_map/ppermute | solution.py:216
  61.0 5.9 %copy-start.1 = (bf16[1024,512]{1,0:T(8,128)(2,1)S(1)}, bf16[1024,512]{1,0:T(8,128)(2,1)}, u32[]{:S(2)}) copy-start(bf16[1024,512]{1,0:T(8,128)(2,1)} %copy-done) | copy-start | bytes 3145732
  61.1 5.9 %copy-start.3 = (bf16[1024,512]{1,0:T(8,128)(2,1)S(1)}, bf16[1024,512]{1,0:T(8,128)(2,1)}, u32[]{:S(2)}) copy-start(bf16[1024,512]{1,0:T(8,128)(2,1)} %copy-done.2) | copy-start | bytes 3145732
  61.1 15.3 %collective-permute-start.12 = (bf16[352,512]{1,0:T(8,128)(2,1)S(1)}, bf16[352,512]{1,0:T(8,128)(2,1)S(1)}, u32[]{:S(2)}, u32[]{:S(2)}) collective-permute-start(bf16[352,512]{1,0:T(8,128)(2,1)S(1)} %fusion.8), channel_id=1, source_target_pairs={{0,4},{1,5},{2,6},{3,7},{4,8},{5,9},{6,10},{7,11},{8,12},{9,13},{1... | collective-permute-start | bytes 1081352 | tf_op jit(solution)/shard_map/ppermute | solution.py:216
  71.0 26.8 %collective-permute-start.8 = (bf16[2,352,512]{2,1,0:T(8,128)(2,1)S(1)}, bf16[2,352,512]{2,1,0:T(8,128)(2,1)S(1)}, u32[]{:S(2)}, u32[]{:S(2)}) collective-permute-start(bf16[2,352,512]{2,1,0:T(8,128)(2,1)S(1)} %get-tuple-element.33), channel_id=1, source_target_pairs={{0,4},{1,5},{2,6},{3,7},{4,8},{5,9},{6,10},{7,11},{8,12},{9,13},{1... | collective-permute-start | bytes 2162696 | tf_op jit(solution)/shard_map/ppermute | solution.py:216
  71.2 26.5 %collective-permute-start.9 = (bf16[2,352,512]{2,1,0:T(8,128)(2,1)S(1)}, bf16[2,352,512]{2,1,0:T(8,128)(2,1)S(1)}, u32[]{:S(2)}, u32[]{:S(2)}) collective-permute-start(bf16[2,352,512]{2,1,0:T(8,128)(2,1)S(1)} %get-tuple-element.34), channel_id=1, source_target_pairs={{0,12},{1,13},{2,14},{3,15},{4,0},{5,1},{6,2},{7,3},{8,4},{9,5},{1... | collective-permute-start | bytes 2162696 | tf_op jit(solution)/shard_map/ppermute | solution.py:216
  77.5 16.7 %collective-permute-start.16 = (bf16[160,512]{1,0:T(8,128)(2,1)S(1)}, bf16[160,512]{1,0:T(8,128)(2,1)S(1)}, u32[]{:S(2)}, u32[]{:S(2)}) collective-permute-start(bf16[160,512]{1,0:T(8,128)(2,1)S(1)} %get-tuple-element.51), channel_id=1, source_target_pairs={{0,4},{1,5},{2,6},{3,7},{4,8},{5,9},{6,10},{7,11},{8,12},{9,13},{1... | collective-permute-start | bytes 491528 | tf_op jit(solution)/shard_map/ppermute | solution.py:216
  77.8 16.3 %collective-permute-start.18 = (bf16[160,512]{1,0:T(8,128)(2,1)S(1)}, bf16[160,512]{1,0:T(8,128)(2,1)S(1)}, u32[]{:S(2)}, u32[]{:S(2)}) collective-permute-start(bf16[160,512]{1,0:T(8,128)(2,1)S(1)} %get-tuple-element.52), channel_id=1, source_target_pairs={{0,12},{1,13},{2,14},{3,15},{4,0},{5,1},{6,2},{7,3},{8,4},{9,5},{1... | collective-permute-start | bytes 491528 | tf_op jit(solution)/shard_map/ppermute | solution.py:216
  81.1 23.3 %collective-permute-start.14 = (bf16[2,352,512]{2,1,0:T(8,128)(2,1)S(1)}, bf16[2,352,512]{2,1,0:T(8,128)(2,1)S(1)}, u32[]{:S(2)}, u32[]{:S(2)}) collective-permute-start(bf16[2,352,512]{2,1,0:T(8,128)(2,1)S(1)} %pad_maximum_fusion.1), channel_id=1, source_target_pairs={{0,2},{1,3},{2,0},{3,1},{4,6},{5,7},{6,4},{7,5},{8,10},{9,11},{10,... | collective-permute-start | bytes 2162696 | tf_op jit(solution)/shard_map/ppermute | solution.py:216
  94.4 9.8 %collective-permute-start.17 = (bf16[320,512]{1,0:T(8,128)(2,1)S(1)}, bf16[320,512]{1,0:T(8,128)(2,1)S(1)}, u32[]{:S(2)}, u32[]{:S(2)}) collective-permute-start(bf16[320,512]{1,0:T(8,128)(2,1)S(1)} %get-tuple-element.49), channel_id=1, source_target_pairs={{0,4},{1,5},{2,6},{3,7},{4,8},{5,9},{6,10},{7,11},{8,12},{9,13},{1... | collective-permute-start | bytes 983048 | tf_op jit(solution)/shard_map/ppermute | solution.py:216
  94.5 9.8 %collective-permute-start.19 = (bf16[320,512]{1,0:T(8,128)(2,1)S(1)}, bf16[320,512]{1,0:T(8,128)(2,1)S(1)}, u32[]{:S(2)}, u32[]{:S(2)}) collective-permute-start(bf16[320,512]{1,0:T(8,128)(2,1)S(1)} %get-tuple-element.50), channel_id=1, source_target_pairs={{0,12},{1,13},{2,14},{3,15},{4,0},{5,1},{6,2},{7,3},{8,4},{9,5},{1... | collective-permute-start | bytes 983048 | tf_op jit(solution)/shard_map/ppermute | solution.py:216

commit v10 on v9

--- a/solution.py
+++ b/solution.py
@@ -332,7 +332,7 @@
         [b] * 4,
         [up2, down2],
     )
-    last = (cols, lax.optimization_barrier((mine, stay_a))[0]) + operands[2:]
+    last = (cols, lax.optimization_barrier((mine, stay_a, up, down))[0]) + operands[2:]
     (near,) = project(last, [((dy, 0), [(z, 0)]) for dy in (2, 3, 1, 0)], [Z_TOK])
     half = Z_TOK // 2
     s2a, s2b = total(near[0, :half], far[2, :half]), total(near[0, half:], far[2, half:])

time: 106 us -> 106 us (level)
  waiting for transfers between devices: 29.6 us -> 27.9 us
    ppermute x20, waiting for transfers between devices: 29.6 us -> 27.9 us  [spread(): return lax.ppermute(x, axis, [(i, j) for i, j in pairs if j is not None])]
  transfers between devices with their start and end apart: 20 -> 20, of which waited for: 10 -> 11; matrix products, arithmetic and copies ran while one was open for 2% -> 2% of each run, Pallas kernels for 32% -> 32%
where the time goes in v10:
time: 106 us; the launch traced here: 105 us
  Pallas kernels  37.2 us (35%)
  starting transfers between devices  34 us (32%)
  waiting for transfers between devices  27.9 us (26%)
  other arithmetic  3.24 us (3%)
  local copies, waits for them, and re-layouts  2.57 us (2%)
    ppermute x20, starting transfers between devices, spread(): return lax.ppermute(x, axis, [(i, j) for i, j in pairs if j is not None])  34 us
    ppermute x20, waiting for transfers between devices, spread(): return lax.ppermute(x, axis, [(i, j) for i, j in pairs if j is not None])  27.9 us
    pallas_call x5, Pallas kernels, project(): pl.pallas_call(functools.partial(project_kernel, laid, len(added)), in_sp...  23 us
    pallas_call x1, Pallas kernels, gated(): pl.pallas_call(gate_kernel, grid=(width // LANES,), in_specs=[pl.BlockSpe...  7.8 us
    pallas_call x1, Pallas kernels, states(): pl.pallas_call(state_kernel, grid=(width // LANES,), in_specs=[pl.BlockSp...  6.41 us
    unnamed x18, local copies, waits for them, and re-layouts  2.57 us
  transfers between devices with their start and end apart: 20, of which 11 were waited for; matrix products, arithmetic and copies ran while one was open for 2% of the time, Pallas kernels for 32%

profile of v10, /device:TPU:0, one launch (start us, length us, event | category | flops | bytes accessed | tf_op | source)
XLA Modules:
  0.0 105.1 jit_solution(11797352325629104699)
XLA Ops:
  0.0 0.0 collective-permute-start.5
  0.0 6.4 %states.1 = (f32[128,8,512]{2,1,0:T(8,128)}, bf16[32,512]{1,0:T(8,128)(2,1)}, f32[16,8,512]{2,1,0:T(8,128)}) custom-call(bf16[3,1024,512]{2,1,0:T(8,128)(2,1)} %bitcast.44, bf16[3,1024,512]{2,1,0:T(8,128)(2,1)} %bitcast.45, bf16[3,1024,512]{2,1,0:T(8,128)(2,1)} %bitcast.46, f32[3,3,512]{2,1,0:T(4,128)} %sf_ref.3, f32[16,512]{1,0:T(8,128)} %rate_ref.3), custom_call_target="tpu_custom_call" | custom-call | tf_op jit(solution)/shard_map/states/pallas_call | solution.py:157
  6.4 2.0 %collective-permute-start = (bf16[32,512]{1,0:T(8,128)(2,1)}, bf16[32,512]{1,0:T(8,128)(2,1)S(1)}, u32[]{:S(2)}, u32[]{:S(2)}) collective-permute-start(bf16[32,512]{1,0:T(8,128)(2,1)} %get-tuple-element.29), channel_id=1, source_target_pairs={{0,64},{16,80},{32,96},{48,112},{64,0},{80,16},{96,32},{112,48},{1... | collective-permute-start | bytes 98312 | tf_op jit(solution)/shard_map/ppermute | solution.py:216
  8.4 2.3 %collective-permute-done = bf16[32,512]{1,0:T(8,128)(2,1)S(1)} collective-permute-done((bf16[32,512]{1,0:T(8,128)(2,1)}, bf16[32,512]{1,0:T(8,128)(2,1)S(1)}, u32[]{:S(2)}, u32[]{:S(2)}) %collective-permute-start) | collective-permute-done | bytes 32800 | tf_op jit(solution)/shard_map/ppermute | solution.py:216
  10.7 0.8 pad_maximum_fusion.2.refs_0_
  11.5 1.5 %collective-permute-start.1 = (bf16[2,32,512]{2,1,0:T(8,128)(2,1)S(1)}, bf16[2,32,512]{2,1,0:T(8,128)(2,1)S(1)}, u32[]{:S(2)}, u32[]{:S(2)}) collective-permute-start(bf16[2,32,512]{2,1,0:T(8,128)(2,1)S(1)} %pad_maximum_fusion.2.refs_0_), channel_id=1, source_target_pairs={{0,16},{16,32},{32,48},{48,0},{64,80},{80,96},{96,112},{112,64},{1... | collective-permute-start | bytes 196616 | tf_op jit(solution)/shard_map/ppermute | solution.py:216
  13.0 2.7 %collective-permute-start.2 = (bf16[2,32,512]{2,1,0:T(8,128)(2,1)S(1)}, bf16[2,32,512]{2,1,0:T(8,128)(2,1)S(1)}, u32[]{:S(2)}, u32[]{:S(2)}) collective-permute-start(bf16[2,32,512]{2,1,0:T(8,128)(2,1)S(1)} %pad_maximum_fusion.2.refs_0_), channel_id=1, source_target_pairs={{0,32},{16,48},{32,0},{48,16},{64,96},{80,112},{96,64},{112,80},{1... | collective-permute-start | bytes 196616 | tf_op jit(solution)/shard_map/ppermute | solution.py:216
  15.7 1.4 %collective-permute-start.3 = (bf16[2,32,512]{2,1,0:T(8,128)(2,1)S(1)}, bf16[2,32,512]{2,1,0:T(8,128)(2,1)S(1)}, u32[]{:S(2)}, u32[]{:S(2)}) collective-permute-start(bf16[2,32,512]{2,1,0:T(8,128)(2,1)S(1)} %pad_maximum_fusion.2.refs_0_), channel_id=1, source_target_pairs={{0,48},{16,0},{32,16},{48,32},{64,112},{80,64},{96,80},{112,96},{1... | collective-permute-start | bytes 196616 | tf_op jit(solution)/shard_map/ppermute | solution.py:216
  17.1 0.4 collective-permute-done.1.refs_1_
  17.6 1.3 %collective-permute-done.2.refs_2_ = bf16[2,32,512]{2,1,0:T(8,128)(2,1)S(1)} collective-permute-done((bf16[2,32,512]{2,1,0:T(8,128)(2,1)S(1)}, bf16[2,32,512]{2,1,0:T(8,128)(2,1)S(1)}, u32[]{:S(2)}, u32[]{:S(2)}) %collective-permute-start.2) | collective-permute-done | bytes 65568 | tf_op jit(solution)/shard_map/ppermute | solution.py:216
  18.9 1.1 %collective-permute-done.3.refs_3_ = bf16[2,32,512]{2,1,0:T(8,128)(2,1)S(1)} collective-permute-done((bf16[2,32,512]{2,1,0:T(8,128)(2,1)S(1)}, bf16[2,32,512]{2,1,0:T(8,128)(2,1)S(1)}, u32[]{:S(2)}, u32[]{:S(2)}) %collective-permute-start.3) | collective-permute-done | bytes 65568 | tf_op jit(solution)/shard_map/ppermute | solution.py:216
  20.0 0.0 copy-done.6
  20.0 0.0 copy-done.7
  20.0 1.6 %copy-done.4 = f32[128,8,512]{2,1,0:T(8,128)S(1)} copy-done((f32[128,8,512]{2,1,0:T(8,128)S(1)}, f32[128,8,512]{2,1,0:T(8,128)}, u32[]{:S(2)}) %copy-start.4) | copy-done | bytes 2097176
  21.6 0.9 copy-done.5
  22.5 7.8 %gated.1.g_ref = bf16[1024,512]{1,0:T(8,128)(2,1)S(1)} custom-call(s32[1]{0:T(128)} %bitcast.at_ref, bf16[3,1024,512]{2,1,0:T(8,128)(2,1)} %bitcast.47, f32[3,3,512]{2,1,0:T(4,128)S(1)} %copy-done.7, f32[16,512]{1,0:T(8,128)S(1)} %copy-done.6, f32[16,512]{1,0:T(8,128)S(1)} %copy-done.8, f32[128,8,512]{2,1,0:T(8,128)S(1)} %copy-done.4, ...), custom_call_target="tpu_custom_call" | custom-call | tf_op jit(solution)/shard_map/gated/pallas_call | solution.py:189
  30.3 0.0 copy-start
  30.3 0.1 collective-permute-start.4
  30.5 2.6 %collective-permute-done.4.gp_ref = bf16[1024,512]{1,0:T(8,128)(2,1)S(1)} collective-permute-done((bf16[1024,512]{1,0:T(8,128)(2,1)S(1)}, bf16[1024,512]{1,0:T(8,128)(2,1)S(1)}, u32[]{:S(2)}, u32[]{:S(2)}) %collective-permute-start.4) | collective-permute-done | bytes 1048608 | tf_op jit(solution)/shard_map/ppermute | solution.py:216
  33.1 0.0 collective-permute-done.5.wp_ref
  33.1 3.8 %project.5 = (bf16[2,352,512]{2,1,0:T(8,128)(2,1)S(1)}, bf16[2,352,512]{2,1,0:T(8,128)(2,1)S(1)}) custom-call(s32[8]{0:T(128)S(1)} %fusion.21.cols_ref, bf16[1024,512]{1,0:T(8,128)(2,1)S(1)} %gated.1.g_ref, bf16[1024,512]{1,0:T(8,128)(2,1)S(1)} %collective-permute-done.4.gp_ref, bf16[512,8192]{1,0:T(8,128)(2,1)} %w_ref.9, ...), custom_call_target="tpu_custom_call" | custom-call | tf_op jit(solution)/shard_map/project/pallas_call | solution.py:279
  36.8 3.1 %collective-permute-start.7 = (bf16[2,352,512]{2,1,0:T(8,128)(2,1)S(1)}, bf16[2,352,512]{2,1,0:T(8,128)(2,1)S(1)}, u32[]{:S(2)}, u32[]{:S(2)}) collective-permute-start(bf16[2,352,512]{2,1,0:T(8,128)(2,1)S(1)} %get-tuple-element.31), channel_id=1, source_target_pairs={{0,12},{1,13},{2,14},{3,15},{4,0},{5,1},{6,2},{7,3},{8,4},{9,5},{1... | collective-permute-start | bytes 2162696 | tf_op jit(solution)/shard_map/ppermute | solution.py:216
  40.0 0.0 collective-permute-start.6
  40.0 4.0 %project.9 = bf16[4,320,512]{2,1,0:T(8,128)(2,1)S(1)} custom-call(s32[8]{0:T(128)S(1)} %fusion.21.cols_ref, bf16[1024,512]{1,0:T(8,128)(2,1)S(1)} %gated.1.g_ref, bf16[1024,512]{1,0:T(8,128)(2,1)S(1)} %collective-permute-done.4.gp_ref, bf16[512,8192]{1,0:T(8,128)(2,1)} %w_ref.9, bf16[512,8192]{1,0:T(8,128)(2,1)} %collective-permute-done.5.wp_ref), custom_call_target="tpu_custom_call" | custom-call | tf_op jit(solution)/shard_map/project/pallas_call | solution.py:279
  44.0 3.9 %collective-permute-start.15 = (bf16[4,320,512]{2,1,0:T(8,128)(2,1)S(1)}, bf16[4,320,512]{2,1,0:T(8,128)(2,1)S(1)}, u32[]{:S(2)}, u32[]{:S(2)}) collective-permute-start(bf16[4,320,512]{2,1,0:T(8,128)(2,1)S(1)} %project.9), channel_id=1, source_target_pairs={{0,2},{1,3},{2,0},{3,1},{4,6},{5,7},{6,4},{7,5},{8,10},{9,11},{10,... | collective-permute-start | bytes 3932168 | tf_op jit(solution)/shard_map/ppermute | solution.py:216
  47.8 5.5 %project.7 = (bf16[1,352,512]{2,1,0:T(8,128)(2,1)S(1)}, bf16[1,352,512]{2,1,0:T(8,128)(2,1)S(1)}, bf16[1,352,512]{2,1,0:T(8,128)(2,1)S(1)}, bf16[1,352,512]{2,1,...) custom-call(s32[8]{0:T(128)S(1)} %fusion.21.cols_ref, ...), custom_call_target="tpu_custom_call" | custom-call | tf_op jit(solution)/shard_map/project/pallas_call | solution.py:279
  53.3 0.7 collective-permute-start.10
  54.0 2.7 %collective-permute-start.11 = (bf16[352,512]{1,0:T(8,128)(2,1)S(1)}, bf16[352,512]{1,0:T(8,128)(2,1)S(1)}, u32[]{:S(2)}, u32[]{:S(2)}) collective-permute-start(bf16[352,512]{1,0:T(8,128)(2,1)S(1)} %bitcast.42), channel_id=1, source_target_pairs={{0,12},{1,13},{2,14},{3,15},{4,0},{5,1},{6,2},{7,3},{8,4},{9,5},{1... | collective-permute-start | bytes 1081352 | tf_op jit(solution)/shard_map/ppermute | solution.py:216
  56.7 0.0 collective-permute-done.7.refs_1_
  56.7 0.1 fusion.9
  56.8 2.7 %collective-permute-start.13 = (bf16[352,512]{1,0:T(8,128)(2,1)S(1)}, bf16[352,512]{1,0:T(8,128)(2,1)S(1)}, u32[]{:S(2)}, u32[]{:S(2)}) collective-permute-start(bf16[352,512]{1,0:T(8,128)(2,1)S(1)} %fusion.9), channel_id=1, source_target_pairs={{0,12},{1,13},{2,14},{3,15},{4,0},{5,1},{6,2},{7,3},{8,4},{9,5},{1... | collective-permute-start | bytes 1081352 | tf_op jit(solution)/shard_map/ppermute | solution.py:216
  59.5 0.7 collective-permute-done.6.refs_0_
  60.2 0.1 fusion.8
  60.3 0.0 copy-start.1
  60.3 0.0 copy-start.3
  60.3 0.1 collective-permute-start.12
  60.4 5.8 %project.6 = (bf16[2,352,512]{2,1,0:T(8,128)(2,1)S(1)}, bf16[2,352,512]{2,1,0:T(8,128)(2,1)S(1)}, bf16[1,352,512]{2,1,0:T(8,128)(2,1)S(1)}, bf16[1,352,512]{2,1,0:T(8,128)(2,1)S(1)}) custom-call(s32[8]{0:T(128)S(1)} %fusion.21.cols_ref, bf16[1024,512]{1,0:T(8,128)(2,1)} %copy-done, bf16[1024,512]{1,0:T(8,128)(2,1)} %copy-done.2, bf16[512,8192]{1,0:T(8,128)(2,1)} %w_ref.9, ...), custom_call_target="tpu_custom_call" | custom-call | tf_op jit(solution)/shard_map/project/pallas_call | solution.py:279
  66.2 1.7 %collective-permute-done.10 = bf16[352,512]{1,0:T(8,128)(2,1)S(1)} collective-permute-done((bf16[352,512]{1,0:T(8,128)(2,1)S(1)}, bf16[352,512]{1,0:T(8,128)(2,1)S(1)}, u32[]{:S(2)}, u32[]{:S(2)}) %collective-permute-start.10) | collective-permute-done | bytes 360480 | tf_op jit(solution)/shard_map/ppermute | solution.py:216
  67.9 0.0 collective-permute-start.8
  67.9 0.0 collective-permute-done.11
  67.9 3.2 %collective-permute-start.9 = (bf16[2,352,512]{2,1,0:T(8,128)(2,1)S(1)}, bf16[2,352,512]{2,1,0:T(8,128)(2,1)S(1)}, u32[]{:S(2)}, u32[]{:S(2)}) collective-permute-start(bf16[2,352,512]{2,1,0:T(8,128)(2,1)S(1)} %get-tuple-element.34), channel_id=1, source_target_pairs={{0,12},{1,13},{2,14},{3,15},{4,0},{5,1},{6,2},{7,3},{8,4},{9,5},{1... | collective-permute-start | bytes 2162696 | tf_op jit(solution)/shard_map/ppermute | solution.py:216
  71.2 4.0 %project.8 = bf16[4,320,512]{2,1,0:T(8,128)(2,1)S(1)} custom-call(s32[8]{0:T(128)S(1)} %fusion.21.cols_ref, bf16[1024,512]{1,0:T(8,128)(2,1)S(1)} %copy-done.1, bf16[1024,512]{1,0:T(8,128)(2,1)S(1)} %copy-done.3, bf16[512,8192]{1,0:T(8,128)(2,1)} %w_ref.9, bf16[512,8192]{1,0:T(8,128)(2,1)} %collective-permute-done.5.wp_ref), custom_call_target="tpu_custom_call" | custom-call | tf_op jit(solution)/shard_map/project/pallas_call | solution.py:279
  75.2 0.0 collective-permute-done.13
  75.2 0.5 collective-permute-done.12
  75.6 1.0 collective-permute-done.15
  76.6 0.1 fusion.14
  76.7 0.4 collective-permute-start.16
  77.1 2.9 %collective-permute-start.18 = (bf16[160,512]{1,0:T(8,128)(2,1)S(1)}, bf16[160,512]{1,0:T(8,128)(2,1)S(1)}, u32[]{:S(2)}, u32[]{:S(2)}) collective-permute-start(bf16[160,512]{1,0:T(8,128)(2,1)S(1)} %get-tuple-element.52), channel_id=1, source_target_pairs={{0,12},{1,13},{2,14},{3,15},{4,0},{5,1},{6,2},{7,3},{8,4},{9,5},{1... | collective-permute-start | bytes 491528 | tf_op jit(solution)/shard_map/ppermute | solution.py:216
  80.0 0.3 fusion.12
  80.3 0.1 pad_maximum_fusion.1
  80.4 3.3 %collective-permute-start.14 = (bf16[2,352,512]{2,1,0:T(8,128)(2,1)S(1)}, bf16[2,352,512]{2,1,0:T(8,128)(2,1)S(1)}, u32[]{:S(2)}, u32[]{:S(2)}) collective-permute-start(bf16[2,352,512]{2,1,0:T(8,128)(2,1)S(1)} %pad_maximum_fusion.1), channel_id=1, source_target_pairs={{0,2},{1,3},{2,0},{3,1},{4,6},{5,7},{6,4},{7,5},{8,10},{9,11},{10,... | collective-permute-start | bytes 2162696 | tf_op jit(solution)/shard_map/ppermute | solution.py:216
  83.7 9.7 %collective-permute-done.16 = bf16[160,512]{1,0:T(8,128)(2,1)S(1)} collective-permute-done((bf16[160,512]{1,0:T(8,128)(2,1)S(1)}, bf16[160,512]{1,0:T(8,128)(2,1)S(1)}, u32[]{:S(2)}, u32[]{:S(2)}) %collective-permute-start.16) | collective-permute-done | bytes 163872 | tf_op jit(solution)/shard_map/ppermute | solution.py:216
  93.4 0.0 collective-permute-done.18
  93.4 0.2 fusion.5
  93.7 0.1 collective-permute-start.17
  93.8 3.2 %collective-permute-start.19 = (bf16[320,512]{1,0:T(8,128)(2,1)S(1)}, bf16[320,512]{1,0:T(8,128)(2,1)S(1)}, u32[]{:S(2)}, u32[]{:S(2)}) collective-permute-start(bf16[320,512]{1,0:T(8,128)(2,1)S(1)} %get-tuple-element.50), channel_id=1, source_target_pairs={{0,12},{1,13},{2,14},{3,15},{4,0},{5,1},{6,2},{7,3},{8,4},{9,5},{1... | collective-permute-start | bytes 983048 | tf_op jit(solution)/shard_map/ppermute | solution.py:216
  97.0 0.0 collective-permute-done.8
  97.0 0.0 collective-permute-done.9
  97.0 6.5 %collective-permute-done.17 = bf16[320,512]{1,0:T(8,128)(2,1)S(1)} collective-permute-done((bf16[320,512]{1,0:T(8,128)(2,1)S(1)}, bf16[320,512]{1,0:T(8,128)(2,1)S(1)}, u32[]{:S(2)}, u32[]{:S(2)}) %collective-permute-start.17) | collective-permute-done | bytes 327712 | tf_op jit(solution)/shard_map/ppermute | solution.py:216
  103.5 0.0 collective-permute-done.19
  103.5 0.2 fusion.7
  103.7 0.0 collective-permute-done.14
  103.7 0.4 fusion.10
  104.1 1.0 pad_maximum_fusion
  (12 shorter events, 0.0 us)
Async XLA Ops:
  0.0 33.1 %collective-permute-start.5 = (bf16[512,8192]{1,0:T(8,128)(2,1)}, bf16[512,8192]{1,0:T(8,128)(2,1)}, u32[]{:S(2)}, u32[]{:S(2)}) collective-permute-start(bf16[512,8192]{1,0:T(8,128)(2,1)} %w_ref.9), channel_id=1, source_target_pairs={{0,1},{1,0},{2,3},{3,2},{4,5},{5,4},{6,7},{7,6},{8,9},{9,8},{10,11... | collective-permute-start | bytes 25165832 | tf_op jit(solution)/shard_map/ppermute | solution.py:216
  0.0 19.9 %copy-start.6 = (f32[16,512]{1,0:T(8,128)S(1)}, f32[16,512]{1,0:T(8,128)}, u32[]{:S(2)}) copy-start(f32[16,512]{1,0:T(8,128)} %rate_ref.3) | copy-start | bytes 98308
  0.0 19.9 %copy-start.7 = (f32[3,3,512]{2,1,0:T(4,128)S(1)}, f32[3,3,512]{2,1,0:T(4,128)}, u32[]{:S(2)}) copy-start(f32[3,3,512]{2,1,0:T(4,128)} %sf_ref.3) | copy-start | bytes 55300
  0.0 19.9 %copy-start.8 = (f32[16,512]{1,0:T(8,128)S(1)}, f32[16,512]{1,0:T(8,128)}, u32[]{:S(2)}) copy-start(f32[16,512]{1,0:T(8,128)} %res_ref.1) | copy-start | bytes 98308
  6.4 4.3 %collective-permute-start = (bf16[32,512]{1,0:T(8,128)(2,1)}, bf16[32,512]{1,0:T(8,128)(2,1)S(1)}, u32[]{:S(2)}, u32[]{:S(2)}) collective-permute-start(bf16[32,512]{1,0:T(8,128)(2,1)} %get-tuple-element.29), channel_id=1, source_target_pairs={{0,64},{16,80},{32,96},{48,112},{64,0},{80,16},{96,32},{112,48},{1... | collective-permute-start | bytes 98312 | tf_op jit(solution)/shard_map/ppermute | solution.py:216
  11.5 6.1 %collective-permute-start.1 = (bf16[2,32,512]{2,1,0:T(8,128)(2,1)S(1)}, bf16[2,32,512]{2,1,0:T(8,128)(2,1)S(1)}, u32[]{:S(2)}, u32[]{:S(2)}) collective-permute-start(bf16[2,32,512]{2,1,0:T(8,128)(2,1)S(1)} %pad_maximum_fusion.2.refs_0_), channel_id=1, source_target_pairs={{0,16},{16,32},{32,48},{48,0},{64,80},{80,96},{96,112},{112,64},{1... | collective-permute-start | bytes 196616 | tf_op jit(solution)/shard_map/ppermute | solution.py:216
  13.0 5.9 %collective-permute-start.2 = (bf16[2,32,512]{2,1,0:T(8,128)(2,1)S(1)}, bf16[2,32,512]{2,1,0:T(8,128)(2,1)S(1)}, u32[]{:S(2)}, u32[]{:S(2)}) collective-permute-start(bf16[2,32,512]{2,1,0:T(8,128)(2,1)S(1)} %pad_maximum_fusion.2.refs_0_), channel_id=1, source_target_pairs={{0,32},{16,48},{32,0},{48,16},{64,96},{80,112},{96,64},{112,80},{1... | collective-permute-start | bytes 196616 | tf_op jit(solution)/shard_map/ppermute | solution.py:216
  15.7 4.3 %collective-permute-start.3 = (bf16[2,32,512]{2,1,0:T(8,128)(2,1)S(1)}, bf16[2,32,512]{2,1,0:T(8,128)(2,1)S(1)}, u32[]{:S(2)}, u32[]{:S(2)}) collective-permute-start(bf16[2,32,512]{2,1,0:T(8,128)(2,1)S(1)} %pad_maximum_fusion.2.refs_0_), channel_id=1, source_target_pairs={{0,48},{16,0},{32,16},{48,32},{64,112},{80,64},{96,80},{112,96},{1... | collective-permute-start | bytes 196616 | tf_op jit(solution)/shard_map/ppermute | solution.py:216
  20.0 1.6 %copy-start.4 = (f32[128,8,512]{2,1,0:T(8,128)S(1)}, f32[128,8,512]{2,1,0:T(8,128)}, u32[]{:S(2)}) copy-start(f32[128,8,512]{2,1,0:T(8,128)} %get-tuple-element.27.p_ref) | copy-start | bytes 6291460
  21.6 0.9 copy-start.5
  30.3 17.5 %copy-start = (bf16[1024,512]{1,0:T(8,128)(2,1)}, bf16[1024,512]{1,0:T(8,128)(2,1)S(1)}, u32[]{:S(2)}) copy-start(bf16[1024,512]{1,0:T(8,128)(2,1)S(1)} %gated.1.g_ref) | copy-start | bytes 3145732
  30.3 2.7 %collective-permute-start.4 = (bf16[1024,512]{1,0:T(8,128)(2,1)S(1)}, bf16[1024,512]{1,0:T(8,128)(2,1)S(1)}, u32[]{:S(2)}, u32[]{:S(2)}) collective-permute-start(bf16[1024,512]{1,0:T(8,128)(2,1)S(1)} %gated.1.g_ref), channel_id=1, source_target_pairs={{0,1},{1,0},{2,3},{3,2},{4,5},{5,4},{6,7},{7,6},{8,9},{9,8},{10,11... | collective-permute-start | bytes 3145736 | tf_op jit(solution)/shard_map/ppermute | solution.py:216
  33.1 6.9 %copy-start.2 = (bf16[1024,512]{1,0:T(8,128)(2,1)}, bf16[1024,512]{1,0:T(8,128)(2,1)S(1)}, u32[]{:S(2)}) copy-start(bf16[1024,512]{1,0:T(8,128)(2,1)S(1)} %collective-permute-done.4.gp_ref) | copy-start | bytes 3145732
  36.8 19.9 %collective-permute-start.7 = (bf16[2,352,512]{2,1,0:T(8,128)(2,1)S(1)}, bf16[2,352,512]{2,1,0:T(8,128)(2,1)S(1)}, u32[]{:S(2)}, u32[]{:S(2)}) collective-permute-start(bf16[2,352,512]{2,1,0:T(8,128)(2,1)S(1)} %get-tuple-element.31), channel_id=1, source_target_pairs={{0,12},{1,13},{2,14},{3,15},{4,0},{5,1},{6,2},{7,3},{8,4},{9,5},{1... | collective-permute-start | bytes 2162696 | tf_op jit(solution)/shard_map/ppermute | solution.py:216
  40.0 20.2 %collective-permute-start.6 = (bf16[2,352,512]{2,1,0:T(8,128)(2,1)S(1)}, bf16[2,352,512]{2,1,0:T(8,128)(2,1)S(1)}, u32[]{:S(2)}, u32[]{:S(2)}) collective-permute-start(bf16[2,352,512]{2,1,0:T(8,128)(2,1)S(1)} %get-tuple-element.30), channel_id=1, source_target_pairs={{0,4},{1,5},{2,6},{3,7},{4,8},{5,9},{6,10},{7,11},{8,12},{9,13},{1... | collective-permute-start | bytes 2162696 | tf_op jit(solution)/shard_map/ppermute | solution.py:216
  44.0 32.7 %collective-permute-start.15 = (bf16[4,320,512]{2,1,0:T(8,128)(2,1)S(1)}, bf16[4,320,512]{2,1,0:T(8,128)(2,1)S(1)}, u32[]{:S(2)}, u32[]{:S(2)}) collective-permute-start(bf16[4,320,512]{2,1,0:T(8,128)(2,1)S(1)} %project.9), channel_id=1, source_target_pairs={{0,2},{1,3},{2,0},{3,1},{4,6},{5,7},{6,4},{7,5},{8,10},{9,11},{10,... | collective-permute-start | bytes 3932168 | tf_op jit(solution)/shard_map/ppermute | solution.py:216
  53.3 14.6 %collective-permute-start.10 = (bf16[352,512]{1,0:T(8,128)(2,1)S(1)}, bf16[352,512]{1,0:T(8,128)(2,1)S(1)}, u32[]{:S(2)}, u32[]{:S(2)}) collective-permute-start(bf16[352,512]{1,0:T(8,128)(2,1)S(1)} %bitcast.43), channel_id=1, source_target_pairs={{0,4},{1,5},{2,6},{3,7},{4,8},{5,9},{6,10},{7,11},{8,12},{9,13},{1... | collective-permute-start | bytes 1081352 | tf_op jit(solution)/shard_map/ppermute | solution.py:216
  54.0 14.0 %collective-permute-start.11 = (bf16[352,512]{1,0:T(8,128)(2,1)S(1)}, bf16[352,512]{1,0:T(8,128)(2,1)S(1)}, u32[]{:S(2)}, u32[]{:S(2)}) collective-permute-start(bf16[352,512]{1,0:T(8,128)(2,1)S(1)} %bitcast.42), channel_id=1, source_target_pairs={{0,12},{1,13},{2,14},{3,15},{4,0},{5,1},{6,2},{7,3},{8,4},{9,5},{1... | collective-permute-start | bytes 1081352 | tf_op jit(solution)/shard_map/ppermute | solution.py:216
  56.8 18.4 %collective-permute-start.13 = (bf16[352,512]{1,0:T(8,128)(2,1)S(1)}, bf16[352,512]{1,0:T(8,128)(2,1)S(1)}, u32[]{:S(2)}, u32[]{:S(2)}) collective-permute-start(bf16[352,512]{1,0:T(8,128)(2,1)S(1)} %fusion.9), channel_id=1, source_target_pairs={{0,12},{1,13},{2,14},{3,15},{4,0},{5,1},{6,2},{7,3},{8,4},{9,5},{1... | collective-permute-start | bytes 1081352 | tf_op jit(solution)/shard_map/ppermute | solution.py:216
  60.3 10.9 %copy-start.1 = (bf16[1024,512]{1,0:T(8,128)(2,1)S(1)}, bf16[1024,512]{1,0:T(8,128)(2,1)}, u32[]{:S(2)}) copy-start(bf16[1024,512]{1,0:T(8,128)(2,1)} %copy-done) | copy-start | bytes 3145732
  60.3 10.9 %copy-start.3 = (bf16[1024,512]{1,0:T(8,128)(2,1)S(1)}, bf16[1024,512]{1,0:T(8,128)(2,1)}, u32[]{:S(2)}) copy-start(bf16[1024,512]{1,0:T(8,128)(2,1)} %copy-done.2) | copy-start | bytes 3145732
  60.3 15.3 %collective-permute-start.12 = (bf16[352,512]{1,0:T(8,128)(2,1)S(1)}, bf16[352,512]{1,0:T(8,128)(2,1)S(1)}, u32[]{:S(2)}, u32[]{:S(2)}) collective-permute-start(bf16[352,512]{1,0:T(8,128)(2,1)S(1)} %fusion.8), channel_id=1, source_target_pairs={{0,4},{1,5},{2,6},{3,7},{4,8},{5,9},{6,10},{7,11},{8,12},{9,13},{1... | collective-permute-start | bytes 1081352 | tf_op jit(solution)/shard_map/ppermute | solution.py:216
  67.9 29.1 %collective-permute-start.8 = (bf16[2,352,512]{2,1,0:T(8,128)(2,1)S(1)}, bf16[2,352,512]{2,1,0:T(8,128)(2,1)S(1)}, u32[]{:S(2)}, u32[]{:S(2)}) collective-permute-start(bf16[2,352,512]{2,1,0:T(8,128)(2,1)S(1)} %get-tuple-element.33), channel_id=1, source_target_pairs={{0,4},{1,5},{2,6},{3,7},{4,8},{5,9},{6,10},{7,11},{8,12},{9,13},{1... | collective-permute-start | bytes 2162696 | tf_op jit(solution)/shard_map/ppermute | solution.py:216
  67.9 29.1 %collective-permute-start.9 = (bf16[2,352,512]{2,1,0:T(8,128)(2,1)S(1)}, bf16[2,352,512]{2,1,0:T(8,128)(2,1)S(1)}, u32[]{:S(2)}, u32[]{:S(2)}) collective-permute-start(bf16[2,352,512]{2,1,0:T(8,128)(2,1)S(1)} %get-tuple-element.34), channel_id=1, source_target_pairs={{0,12},{1,13},{2,14},{3,15},{4,0},{5,1},{6,2},{7,3},{8,4},{9,5},{1... | collective-permute-start | bytes 2162696 | tf_op jit(solution)/shard_map/ppermute | solution.py:216
  76.7 16.7 %collective-permute-start.16 = (bf16[160,512]{1,0:T(8,128)(2,1)S(1)}, bf16[160,512]{1,0:T(8,128)(2,1)S(1)}, u32[]{:S(2)}, u32[]{:S(2)}) collective-permute-start(bf16[160,512]{1,0:T(8,128)(2,1)S(1)} %get-tuple-element.51), channel_id=1, source_target_pairs={{0,4},{1,5},{2,6},{3,7},{4,8},{5,9},{6,10},{7,11},{8,12},{9,13},{1... | collective-permute-start | bytes 491528 | tf_op jit(solution)/shard_map/ppermute | solution.py:216
  77.1 16.3 %collective-permute-start.18 = (bf16[160,512]{1,0:T(8,128)(2,1)S(1)}, bf16[160,512]{1,0:T(8,128)(2,1)S(1)}, u32[]{:S(2)}, u32[]{:S(2)}) collective-permute-start(bf16[160,512]{1,0:T(8,128)(2,1)S(1)} %get-tuple-element.52), channel_id=1, source_target_pairs={{0,12},{1,13},{2,14},{3,15},{4,0},{5,1},{6,2},{7,3},{8,4},{9,5},{1... | collective-permute-start | bytes 491528 | tf_op jit(solution)/shard_map/ppermute | solution.py:216
  80.4 23.3 %collective-permute-start.14 = (bf16[2,352,512]{2,1,0:T(8,128)(2,1)S(1)}, bf16[2,352,512]{2,1,0:T(8,128)(2,1)S(1)}, u32[]{:S(2)}, u32[]{:S(2)}) collective-permute-start(bf16[2,352,512]{2,1,0:T(8,128)(2,1)S(1)} %pad_maximum_fusion.1), channel_id=1, source_target_pairs={{0,2},{1,3},{2,0},{3,1},{4,6},{5,7},{6,4},{7,5},{8,10},{9,11},{10,... | collective-permute-start | bytes 2162696 | tf_op jit(solution)/shard_map/ppermute | solution.py:216
  93.7 9.8 %collective-permute-start.17 = (bf16[320,512]{1,0:T(8,128)(2,1)S(1)}, bf16[320,512]{1,0:T(8,128)(2,1)S(1)}, u32[]{:S(2)}, u32[]{:S(2)}) collective-permute-start(bf16[320,512]{1,0:T(8,128)(2,1)S(1)} %get-tuple-element.49), channel_id=1, source_target_pairs={{0,4},{1,5},{2,6},{3,7},{4,8},{5,9},{6,10},{7,11},{8,12},{9,13},{1... | collective-permute-start | bytes 983048 | tf_op jit(solution)/shard_map/ppermute | solution.py:216
  93.8 9.8 %collective-permute-start.19 = (bf16[320,512]{1,0:T(8,128)(2,1)S(1)}, bf16[320,512]{1,0:T(8,128)(2,1)S(1)}, u32[]{:S(2)}, u32[]{:S(2)}) collective-permute-start(bf16[320,512]{1,0:T(8,128)(2,1)S(1)} %get-tuple-element.50), channel_id=1, source_target_pairs={{0,12},{1,13},{2,14},{3,15},{4,0},{5,1},{6,2},{7,3},{8,4},{9,5},{1... | collective-permute-start | bytes 983048 | tf_op jit(solution)/shard_map/ppermute | solution.py:216

commit v11 on v10

--- a/solution.py
+++ b/solution.py
@@ -32,9 +32,9 @@
         rows_ref[pl.ds(at - 2, 2), :] = before
 
 
-def state_kernel(key_ref, val_ref, query_ref, sf_ref, rate_ref, p_ref, told_ref, start_ref, xs, told):
+def state_kernel(key_ref, val_ref, query_ref, sf_ref, rate_ref, p_ref, told_ref, xs, told):
     n_modes = rate_ref.shape[0]
-    steps = p_ref.shape[0]
+    steps = p_ref.shape[0] - n_modes
     rows = lax.broadcasted_iota(jnp.int32, (SUBS, LANES), 0)
     none = jnp.zeros((2, LANES), f32)
     for j in range(2):
@@ -65,7 +65,7 @@
         rate = jnp.broadcast_to(rate_ref[pl.ds(r, 1), :], (SUBS, LANES))
         scanned = row_scan(state[r], jnp.exp(-rate * steps), rows)
         told[pl.ds(r, 1), :] = scanned[SUBS - 1 :]
-        start_ref[r] = jnp.where(rows >= 1, pltpu.roll(scanned, 1, axis=0), 0.0)
+        p_ref[steps + r] = jnp.where(rows >= 1, pltpu.roll(scanned, 1, axis=0), 0.0)
     end = (SUBS - 1) * (steps + PAD) + PAD + steps
     told[pl.ds(LAST, PAYLOAD - LAST), :] = jnp.zeros((PAYLOAD - LAST, LANES), f32)
     told[pl.ds(LAST, 2), :] = query_ref[0].astype(f32)[14:]
@@ -75,10 +75,10 @@
     told_ref[...] = told[...].astype(bf16)
 
 
-def gate_kernel(at_ref, x_ref, sf_ref, rate_ref, res_ref, p_ref, start_ref, *refs):
+def gate_kernel(at_ref, x_ref, sf_ref, rate_ref, res_ref, p_ref, *refs):
     told_refs, (out_ref, xs, ys, told) = refs[:-4], refs[-4:]
     n_modes = rate_ref.shape[0]
-    steps = p_ref.shape[0]
+    steps = p_ref.shape[0] - n_modes
     n_tok = SUBS * steps
     me = at_ref[0]
     rows = lax.broadcasted_iota(jnp.int32, (SUBS, LANES), 0)
@@ -118,7 +118,7 @@
         gain.append(jnp.broadcast_to(res_ref[pl.ds(r, 1), :], (SUBS, LANES)))
         passed = (rows * steps).astype(f32)
         mine = jnp.exp(-rate * (passed - 1.0)) * p_first[0] + jnp.exp(-rate * (passed - 2.0)) * p_first[1]
-        state0.append(start_ref[r] + jnp.exp(-rate * passed) * enter + jnp.where(rows >= 1, mine, 0.0))
+        state0.append(p_ref[steps + r] + jnp.exp(-rate * passed) * enter + jnp.where(rows >= 1, mine, 0.0))
 
     def tap(at):
         return xs[pl.ds(PAD + at, SUBS, stride=steps + PAD), :]
@@ -165,14 +165,12 @@
             pl.BlockSpec((modes, LANES), col),
         ],
         out_specs=[
-            pl.BlockSpec((steps, SUBS, LANES), three),
+            pl.BlockSpec((steps + modes, SUBS, LANES), three),
             pl.BlockSpec((PAYLOAD, LANES), col),
-            pl.BlockSpec((modes, SUBS, LANES), three),
         ],
         out_shape=[
-            jax.ShapeDtypeStruct((steps, SUBS, width), f32),
+            jax.ShapeDtypeStruct((steps + modes, SUBS, width), f32),
             jax.ShapeDtypeStruct((PAYLOAD, width), bf16),
-            jax.ShapeDtypeStruct((modes, SUBS, width), f32),
         ],
         scratch_shapes=[pltpu.VMEM((2, n_tok + SUBS * PAD, LANES), f32), pltpu.VMEM((PAYLOAD, LANES), f32)],
         compiler_params=pltpu.CompilerParams(vmem_limit_bytes=60 << 20),
@@ -180,7 +178,7 @@
     )(x, x, x, sf, rate)
 
 
-def gated(at, x, sf, rate, res, p, start, told):
+def gated(at, x, sf, rate, res, p, told):
     _, n_tok, width = x.shape
     modes = rate.shape[0]
     steps = n_tok // SUBS
@@ -195,8 +193,7 @@
             pl.BlockSpec((3, 3, LANES), three),
             pl.BlockSpec((modes, LANES), col),
             pl.BlockSpec((modes, LANES), col),
-            pl.BlockSpec((steps, SUBS, LANES), three),
-            pl.BlockSpec((modes, SUBS, LANES), three),
+            pl.BlockSpec((steps + modes, SUBS, LANES), three),
         ]
         + [pl.BlockSpec((2, PAYLOAD, LANES), three)] * len(told),
         out_specs=pl.BlockSpec((n_tok, LANES), col),
@@ -208,7 +205,7 @@
         ],
         compiler_params=pltpu.CompilerParams(vmem_limit_bytes=48 << 20),
         name="gated",
-    )(at, x, sf, rate, res, p, start, *told)
+    )(at, x, sf, rate, res, p, *told)
 
 
 def spread(x, axis, target):
@@ -238,26 +235,25 @@
 
 def project_kernel(plan, n_added, cols_ref, g_ref, gp_ref, w_ref, wp_ref, *refs):
     added, refs = refs[:n_added], refs[n_added:]
-    out_refs, (acts, weights, act_sems, weight_sems) = refs[:-4], refs[-4:]
+    out_refs, (weights, sems) = refs[:-2], refs[-2:]
     depth = g_ref.shape[1]
-    act_copies = [pltpu.make_async_copy(r, acts.at[j], act_sems.at[j]) for j, r in enumerate((g_ref, gp_ref))]
     copies = []
     for k, (col, _) in enumerate(plan):
         at = pl.ds(pl.multiple_of(cols_ref[col] * depth, depth), depth)
         pair = [
-            pltpu.make_async_copy(source.at[:, at], weights.at[k, j], weight_sems.at[k, j])
+            pltpu.make_async_copy(source.at[:, at], weights.at[k, j], sems.at[k, j])
             for j, source in enumerate((w_ref, wp_ref))
         ]
-        for copy in act_copies + pair if k == 0 else pair:
+        for copy in pair:
             copy.start()
         copies.append(pair)
     for k, (_, pieces) in enumerate(plan):
-        for copy in act_copies + copies[k] if k == 0 else copies[k]:
+        for copy in copies[k]:
             copy.wait()
         for first, count, out, slot, extra in pieces:
             rows = pl.ds(first, count)
-            acc = jnp.dot(acts[0, rows, :], weights[k, 0], preferred_element_type=f32)
-            acc = acc + jnp.dot(acts[1, rows, :], weights[k, 1], preferred_element_type=f32)
+            acc = jnp.dot(g_ref[rows, :], weights[k, 0], preferred_element_type=f32)
+            acc = acc + jnp.dot(gp_ref[rows, :], weights[k, 1], preferred_element_type=f32)
             if extra is not None:
                 acc = acc + added[extra[0]][extra[1]].astype(f32)
             out_refs[out][slot] = acc.astype(bf16)
@@ -265,7 +261,7 @@
 
 def project(operands, plan, counts, added=(), limit=50):
     cols, g, gp, w, wp = operands
-    n_tok, depth = g.shape
+    depth = g.shape[1]
     slots = [0] * len(counts)
     laid = []
     for (dy, dz), pieces in plan:
@@ -278,13 +274,11 @@
     anywhere = pl.BlockSpec(memory_space=pl.ANY)
     return pl.pallas_call(
         functools.partial(project_kernel, laid, len(added)),
-        in_specs=[pl.BlockSpec(memory_space=pltpu.SMEM)] + [anywhere] * 4 + [vmem] * len(added),
+        in_specs=[pl.BlockSpec(memory_space=pltpu.SMEM)] + [vmem] * 2 + [anywhere] * 2 + [vmem] * len(added),
         out_specs=[vmem] * len(counts),
         out_shape=[jax.ShapeDtypeStruct((n, count, depth), bf16) for n, count in zip(slots, counts)],
         scratch_shapes=[
-            pltpu.VMEM((2, n_tok, depth), bf16),
             pltpu.VMEM((len(plan), 2, depth, depth), bf16),
-            pltpu.SemaphoreType.DMA((2,)),
             pltpu.SemaphoreType.DMA((len(plan), 2)),
         ],
         compiler_params=pltpu.CompilerParams(vmem_limit_bytes=limit << 20),
@@ -296,7 +290,7 @@
     return sum(p.astype(f32) for p in parts).astype(bf16)
 
 
-Z_TOK = 320
+Z_TOK = 384
 
 
 def per_device(features, short_filter, decay_rate, residues, out_weight):
@@ -306,11 +300,11 @@
     me = lax.axis_index("ch")
     steps = jnp.arange(8, dtype=jnp.int32)
     cols = (me // 4 + steps // 2) % 4 * 4 + (me // 2 + steps) % 2 * 2 + me % 2
-    product, told, start = states(x, short_filter, decay_rate)
+    product, told = states(x, short_filter, decay_rate)
     told = jnp.stack([told, to_near_z(told)])
     heard = [told] + [to_x(told, n) for n in (1, 2, 3)]
     at = lax.axis_index("ctx").astype(jnp.int32)[None]
-    mine = gated(at, x, short_filter, decay_rate, residues, product, start, heard)
+    mine = gated(at, x, short_filter, decay_rate, residues, product, heard)
     operands = (cols, mine, to_core(mine), out_weight, weight_pair)
     n_y = n_tok - Z_TOK
     a, b, z = 0, n_y // 2, n_y

time: 106 us -> 104 us (0.981)
  other arithmetic: 3.24 us -> 6.4 us
  waiting for transfers between devices: 27.9 us -> 25.3 us
  Pallas kernels: 37.2 us -> 35.8 us
    convert_element_type x5, other arithmetic: 0.66 us -> 3.89 us  [total(): return sum((p.astype(f32) for p in parts)).astype(bf16)]
    ppermute x20, waiting for transfers between devices: 27.9 us -> 25.3 us  [spread(): return lax.ppermute(x, axis, [(i, j) for i, j in pairs if j is not None])]
    pallas_call x5, Pallas kernels: 23 us -> 21.5 us  [project(): pl.pallas_call(functools.partial(project_kernel, laid, len(added)), in_sp...]
    unnamed x18 -> x16, local copies, waits for them, and re-layouts: 2.57 us -> 1.69 us
  transfers between devices with their start and end apart: 20 -> 20, of which waited for: 11 -> 11; matrix products, arithmetic and copies ran while one was open for 2% -> 4% of each run, Pallas kernels for 32% -> 31%
where the time goes in v11:
time: 104 us
  Pallas kernels  35.8 us (34%)
  starting transfers between devices  34.5 us (33%)
  waiting for transfers between devices  25.3 us (24%)
  other arithmetic  6.4 us (6%)
  local copies, waits for them, and re-layouts  1.69 us (2%)
    ppermute x20, starting transfers between devices, spread(): return lax.ppermute(x, axis, [(i, j) for i, j in pairs if j is not None])  34.5 us
    ppermute x20, waiting for transfers between devices, spread(): return lax.ppermute(x, axis, [(i, j) for i, j in pairs if j is not None])  25.3 us
    pallas_call x5, Pallas kernels, project(): pl.pallas_call(functools.partial(project_kernel, laid, len(added)), in_sp...  21.5 us
    pallas_call x1, Pallas kernels, gated(): pl.pallas_call(gate_kernel, grid=(width // LANES,), in_specs=[pl.BlockSpe...  7.79 us
    pallas_call x1, Pallas kernels, states(): pl.pallas_call(state_kernel, grid=(width // LANES,), in_specs=[pl.BlockSp...  6.54 us
    convert_element_type x5, other arithmetic, total(): return sum((p.astype(f32) for p in parts)).astype(bf16)  3.89 us
  transfers between devices with their start and end apart: 20, of which 11 were waited for; matrix products, arithmetic and copies ran while one was open for 4% of the time, Pallas kernels for 31%

profile of v11, /device:TPU:0, one launch (start us, length us, event | category | flops | bytes accessed | tf_op | source)
XLA Modules:
  0.0 103.9 jit_solution(14572317744514668722)
XLA Ops:
  0.0 0.0 collective-permute-start.5
  0.0 6.5 %states.1 = (f32[144,8,512]{2,1,0:T(8,128)}, bf16[32,512]{1,0:T(8,128)(2,1)}) custom-call(bf16[3,1024,512]{2,1,0:T(8,128)(2,1)} %bitcast.44, bf16[3,1024,512]{2,1,0:T(8,128)(2,1)} %bitcast.45, bf16[3,1024,512]{2,1,0:T(8,128)(2,1)} %bitcast.46, f32[3,3,512]{2,1,0:T(4,128)} %sf_ref.3, f32[16,512]{1,0:T(8,128)} %rate_ref.3), custom_call_target="tpu_custom_call" | custom-call | tf_op jit(solution)/shard_map/states/pallas_call | solution.py:157
  6.5 2.0 %collective-permute-start = (bf16[32,512]{1,0:T(8,128)(2,1)}, bf16[32,512]{1,0:T(8,128)(2,1)S(1)}, u32[]{:S(2)}, u32[]{:S(2)}) collective-permute-start(bf16[32,512]{1,0:T(8,128)(2,1)} %get-tuple-element.27), channel_id=1, source_target_pairs={{0,64},{16,80},{32,96},{48,112},{64,0},{80,16},{96,32},{112,48},{1... | collective-permute-start | bytes 98312 | tf_op jit(solution)/shard_map/ppermute | solution.py:213
  8.6 2.3 %collective-permute-done = bf16[32,512]{1,0:T(8,128)(2,1)S(1)} collective-permute-done((bf16[32,512]{1,0:T(8,128)(2,1)}, bf16[32,512]{1,0:T(8,128)(2,1)S(1)}, u32[]{:S(2)}, u32[]{:S(2)}) %collective-permute-start) | collective-permute-done | bytes 32800 | tf_op jit(solution)/shard_map/ppermute | solution.py:213
  10.8 0.8 pad_maximum_fusion.2.refs_0_
  11.6 1.5 %collective-permute-start.1 = (bf16[2,32,512]{2,1,0:T(8,128)(2,1)S(1)}, bf16[2,32,512]{2,1,0:T(8,128)(2,1)S(1)}, u32[]{:S(2)}, u32[]{:S(2)}) collective-permute-start(bf16[2,32,512]{2,1,0:T(8,128)(2,1)S(1)} %pad_maximum_fusion.2.refs_0_), channel_id=1, source_target_pairs={{0,16},{16,32},{32,48},{48,0},{64,80},{80,96},{96,112},{112,64},{1... | collective-permute-start | bytes 196616 | tf_op jit(solution)/shard_map/ppermute | solution.py:213
  13.1 2.7 %collective-permute-start.2 = (bf16[2,32,512]{2,1,0:T(8,128)(2,1)S(1)}, bf16[2,32,512]{2,1,0:T(8,128)(2,1)S(1)}, u32[]{:S(2)}, u32[]{:S(2)}) collective-permute-start(bf16[2,32,512]{2,1,0:T(8,128)(2,1)S(1)} %pad_maximum_fusion.2.refs_0_), channel_id=1, source_target_pairs={{0,32},{16,48},{32,0},{48,16},{64,96},{80,112},{96,64},{112,80},{1... | collective-permute-start | bytes 196616 | tf_op jit(solution)/shard_map/ppermute | solution.py:213
  15.8 1.4 %collective-permute-start.3 = (bf16[2,32,512]{2,1,0:T(8,128)(2,1)S(1)}, bf16[2,32,512]{2,1,0:T(8,128)(2,1)S(1)}, u32[]{:S(2)}, u32[]{:S(2)}) collective-permute-start(bf16[2,32,512]{2,1,0:T(8,128)(2,1)S(1)} %pad_maximum_fusion.2.refs_0_), channel_id=1, source_target_pairs={{0,48},{16,0},{32,16},{48,32},{64,112},{80,64},{96,80},{112,96},{1... | collective-permute-start | bytes 196616 | tf_op jit(solution)/shard_map/ppermute | solution.py:213
  17.2 0.4 collective-permute-done.1.refs_1_
  17.7 1.3 %collective-permute-done.2.refs_2_ = bf16[2,32,512]{2,1,0:T(8,128)(2,1)S(1)} collective-permute-done((bf16[2,32,512]{2,1,0:T(8,128)(2,1)S(1)}, bf16[2,32,512]{2,1,0:T(8,128)(2,1)S(1)}, u32[]{:S(2)}, u32[]{:S(2)}) %collective-permute-start.2) | collective-permute-done | bytes 65568 | tf_op jit(solution)/shard_map/ppermute | solution.py:213
  19.0 1.1 %collective-permute-done.3.refs_3_ = bf16[2,32,512]{2,1,0:T(8,128)(2,1)S(1)} collective-permute-done((bf16[2,32,512]{2,1,0:T(8,128)(2,1)S(1)}, bf16[2,32,512]{2,1,0:T(8,128)(2,1)S(1)}, u32[]{:S(2)}, u32[]{:S(2)}) %collective-permute-start.3) | collective-permute-done | bytes 65568 | tf_op jit(solution)/shard_map/ppermute | solution.py:213
  20.1 0.0 copy-done.5
  20.1 0.0 copy-done.6
  20.1 0.0 copy-done.7
  20.1 0.0 copy-start.4
  20.1 1.7 %copy-done.4 = f32[144,8,512]{2,1,0:T(8,128)S(1)} copy-done((f32[144,8,512]{2,1,0:T(8,128)S(1)}, f32[144,8,512]{2,1,0:T(8,128)}, u32[]{:S(2)}) %copy-start.4) | copy-done | bytes 2359320
  21.8 7.8 %gated.1.g_ref = bf16[1024,512]{1,0:T(8,128)(2,1)S(1)} custom-call(s32[1]{0:T(128)} %bitcast.at_ref, bf16[3,1024,512]{2,1,0:T(8,128)(2,1)} %bitcast.47, f32[3,3,512]{2,1,0:T(4,128)S(1)} %copy-done.6, f32[16,512]{1,0:T(8,128)S(1)} %copy-done.5, f32[16,512]{1,0:T(8,128)S(1)} %copy-done.7, f32[144,8,512]{2,1,0:T(8,128)S(1)} %copy-done.4, ...), custom_call_target="tpu_custom_call" | custom-call | tf_op jit(solution)/shard_map/gated/pallas_call | solution.py:187
  29.6 0.0 copy-start
  29.6 0.1 collective-permute-start.4
  29.7 2.6 %collective-permute-done.4.gp_ref = bf16[1024,512]{1,0:T(8,128)(2,1)S(1)} collective-permute-done((bf16[1024,512]{1,0:T(8,128)(2,1)S(1)}, bf16[1024,512]{1,0:T(8,128)(2,1)S(1)}, u32[]{:S(2)}, u32[]{:S(2)}) %collective-permute-start.4) | collective-permute-done | bytes 1048608 | tf_op jit(solution)/shard_map/ppermute | solution.py:213
  32.3 0.0 collective-permute-done.5.wp_ref
  32.3 3.5 %project.5 = (bf16[2,320,512]{2,1,0:T(8,128)(2,1)S(1)}, bf16[2,320,512]{2,1,0:T(8,128)(2,1)S(1)}) custom-call(s32[8]{0:T(128)S(1)} %fusion.21.cols_ref, bf16[1024,512]{1,0:T(8,128)(2,1)S(1)} %gated.1.g_ref, bf16[1024,512]{1,0:T(8,128)(2,1)S(1)} %collective-permute-done.4.gp_ref, bf16[512,8192]{1,0:T(8,128)(2,1)} %w_ref.9, ...), custom_call_target="tpu_custom_call" | custom-call | tf_op jit(solution)/shard_map/project/pallas_call | solution.py:275
  35.8 3.1 %collective-permute-start.7 = (bf16[2,320,512]{2,1,0:T(8,128)(2,1)S(1)}, bf16[2,320,512]{2,1,0:T(8,128)(2,1)S(1)}, u32[]{:S(2)}, u32[]{:S(2)}) collective-permute-start(bf16[2,320,512]{2,1,0:T(8,128)(2,1)S(1)} %get-tuple-element.29), channel_id=1, source_target_pairs={{0,12},{1,13},{2,14},{3,15},{4,0},{5,1},{6,2},{7,3},{8,4},{9,5},{1... | collective-permute-start | bytes 1966088 | tf_op jit(solution)/shard_map/ppermute | solution.py:213
  38.9 0.0 collective-permute-start.6
  38.9 4.1 %project.9 = bf16[4,384,512]{2,1,0:T(8,128)(2,1)S(1)} custom-call(s32[8]{0:T(128)S(1)} %fusion.21.cols_ref, bf16[1024,512]{1,0:T(8,128)(2,1)S(1)} %gated.1.g_ref, bf16[1024,512]{1,0:T(8,128)(2,1)S(1)} %collective-permute-done.4.gp_ref, bf16[512,8192]{1,0:T(8,128)(2,1)} %w_ref.9, bf16[512,8192]{1,0:T(8,128)(2,1)} %collective-permute-done.5.wp_ref), custom_call_target="tpu_custom_call" | custom-call | tf_op jit(solution)/shard_map/project/pallas_call | solution.py:275
  43.0 3.9 %collective-permute-start.15 = (bf16[4,384,512]{2,1,0:T(8,128)(2,1)S(1)}, bf16[4,384,512]{2,1,0:T(8,128)(2,1)}, u32[]{:S(2)}, u32[]{:S(2)}) collective-permute-start(bf16[4,384,512]{2,1,0:T(8,128)(2,1)S(1)} %project.9), channel_id=1, source_target_pairs={{0,2},{1,3},{2,0},{3,1},{4,6},{5,7},{6,4},{7,5},{8,10},{9,11},{10,... | collective-permute-start | bytes 4718600 | tf_op jit(solution)/shard_map/ppermute | solution.py:213
  46.9 4.3 %project.7 = (bf16[1,320,512]{2,1,0:T(8,128)(2,1)S(1)}, bf16[1,320,512]{2,1,0:T(8,128)(2,1)S(1)}, bf16[1,320,512]{2,1,0:T(8,128)(2,1)S(1)}, bf16[1,320,512]{2,1,...) custom-call(s32[8]{0:T(128)S(1)} %fusion.21.cols_ref, ...), custom_call_target="tpu_custom_call" | custom-call | tf_op jit(solution)/shard_map/project/pallas_call | solution.py:275
  51.2 0.7 collective-permute-start.10
  51.9 2.7 %collective-permute-start.11 = (bf16[320,512]{1,0:T(8,128)(2,1)S(1)}, bf16[320,512]{1,0:T(8,128)(2,1)S(1)}, u32[]{:S(2)}, u32[]{:S(2)}) collective-permute-start(bf16[320,512]{1,0:T(8,128)(2,1)S(1)} %bitcast.42), channel_id=1, source_target_pairs={{0,12},{1,13},{2,14},{3,15},{4,0},{5,1},{6,2},{7,3},{8,4},{9,5},{1... | collective-permute-start | bytes 983048 | tf_op jit(solution)/shard_map/ppermute | solution.py:213
  54.6 0.0 collective-permute-done.7.refs_1_
  54.6 0.1 fusion.9
  54.7 2.3 %collective-permute-start.13 = (bf16[320,512]{1,0:T(8,128)(2,1)S(1)}, bf16[320,512]{1,0:T(8,128)(2,1)S(1)}, u32[]{:S(2)}, u32[]{:S(2)}) collective-permute-start(bf16[320,512]{1,0:T(8,128)(2,1)S(1)} %fusion.9), channel_id=1, source_target_pairs={{0,12},{1,13},{2,14},{3,15},{4,0},{5,1},{6,2},{7,3},{8,4},{9,5},{1... | collective-permute-start | bytes 983048 | tf_op jit(solution)/shard_map/ppermute | solution.py:213
  57.0 0.7 collective-permute-done.6.refs_0_
  57.7 0.1 fusion.8
  57.8 0.0 copy-start.1
  57.8 0.1 collective-permute-start.12
  57.9 5.5 %project.6 = (bf16[2,320,512]{2,1,0:T(8,128)(2,1)S(1)}, bf16[2,320,512]{2,1,0:T(8,128)(2,1)S(1)}, bf16[1,320,512]{2,1,0:T(8,128)(2,1)S(1)}, bf16[1,320,512]{2,1,0:T(8,128)(2,1)S(1)}) custom-call(s32[8]{0:T(128)S(1)} %fusion.21.cols_ref, bf16[1024,512]{1,0:T(8,128)(2,1)} %copy-done, bf16[1024,512]{1,0:T(8,128)(2,1)} %copy-done.2, bf16[512,8192]{1,0:T(8,128)(2,1)} %w_ref.9, ...), custom_call_target="tpu_custom_call" | custom-call | tf_op jit(solution)/shard_map/project/pallas_call | solution.py:275
  63.4 1.3 %collective-permute-done.10 = bf16[320,512]{1,0:T(8,128)(2,1)S(1)} collective-permute-done((bf16[320,512]{1,0:T(8,128)(2,1)S(1)}, bf16[320,512]{1,0:T(8,128)(2,1)S(1)}, u32[]{:S(2)}, u32[]{:S(2)}) %collective-permute-start.10) | collective-permute-done | bytes 327712 | tf_op jit(solution)/shard_map/ppermute | solution.py:213
  64.7 0.0 collective-permute-start.8
  64.7 0.0 collective-permute-done.11
  64.7 3.2 %collective-permute-start.9 = (bf16[2,320,512]{2,1,0:T(8,128)(2,1)S(1)}, bf16[2,320,512]{2,1,0:T(8,128)(2,1)S(1)}, u32[]{:S(2)}, u32[]{:S(2)}) collective-permute-start(bf16[2,320,512]{2,1,0:T(8,128)(2,1)S(1)} %get-tuple-element.32), channel_id=1, source_target_pairs={{0,12},{1,13},{2,14},{3,15},{4,0},{5,1},{6,2},{7,3},{8,4},{9,5},{1... | collective-permute-start | bytes 1966088 | tf_op jit(solution)/shard_map/ppermute | solution.py:213
  68.0 4.1 %project.8 = bf16[4,384,512]{2,1,0:T(8,128)(2,1)S(1)} custom-call(s32[8]{0:T(128)S(1)} %fusion.21.cols_ref, bf16[1024,512]{1,0:T(8,128)(2,1)S(1)} %copy-done.1, bf16[1024,512]{1,0:T(8,128)(2,1)S(1)} %copy-done.3, bf16[512,8192]{1,0:T(8,128)(2,1)} %w_ref.9, bf16[512,8192]{1,0:T(8,128)(2,1)} %collective-permute-done.5.wp_ref), custom_call_target="tpu_custom_call" | custom-call | tf_op jit(solution)/shard_map/project/pallas_call | solution.py:275
  72.1 0.0 collective-permute-done.13
  72.1 0.0 collective-permute-done.12
  72.1 0.3 fusion.12
  72.4 0.1 pad_maximum_fusion.1
  72.5 3.9 %collective-permute-start.14 = (bf16[2,320,512]{2,1,0:T(8,128)(2,1)S(1)}, bf16[2,320,512]{2,1,0:T(8,128)(2,1)S(1)}, u32[]{:S(2)}, u32[]{:S(2)}) collective-permute-start(bf16[2,320,512]{2,1,0:T(8,128)(2,1)S(1)} %pad_maximum_fusion.1), channel_id=1, source_target_pairs={{0,2},{1,3},{2,0},{3,1},{4,6},{5,7},{6,4},{7,5},{8,10},{9,11},{10,... | collective-permute-start | bytes 1966088 | tf_op jit(solution)/shard_map/ppermute | solution.py:213
  76.3 5.9 %collective-permute-done.15 = bf16[4,384,512]{2,1,0:T(8,128)(2,1)} collective-permute-done((bf16[4,384,512]{2,1,0:T(8,128)(2,1)S(1)}, bf16[4,384,512]{2,1,0:T(8,128)(2,1)}, u32[]{:S(2)}, u32[]{:S(2)}) %collective-permute-start.15) | collective-permute-done | bytes 1572896 | tf_op jit(solution)/shard_map/ppermute | solution.py:213
  82.2 1.1 %fusion.14 = (bf16[192,512]{1,0:T(8,128)(2,1)S(1)}, bf16[192,512]{1,0:T(8,128)(2,1)S(1)}) fusion(bf16[4,384,512]{2,1,0:T(8,128)(2,1)} %collective-permute-done.15, bf16[4,384,512]{2,1,0:T(8,128)(2,1)S(1)} %project.8), kind=kLoop, calls=%fused_computation.27 | loop fusion | flops 786432 | bytes 1179648 | tf_op jit(solution)/shard_map/convert_element_type | solution.py:290
  83.3 0.7 collective-permute-start.16
  84.0 2.7 %collective-permute-start.18 = (bf16[192,512]{1,0:T(8,128)(2,1)S(1)}, bf16[192,512]{1,0:T(8,128)(2,1)S(1)}, u32[]{:S(2)}, u32[]{:S(2)}) collective-permute-start(bf16[192,512]{1,0:T(8,128)(2,1)S(1)} %get-tuple-element.50), channel_id=1, source_target_pairs={{0,12},{1,13},{2,14},{3,15},{4,0},{5,1},{6,2},{7,3},{8,4},{9,5},{1... | collective-permute-start | bytes 589832 | tf_op jit(solution)/shard_map/ppermute | solution.py:213
  86.8 3.6 %collective-permute-done.16 = bf16[192,512]{1,0:T(8,128)(2,1)S(1)} collective-permute-done((bf16[192,512]{1,0:T(8,128)(2,1)S(1)}, bf16[192,512]{1,0:T(8,128)(2,1)S(1)}, u32[]{:S(2)}, u32[]{:S(2)}) %collective-permute-start.16) | collective-permute-done | bytes 196640 | tf_op jit(solution)/shard_map/ppermute | solution.py:213
  90.3 0.0 collective-permute-done.18
  90.3 1.4 %fusion.1 = (bf16[384,512]{1,0:T(8,128)(2,1)S(1)}, bf16[384,512]{1,0:T(8,128)(2,1)S(1)}) fusion(bf16[4,384,512]{2,1,0:T(8,128)(2,1)} %collective-permute-done.15, bf16[4,384,512]{2,1,0:T(8,128)(2,1)S(1)} %project.8, bf16[192,512]{1,0:T(8,128)(2,1)S(1)} %collective-permute-done.16, bf16[192,512]{1,0:T(8,128)(2,1)S(1)} %collective-permute-done.18), kind=kLoop, calls=%fused_computation.4 | loop fusion | flops 2359296 | bytes 2752512 | tf_op jit(solution)/shard_map/convert_element_type | solution.py:290
  91.7 1.5 %collective-permute-start.17 = (bf16[384,512]{1,0:T(8,128)(2,1)S(1)}, bf16[384,512]{1,0:T(8,128)(2,1)S(1)}, u32[]{:S(2)}, u32[]{:S(2)}) collective-permute-start(bf16[384,512]{1,0:T(8,128)(2,1)S(1)} %get-tuple-element.47), channel_id=1, source_target_pairs={{0,4},{1,5},{2,6},{3,7},{4,8},{5,9},{6,10},{7,11},{8,12},{9,13},{1... | collective-permute-start | bytes 1179656 | tf_op jit(solution)/shard_map/ppermute | solution.py:213
  93.2 2.0 %collective-permute-start.19 = (bf16[384,512]{1,0:T(8,128)(2,1)S(1)}, bf16[384,512]{1,0:T(8,128)(2,1)S(1)}, u32[]{:S(2)}, u32[]{:S(2)}) collective-permute-start(bf16[384,512]{1,0:T(8,128)(2,1)S(1)} %get-tuple-element.48), channel_id=1, source_target_pairs={{0,12},{1,13},{2,14},{3,15},{4,0},{5,1},{6,2},{7,3},{8,4},{9,5},{1... | collective-permute-start | bytes 1179656 | tf_op jit(solution)/shard_map/ppermute | solution.py:213
  95.2 0.0 collective-permute-done.8
  95.2 0.0 collective-permute-done.9
  95.2 0.2 collective-permute-done.14
  95.4 0.4 fusion.10
  95.7 5.9 %collective-permute-done.17 = bf16[384,512]{1,0:T(8,128)(2,1)S(1)} collective-permute-done((bf16[384,512]{1,0:T(8,128)(2,1)S(1)}, bf16[384,512]{1,0:T(8,128)(2,1)S(1)}, u32[]{:S(2)}, u32[]{:S(2)}) %collective-permute-start.17) | collective-permute-done | bytes 393248 | tf_op jit(solution)/shard_map/ppermute | solution.py:213
  101.6 0.0 collective-permute-done.19
  101.6 1.2 %fusion.3 = bf16[384,512]{1,0:T(8,128)(2,1)S(1)} fusion(bf16[384,512]{1,0:T(8,128)(2,1)S(1)} %collective-permute-done.19, bf16[384,512]{1,0:T(8,128)(2,1)S(1)} %collective-permute-done.17, bf16[4,384,512]{2,1,0:T(8,128)(2,1)} %collective-permute-done.15, bf16[4,384,512]{2,1,0:T(8,128)(2,1)S(1)} %project.8), kind=kLoop, calls=%fused_computation.7 | loop fusion | flops 1572864 | bytes 1966080 | tf_op jit(solution)/shard_map/convert_element_type | solution.py:290
  102.8 1.0 %pad_maximum_fusion = bf16[1024,512]{1,0:T(8,128)(2,1)} fusion(bf16[384,512]{1,0:T(8,128)(2,1)S(1)} %fusion.3, bf16[320,512]{1,0:T(8,128)(2,1)S(1)} %get-tuple-element.52, bf16[320,512]{1,0:T(8,128)(2,1)S(1)} %get-tuple-element.51), kind=kLoop, calls=%fused_computation | loop fusion | flops 3145728 | bytes 2097152 | tf_op jit(solution)/shard_map/concatenate | solution.py:344
  (10 shorter events, 0.0 us)
Async XLA Ops:
  0.0 32.3 %collective-permute-start.5 = (bf16[512,8192]{1,0:T(8,128)(2,1)}, bf16[512,8192]{1,0:T(8,128)(2,1)}, u32[]{:S(2)}, u32[]{:S(2)}) collective-permute-start(bf16[512,8192]{1,0:T(8,128)(2,1)} %w_ref.9), channel_id=1, source_target_pairs={{0,1},{1,0},{2,3},{3,2},{4,5},{5,4},{6,7},{7,6},{8,9},{9,8},{10,11... | collective-permute-start | bytes 25165832 | tf_op jit(solution)/shard_map/ppermute | solution.py:213
  0.0 20.1 %copy-start.5 = (f32[16,512]{1,0:T(8,128)S(1)}, f32[16,512]{1,0:T(8,128)}, u32[]{:S(2)}) copy-start(f32[16,512]{1,0:T(8,128)} %rate_ref.3) | copy-start | bytes 98308
  0.0 20.1 %copy-start.6 = (f32[3,3,512]{2,1,0:T(4,128)S(1)}, f32[3,3,512]{2,1,0:T(4,128)}, u32[]{:S(2)}) copy-start(f32[3,3,512]{2,1,0:T(4,128)} %sf_ref.3) | copy-start | bytes 55300
  0.0 20.1 %copy-start.7 = (f32[16,512]{1,0:T(8,128)S(1)}, f32[16,512]{1,0:T(8,128)}, u32[]{:S(2)}) copy-start(f32[16,512]{1,0:T(8,128)} %res_ref.1) | copy-start | bytes 98308
  6.5 4.3 %collective-permute-start = (bf16[32,512]{1,0:T(8,128)(2,1)}, bf16[32,512]{1,0:T(8,128)(2,1)S(1)}, u32[]{:S(2)}, u32[]{:S(2)}) collective-permute-start(bf16[32,512]{1,0:T(8,128)(2,1)} %get-tuple-element.27), channel_id=1, source_target_pairs={{0,64},{16,80},{32,96},{48,112},{64,0},{80,16},{96,32},{112,48},{1... | collective-permute-start | bytes 98312 | tf_op jit(solution)/shard_map/ppermute | solution.py:213
  11.6 6.1 %collective-permute-start.1 = (bf16[2,32,512]{2,1,0:T(8,128)(2,1)S(1)}, bf16[2,32,512]{2,1,0:T(8,128)(2,1)S(1)}, u32[]{:S(2)}, u32[]{:S(2)}) collective-permute-start(bf16[2,32,512]{2,1,0:T(8,128)(2,1)S(1)} %pad_maximum_fusion.2.refs_0_), channel_id=1, source_target_pairs={{0,16},{16,32},{32,48},{48,0},{64,80},{80,96},{96,112},{112,64},{1... | collective-permute-start | bytes 196616 | tf_op jit(solution)/shard_map/ppermute | solution.py:213
  13.1 5.9 %collective-permute-start.2 = (bf16[2,32,512]{2,1,0:T(8,128)(2,1)S(1)}, bf16[2,32,512]{2,1,0:T(8,128)(2,1)S(1)}, u32[]{:S(2)}, u32[]{:S(2)}) collective-permute-start(bf16[2,32,512]{2,1,0:T(8,128)(2,1)S(1)} %pad_maximum_fusion.2.refs_0_), channel_id=1, source_target_pairs={{0,32},{16,48},{32,0},{48,16},{64,96},{80,112},{96,64},{112,80},{1... | collective-permute-start | bytes 196616 | tf_op jit(solution)/shard_map/ppermute | solution.py:213
  15.8 4.3 %collective-permute-start.3 = (bf16[2,32,512]{2,1,0:T(8,128)(2,1)S(1)}, bf16[2,32,512]{2,1,0:T(8,128)(2,1)S(1)}, u32[]{:S(2)}, u32[]{:S(2)}) collective-permute-start(bf16[2,32,512]{2,1,0:T(8,128)(2,1)S(1)} %pad_maximum_fusion.2.refs_0_), channel_id=1, source_target_pairs={{0,48},{16,0},{32,16},{48,32},{64,112},{80,64},{96,80},{112,96},{1... | collective-permute-start | bytes 196616 | tf_op jit(solution)/shard_map/ppermute | solution.py:213
  20.1 1.7 %copy-start.4 = (f32[144,8,512]{2,1,0:T(8,128)S(1)}, f32[144,8,512]{2,1,0:T(8,128)}, u32[]{:S(2)}) copy-start(f32[144,8,512]{2,1,0:T(8,128)} %get-tuple-element.26.p_ref) | copy-start | bytes 7077892
  29.6 17.3 %copy-start = (bf16[1024,512]{1,0:T(8,128)(2,1)}, bf16[1024,512]{1,0:T(8,128)(2,1)S(1)}, u32[]{:S(2)}) copy-start(bf16[1024,512]{1,0:T(8,128)(2,1)S(1)} %gated.1.g_ref) | copy-start | bytes 3145732
  29.6 2.7 %collective-permute-start.4 = (bf16[1024,512]{1,0:T(8,128)(2,1)S(1)}, bf16[1024,512]{1,0:T(8,128)(2,1)S(1)}, u32[]{:S(2)}, u32[]{:S(2)}) collective-permute-start(bf16[1024,512]{1,0:T(8,128)(2,1)S(1)} %gated.1.g_ref), channel_id=1, source_target_pairs={{0,1},{1,0},{2,3},{3,2},{4,5},{5,4},{6,7},{7,6},{8,9},{9,8},{10,11... | collective-permute-start | bytes 3145736 | tf_op jit(solution)/shard_map/ppermute | solution.py:213
  32.3 14.6 %copy-start.2 = (bf16[1024,512]{1,0:T(8,128)(2,1)}, bf16[1024,512]{1,0:T(8,128)(2,1)S(1)}, u32[]{:S(2)}) copy-start(bf16[1024,512]{1,0:T(8,128)(2,1)S(1)} %collective-permute-done.4.gp_ref) | copy-start | bytes 3145732
  35.8 18.8 %collective-permute-start.7 = (bf16[2,320,512]{2,1,0:T(8,128)(2,1)S(1)}, bf16[2,320,512]{2,1,0:T(8,128)(2,1)S(1)}, u32[]{:S(2)}, u32[]{:S(2)}) collective-permute-start(bf16[2,320,512]{2,1,0:T(8,128)(2,1)S(1)} %get-tuple-element.29), channel_id=1, source_target_pairs={{0,12},{1,13},{2,14},{3,15},{4,0},{5,1},{6,2},{7,3},{8,4},{9,5},{1... | collective-permute-start | bytes 1966088 | tf_op jit(solution)/shard_map/ppermute | solution.py:213
  38.9 18.8 %collective-permute-start.6 = (bf16[2,320,512]{2,1,0:T(8,128)(2,1)S(1)}, bf16[2,320,512]{2,1,0:T(8,128)(2,1)S(1)}, u32[]{:S(2)}, u32[]{:S(2)}) collective-permute-start(bf16[2,320,512]{2,1,0:T(8,128)(2,1)S(1)} %get-tuple-element.28), channel_id=1, source_target_pairs={{0,4},{1,5},{2,6},{3,7},{4,8},{5,9},{6,10},{7,11},{8,12},{9,13},{1... | collective-permute-start | bytes 1966088 | tf_op jit(solution)/shard_map/ppermute | solution.py:213
  43.0 39.2 %collective-permute-start.15 = (bf16[4,384,512]{2,1,0:T(8,128)(2,1)S(1)}, bf16[4,384,512]{2,1,0:T(8,128)(2,1)}, u32[]{:S(2)}, u32[]{:S(2)}) collective-permute-start(bf16[4,384,512]{2,1,0:T(8,128)(2,1)S(1)} %project.9), channel_id=1, source_target_pairs={{0,2},{1,3},{2,0},{3,1},{4,6},{5,7},{6,4},{7,5},{8,10},{9,11},{10,... | collective-permute-start | bytes 4718600 | tf_op jit(solution)/shard_map/ppermute | solution.py:213
  51.2 13.5 %collective-permute-start.10 = (bf16[320,512]{1,0:T(8,128)(2,1)S(1)}, bf16[320,512]{1,0:T(8,128)(2,1)S(1)}, u32[]{:S(2)}, u32[]{:S(2)}) collective-permute-start(bf16[320,512]{1,0:T(8,128)(2,1)S(1)} %bitcast.43), channel_id=1, source_target_pairs={{0,4},{1,5},{2,6},{3,7},{4,8},{5,9},{6,10},{7,11},{8,12},{9,13},{1... | collective-permute-start | bytes 983048 | tf_op jit(solution)/shard_map/ppermute | solution.py:213
  51.9 12.8 %collective-permute-start.11 = (bf16[320,512]{1,0:T(8,128)(2,1)S(1)}, bf16[320,512]{1,0:T(8,128)(2,1)S(1)}, u32[]{:S(2)}, u32[]{:S(2)}) collective-permute-start(bf16[320,512]{1,0:T(8,128)(2,1)S(1)} %bitcast.42), channel_id=1, source_target_pairs={{0,12},{1,13},{2,14},{3,15},{4,0},{5,1},{6,2},{7,3},{8,4},{9,5},{1... | collective-permute-start | bytes 983048 | tf_op jit(solution)/shard_map/ppermute | solution.py:213
  54.7 17.4 %collective-permute-start.13 = (bf16[320,512]{1,0:T(8,128)(2,1)S(1)}, bf16[320,512]{1,0:T(8,128)(2,1)S(1)}, u32[]{:S(2)}, u32[]{:S(2)}) collective-permute-start(bf16[320,512]{1,0:T(8,128)(2,1)S(1)} %fusion.9), channel_id=1, source_target_pairs={{0,12},{1,13},{2,14},{3,15},{4,0},{5,1},{6,2},{7,3},{8,4},{9,5},{1... | collective-permute-start | bytes 983048 | tf_op jit(solution)/shard_map/ppermute | solution.py:213
  57.8 10.2 %copy-start.1 = (bf16[1024,512]{1,0:T(8,128)(2,1)S(1)}, bf16[1024,512]{1,0:T(8,128)(2,1)}, u32[]{:S(2)}) copy-start(bf16[1024,512]{1,0:T(8,128)(2,1)} %copy-done) | copy-start | bytes 3145732
  57.8 10.2 %copy-start.3 = (bf16[1024,512]{1,0:T(8,128)(2,1)S(1)}, bf16[1024,512]{1,0:T(8,128)(2,1)}, u32[]{:S(2)}) copy-start(bf16[1024,512]{1,0:T(8,128)(2,1)} %copy-done.2) | copy-start | bytes 3145732
  57.8 14.3 %collective-permute-start.12 = (bf16[320,512]{1,0:T(8,128)(2,1)S(1)}, bf16[320,512]{1,0:T(8,128)(2,1)S(1)}, u32[]{:S(2)}, u32[]{:S(2)}) collective-permute-start(bf16[320,512]{1,0:T(8,128)(2,1)S(1)} %fusion.8), channel_id=1, source_target_pairs={{0,4},{1,5},{2,6},{3,7},{4,8},{5,9},{6,10},{7,11},{8,12},{9,13},{1... | collective-permute-start | bytes 983048 | tf_op jit(solution)/shard_map/ppermute | solution.py:213
  64.7 30.5 %collective-permute-start.8 = (bf16[2,320,512]{2,1,0:T(8,128)(2,1)S(1)}, bf16[2,320,512]{2,1,0:T(8,128)(2,1)S(1)}, u32[]{:S(2)}, u32[]{:S(2)}) collective-permute-start(bf16[2,320,512]{2,1,0:T(8,128)(2,1)S(1)} %get-tuple-element.31), channel_id=1, source_target_pairs={{0,4},{1,5},{2,6},{3,7},{4,8},{5,9},{6,10},{7,11},{8,12},{9,13},{1... | collective-permute-start | bytes 1966088 | tf_op jit(solution)/shard_map/ppermute | solution.py:213
  64.7 30.5 %collective-permute-start.9 = (bf16[2,320,512]{2,1,0:T(8,128)(2,1)S(1)}, bf16[2,320,512]{2,1,0:T(8,128)(2,1)S(1)}, u32[]{:S(2)}, u32[]{:S(2)}) collective-permute-start(bf16[2,320,512]{2,1,0:T(8,128)(2,1)S(1)} %get-tuple-element.32), channel_id=1, source_target_pairs={{0,12},{1,13},{2,14},{3,15},{4,0},{5,1},{6,2},{7,3},{8,4},{9,5},{1... | collective-permute-start | bytes 1966088 | tf_op jit(solution)/shard_map/ppermute | solution.py:213
  72.5 22.9 %collective-permute-start.14 = (bf16[2,320,512]{2,1,0:T(8,128)(2,1)S(1)}, bf16[2,320,512]{2,1,0:T(8,128)(2,1)S(1)}, u32[]{:S(2)}, u32[]{:S(2)}) collective-permute-start(bf16[2,320,512]{2,1,0:T(8,128)(2,1)S(1)} %pad_maximum_fusion.1), channel_id=1, source_target_pairs={{0,2},{1,3},{2,0},{3,1},{4,6},{5,7},{6,4},{7,5},{8,10},{9,11},{10,... | collective-permute-start | bytes 1966088 | tf_op jit(solution)/shard_map/ppermute | solution.py:213
  83.3 7.0 %collective-permute-start.16 = (bf16[192,512]{1,0:T(8,128)(2,1)S(1)}, bf16[192,512]{1,0:T(8,128)(2,1)S(1)}, u32[]{:S(2)}, u32[]{:S(2)}) collective-permute-start(bf16[192,512]{1,0:T(8,128)(2,1)S(1)} %get-tuple-element.49), channel_id=1, source_target_pairs={{0,4},{1,5},{2,6},{3,7},{4,8},{5,9},{6,10},{7,11},{8,12},{9,13},{1... | collective-permute-start | bytes 589832 | tf_op jit(solution)/shard_map/ppermute | solution.py:213
  84.0 6.3 %collective-permute-start.18 = (bf16[192,512]{1,0:T(8,128)(2,1)S(1)}, bf16[192,512]{1,0:T(8,128)(2,1)S(1)}, u32[]{:S(2)}, u32[]{:S(2)}) collective-permute-start(bf16[192,512]{1,0:T(8,128)(2,1)S(1)} %get-tuple-element.50), channel_id=1, source_target_pairs={{0,12},{1,13},{2,14},{3,15},{4,0},{5,1},{6,2},{7,3},{8,4},{9,5},{1... | collective-permute-start | bytes 589832 | tf_op jit(solution)/shard_map/ppermute | solution.py:213
  91.7 9.9 %collective-permute-start.17 = (bf16[384,512]{1,0:T(8,128)(2,1)S(1)}, bf16[384,512]{1,0:T(8,128)(2,1)S(1)}, u32[]{:S(2)}, u32[]{:S(2)}) collective-permute-start(bf16[384,512]{1,0:T(8,128)(2,1)S(1)} %get-tuple-element.47), channel_id=1, source_target_pairs={{0,4},{1,5},{2,6},{3,7},{4,8},{5,9},{6,10},{7,11},{8,12},{9,13},{1... | collective-permute-start | bytes 1179656 | tf_op jit(solution)/shard_map/ppermute | solution.py:213
  93.2 8.4 %collective-permute-start.19 = (bf16[384,512]{1,0:T(8,128)(2,1)S(1)}, bf16[384,512]{1,0:T(8,128)(2,1)S(1)}, u32[]{:S(2)}, u32[]{:S(2)}) collective-permute-start(bf16[384,512]{1,0:T(8,128)(2,1)S(1)} %get-tuple-element.48), channel_id=1, source_target_pairs={{0,12},{1,13},{2,14},{3,15},{4,0},{5,1},{6,2},{7,3},{8,4},{9,5},{1... | collective-permute-start | bytes 1179656 | tf_op jit(solution)/shard_map/ppermute | solution.py:213

commit v12 on v11

--- a/solution.py
+++ b/solution.py
@@ -259,7 +259,7 @@
             out_refs[out][slot] = acc.astype(bf16)
 
 
-def project(operands, plan, counts, added=(), limit=50):
+def project(operands, plan, counts, added=(), limit=48):
     cols, g, gp, w, wp = operands
     depth = g.shape[1]
     slots = [0] * len(counts)
@@ -309,7 +309,7 @@
     n_y = n_tok - Z_TOK
     a, b, z = 0, n_y // 2, n_y
 
-    up2, down2 = project(operands, [((2, dz), [(a, 0), (b, 1)]) for dz in (1, 0)], [b, b], limit=50)
+    up2, down2 = project(operands, [((2, dz), [(a, 0), (b, 1)]) for dz in (1, 0)], [b, b], limit=48)
     up2, down2 = to_y(up2, 1), to_y(down2, -1)
     (far,) = project(operands, [((dy, 1), [(z, 0)]) for dy in (0, 1, 2, 3)], [Z_TOK])
     far = to_far_z(far)

time: 104 us -> 101 us (0.971)
  other arithmetic: 6.4 us -> 3.26 us
  waiting for transfers between devices: 25.3 us -> 26.4 us
  Pallas kernels: 35.8 us -> 34.7 us
    convert_element_type x5, other arithmetic: 3.89 us -> 0.76 us  [total(): return sum((p.astype(f32) for p in parts)).astype(bf16)]
    pallas_call x5, Pallas kernels: 21.5 us -> 20.4 us  [project(): pl.pallas_call(functools.partial(project_kernel, laid, len(added)), in_sp...]
    ppermute x20, waiting for transfers between devices: 25.3 us -> 26.4 us  [spread(): return lax.ppermute(x, axis, [(i, j) for i, j in pairs if j is not None])]
  transfers between devices with their start and end apart: 20 -> 20, of which waited for: 11 -> 11; matrix products, arithmetic and copies ran while one was open for 4% -> 2% of each run, Pallas kernels for 31% -> 31%
where the time goes in v12:
time: 101 us
  Pallas kernels  34.7 us (34%)
  starting transfers between devices  34.5 us (34%)
  waiting for transfers between devices  26.4 us (26%)
  other arithmetic  3.26 us (3%)
  local copies, waits for them, and re-layouts  1.67 us (2%)
    ppermute x20, starting transfers between devices, spread(): return lax.ppermute(x, axis, [(i, j) for i, j in pairs if j is not None])  34.5 us
    ppermute x20, waiting for transfers between devices, spread(): return lax.ppermute(x, axis, [(i, j) for i, j in pairs if j is not None])  26.4 us
    pallas_call x5, Pallas kernels, project(): pl.pallas_call(functools.partial(project_kernel, laid, len(added)), in_sp...  20.4 us
    pallas_call x1, Pallas kernels, gated(): pl.pallas_call(gate_kernel, grid=(width // LANES,), in_specs=[pl.BlockSpe...  7.79 us
    pallas_call x1, Pallas kernels, states(): pl.pallas_call(state_kernel, grid=(width // LANES,), in_specs=[pl.BlockSp...  6.53 us
  transfers between devices with their start and end apart: 20, of which 11 were waited for; matrix products, arithmetic and copies ran while one was open for 2% of the time, Pallas kernels for 31%

profile of v12, /device:TPU:0, one launch (start us, length us, event | category | flops | bytes accessed | tf_op | source)
XLA Modules:
  0.0 100.7 jit_solution(257696358059668185)
XLA Ops:
  0.0 0.0 collective-permute-start.5
  0.0 0.0 copy-start.1
  0.0 0.0 copy-start.3
  0.0 6.5 %states.1 = (f32[144,8,512]{2,1,0:T(8,128)}, bf16[32,512]{1,0:T(8,128)(2,1)}) custom-call(bf16[3,1024,512]{2,1,0:T(8,128)(2,1)} %bitcast.44, bf16[3,1024,512]{2,1,0:T(8,128)(2,1)} %bitcast.45, bf16[3,1024,512]{2,1,0:T(8,128)(2,1)} %bitcast.46, f32[3,3,512]{2,1,0:T(4,128)} %sf_ref.3, f32[16,512]{1,0:T(8,128)} %rate_ref.3), custom_call_target="tpu_custom_call" | custom-call | tf_op jit(solution)/shard_map/states/pallas_call | solution.py:157
  6.5 2.0 %collective-permute-start = (bf16[32,512]{1,0:T(8,128)(2,1)}, bf16[32,512]{1,0:T(8,128)(2,1)S(1)}, u32[]{:S(2)}, u32[]{:S(2)}) collective-permute-start(bf16[32,512]{1,0:T(8,128)(2,1)} %get-tuple-element.27), channel_id=1, source_target_pairs={{0,64},{16,80},{32,96},{48,112},{64,0},{80,16},{96,32},{112,48},{1... | collective-permute-start | bytes 98312 | tf_op jit(solution)/shard_map/ppermute | solution.py:213
  8.5 2.3 %collective-permute-done = bf16[32,512]{1,0:T(8,128)(2,1)S(1)} collective-permute-done((bf16[32,512]{1,0:T(8,128)(2,1)}, bf16[32,512]{1,0:T(8,128)(2,1)S(1)}, u32[]{:S(2)}, u32[]{:S(2)}) %collective-permute-start) | collective-permute-done | bytes 32800 | tf_op jit(solution)/shard_map/ppermute | solution.py:213
  10.8 0.8 pad_maximum_fusion.2.refs_0_
  11.6 1.5 %collective-permute-start.1 = (bf16[2,32,512]{2,1,0:T(8,128)(2,1)S(1)}, bf16[2,32,512]{2,1,0:T(8,128)(2,1)S(1)}, u32[]{:S(2)}, u32[]{:S(2)}) collective-permute-start(bf16[2,32,512]{2,1,0:T(8,128)(2,1)S(1)} %pad_maximum_fusion.2.refs_0_), channel_id=1, source_target_pairs={{0,16},{16,32},{32,48},{48,0},{64,80},{80,96},{96,112},{112,64},{1... | collective-permute-start | bytes 196616 | tf_op jit(solution)/shard_map/ppermute | solution.py:213
  13.1 2.7 %collective-permute-start.2 = (bf16[2,32,512]{2,1,0:T(8,128)(2,1)S(1)}, bf16[2,32,512]{2,1,0:T(8,128)(2,1)S(1)}, u32[]{:S(2)}, u32[]{:S(2)}) collective-permute-start(bf16[2,32,512]{2,1,0:T(8,128)(2,1)S(1)} %pad_maximum_fusion.2.refs_0_), channel_id=1, source_target_pairs={{0,32},{16,48},{32,0},{48,16},{64,96},{80,112},{96,64},{112,80},{1... | collective-permute-start | bytes 196616 | tf_op jit(solution)/shard_map/ppermute | solution.py:213
  15.8 1.4 %collective-permute-start.3 = (bf16[2,32,512]{2,1,0:T(8,128)(2,1)S(1)}, bf16[2,32,512]{2,1,0:T(8,128)(2,1)S(1)}, u32[]{:S(2)}, u32[]{:S(2)}) collective-permute-start(bf16[2,32,512]{2,1,0:T(8,128)(2,1)S(1)} %pad_maximum_fusion.2.refs_0_), channel_id=1, source_target_pairs={{0,48},{16,0},{32,16},{48,32},{64,112},{80,64},{96,80},{112,96},{1... | collective-permute-start | bytes 196616 | tf_op jit(solution)/shard_map/ppermute | solution.py:213
  17.2 0.4 collective-permute-done.1.refs_1_
  17.7 1.3 %collective-permute-done.2.refs_2_ = bf16[2,32,512]{2,1,0:T(8,128)(2,1)S(1)} collective-permute-done((bf16[2,32,512]{2,1,0:T(8,128)(2,1)S(1)}, bf16[2,32,512]{2,1,0:T(8,128)(2,1)S(1)}, u32[]{:S(2)}, u32[]{:S(2)}) %collective-permute-start.2) | collective-permute-done | bytes 65568 | tf_op jit(solution)/shard_map/ppermute | solution.py:213
  19.0 1.1 %collective-permute-done.3.refs_3_ = bf16[2,32,512]{2,1,0:T(8,128)(2,1)S(1)} collective-permute-done((bf16[2,32,512]{2,1,0:T(8,128)(2,1)S(1)}, bf16[2,32,512]{2,1,0:T(8,128)(2,1)S(1)}, u32[]{:S(2)}, u32[]{:S(2)}) %collective-permute-start.3) | collective-permute-done | bytes 65568 | tf_op jit(solution)/shard_map/ppermute | solution.py:213
  20.1 0.0 copy-done.1
  20.1 0.0 copy-done.2
  20.1 0.0 copy-done.3
  20.1 0.0 copy-start
  20.1 1.7 %copy-done = f32[144,8,512]{2,1,0:T(8,128)S(1)} copy-done((f32[144,8,512]{2,1,0:T(8,128)S(1)}, f32[144,8,512]{2,1,0:T(8,128)}, u32[]{:S(2)}) %copy-start) | copy-done | bytes 2359320
  21.7 7.8 %gated.1.g_ref = bf16[1024,512]{1,0:T(8,128)(2,1)S(1)} custom-call(s32[1]{0:T(128)} %bitcast.at_ref, bf16[3,1024,512]{2,1,0:T(8,128)(2,1)} %bitcast.47, f32[3,3,512]{2,1,0:T(4,128)S(1)} %copy-done.2, f32[16,512]{1,0:T(8,128)S(1)} %copy-done.1, f32[16,512]{1,0:T(8,128)S(1)} %copy-done.3, f32[144,8,512]{2,1,0:T(8,128)S(1)} %copy-done, ...), custom_call_target="tpu_custom_call" | custom-call | tf_op jit(solution)/shard_map/gated/pallas_call | solution.py:187
  29.6 0.1 collective-permute-start.4
  29.7 2.6 %collective-permute-done.4.gp_ref = bf16[1024,512]{1,0:T(8,128)(2,1)S(1)} collective-permute-done((bf16[1024,512]{1,0:T(8,128)(2,1)S(1)}, bf16[1024,512]{1,0:T(8,128)(2,1)S(1)}, u32[]{:S(2)}, u32[]{:S(2)}) %collective-permute-start.4) | collective-permute-done | bytes 1048608 | tf_op jit(solution)/shard_map/ppermute | solution.py:213
  32.3 0.0 collective-permute-done.5.wp_ref
  32.3 3.5 %project.5 = (bf16[2,320,512]{2,1,0:T(8,128)(2,1)S(1)}, bf16[2,320,512]{2,1,0:T(8,128)(2,1)S(1)}) custom-call(s32[8]{0:T(128)S(1)} %fusion.21.cols_ref, bf16[1024,512]{1,0:T(8,128)(2,1)S(1)} %gated.1.g_ref, bf16[1024,512]{1,0:T(8,128)(2,1)S(1)} %collective-permute-done.4.gp_ref, bf16[512,8192]{1,0:T(8,128)(2,1)} %w_ref.9, ...), custom_call_target="tpu_custom_call" | custom-call | tf_op jit(solution)/shard_map/project/pallas_call | solution.py:275
  35.8 3.1 %collective-permute-start.7 = (bf16[2,320,512]{2,1,0:T(8,128)(2,1)S(1)}, bf16[2,320,512]{2,1,0:T(8,128)(2,1)S(1)}, u32[]{:S(2)}, u32[]{:S(2)}) collective-permute-start(bf16[2,320,512]{2,1,0:T(8,128)(2,1)S(1)} %get-tuple-element.29), channel_id=1, source_target_pairs={{0,12},{1,13},{2,14},{3,15},{4,0},{5,1},{6,2},{7,3},{8,4},{9,5},{1... | collective-permute-start | bytes 1966088 | tf_op jit(solution)/shard_map/ppermute | solution.py:213
  38.9 0.0 collective-permute-start.6
  38.9 4.1 %project.9 = bf16[4,384,512]{2,1,0:T(8,128)(2,1)S(1)} custom-call(s32[8]{0:T(128)S(1)} %fusion.21.cols_ref, bf16[1024,512]{1,0:T(8,128)(2,1)S(1)} %gated.1.g_ref, bf16[1024,512]{1,0:T(8,128)(2,1)S(1)} %collective-permute-done.4.gp_ref, bf16[512,8192]{1,0:T(8,128)(2,1)} %w_ref.9, bf16[512,8192]{1,0:T(8,128)(2,1)} %collective-permute-done.5.wp_ref), custom_call_target="tpu_custom_call" | custom-call | tf_op jit(solution)/shard_map/project/pallas_call | solution.py:275
  43.0 3.9 %collective-permute-start.15 = (bf16[4,384,512]{2,1,0:T(8,128)(2,1)S(1)}, bf16[4,384,512]{2,1,0:T(8,128)(2,1)S(1)}, u32[]{:S(2)}, u32[]{:S(2)}) collective-permute-start(bf16[4,384,512]{2,1,0:T(8,128)(2,1)S(1)} %project.9), channel_id=1, source_target_pairs={{0,2},{1,3},{2,0},{3,1},{4,6},{5,7},{6,4},{7,5},{8,10},{9,11},{10,... | collective-permute-start | bytes 4718600 | tf_op jit(solution)/shard_map/ppermute | solution.py:213
  46.9 4.3 %project.7 = (bf16[1,320,512]{2,1,0:T(8,128)(2,1)S(1)}, bf16[1,320,512]{2,1,0:T(8,128)(2,1)S(1)}, bf16[1,320,512]{2,1,0:T(8,128)(2,1)S(1)}, bf16[1,320,512]{2,1,...) custom-call(s32[8]{0:T(128)S(1)} %fusion.21.cols_ref, ...), custom_call_target="tpu_custom_call" | custom-call | tf_op jit(solution)/shard_map/project/pallas_call | solution.py:275
  51.2 0.7 collective-permute-start.10
  51.9 2.7 %collective-permute-start.11 = (bf16[320,512]{1,0:T(8,128)(2,1)S(1)}, bf16[320,512]{1,0:T(8,128)(2,1)S(1)}, u32[]{:S(2)}, u32[]{:S(2)}) collective-permute-start(bf16[320,512]{1,0:T(8,128)(2,1)S(1)} %bitcast.42), channel_id=1, source_target_pairs={{0,12},{1,13},{2,14},{3,15},{4,0},{5,1},{6,2},{7,3},{8,4},{9,5},{1... | collective-permute-start | bytes 983048 | tf_op jit(solution)/shard_map/ppermute | solution.py:213
  54.6 0.0 collective-permute-done.7.refs_1_
  54.6 0.1 fusion.9
  54.7 2.3 %collective-permute-start.13 = (bf16[320,512]{1,0:T(8,128)(2,1)S(1)}, bf16[320,512]{1,0:T(8,128)(2,1)S(1)}, u32[]{:S(2)}, u32[]{:S(2)}) collective-permute-start(bf16[320,512]{1,0:T(8,128)(2,1)S(1)} %fusion.9), channel_id=1, source_target_pairs={{0,12},{1,13},{2,14},{3,15},{4,0},{5,1},{6,2},{7,3},{8,4},{9,5},{1... | collective-permute-start | bytes 983048 | tf_op jit(solution)/shard_map/ppermute | solution.py:213
  57.0 0.7 collective-permute-done.6.refs_0_
  57.7 0.1 fusion.8
  57.8 0.1 collective-permute-start.12
  57.9 4.3 %project.6 = (bf16[2,320,512]{2,1,0:T(8,128)(2,1)S(1)}, bf16[2,320,512]{2,1,0:T(8,128)(2,1)S(1)}, bf16[1,320,512]{2,1,0:T(8,128)(2,1)S(1)}, bf16[1,320,512]{2,1,0:T(8,128)(2,1)S(1)}) custom-call(s32[8]{0:T(128)S(1)} %fusion.21.cols_ref, bf16[1024,512]{1,0:T(8,128)(2,1)S(1)} %gated.1.g_ref, bf16[1024,512]{1,0:T(8,128)(2,1)S(1)} %collective-permute-done.4.gp_ref, ...), custom_call_target="tpu_custom_call" | custom-call | tf_op jit(solution)/shard_map/project/pallas_call | solution.py:275
  62.2 2.5 %collective-permute-done.10 = bf16[320,512]{1,0:T(8,128)(2,1)S(1)} collective-permute-done((bf16[320,512]{1,0:T(8,128)(2,1)S(1)}, bf16[320,512]{1,0:T(8,128)(2,1)S(1)}, u32[]{:S(2)}, u32[]{:S(2)}) %collective-permute-start.10) | collective-permute-done | bytes 327712 | tf_op jit(solution)/shard_map/ppermute | solution.py:213
  64.7 0.0 collective-permute-start.8
  64.7 0.0 collective-permute-done.11
  64.7 3.2 %collective-permute-start.9 = (bf16[2,320,512]{2,1,0:T(8,128)(2,1)S(1)}, bf16[2,320,512]{2,1,0:T(8,128)(2,1)S(1)}, u32[]{:S(2)}, u32[]{:S(2)}) collective-permute-start(bf16[2,320,512]{2,1,0:T(8,128)(2,1)S(1)} %get-tuple-element.32), channel_id=1, source_target_pairs={{0,12},{1,13},{2,14},{3,15},{4,0},{5,1},{6,2},{7,3},{8,4},{9,5},{1... | collective-permute-start | bytes 1966088 | tf_op jit(solution)/shard_map/ppermute | solution.py:213
  67.9 4.1 %project.8 = bf16[4,384,512]{2,1,0:T(8,128)(2,1)S(1)} custom-call(s32[8]{0:T(128)S(1)} %fusion.21.cols_ref, bf16[1024,512]{1,0:T(8,128)(2,1)S(1)} %gated.1.g_ref, bf16[1024,512]{1,0:T(8,128)(2,1)S(1)} %collective-permute-done.4.gp_ref, bf16[512,8192]{1,0:T(8,128)(2,1)} %w_ref.9, bf16[512,8192]{1,0:T(8,128)(2,1)} %collective-permute-done.5.wp_ref), custom_call_target="tpu_custom_call" | custom-call | tf_op jit(solution)/shard_map/project/pallas_call | solution.py:275
  72.1 0.0 collective-permute-done.13
  72.1 0.0 collective-permute-done.12
  72.1 0.3 fusion.12
  72.4 0.1 pad_maximum_fusion.1
  72.4 3.9 %collective-permute-start.14 = (bf16[2,320,512]{2,1,0:T(8,128)(2,1)S(1)}, bf16[2,320,512]{2,1,0:T(8,128)(2,1)S(1)}, u32[]{:S(2)}, u32[]{:S(2)}) collective-permute-start(bf16[2,320,512]{2,1,0:T(8,128)(2,1)S(1)} %pad_maximum_fusion.1), channel_id=1, source_target_pairs={{0,2},{1,3},{2,0},{3,1},{4,6},{5,7},{6,4},{7,5},{8,10},{9,11},{10,... | collective-permute-start | bytes 1966088 | tf_op jit(solution)/shard_map/ppermute | solution.py:213
  76.3 5.8 %collective-permute-done.15 = bf16[4,384,512]{2,1,0:T(8,128)(2,1)S(1)} collective-permute-done((bf16[4,384,512]{2,1,0:T(8,128)(2,1)S(1)}, bf16[4,384,512]{2,1,0:T(8,128)(2,1)S(1)}, u32[]{:S(2)}, u32[]{:S(2)}) %collective-permute-start.15) | collective-permute-done | bytes 1572896 | tf_op jit(solution)/shard_map/ppermute | solution.py:213
  82.1 0.1 fusion.14
  82.2 0.7 collective-permute-start.16
  82.9 2.7 %collective-permute-start.18 = (bf16[192,512]{1,0:T(8,128)(2,1)S(1)}, bf16[192,512]{1,0:T(8,128)(2,1)S(1)}, u32[]{:S(2)}, u32[]{:S(2)}) collective-permute-start(bf16[192,512]{1,0:T(8,128)(2,1)S(1)} %get-tuple-element.50), channel_id=1, source_target_pairs={{0,12},{1,13},{2,14},{3,15},{4,0},{5,1},{6,2},{7,3},{8,4},{9,5},{1... | collective-permute-start | bytes 589832 | tf_op jit(solution)/shard_map/ppermute | solution.py:213
  85.6 3.6 %collective-permute-done.16 = bf16[192,512]{1,0:T(8,128)(2,1)S(1)} collective-permute-done((bf16[192,512]{1,0:T(8,128)(2,1)S(1)}, bf16[192,512]{1,0:T(8,128)(2,1)S(1)}, u32[]{:S(2)}, u32[]{:S(2)}) %collective-permute-start.16) | collective-permute-done | bytes 196640 | tf_op jit(solution)/shard_map/ppermute | solution.py:213
  89.2 0.0 collective-permute-done.18
  89.2 0.3 fusion.1
  89.5 1.5 %collective-permute-start.17 = (bf16[384,512]{1,0:T(8,128)(2,1)S(1)}, bf16[384,512]{1,0:T(8,128)(2,1)S(1)}, u32[]{:S(2)}, u32[]{:S(2)}) collective-permute-start(bf16[384,512]{1,0:T(8,128)(2,1)S(1)} %get-tuple-element.47), channel_id=1, source_target_pairs={{0,4},{1,5},{2,6},{3,7},{4,8},{5,9},{6,10},{7,11},{8,12},{9,13},{1... | collective-permute-start | bytes 1179656 | tf_op jit(solution)/shard_map/ppermute | solution.py:213
  91.0 2.0 %collective-permute-start.19 = (bf16[384,512]{1,0:T(8,128)(2,1)S(1)}, bf16[384,512]{1,0:T(8,128)(2,1)S(1)}, u32[]{:S(2)}, u32[]{:S(2)}) collective-permute-start(bf16[384,512]{1,0:T(8,128)(2,1)S(1)} %get-tuple-element.48), channel_id=1, source_target_pairs={{0,12},{1,13},{2,14},{3,15},{4,0},{5,1},{6,2},{7,3},{8,4},{9,5},{1... | collective-permute-start | bytes 1179656 | tf_op jit(solution)/shard_map/ppermute | solution.py:213
  92.9 0.0 collective-permute-done.8
  93.0 0.0 collective-permute-done.9
  93.0 2.4 %collective-permute-done.14 = bf16[2,320,512]{2,1,0:T(8,128)(2,1)S(1)} collective-permute-done((bf16[2,320,512]{2,1,0:T(8,128)(2,1)S(1)}, bf16[2,320,512]{2,1,0:T(8,128)(2,1)S(1)}, u32[]{:S(2)}, u32[]{:S(2)}) %collective-permute-start.14) | collective-permute-done | bytes 655392 | tf_op jit(solution)/shard_map/ppermute | solution.py:213
  95.3 0.4 fusion.10
  95.7 3.8 %collective-permute-done.17 = bf16[384,512]{1,0:T(8,128)(2,1)S(1)} collective-permute-done((bf16[384,512]{1,0:T(8,128)(2,1)S(1)}, bf16[384,512]{1,0:T(8,128)(2,1)S(1)}, u32[]{:S(2)}, u32[]{:S(2)}) %collective-permute-start.17) | collective-permute-done | bytes 393248 | tf_op jit(solution)/shard_map/ppermute | solution.py:213
  99.5 0.0 collective-permute-done.19
  99.5 0.2 fusion.3
  99.7 1.0 %pad_maximum_fusion = bf16[1024,512]{1,0:T(8,128)(2,1)} fusion(bf16[384,512]{1,0:T(8,128)(2,1)S(1)} %fusion.3, bf16[320,512]{1,0:T(8,128)(2,1)S(1)} %get-tuple-element.52, bf16[320,512]{1,0:T(8,128)(2,1)S(1)} %get-tuple-element.51), kind=kLoop, calls=%fused_computation | loop fusion | flops 3145728 | bytes 2097152 | tf_op jit(solution)/shard_map/concatenate | solution.py:344
  (2 shorter events, 0.0 us)
Async XLA Ops:
  0.0 32.3 %collective-permute-start.5 = (bf16[512,8192]{1,0:T(8,128)(2,1)}, bf16[512,8192]{1,0:T(8,128)(2,1)}, u32[]{:S(2)}, u32[]{:S(2)}) collective-permute-start(bf16[512,8192]{1,0:T(8,128)(2,1)} %w_ref.9), channel_id=1, source_target_pairs={{0,1},{1,0},{2,3},{3,2},{4,5},{5,4},{6,7},{7,6},{8,9},{9,8},{10,11... | collective-permute-start | bytes 25165832 | tf_op jit(solution)/shard_map/ppermute | solution.py:213
  0.0 20.1 %copy-start.1 = (f32[16,512]{1,0:T(8,128)S(1)}, f32[16,512]{1,0:T(8,128)}, u32[]{:S(2)}) copy-start(f32[16,512]{1,0:T(8,128)} %rate_ref.3) | copy-start | bytes 98308
  0.0 20.1 %copy-start.2 = (f32[3,3,512]{2,1,0:T(4,128)S(1)}, f32[3,3,512]{2,1,0:T(4,128)}, u32[]{:S(2)}) copy-start(f32[3,3,512]{2,1,0:T(4,128)} %sf_ref.3) | copy-start | bytes 55300
  0.0 20.1 %copy-start.3 = (f32[16,512]{1,0:T(8,128)S(1)}, f32[16,512]{1,0:T(8,128)}, u32[]{:S(2)}) copy-start(f32[16,512]{1,0:T(8,128)} %res_ref.1) | copy-start | bytes 98308
  6.5 4.3 %collective-permute-start = (bf16[32,512]{1,0:T(8,128)(2,1)}, bf16[32,512]{1,0:T(8,128)(2,1)S(1)}, u32[]{:S(2)}, u32[]{:S(2)}) collective-permute-start(bf16[32,512]{1,0:T(8,128)(2,1)} %get-tuple-element.27), channel_id=1, source_target_pairs={{0,64},{16,80},{32,96},{48,112},{64,0},{80,16},{96,32},{112,48},{1... | collective-permute-start | bytes 98312 | tf_op jit(solution)/shard_map/ppermute | solution.py:213
  11.6 6.1 %collective-permute-start.1 = (bf16[2,32,512]{2,1,0:T(8,128)(2,1)S(1)}, bf16[2,32,512]{2,1,0:T(8,128)(2,1)S(1)}, u32[]{:S(2)}, u32[]{:S(2)}) collective-permute-start(bf16[2,32,512]{2,1,0:T(8,128)(2,1)S(1)} %pad_maximum_fusion.2.refs_0_), channel_id=1, source_target_pairs={{0,16},{16,32},{32,48},{48,0},{64,80},{80,96},{96,112},{112,64},{1... | collective-permute-start | bytes 196616 | tf_op jit(solution)/shard_map/ppermute | solution.py:213
  13.1 5.9 %collective-permute-start.2 = (bf16[2,32,512]{2,1,0:T(8,128)(2,1)S(1)}, bf16[2,32,512]{2,1,0:T(8,128)(2,1)S(1)}, u32[]{:S(2)}, u32[]{:S(2)}) collective-permute-start(bf16[2,32,512]{2,1,0:T(8,128)(2,1)S(1)} %pad_maximum_fusion.2.refs_0_), channel_id=1, source_target_pairs={{0,32},{16,48},{32,0},{48,16},{64,96},{80,112},{96,64},{112,80},{1... | collective-permute-start | bytes 196616 | tf_op jit(solution)/shard_map/ppermute | solution.py:213
  15.8 4.3 %collective-permute-start.3 = (bf16[2,32,512]{2,1,0:T(8,128)(2,1)S(1)}, bf16[2,32,512]{2,1,0:T(8,128)(2,1)S(1)}, u32[]{:S(2)}, u32[]{:S(2)}) collective-permute-start(bf16[2,32,512]{2,1,0:T(8,128)(2,1)S(1)} %pad_maximum_fusion.2.refs_0_), channel_id=1, source_target_pairs={{0,48},{16,0},{32,16},{48,32},{64,112},{80,64},{96,80},{112,96},{1... | collective-permute-start | bytes 196616 | tf_op jit(solution)/shard_map/ppermute | solution.py:213
  20.1 1.7 %copy-start = (f32[144,8,512]{2,1,0:T(8,128)S(1)}, f32[144,8,512]{2,1,0:T(8,128)}, u32[]{:S(2)}) copy-start(f32[144,8,512]{2,1,0:T(8,128)} %get-tuple-element.26.p_ref) | copy-start | bytes 7077892
  29.6 2.7 %collective-permute-start.4 = (bf16[1024,512]{1,0:T(8,128)(2,1)S(1)}, bf16[1024,512]{1,0:T(8,128)(2,1)S(1)}, u32[]{:S(2)}, u32[]{:S(2)}) collective-permute-start(bf16[1024,512]{1,0:T(8,128)(2,1)S(1)} %gated.1.g_ref), channel_id=1, source_target_pairs={{0,1},{1,0},{2,3},{3,2},{4,5},{5,4},{6,7},{7,6},{8,9},{9,8},{10,11... | collective-permute-start | bytes 3145736 | tf_op jit(solution)/shard_map/ppermute | solution.py:213
  35.8 18.8 %collective-permute-start.7 = (bf16[2,320,512]{2,1,0:T(8,128)(2,1)S(1)}, bf16[2,320,512]{2,1,0:T(8,128)(2,1)S(1)}, u32[]{:S(2)}, u32[]{:S(2)}) collective-permute-start(bf16[2,320,512]{2,1,0:T(8,128)(2,1)S(1)} %get-tuple-element.29), channel_id=1, source_target_pairs={{0,12},{1,13},{2,14},{3,15},{4,0},{5,1},{6,2},{7,3},{8,4},{9,5},{1... | collective-permute-start | bytes 1966088 | tf_op jit(solution)/shard_map/ppermute | solution.py:213
  38.9 18.8 %collective-permute-start.6 = (bf16[2,320,512]{2,1,0:T(8,128)(2,1)S(1)}, bf16[2,320,512]{2,1,0:T(8,128)(2,1)S(1)}, u32[]{:S(2)}, u32[]{:S(2)}) collective-permute-start(bf16[2,320,512]{2,1,0:T(8,128)(2,1)S(1)} %get-tuple-element.28), channel_id=1, source_target_pairs={{0,4},{1,5},{2,6},{3,7},{4,8},{5,9},{6,10},{7,11},{8,12},{9,13},{1... | collective-permute-start | bytes 1966088 | tf_op jit(solution)/shard_map/ppermute | solution.py:213
  43.0 39.1 %collective-permute-start.15 = (bf16[4,384,512]{2,1,0:T(8,128)(2,1)S(1)}, bf16[4,384,512]{2,1,0:T(8,128)(2,1)S(1)}, u32[]{:S(2)}, u32[]{:S(2)}) collective-permute-start(bf16[4,384,512]{2,1,0:T(8,128)(2,1)S(1)} %project.9), channel_id=1, source_target_pairs={{0,2},{1,3},{2,0},{3,1},{4,6},{5,7},{6,4},{7,5},{8,10},{9,11},{10,... | collective-permute-start | bytes 4718600 | tf_op jit(solution)/shard_map/ppermute | solution.py:213
  51.2 13.5 %collective-permute-start.10 = (bf16[320,512]{1,0:T(8,128)(2,1)S(1)}, bf16[320,512]{1,0:T(8,128)(2,1)S(1)}, u32[]{:S(2)}, u32[]{:S(2)}) collective-permute-start(bf16[320,512]{1,0:T(8,128)(2,1)S(1)} %bitcast.43), channel_id=1, source_target_pairs={{0,4},{1,5},{2,6},{3,7},{4,8},{5,9},{6,10},{7,11},{8,12},{9,13},{1... | collective-permute-start | bytes 983048 | tf_op jit(solution)/shard_map/ppermute | solution.py:213
  51.9 12.8 %collective-permute-start.11 = (bf16[320,512]{1,0:T(8,128)(2,1)S(1)}, bf16[320,512]{1,0:T(8,128)(2,1)S(1)}, u32[]{:S(2)}, u32[]{:S(2)}) collective-permute-start(bf16[320,512]{1,0:T(8,128)(2,1)S(1)} %bitcast.42), channel_id=1, source_target_pairs={{0,12},{1,13},{2,14},{3,15},{4,0},{5,1},{6,2},{7,3},{8,4},{9,5},{1... | collective-permute-start | bytes 983048 | tf_op jit(solution)/shard_map/ppermute | solution.py:213
  54.7 17.4 %collective-permute-start.13 = (bf16[320,512]{1,0:T(8,128)(2,1)S(1)}, bf16[320,512]{1,0:T(8,128)(2,1)S(1)}, u32[]{:S(2)}, u32[]{:S(2)}) collective-permute-start(bf16[320,512]{1,0:T(8,128)(2,1)S(1)} %fusion.9), channel_id=1, source_target_pairs={{0,12},{1,13},{2,14},{3,15},{4,0},{5,1},{6,2},{7,3},{8,4},{9,5},{1... | collective-permute-start | bytes 983048 | tf_op jit(solution)/shard_map/ppermute | solution.py:213
  57.8 14.3 %collective-permute-start.12 = (bf16[320,512]{1,0:T(8,128)(2,1)S(1)}, bf16[320,512]{1,0:T(8,128)(2,1)S(1)}, u32[]{:S(2)}, u32[]{:S(2)}) collective-permute-start(bf16[320,512]{1,0:T(8,128)(2,1)S(1)} %fusion.8), channel_id=1, source_target_pairs={{0,4},{1,5},{2,6},{3,7},{4,8},{5,9},{6,10},{7,11},{8,12},{9,13},{1... | collective-permute-start | bytes 983048 | tf_op jit(solution)/shard_map/ppermute | solution.py:213
  64.7 28.2 %collective-permute-start.8 = (bf16[2,320,512]{2,1,0:T(8,128)(2,1)S(1)}, bf16[2,320,512]{2,1,0:T(8,128)(2,1)S(1)}, u32[]{:S(2)}, u32[]{:S(2)}) collective-permute-start(bf16[2,320,512]{2,1,0:T(8,128)(2,1)S(1)} %get-tuple-element.31), channel_id=1, source_target_pairs={{0,4},{1,5},{2,6},{3,7},{4,8},{5,9},{6,10},{7,11},{8,12},{9,13},{1... | collective-permute-start | bytes 1966088 | tf_op jit(solution)/shard_map/ppermute | solution.py:213
  64.7 28.2 %collective-permute-start.9 = (bf16[2,320,512]{2,1,0:T(8,128)(2,1)S(1)}, bf16[2,320,512]{2,1,0:T(8,128)(2,1)S(1)}, u32[]{:S(2)}, u32[]{:S(2)}) collective-permute-start(bf16[2,320,512]{2,1,0:T(8,128)(2,1)S(1)} %get-tuple-element.32), channel_id=1, source_target_pairs={{0,12},{1,13},{2,14},{3,15},{4,0},{5,1},{6,2},{7,3},{8,4},{9,5},{1... | collective-permute-start | bytes 1966088 | tf_op jit(solution)/shard_map/ppermute | solution.py:213
  72.4 22.9 %collective-permute-start.14 = (bf16[2,320,512]{2,1,0:T(8,128)(2,1)S(1)}, bf16[2,320,512]{2,1,0:T(8,128)(2,1)S(1)}, u32[]{:S(2)}, u32[]{:S(2)}) collective-permute-start(bf16[2,320,512]{2,1,0:T(8,128)(2,1)S(1)} %pad_maximum_fusion.1), channel_id=1, source_target_pairs={{0,2},{1,3},{2,0},{3,1},{4,6},{5,7},{6,4},{7,5},{8,10},{9,11},{10,... | collective-permute-start | bytes 1966088 | tf_op jit(solution)/shard_map/ppermute | solution.py:213
  82.2 7.0 %collective-permute-start.16 = (bf16[192,512]{1,0:T(8,128)(2,1)S(1)}, bf16[192,512]{1,0:T(8,128)(2,1)S(1)}, u32[]{:S(2)}, u32[]{:S(2)}) collective-permute-start(bf16[192,512]{1,0:T(8,128)(2,1)S(1)} %get-tuple-element.49), channel_id=1, source_target_pairs={{0,4},{1,5},{2,6},{3,7},{4,8},{5,9},{6,10},{7,11},{8,12},{9,13},{1... | collective-permute-start | bytes 589832 | tf_op jit(solution)/shard_map/ppermute | solution.py:213
  82.9 6.3 %collective-permute-start.18 = (bf16[192,512]{1,0:T(8,128)(2,1)S(1)}, bf16[192,512]{1,0:T(8,128)(2,1)S(1)}, u32[]{:S(2)}, u32[]{:S(2)}) collective-permute-start(bf16[192,512]{1,0:T(8,128)(2,1)S(1)} %get-tuple-element.50), channel_id=1, source_target_pairs={{0,12},{1,13},{2,14},{3,15},{4,0},{5,1},{6,2},{7,3},{8,4},{9,5},{1... | collective-permute-start | bytes 589832 | tf_op jit(solution)/shard_map/ppermute | solution.py:213
  89.5 10.0 %collective-permute-start.17 = (bf16[384,512]{1,0:T(8,128)(2,1)S(1)}, bf16[384,512]{1,0:T(8,128)(2,1)S(1)}, u32[]{:S(2)}, u32[]{:S(2)}) collective-permute-start(bf16[384,512]{1,0:T(8,128)(2,1)S(1)} %get-tuple-element.47), channel_id=1, source_target_pairs={{0,4},{1,5},{2,6},{3,7},{4,8},{5,9},{6,10},{7,11},{8,12},{9,13},{1... | collective-permute-start | bytes 1179656 | tf_op jit(solution)/shard_map/ppermute | solution.py:213
  91.0 8.5 %collective-permute-start.19 = (bf16[384,512]{1,0:T(8,128)(2,1)S(1)}, bf16[384,512]{1,0:T(8,128)(2,1)S(1)}, u32[]{:S(2)}, u32[]{:S(2)}) collective-permute-start(bf16[384,512]{1,0:T(8,128)(2,1)S(1)} %get-tuple-element.48), channel_id=1, source_target_pairs={{0,12},{1,13},{2,14},{3,15},{4,0},{5,1},{6,2},{7,3},{8,4},{9,5},{1... | collective-permute-start | bytes 1179656 | tf_op jit(solution)/shard_map/ppermute | solution.py:213

commit v13 on v12

--- a/solution.py
+++ b/solution.py
@@ -203,7 +203,7 @@
             pltpu.VMEM((n_tok + SUBS * PAD, LANES), f32),
             pltpu.VMEM((2 * len(told) + 1, PAYLOAD, LANES), f32),
         ],
-        compiler_params=pltpu.CompilerParams(vmem_limit_bytes=48 << 20),
+        compiler_params=pltpu.CompilerParams(vmem_limit_bytes=52 << 20),
         name="gated",
     )(at, x, sf, rate, res, p, *told)
 

time: 101 us -> 99.5 us (0.985)
  local copies, waits for them, and re-layouts: 1.67 us -> 0.01 us
    unnamed x8 -> x6, local copies, waits for them, and re-layouts: 1.67 us -> 0.01 us
  transfers between devices with their start and end apart: 20 -> 20, of which waited for: 11 -> 11; matrix products, arithmetic and copies ran while one was open for 2% -> 2% of each run, Pallas kernels for 31% -> 32%
where the time goes in v13:
time: 99.5 us; the launch traced here: 99.2 us
  Pallas kernels  34.8 us (35%)
  starting transfers between devices  34.5 us (35%)
  waiting for transfers between devices  26.4 us (27%)
  other arithmetic  3.26 us (3%)
    ppermute x20, starting transfers between devices, spread(): return lax.ppermute(x, axis, [(i, j) for i, j in pairs if j is not None])  34.5 us
    ppermute x20, waiting for transfers between devices, spread(): return lax.ppermute(x, axis, [(i, j) for i, j in pairs if j is not None])  26.4 us
    pallas_call x5, Pallas kernels, project(): pl.pallas_call(functools.partial(project_kernel, laid, len(added)), in_sp...  20.4 us
    pallas_call x1, Pallas kernels, gated(): pl.pallas_call(gate_kernel, grid=(width // LANES,), in_specs=[pl.BlockSpe...  7.94 us
    pallas_call x1, Pallas kernels, states(): pl.pallas_call(state_kernel, grid=(width // LANES,), in_specs=[pl.BlockSp...  6.54 us
  transfers between devices with their start and end apart: 20, of which 11 were waited for; matrix products, arithmetic and copies ran while one was open for 2% of the time, Pallas kernels for 32%

profile of v13, /device:TPU:0, one launch (start us, length us, event | category | flops | bytes accessed | tf_op | source)
XLA Modules:
  0.0 99.2 jit_solution(5337720470522679365)
XLA Ops:
  0.0 0.0 collective-permute-start.5
  0.0 0.0 copy-start
  0.0 0.0 copy-start.1
  0.0 0.0 copy-start.2
  0.0 6.5 %states.1 = (f32[144,8,512]{2,1,0:T(8,128)}, bf16[32,512]{1,0:T(8,128)(2,1)}) custom-call(bf16[3,1024,512]{2,1,0:T(8,128)(2,1)} %bitcast.44, bf16[3,1024,512]{2,1,0:T(8,128)(2,1)} %bitcast.45, bf16[3,1024,512]{2,1,0:T(8,128)(2,1)} %bitcast.46, f32[3,3,512]{2,1,0:T(4,128)} %sf_ref.3, f32[16,512]{1,0:T(8,128)} %rate_ref.3), custom_call_target="tpu_custom_call" | custom-call | tf_op jit(solution)/shard_map/states/pallas_call | solution.py:157
  6.5 2.0 %collective-permute-start = (bf16[32,512]{1,0:T(8,128)(2,1)}, bf16[32,512]{1,0:T(8,128)(2,1)S(1)}, u32[]{:S(2)}, u32[]{:S(2)}) collective-permute-start(bf16[32,512]{1,0:T(8,128)(2,1)} %get-tuple-element.27), channel_id=1, source_target_pairs={{0,64},{16,80},{32,96},{48,112},{64,0},{80,16},{96,32},{112,48},{1... | collective-permute-start | bytes 98312 | tf_op jit(solution)/shard_map/ppermute | solution.py:213
  8.5 2.3 %collective-permute-done = bf16[32,512]{1,0:T(8,128)(2,1)S(1)} collective-permute-done((bf16[32,512]{1,0:T(8,128)(2,1)}, bf16[32,512]{1,0:T(8,128)(2,1)S(1)}, u32[]{:S(2)}, u32[]{:S(2)}) %collective-permute-start) | collective-permute-done | bytes 32800 | tf_op jit(solution)/shard_map/ppermute | solution.py:213
  10.8 0.8 pad_maximum_fusion.2.refs_0_
  11.6 1.5 %collective-permute-start.1 = (bf16[2,32,512]{2,1,0:T(8,128)(2,1)S(1)}, bf16[2,32,512]{2,1,0:T(8,128)(2,1)S(1)}, u32[]{:S(2)}, u32[]{:S(2)}) collective-permute-start(bf16[2,32,512]{2,1,0:T(8,128)(2,1)S(1)} %pad_maximum_fusion.2.refs_0_), channel_id=1, source_target_pairs={{0,16},{16,32},{32,48},{48,0},{64,80},{80,96},{96,112},{112,64},{1... | collective-permute-start | bytes 196616 | tf_op jit(solution)/shard_map/ppermute | solution.py:213
  13.1 2.7 %collective-permute-start.2 = (bf16[2,32,512]{2,1,0:T(8,128)(2,1)S(1)}, bf16[2,32,512]{2,1,0:T(8,128)(2,1)S(1)}, u32[]{:S(2)}, u32[]{:S(2)}) collective-permute-start(bf16[2,32,512]{2,1,0:T(8,128)(2,1)S(1)} %pad_maximum_fusion.2.refs_0_), channel_id=1, source_target_pairs={{0,32},{16,48},{32,0},{48,16},{64,96},{80,112},{96,64},{112,80},{1... | collective-permute-start | bytes 196616 | tf_op jit(solution)/shard_map/ppermute | solution.py:213
  15.8 1.4 %collective-permute-start.3 = (bf16[2,32,512]{2,1,0:T(8,128)(2,1)S(1)}, bf16[2,32,512]{2,1,0:T(8,128)(2,1)S(1)}, u32[]{:S(2)}, u32[]{:S(2)}) collective-permute-start(bf16[2,32,512]{2,1,0:T(8,128)(2,1)S(1)} %pad_maximum_fusion.2.refs_0_), channel_id=1, source_target_pairs={{0,48},{16,0},{32,16},{48,32},{64,112},{80,64},{96,80},{112,96},{1... | collective-permute-start | bytes 196616 | tf_op jit(solution)/shard_map/ppermute | solution.py:213
  17.2 0.4 collective-permute-done.1.refs_1_
  17.7 1.3 %collective-permute-done.2.refs_2_ = bf16[2,32,512]{2,1,0:T(8,128)(2,1)S(1)} collective-permute-done((bf16[2,32,512]{2,1,0:T(8,128)(2,1)S(1)}, bf16[2,32,512]{2,1,0:T(8,128)(2,1)S(1)}, u32[]{:S(2)}, u32[]{:S(2)}) %collective-permute-start.2) | collective-permute-done | bytes 65568 | tf_op jit(solution)/shard_map/ppermute | solution.py:213
  19.0 1.1 %collective-permute-done.3.refs_3_ = bf16[2,32,512]{2,1,0:T(8,128)(2,1)S(1)} collective-permute-done((bf16[2,32,512]{2,1,0:T(8,128)(2,1)S(1)}, bf16[2,32,512]{2,1,0:T(8,128)(2,1)S(1)}, u32[]{:S(2)}, u32[]{:S(2)}) %collective-permute-start.3) | collective-permute-done | bytes 65568 | tf_op jit(solution)/shard_map/ppermute | solution.py:213
  20.1 0.0 copy-done
  20.1 0.0 copy-done.1
  20.1 0.0 copy-done.2
  20.1 7.9 %gated.1.g_ref = bf16[1024,512]{1,0:T(8,128)(2,1)S(1)} custom-call(s32[1]{0:T(128)} %bitcast.at_ref, bf16[3,1024,512]{2,1,0:T(8,128)(2,1)} %bitcast.47, f32[3,3,512]{2,1,0:T(4,128)S(1)} %copy-done.1, f32[16,512]{1,0:T(8,128)S(1)} %copy-done, f32[16,512]{1,0:T(8,128)S(1)} %copy-done.2, f32[144,8,512]{2,1,0:T(8,128)} %get-tuple-element.26.p_ref, ...), custom_call_target="tpu_custom_call" | custom-call | tf_op jit(solution)/shard_map/gated/pallas_call | solution.py:187
  28.0 0.1 collective-permute-start.4
  28.2 2.6 %collective-permute-done.4.gp_ref = bf16[1024,512]{1,0:T(8,128)(2,1)S(1)} collective-permute-done((bf16[1024,512]{1,0:T(8,128)(2,1)S(1)}, bf16[1024,512]{1,0:T(8,128)(2,1)S(1)}, u32[]{:S(2)}, u32[]{:S(2)}) %collective-permute-start.4) | collective-permute-done | bytes 1048608 | tf_op jit(solution)/shard_map/ppermute | solution.py:213
  30.8 0.0 collective-permute-done.5.wp_ref
  30.8 3.5 %project.5 = (bf16[2,320,512]{2,1,0:T(8,128)(2,1)S(1)}, bf16[2,320,512]{2,1,0:T(8,128)(2,1)S(1)}) custom-call(s32[8]{0:T(128)S(1)} %fusion.21.cols_ref, bf16[1024,512]{1,0:T(8,128)(2,1)S(1)} %gated.1.g_ref, bf16[1024,512]{1,0:T(8,128)(2,1)S(1)} %collective-permute-done.4.gp_ref, bf16[512,8192]{1,0:T(8,128)(2,1)} %w_ref.9, ...), custom_call_target="tpu_custom_call" | custom-call | tf_op jit(solution)/shard_map/project/pallas_call | solution.py:275
  34.3 3.1 %collective-permute-start.7 = (bf16[2,320,512]{2,1,0:T(8,128)(2,1)S(1)}, bf16[2,320,512]{2,1,0:T(8,128)(2,1)S(1)}, u32[]{:S(2)}, u32[]{:S(2)}) collective-permute-start(bf16[2,320,512]{2,1,0:T(8,128)(2,1)S(1)} %get-tuple-element.29), channel_id=1, source_target_pairs={{0,12},{1,13},{2,14},{3,15},{4,0},{5,1},{6,2},{7,3},{8,4},{9,5},{1... | collective-permute-start | bytes 1966088 | tf_op jit(solution)/shard_map/ppermute | solution.py:213
  37.3 0.0 collective-permute-start.6
  37.3 4.1 %project.9 = bf16[4,384,512]{2,1,0:T(8,128)(2,1)S(1)} custom-call(s32[8]{0:T(128)S(1)} %fusion.21.cols_ref, bf16[1024,512]{1,0:T(8,128)(2,1)S(1)} %gated.1.g_ref, bf16[1024,512]{1,0:T(8,128)(2,1)S(1)} %collective-permute-done.4.gp_ref, bf16[512,8192]{1,0:T(8,128)(2,1)} %w_ref.9, bf16[512,8192]{1,0:T(8,128)(2,1)} %collective-permute-done.5.wp_ref), custom_call_target="tpu_custom_call" | custom-call | tf_op jit(solution)/shard_map/project/pallas_call | solution.py:275
  41.5 3.9 %collective-permute-start.15 = (bf16[4,384,512]{2,1,0:T(8,128)(2,1)S(1)}, bf16[4,384,512]{2,1,0:T(8,128)(2,1)S(1)}, u32[]{:S(2)}, u32[]{:S(2)}) collective-permute-start(bf16[4,384,512]{2,1,0:T(8,128)(2,1)S(1)} %project.9), channel_id=1, source_target_pairs={{0,2},{1,3},{2,0},{3,1},{4,6},{5,7},{6,4},{7,5},{8,10},{9,11},{10,... | collective-permute-start | bytes 4718600 | tf_op jit(solution)/shard_map/ppermute | solution.py:213
  45.4 4.3 %project.7 = (bf16[1,320,512]{2,1,0:T(8,128)(2,1)S(1)}, bf16[1,320,512]{2,1,0:T(8,128)(2,1)S(1)}, bf16[1,320,512]{2,1,0:T(8,128)(2,1)S(1)}, bf16[1,320,512]{2,1,...) custom-call(s32[8]{0:T(128)S(1)} %fusion.21.cols_ref, ...), custom_call_target="tpu_custom_call" | custom-call | tf_op jit(solution)/shard_map/project/pallas_call | solution.py:275
  49.7 0.7 collective-permute-start.10
  50.4 2.7 %collective-permute-start.11 = (bf16[320,512]{1,0:T(8,128)(2,1)S(1)}, bf16[320,512]{1,0:T(8,128)(2,1)S(1)}, u32[]{:S(2)}, u32[]{:S(2)}) collective-permute-start(bf16[320,512]{1,0:T(8,128)(2,1)S(1)} %bitcast.42), channel_id=1, source_target_pairs={{0,12},{1,13},{2,14},{3,15},{4,0},{5,1},{6,2},{7,3},{8,4},{9,5},{1... | collective-permute-start | bytes 983048 | tf_op jit(solution)/shard_map/ppermute | solution.py:213
  53.1 0.0 collective-permute-done.7.refs_1_
  53.1 0.1 fusion.9
  53.2 2.3 %collective-permute-start.13 = (bf16[320,512]{1,0:T(8,128)(2,1)S(1)}, bf16[320,512]{1,0:T(8,128)(2,1)S(1)}, u32[]{:S(2)}, u32[]{:S(2)}) collective-permute-start(bf16[320,512]{1,0:T(8,128)(2,1)S(1)} %fusion.9), channel_id=1, source_target_pairs={{0,12},{1,13},{2,14},{3,15},{4,0},{5,1},{6,2},{7,3},{8,4},{9,5},{1... | collective-permute-start | bytes 983048 | tf_op jit(solution)/shard_map/ppermute | solution.py:213
  55.5 0.7 collective-permute-done.6.refs_0_
  56.2 0.1 fusion.8
  56.3 0.1 collective-permute-start.12
  56.3 4.3 %project.6 = (bf16[2,320,512]{2,1,0:T(8,128)(2,1)S(1)}, bf16[2,320,512]{2,1,0:T(8,128)(2,1)S(1)}, bf16[1,320,512]{2,1,0:T(8,128)(2,1)S(1)}, bf16[1,320,512]{2,1,0:T(8,128)(2,1)S(1)}) custom-call(s32[8]{0:T(128)S(1)} %fusion.21.cols_ref, bf16[1024,512]{1,0:T(8,128)(2,1)S(1)} %gated.1.g_ref, bf16[1024,512]{1,0:T(8,128)(2,1)S(1)} %collective-permute-done.4.gp_ref, ...), custom_call_target="tpu_custom_call" | custom-call | tf_op jit(solution)/shard_map/project/pallas_call | solution.py:275
  60.7 2.5 %collective-permute-done.10 = bf16[320,512]{1,0:T(8,128)(2,1)S(1)} collective-permute-done((bf16[320,512]{1,0:T(8,128)(2,1)S(1)}, bf16[320,512]{1,0:T(8,128)(2,1)S(1)}, u32[]{:S(2)}, u32[]{:S(2)}) %collective-permute-start.10) | collective-permute-done | bytes 327712 | tf_op jit(solution)/shard_map/ppermute | solution.py:213
  63.2 0.0 collective-permute-start.8
  63.2 0.0 collective-permute-done.11
  63.2 3.2 %collective-permute-start.9 = (bf16[2,320,512]{2,1,0:T(8,128)(2,1)S(1)}, bf16[2,320,512]{2,1,0:T(8,128)(2,1)S(1)}, u32[]{:S(2)}, u32[]{:S(2)}) collective-permute-start(bf16[2,320,512]{2,1,0:T(8,128)(2,1)S(1)} %get-tuple-element.32), channel_id=1, source_target_pairs={{0,12},{1,13},{2,14},{3,15},{4,0},{5,1},{6,2},{7,3},{8,4},{9,5},{1... | collective-permute-start | bytes 1966088 | tf_op jit(solution)/shard_map/ppermute | solution.py:213
  66.4 4.1 %project.8 = bf16[4,384,512]{2,1,0:T(8,128)(2,1)S(1)} custom-call(s32[8]{0:T(128)S(1)} %fusion.21.cols_ref, bf16[1024,512]{1,0:T(8,128)(2,1)S(1)} %gated.1.g_ref, bf16[1024,512]{1,0:T(8,128)(2,1)S(1)} %collective-permute-done.4.gp_ref, bf16[512,8192]{1,0:T(8,128)(2,1)} %w_ref.9, bf16[512,8192]{1,0:T(8,128)(2,1)} %collective-permute-done.5.wp_ref), custom_call_target="tpu_custom_call" | custom-call | tf_op jit(solution)/shard_map/project/pallas_call | solution.py:275
  70.6 0.0 collective-permute-done.13
  70.6 0.0 collective-permute-done.12
  70.6 0.3 fusion.12
  70.8 0.1 pad_maximum_fusion.1
  70.9 3.9 %collective-permute-start.14 = (bf16[2,320,512]{2,1,0:T(8,128)(2,1)S(1)}, bf16[2,320,512]{2,1,0:T(8,128)(2,1)S(1)}, u32[]{:S(2)}, u32[]{:S(2)}) collective-permute-start(bf16[2,320,512]{2,1,0:T(8,128)(2,1)S(1)} %pad_maximum_fusion.1), channel_id=1, source_target_pairs={{0,2},{1,3},{2,0},{3,1},{4,6},{5,7},{6,4},{7,5},{8,10},{9,11},{10,... | collective-permute-start | bytes 1966088 | tf_op jit(solution)/shard_map/ppermute | solution.py:213
  74.8 5.8 %collective-permute-done.15 = bf16[4,384,512]{2,1,0:T(8,128)(2,1)S(1)} collective-permute-done((bf16[4,384,512]{2,1,0:T(8,128)(2,1)S(1)}, bf16[4,384,512]{2,1,0:T(8,128)(2,1)S(1)}, u32[]{:S(2)}, u32[]{:S(2)}) %collective-permute-start.15) | collective-permute-done | bytes 1572896 | tf_op jit(solution)/shard_map/ppermute | solution.py:213
  80.6 0.1 fusion.14
  80.7 0.7 collective-permute-start.16
  81.4 2.7 %collective-permute-start.18 = (bf16[192,512]{1,0:T(8,128)(2,1)S(1)}, bf16[192,512]{1,0:T(8,128)(2,1)S(1)}, u32[]{:S(2)}, u32[]{:S(2)}) collective-permute-start(bf16[192,512]{1,0:T(8,128)(2,1)S(1)} %get-tuple-element.50), channel_id=1, source_target_pairs={{0,12},{1,13},{2,14},{3,15},{4,0},{5,1},{6,2},{7,3},{8,4},{9,5},{1... | collective-permute-start | bytes 589832 | tf_op jit(solution)/shard_map/ppermute | solution.py:213
  84.1 3.6 %collective-permute-done.16 = bf16[192,512]{1,0:T(8,128)(2,1)S(1)} collective-permute-done((bf16[192,512]{1,0:T(8,128)(2,1)S(1)}, bf16[192,512]{1,0:T(8,128)(2,1)S(1)}, u32[]{:S(2)}, u32[]{:S(2)}) %collective-permute-start.16) | collective-permute-done | bytes 196640 | tf_op jit(solution)/shard_map/ppermute | solution.py:213
  87.7 0.0 collective-permute-done.18
  87.7 0.3 fusion.1
  88.0 1.5 %collective-permute-start.17 = (bf16[384,512]{1,0:T(8,128)(2,1)S(1)}, bf16[384,512]{1,0:T(8,128)(2,1)S(1)}, u32[]{:S(2)}, u32[]{:S(2)}) collective-permute-start(bf16[384,512]{1,0:T(8,128)(2,1)S(1)} %get-tuple-element.47), channel_id=1, source_target_pairs={{0,4},{1,5},{2,6},{3,7},{4,8},{5,9},{6,10},{7,11},{8,12},{9,13},{1... | collective-permute-start | bytes 1179656 | tf_op jit(solution)/shard_map/ppermute | solution.py:213
  89.5 2.0 %collective-permute-start.19 = (bf16[384,512]{1,0:T(8,128)(2,1)S(1)}, bf16[384,512]{1,0:T(8,128)(2,1)S(1)}, u32[]{:S(2)}, u32[]{:S(2)}) collective-permute-start(bf16[384,512]{1,0:T(8,128)(2,1)S(1)} %get-tuple-element.48), channel_id=1, source_target_pairs={{0,12},{1,13},{2,14},{3,15},{4,0},{5,1},{6,2},{7,3},{8,4},{9,5},{1... | collective-permute-start | bytes 1179656 | tf_op jit(solution)/shard_map/ppermute | solution.py:213
  91.4 0.0 collective-permute-done.8
  91.4 0.0 collective-permute-done.9
  91.4 2.4 %collective-permute-done.14 = bf16[2,320,512]{2,1,0:T(8,128)(2,1)S(1)} collective-permute-done((bf16[2,320,512]{2,1,0:T(8,128)(2,1)S(1)}, bf16[2,320,512]{2,1,0:T(8,128)(2,1)S(1)}, u32[]{:S(2)}, u32[]{:S(2)}) %collective-permute-start.14) | collective-permute-done | bytes 655392 | tf_op jit(solution)/shard_map/ppermute | solution.py:213
  93.8 0.4 fusion.10
  94.2 3.8 %collective-permute-done.17 = bf16[384,512]{1,0:T(8,128)(2,1)S(1)} collective-permute-done((bf16[384,512]{1,0:T(8,128)(2,1)S(1)}, bf16[384,512]{1,0:T(8,128)(2,1)S(1)}, u32[]{:S(2)}, u32[]{:S(2)}) %collective-permute-start.17) | collective-permute-done | bytes 393248 | tf_op jit(solution)/shard_map/ppermute | solution.py:213
  97.9 0.0 collective-permute-done.19
  97.9 0.2 fusion.3
  98.2 1.0 %pad_maximum_fusion = bf16[1024,512]{1,0:T(8,128)(2,1)} fusion(bf16[384,512]{1,0:T(8,128)(2,1)S(1)} %fusion.3, bf16[320,512]{1,0:T(8,128)(2,1)S(1)} %get-tuple-element.52, bf16[320,512]{1,0:T(8,128)(2,1)S(1)} %get-tuple-element.51), kind=kLoop, calls=%fused_computation | loop fusion | flops 3145728 | bytes 2097152 | tf_op jit(solution)/shard_map/concatenate | solution.py:344
  (1 shorter events, 0.0 us)
Async XLA Ops:
  0.0 30.8 %collective-permute-start.5 = (bf16[512,8192]{1,0:T(8,128)(2,1)}, bf16[512,8192]{1,0:T(8,128)(2,1)}, u32[]{:S(2)}, u32[]{:S(2)}) collective-permute-start(bf16[512,8192]{1,0:T(8,128)(2,1)} %w_ref.9), channel_id=1, source_target_pairs={{0,1},{1,0},{2,3},{3,2},{4,5},{5,4},{6,7},{7,6},{8,9},{9,8},{10,11... | collective-permute-start | bytes 25165832 | tf_op jit(solution)/shard_map/ppermute | solution.py:213
  0.0 20.1 %copy-start = (f32[16,512]{1,0:T(8,128)S(1)}, f32[16,512]{1,0:T(8,128)}, u32[]{:S(2)}) copy-start(f32[16,512]{1,0:T(8,128)} %rate_ref.3) | copy-start | bytes 98308
  0.0 20.1 %copy-start.1 = (f32[3,3,512]{2,1,0:T(4,128)S(1)}, f32[3,3,512]{2,1,0:T(4,128)}, u32[]{:S(2)}) copy-start(f32[3,3,512]{2,1,0:T(4,128)} %sf_ref.3) | copy-start | bytes 55300
  0.0 20.1 %copy-start.2 = (f32[16,512]{1,0:T(8,128)S(1)}, f32[16,512]{1,0:T(8,128)}, u32[]{:S(2)}) copy-start(f32[16,512]{1,0:T(8,128)} %res_ref.1) | copy-start | bytes 98308
  6.5 4.3 %collective-permute-start = (bf16[32,512]{1,0:T(8,128)(2,1)}, bf16[32,512]{1,0:T(8,128)(2,1)S(1)}, u32[]{:S(2)}, u32[]{:S(2)}) collective-permute-start(bf16[32,512]{1,0:T(8,128)(2,1)} %get-tuple-element.27), channel_id=1, source_target_pairs={{0,64},{16,80},{32,96},{48,112},{64,0},{80,16},{96,32},{112,48},{1... | collective-permute-start | bytes 98312 | tf_op jit(solution)/shard_map/ppermute | solution.py:213
  11.6 6.1 %collective-permute-start.1 = (bf16[2,32,512]{2,1,0:T(8,128)(2,1)S(1)}, bf16[2,32,512]{2,1,0:T(8,128)(2,1)S(1)}, u32[]{:S(2)}, u32[]{:S(2)}) collective-permute-start(bf16[2,32,512]{2,1,0:T(8,128)(2,1)S(1)} %pad_maximum_fusion.2.refs_0_), channel_id=1, source_target_pairs={{0,16},{16,32},{32,48},{48,0},{64,80},{80,96},{96,112},{112,64},{1... | collective-permute-start | bytes 196616 | tf_op jit(solution)/shard_map/ppermute | solution.py:213
  13.1 5.9 %collective-permute-start.2 = (bf16[2,32,512]{2,1,0:T(8,128)(2,1)S(1)}, bf16[2,32,512]{2,1,0:T(8,128)(2,1)S(1)}, u32[]{:S(2)}, u32[]{:S(2)}) collective-permute-start(bf16[2,32,512]{2,1,0:T(8,128)(2,1)S(1)} %pad_maximum_fusion.2.refs_0_), channel_id=1, source_target_pairs={{0,32},{16,48},{32,0},{48,16},{64,96},{80,112},{96,64},{112,80},{1... | collective-permute-start | bytes 196616 | tf_op jit(solution)/shard_map/ppermute | solution.py:213
  15.8 4.3 %collective-permute-start.3 = (bf16[2,32,512]{2,1,0:T(8,128)(2,1)S(1)}, bf16[2,32,512]{2,1,0:T(8,128)(2,1)S(1)}, u32[]{:S(2)}, u32[]{:S(2)}) collective-permute-start(bf16[2,32,512]{2,1,0:T(8,128)(2,1)S(1)} %pad_maximum_fusion.2.refs_0_), channel_id=1, source_target_pairs={{0,48},{16,0},{32,16},{48,32},{64,112},{80,64},{96,80},{112,96},{1... | collective-permute-start | bytes 196616 | tf_op jit(solution)/shard_map/ppermute | solution.py:213
  28.0 2.7 %collective-permute-start.4 = (bf16[1024,512]{1,0:T(8,128)(2,1)S(1)}, bf16[1024,512]{1,0:T(8,128)(2,1)S(1)}, u32[]{:S(2)}, u32[]{:S(2)}) collective-permute-start(bf16[1024,512]{1,0:T(8,128)(2,1)S(1)} %gated.1.g_ref), channel_id=1, source_target_pairs={{0,1},{1,0},{2,3},{3,2},{4,5},{5,4},{6,7},{7,6},{8,9},{9,8},{10,11... | collective-permute-start | bytes 3145736 | tf_op jit(solution)/shard_map/ppermute | solution.py:213
  34.3 18.8 %collective-permute-start.7 = (bf16[2,320,512]{2,1,0:T(8,128)(2,1)S(1)}, bf16[2,320,512]{2,1,0:T(8,128)(2,1)S(1)}, u32[]{:S(2)}, u32[]{:S(2)}) collective-permute-start(bf16[2,320,512]{2,1,0:T(8,128)(2,1)S(1)} %get-tuple-element.29), channel_id=1, source_target_pairs={{0,12},{1,13},{2,14},{3,15},{4,0},{5,1},{6,2},{7,3},{8,4},{9,5},{1... | collective-permute-start | bytes 1966088 | tf_op jit(solution)/shard_map/ppermute | solution.py:213
  37.3 18.8 %collective-permute-start.6 = (bf16[2,320,512]{2,1,0:T(8,128)(2,1)S(1)}, bf16[2,320,512]{2,1,0:T(8,128)(2,1)S(1)}, u32[]{:S(2)}, u32[]{:S(2)}) collective-permute-start(bf16[2,320,512]{2,1,0:T(8,128)(2,1)S(1)} %get-tuple-element.28), channel_id=1, source_target_pairs={{0,4},{1,5},{2,6},{3,7},{4,8},{5,9},{6,10},{7,11},{8,12},{9,13},{1... | collective-permute-start | bytes 1966088 | tf_op jit(solution)/shard_map/ppermute | solution.py:213
  41.5 39.1 %collective-permute-start.15 = (bf16[4,384,512]{2,1,0:T(8,128)(2,1)S(1)}, bf16[4,384,512]{2,1,0:T(8,128)(2,1)S(1)}, u32[]{:S(2)}, u32[]{:S(2)}) collective-permute-start(bf16[4,384,512]{2,1,0:T(8,128)(2,1)S(1)} %project.9), channel_id=1, source_target_pairs={{0,2},{1,3},{2,0},{3,1},{4,6},{5,7},{6,4},{7,5},{8,10},{9,11},{10,... | collective-permute-start | bytes 4718600 | tf_op jit(solution)/shard_map/ppermute | solution.py:213
  49.7 13.5 %collective-permute-start.10 = (bf16[320,512]{1,0:T(8,128)(2,1)S(1)}, bf16[320,512]{1,0:T(8,128)(2,1)S(1)}, u32[]{:S(2)}, u32[]{:S(2)}) collective-permute-start(bf16[320,512]{1,0:T(8,128)(2,1)S(1)} %bitcast.43), channel_id=1, source_target_pairs={{0,4},{1,5},{2,6},{3,7},{4,8},{5,9},{6,10},{7,11},{8,12},{9,13},{1... | collective-permute-start | bytes 983048 | tf_op jit(solution)/shard_map/ppermute | solution.py:213
  50.4 12.8 %collective-permute-start.11 = (bf16[320,512]{1,0:T(8,128)(2,1)S(1)}, bf16[320,512]{1,0:T(8,128)(2,1)S(1)}, u32[]{:S(2)}, u32[]{:S(2)}) collective-permute-start(bf16[320,512]{1,0:T(8,128)(2,1)S(1)} %bitcast.42), channel_id=1, source_target_pairs={{0,12},{1,13},{2,14},{3,15},{4,0},{5,1},{6,2},{7,3},{8,4},{9,5},{1... | collective-permute-start | bytes 983048 | tf_op jit(solution)/shard_map/ppermute | solution.py:213
  53.2 17.4 %collective-permute-start.13 = (bf16[320,512]{1,0:T(8,128)(2,1)S(1)}, bf16[320,512]{1,0:T(8,128)(2,1)S(1)}, u32[]{:S(2)}, u32[]{:S(2)}) collective-permute-start(bf16[320,512]{1,0:T(8,128)(2,1)S(1)} %fusion.9), channel_id=1, source_target_pairs={{0,12},{1,13},{2,14},{3,15},{4,0},{5,1},{6,2},{7,3},{8,4},{9,5},{1... | collective-permute-start | bytes 983048 | tf_op jit(solution)/shard_map/ppermute | solution.py:213
  56.3 14.3 %collective-permute-start.12 = (bf16[320,512]{1,0:T(8,128)(2,1)S(1)}, bf16[320,512]{1,0:T(8,128)(2,1)S(1)}, u32[]{:S(2)}, u32[]{:S(2)}) collective-permute-start(bf16[320,512]{1,0:T(8,128)(2,1)S(1)} %fusion.8), channel_id=1, source_target_pairs={{0,4},{1,5},{2,6},{3,7},{4,8},{5,9},{6,10},{7,11},{8,12},{9,13},{1... | collective-permute-start | bytes 983048 | tf_op jit(solution)/shard_map/ppermute | solution.py:213
  63.2 28.2 %collective-permute-start.8 = (bf16[2,320,512]{2,1,0:T(8,128)(2,1)S(1)}, bf16[2,320,512]{2,1,0:T(8,128)(2,1)S(1)}, u32[]{:S(2)}, u32[]{:S(2)}) collective-permute-start(bf16[2,320,512]{2,1,0:T(8,128)(2,1)S(1)} %get-tuple-element.31), channel_id=1, source_target_pairs={{0,4},{1,5},{2,6},{3,7},{4,8},{5,9},{6,10},{7,11},{8,12},{9,13},{1... | collective-permute-start | bytes 1966088 | tf_op jit(solution)/shard_map/ppermute | solution.py:213
  63.2 28.2 %collective-permute-start.9 = (bf16[2,320,512]{2,1,0:T(8,128)(2,1)S(1)}, bf16[2,320,512]{2,1,0:T(8,128)(2,1)S(1)}, u32[]{:S(2)}, u32[]{:S(2)}) collective-permute-start(bf16[2,320,512]{2,1,0:T(8,128)(2,1)S(1)} %get-tuple-element.32), channel_id=1, source_target_pairs={{0,12},{1,13},{2,14},{3,15},{4,0},{5,1},{6,2},{7,3},{8,4},{9,5},{1... | collective-permute-start | bytes 1966088 | tf_op jit(solution)/shard_map/ppermute | solution.py:213
  70.9 22.9 %collective-permute-start.14 = (bf16[2,320,512]{2,1,0:T(8,128)(2,1)S(1)}, bf16[2,320,512]{2,1,0:T(8,128)(2,1)S(1)}, u32[]{:S(2)}, u32[]{:S(2)}) collective-permute-start(bf16[2,320,512]{2,1,0:T(8,128)(2,1)S(1)} %pad_maximum_fusion.1), channel_id=1, source_target_pairs={{0,2},{1,3},{2,0},{3,1},{4,6},{5,7},{6,4},{7,5},{8,10},{9,11},{10,... | collective-permute-start | bytes 1966088 | tf_op jit(solution)/shard_map/ppermute | solution.py:213
  80.7 7.0 %collective-permute-start.16 = (bf16[192,512]{1,0:T(8,128)(2,1)S(1)}, bf16[192,512]{1,0:T(8,128)(2,1)S(1)}, u32[]{:S(2)}, u32[]{:S(2)}) collective-permute-start(bf16[192,512]{1,0:T(8,128)(2,1)S(1)} %get-tuple-element.49), channel_id=1, source_target_pairs={{0,4},{1,5},{2,6},{3,7},{4,8},{5,9},{6,10},{7,11},{8,12},{9,13},{1... | collective-permute-start | bytes 589832 | tf_op jit(solution)/shard_map/ppermute | solution.py:213
  81.4 6.3 %collective-permute-start.18 = (bf16[192,512]{1,0:T(8,128)(2,1)S(1)}, bf16[192,512]{1,0:T(8,128)(2,1)S(1)}, u32[]{:S(2)}, u32[]{:S(2)}) collective-permute-start(bf16[192,512]{1,0:T(8,128)(2,1)S(1)} %get-tuple-element.50), channel_id=1, source_target_pairs={{0,12},{1,13},{2,14},{3,15},{4,0},{5,1},{6,2},{7,3},{8,4},{9,5},{1... | collective-permute-start | bytes 589832 | tf_op jit(solution)/shard_map/ppermute | solution.py:213
  88.0 10.0 %collective-permute-start.17 = (bf16[384,512]{1,0:T(8,128)(2,1)S(1)}, bf16[384,512]{1,0:T(8,128)(2,1)S(1)}, u32[]{:S(2)}, u32[]{:S(2)}) collective-permute-start(bf16[384,512]{1,0:T(8,128)(2,1)S(1)} %get-tuple-element.47), channel_id=1, source_target_pairs={{0,4},{1,5},{2,6},{3,7},{4,8},{5,9},{6,10},{7,11},{8,12},{9,13},{1... | collective-permute-start | bytes 1179656 | tf_op jit(solution)/shard_map/ppermute | solution.py:213
  89.5 8.5 %collective-permute-start.19 = (bf16[384,512]{1,0:T(8,128)(2,1)S(1)}, bf16[384,512]{1,0:T(8,128)(2,1)S(1)}, u32[]{:S(2)}, u32[]{:S(2)}) collective-permute-start(bf16[384,512]{1,0:T(8,128)(2,1)S(1)} %get-tuple-element.48), channel_id=1, source_target_pairs={{0,12},{1,13},{2,14},{3,15},{4,0},{5,1},{6,2},{7,3},{8,4},{9,5},{1... | collective-permute-start | bytes 1179656 | tf_op jit(solution)/shard_map/ppermute | solution.py:213
